TPU v7x, 32 devices: a whole 2x2x4 slice. The times are simulated.
32 devices in a mesh: blk: 4 (over z), grp: 8 (over y, x, core).
Axes of the slice: x: 2, y: 2, z: 4, core: 2. Of those that a mesh axis runs over, the one named last changes fastest.
Arguments:
- basis: bfloat16 [8, 512, 1152], P('grp', 'blk'), may hold values from -6 to 6
- coeffs: bfloat16 [2, 1152, 768], replicated, may hold values from -0.1875 to 0.1875
- stiff_blocks: bfloat16 [8, 4, 4, 128, 128], P('grp', 'blk'), as said below
- mass_blocks: bfloat16 [8, 4, 4, 128, 128], P('grp', 'blk'), as said below
- block_cols: int32 [8, 4, 4], P('grp', 'blk'), may hold values from 0 to 3
Outputs:
- basis_out: bfloat16 [8, 512, 1152], P('grp', 'blk')
- ritz_value: float32 [384], replicated
- gram: float32 [1152, 2, 1152], P('grp', None, 'blk')
Inputs may be any that keep to these rules, and one draw needn't show every extreme that they name: block_cols names row blocks of the same substructure. `mass_blocks`: real-valued blocks of order 1 / sqrt(512). `stiff_blocks`: real-valued blocks, of larger size than the mass blocks.
All inputs are finite; a program needn't handle non-finite values.
Results may differ from a plain program's by a relative error of at most 0.02.
Values may be sent and summed in bfloat16 or wider, within the bound.
No kernel may reach another device: no remote copies, remote signals or barrier semaphores. Data moves between devices by JAX's collectives and lax.ppermute only.
A program may use at most 64 MiB of HBM per device.

v0:
```python
import jax
import jax.numpy as jnp
from jax import lax
from jax.sharding import PartitionSpec as P

epsilon = 1e-06


def apply_pair(stiff, mass, cols, field, final):
    columns = field.shape[1]
    block_rows, slots = cols.shape
    edge = stiff.shape[-1]
    own_blocks = field.reshape(block_rows, edge, columns)
    wanted = cols.reshape(-1)

    def take_blocks(arrived):
        arrived_count = arrived.shape[0]
        ident = jnp.arange(arrived_count, dtype=jnp.int32)
        selector = (wanted[:, None] == ident[None, :]).astype(jnp.bfloat16)
        taken = jnp.dot(
            selector, arrived.reshape(arrived_count, -1), preferred_element_type=jnp.float32
        )
        return taken.astype(jnp.bfloat16)

    if final:
        gathered = take_blocks(lax.all_gather(own_blocks, "blk", axis=0, tiled=True))
    else:
        gathered = take_blocks(lax.all_gather(own_blocks, "blk", axis=0, tiled=True))
    gathered = gathered.reshape(block_rows, slots, edge, columns)
    contract = (((1, 3), (1, 2)), ((0,), (0,)))
    stiff_out = lax.dot_general(stiff, gathered, contract, preferred_element_type=jnp.float32)
    mass_out = lax.dot_general(mass, gathered, contract, preferred_element_type=jnp.float32)
    return (
        stiff_out.reshape(block_rows * edge, columns),
        mass_out.reshape(block_rows * edge, columns),
    )


def body(basis, coeffs, stiff_blocks, mass_blocks, block_cols):
    stiff = stiff_blocks[0]
    mass = mass_blocks[0]
    cols = block_cols[0]
    current = basis[0]
    rows_here, columns = current.shape
    mode_count = columns // 3
    total_rows = rows_here * lax.axis_size("blk") * lax.axis_size("grp")
    for sweep in range(coeffs.shape[0]):
        turned = jnp.dot(current, coeffs[sweep], preferred_element_type=jnp.float32).astype(
            jnp.bfloat16
        )
        next_modes = turned[:, :mode_count]
        next_history = turned[:, mode_count:]
        stiff_x, mass_x = apply_pair(stiff, mass, cols, next_modes, False)
        numerator, denominator = lax.psum(
            (jnp.sum(stiff_x * mass_x, axis=0), jnp.sum(mass_x * mass_x, axis=0)), ("blk", "grp")
        )
        ritz_value = numerator / (denominator + epsilon)
        residual = stiff_x - ritz_value * mass_x
        resid_sum = lax.psum(jnp.sum(residual * residual, axis=0), ("blk", "grp"))
        next_search = (residual * lax.rsqrt(resid_sum / total_rows + epsilon)).astype(jnp.bfloat16)
        current = jnp.concatenate([next_modes, next_search, next_history], axis=1)
    stiff_rest, mass_rest = apply_pair(stiff, mass, cols, current[:, mode_count:], True)
    stiff_all = jnp.concatenate(
        [stiff_x.astype(jnp.bfloat16), stiff_rest.astype(jnp.bfloat16)], axis=1
    )
    mass_all = jnp.concatenate(
        [mass_x.astype(jnp.bfloat16), mass_rest.astype(jnp.bfloat16)], axis=1
    )
    inner = (((0,), (0,)), ((), ()))
    gram_stiff = lax.dot_general(current, stiff_all, inner, preferred_element_type=jnp.float32)
    gram_mass = lax.dot_general(current, mass_all, inner, preferred_element_type=jnp.float32)
    by_group = lax.psum_scatter(
        jnp.stack([gram_stiff, gram_mass], axis=1).astype(jnp.bfloat16),
        "grp",
        scatter_dimension=0,
        tiled=True,
    )
    gram = lax.psum_scatter(by_group, "blk", scatter_dimension=2, tiled=True).astype(jnp.float32)
    return (current[None], ritz_value, gram)


def solution(mesh):
    in_specs = (
        P("grp", "blk", None),
        P(),
        P("grp", "blk", None, None, None),
        P("grp", "blk", None, None, None),
        P("grp", "blk", None),
    )
    out_specs = (P("grp", "blk", None), P(), P("grp", None, "blk"))
    return jax.shard_map(body, mesh=mesh, in_specs=in_specs, out_specs=out_specs, check_vma=False)
```

profile of v0, /device:TPU:0, one launch (start us, length us, event | category | flops | bytes accessed | tf_op | source)
XLA Modules:
  0.0 328.8 jit_solution(17541428477707894250)
XLA Ops:
  7.2 0.0 copy-start
  7.2 0.0 copy-start.4
  7.2 0.0 copy-start.2
  7.2 0.0 copy-start.1
  7.2 0.0 reduce-scatter.5.cloned.1.call-start
  7.3 0.9 copy-done
  8.1 1.9 fusion.8
  10.1 16.2 %all-gather = bf16[512,384]{1,0:T(8,128)(2,1)S(1)} all-gather(bf16[128,384]{1,0:T(8,128)(2,1)S(1)} %get-tuple-element.22), channel_id=2, replica_groups=mesh['blk'=4,'grp'=8] {'blk'}, dimensions={0}, use_global_device_ids=true | all-gather | bytes 491520 | tf_op jit(solution)/shard_map/all_gather | solution.py:28
  26.3 0.1 reshape.85
  26.5 0.0 copy-done.4
  26.5 0.4 convolution_convert_fusion.2
  26.9 0.0 copy-done.2
  26.9 0.2 convolution_bitcast_fusion.5
  27.1 0.0 copy-done.1
  27.2 0.2 multiply_reduce_fusion.4
  27.4 40.9 %all-reduce.1 = (f32[384]{0:T(512)S(1)}, f32[384]{0:T(512)S(1)}) all-reduce(f32[384]{0:T(512)S(1)} %get-tuple-element.12, f32[384]{0:T(512)S(1)} %get-tuple-element.11), channel_id=1, replica_groups=mesh['blk'=4,'grp'=8] {'blk','grp'}, use_global_device_ids=true, to_apply=%region_1.0 | all-reduce | flops 768 | bytes 6144 | tf_op jit(solution)/shard_map/psum | solution.py:54
  68.3 0.1 multiply_reduce_fusion.3
  68.3 40.3 %psum.44 = f32[384]{0:T(512)S(1)} all-reduce(f32[384]{0:T(512)S(1)} %multiply_reduce_fusion.3), channel_id=1, replica_groups=mesh['blk'=4,'grp'=8] {'blk','grp'}, use_global_device_ids=true, to_apply=%region_5.0 | all-reduce | flops 384 | bytes 3072 | tf_op jit(solution)/shard_map/psum | solution.py:59
  108.7 1.9 fusion.11
  110.6 14.9 %all-gather.1 = bf16[512,384]{1,0:T(8,128)(2,1)S(1)} all-gather(bf16[128,384]{1,0:T(8,128)(2,1)S(1)} %get-tuple-element.20), channel_id=3, replica_groups=mesh['blk'=4,'grp'=8] {'blk'}, dimensions={0}, use_global_device_ids=true | all-gather | bytes 491520 | tf_op jit(solution)/shard_map/all_gather | solution.py:28
  125.6 0.1 reshape.90
  125.7 0.4 convolution_convert_fusion.1
  126.1 0.2 convolution_bitcast_fusion.3
  126.4 0.2 multiply_reduce_fusion.1
  126.6 39.9 %all-reduce = (f32[384]{0:T(512)S(1)}, f32[384]{0:T(512)S(1)}) all-reduce(f32[384]{0:T(512)S(1)} %get-tuple-element.10, f32[384]{0:T(512)S(1)} %get-tuple-element.9), channel_id=1, replica_groups=mesh['blk'=4,'grp'=8] {'blk','grp'}, use_global_device_ids=true, to_apply=%region_7.0 | all-reduce | flops 768 | bytes 6144 | tf_op jit(solution)/shard_map/psum | solution.py:54
  166.5 0.0 copy-start.3
  166.5 0.1 multiply_reduce_fusion
  166.5 40.4 %psum.47 = f32[384]{0:T(512)S(1)} all-reduce(f32[384]{0:T(512)S(1)} %multiply_reduce_fusion), channel_id=1, replica_groups=mesh['blk'=4,'grp'=8] {'blk','grp'}, use_global_device_ids=true, to_apply=%region_11.0 | all-reduce | flops 384 | bytes 3072 | tf_op jit(solution)/shard_map/psum | solution.py:59
  206.9 0.1 fusion.55
  207.0 18.3 %all-gather.2 = bf16[512,768]{1,0:T(8,128)(2,1)S(1)} all-gather(bf16[128,768]{1,0:T(8,128)(2,1)S(1)} %pad_maximum_fusion.2), channel_id=4, replica_groups=mesh['blk'=4,'grp'=8] {'blk'}, dimensions={0}, use_global_device_ids=true | all-gather | bytes 983040 | tf_op jit(solution)/shard_map/all_gather | solution.py:26
  225.3 0.6 reshape.93
  225.9 0.6 convolution_convert_fusion
  226.5 0.0 copy-done.3
  226.5 0.4 fusion.16
  226.9 0.4 fusion.17
  227.4 0.1 copy.19
  227.5 0.1 copy.20
  227.6 0.9 fusion
  228.5 0.9 fusion.1
  229.4 2.8 pad_maximum_fusion
  232.2 0.0 reduce-scatter.5.cloned.1.call-update
  232.3 0.0 reduce-scatter.7.cloned.1.call-start
  232.3 57.6 %reduce-scatter.5.cloned.1.call-done = bf16[144,2,1152]{2,0,1:T(8,128)(2,1)} async-done(((bf16[1152,2,1152]{2,0,1:T(8,128)(2,1)}), bf16[144,2,1152]{2,0,1:T(8,128)(2,1)}) %reduce-scatter.5.cloned.1.call-update) | async-done | bytes 663568 | tf_op jit(solution)/shard_map/reduce_scatter | solution.py:72
  289.9 3.5 %copy.28 = bf16[144,2,1152]{0,1,2:T(2,128)(2,1)S(1)} copy(bf16[144,2,1152]{2,0,1:T(8,128)(2,1)} %reduce-scatter.5.cloned.1.call-done) | data formatting | bytes 1327104
  293.4 1.5 reshape.107
  294.9 0.0 reduce-scatter.7.cloned.1.call-update
  295.0 0.7 fusion.54
  295.7 24.0 %reduce-scatter.7.cloned.1.call-done = bf16[288,288]{1,0:T(8,128)(2,1)} async-done(((bf16[1152,288]{1,0:T(8,128)(2,1)}), bf16[288,288]{1,0:T(8,128)(2,1)}) %reduce-scatter.7.cloned.1.call-update) | async-done | bytes 165904
  319.7 1.1 reshape.108
  320.8 0.2 copy.29
  321.0 0.9 copy.21
  (8 shorter events, 0.1 us)
Async XLA Ops:
  7.2 1.0 copy-start
  7.2 19.3 %copy-start.4 = (s32[1,1,4]{2,1,0:T(1,128)S(1)}, s32[1,1,4]{2,1,0:T(1,128)}, u32[]{:S(2)}) copy-start(s32[1,1,4]{2,1,0:T(1,128)} %param.9) | copy-start | bytes 52
  7.2 19.7 %copy-start.2 = (bf16[1,1,4,128,128]{4,3,2,1,0:T(8,128)(2,1)S(1)}, bf16[1,1,4,128,128]{4,3,2,1,0:T(8,128)(2,1)}, u32[]{:S(2)}) copy-start(bf16[1,1,4,128,128]{4,3,2,1,0:T(8,128)(2,1)} %param.7) | copy-start | bytes 393220
  7.2 19.9 %copy-start.1 = (bf16[1,1,4,128,128]{4,3,2,1,0:T(8,128)(2,1)S(1)}, bf16[1,1,4,128,128]{4,3,2,1,0:T(8,128)(2,1)}, u32[]{:S(2)}) copy-start(bf16[1,1,4,128,128]{4,3,2,1,0:T(8,128)(2,1)} %param.8) | copy-start | bytes 393220
  7.2 282.7 %reduce-scatter.5.cloned.1.call-start = ((), (), s32[]{:S(2)}) async-start(), calls=%async_computation.2 | async-start | bytes 5971968 | tf_op jit(solution)/shard_map/reduce_scatter | solution.py:72
  166.5 60.0 %copy-start.3 = (f32[384]{0:T(512)}, f32[384]{0:T(512)S(1)}, u32[]{:S(2)}) copy-start(f32[384]{0:T(512)S(1)} %add_divide_fusion) | copy-start | bytes 4612
  232.3 87.4 %reduce-scatter.7.cloned.1.call-start = ((), (), s32[]{:S(2)}) async-start(), calls=%async_computation.3 | async-start | bytes 1105920
Sparse Core Ops, SparseCore 0:
  232.4 57.4 reduce-scatter.4
  295.1 24.5 reduce-scatter.6
where the time goes:
time: 330 us; the launch traced here: 329 us
  blocking collectives  211 us (64%)
  waiting for transfers between devices  81.6 us (25%)
  between operations  14.3 us (4%)
  local copies, waits for them, and re-layouts  9.36 us (3%)
  matrix products  8.84 us (3%)
  other arithmetic  3.82 us (1%)
    psum x2, blocking collectives, body(): lax.psum((jnp.sum(stiff_x * mass_x, axis=0), jnp.sum(mass_x * mass_x, axi...  80.8 us
    psum x2, blocking collectives, body(): resid_sum = lax.psum(jnp.sum(residual * residual, axis=0), ('blk', 'grp'))  80.7 us
    reduce_scatter x1, waiting for transfers between devices, body(): lax.psum_scatter(jnp.stack([gram_stiff, gram_mass], axis=1).astype(jnp.bf...  57.6 us
    all_gather x3, blocking collectives, apply_pair(): lax.all_gather(own_blocks, 'blk', axis=0, tiled=True)  49.4 us
    unnamed x3, waiting for transfers between devices  24 us
    unnamed x15, local copies, waits for them, and re-layouts  8.2 us
  transfers between devices with their start and end apart: 2, of which 2 were waited for; matrix products, arithmetic and copies ran while one was open for 0% of the time, Pallas kernels for 0%

commit v1 on v0

v1 whole, which is shorter than its diff:
```python
import functools

import jax
import jax.numpy as jnp
from jax import lax
from jax.experimental import pallas as pl
from jax.experimental.pallas import tpu as pltpu
from jax.sharding import PartitionSpec as P

epsilon = 1e-06
tiny = 1e-30
f32 = jnp.float32
bf16 = jnp.bfloat16
VMEM_BYTES = 56 * 1024 * 1024


def vmem():
    return pl.BlockSpec(memory_space=pltpu.VMEM)


def smem():
    return pl.BlockSpec(memory_space=pltpu.SMEM)


def block_dot(pieces_k, slots, edge, cols, k, field, lanes):
    half = slots * edge
    top = jnp.concatenate([pieces_k[s * edge : (s + 1) * edge, :] for s in range(slots)], axis=1)
    low = jnp.concatenate(
        [pieces_k[half + s * edge : half + (s + 1) * edge, :] for s in range(slots)], axis=1
    )
    rows = [
        field[pl.ds(pl.multiple_of(cols[k, s] * edge, edge), edge), lanes] for s in range(slots)
    ]
    return jnp.dot(
        jnp.concatenate([top, low], axis=0),
        jnp.concatenate(rows, axis=0),
        preferred_element_type=f32,
    )


def column_stats(stiff_x, mass_x):
    num = jnp.sum(stiff_x * mass_x, axis=0, keepdims=True)
    den = jnp.sum(mass_x * mass_x, axis=0, keepdims=True)
    rest = stiff_x - (num / jnp.maximum(den, tiny)) * mass_x
    return num, den, jnp.sum(rest * rest, axis=0, keepdims=True)


def shift_and_scale(stats, total_rows):
    num, den, about = stats[0:1, :], stats[1:2, :], stats[2:3, :]
    shift = num / (den + epsilon)
    off = shift - num / jnp.maximum(den, tiny)
    scale = lax.rsqrt((about + off * off * den) / total_rows + epsilon)
    return shift, scale


def stats_kernel(nz, slots, edge, modes, rows_of, meta, cols, *refs):
    x_refs, km_refs = refs[:nz], refs[nz : nz + rows_of]
    stats_ref, field, stiff, mass = refs[nz + rows_of :]
    z = meta[0]
    for k in range(nz):
        field[pl.ds(pl.multiple_of((z ^ k) * edge, edge), edge), :] = x_refs[k][...]
    for k in range(rows_of):
        both = block_dot(km_refs[k], slots, edge, cols, k, field, slice(None))
        at = pl.ds(pl.multiple_of((z ^ k) * edge, edge), edge) if rows_of > 1 else slice(None)
        stiff[at, :] = both[:edge]
        mass[at, :] = both[edge:]
    num, den, about = column_stats(stiff[...], mass[...])
    stats_ref[0:1, :] = num
    stats_ref[1:2, :] = den
    stats_ref[2:3, :] = about


def sweep_kernel(nz, slots, edge, modes, total_rows, meta, cols, *refs):
    x_refs, h_refs, km_refs = refs[:nz], refs[nz : 2 * nz], refs[2 * nz : 3 * nz]
    stats, coeffs, turned_ref, stiff_ref, mass_ref, stats_ref, full = refs[3 * nz :]
    z = meta[0]
    at = [pl.ds(pl.multiple_of((z ^ k) * edge, edge), edge) for k in range(nz)]
    for k in range(nz):
        full[at[k], 0:modes] = x_refs[k][...]
        full[at[k], 2 * modes : 3 * modes] = h_refs[k][...]
    shift, scale = shift_and_scale(stats, total_rows)
    for k in range(nz):
        both = block_dot(km_refs[k], slots, edge, cols, k, full, slice(0, modes))
        full[at[k], modes : 2 * modes] = ((both[:edge] - shift * both[edge:]) * scale).astype(bf16)
    turned_ref[...] = jnp.dot(full[...], coeffs[...], preferred_element_type=f32).astype(bf16)
    for k in range(nz):
        both = block_dot(km_refs[k], slots, edge, cols, k, turned_ref, slice(0, modes))
        stiff_ref[at[k], :] = both[:edge]
        mass_ref[at[k], :] = both[edge:]
    num, den, about = column_stats(stiff_ref[...], mass_ref[...])
    stats_ref[0:1, :] = num
    stats_ref[1:2, :] = den
    stats_ref[2:3, :] = about


def gram_kernel(nz, ng, slots, edge, modes, total_rows, split, meta, cols, *refs):
    km_refs = refs[:nz]
    turned, stiff, mass, stats, basis_ref, ritz_ref, gram_ref, full, chosen, applied = refs[nz:]
    z, core, chip = meta[0], meta[1], meta[2]
    at = [pl.ds(pl.multiple_of((z ^ k) * edge, edge), edge) for k in range(nz)]
    width = 3 * modes // nz
    shift, scale = shift_and_scale(stats, total_rows)
    ritz_ref[...] = shift
    full[:, 0:modes] = turned[:, 0:modes]
    full[:, modes : 2 * modes] = ((stiff[...] - shift * mass[...]) * scale).astype(bf16)
    full[:, 2 * modes : 3 * modes] = turned[:, modes : 2 * modes]
    basis_ref[...] = full[at[0], :]
    window = chosen.shape[1]
    start = z * width // 128 * 128
    picked = full[:, pl.ds(pl.multiple_of(start, 128), window)].astype(f32)
    chosen[...] = pltpu.roll(picked, window - (z * width - start), 1).astype(bf16)
    for k in range(nz):
        both = block_dot(km_refs[k], slots, edge, cols, k, chosen, slice(0, width)).astype(bf16)
        applied[at[k], 0:width] = both[:edge]
        applied[at[k], width : 2 * width] = both[edge:]
    gram = lax.dot_general(
        full[...], applied[...], (((0,), (0,)), ((), ())), preferred_element_type=f32
    ).astype(bf16)
    if split:
        rows = 3 * modes // ng
        for q in range(ng):
            gram_ref[(q % 2) ^ core, (q // 2) ^ chip] = gram[q * rows : (q + 1) * rows]
    else:
        gram_ref[...] = gram


def call(kernel, inputs, n_smem, out_shape, scratch, flops):
    return pl.pallas_call(
        kernel,
        out_shape=out_shape,
        in_specs=[smem()] * n_smem + [vmem()] * (len(inputs) - n_smem),
        out_specs=jax.tree.map(lambda _: vmem(), out_shape),
        scratch_shapes=scratch,
        compiler_params=pltpu.CompilerParams(vmem_limit_bytes=VMEM_BYTES),
        cost_estimate=pl.CostEstimate(flops=flops, bytes_accessed=4_000_000, transcendentals=0),
    )(*inputs)


def by_xor(size, k):
    return [(i, i ^ k) for i in range(size)]


def merge(one, two):
    num, den = one[0] + two[0], one[1] + two[1]
    apart = one[0] / jnp.maximum(one[1], tiny) - two[0] / jnp.maximum(two[1], tiny)
    weight = jnp.sqrt(one[1]) * jnp.sqrt(two[1]) * lax.rsqrt(jnp.maximum(den, tiny))
    gap = apart * weight
    return jnp.stack([num, den, (one[2] + two[2]) + gap * gap])


def merge_over(axis, size, stats):
    step = 1
    if axis == "grp" and size >= 8:
        stats = merge(stats, lax.ppermute(stats, axis, by_xor(size, 1)))
        step = 2
        if size == 8:
            got = [lax.ppermute(stats, axis, by_xor(size, 2 * k)) for k in (1, 2, 3)]
            return merge(merge(stats, got[0]), merge(got[1], got[2]))
    while step < size:
        stats = merge(stats, lax.ppermute(stats, axis, by_xor(size, step)))
        step *= 2
    return stats


def gather(x, nz):
    return [x] + [lax.ppermute(x, "blk", by_xor(nz, k)) for k in range(1, nz)]


def body(basis, coeffs, stiff_blocks, mass_blocks, block_cols):
    nz, ng = lax.axis_size("blk"), lax.axis_size("grp")
    z, g = lax.axis_index("blk"), lax.axis_index("grp")
    current = basis[0]
    edge, columns = current.shape
    slots = block_cols.shape[-1]
    modes = columns // 3
    rows = edge * nz
    total_rows = rows * ng
    width = columns // nz

    tag = jnp.pad(block_cols[0, 0].astype(bf16)[None, :], ((0, 15), (0, edge - slots)))
    payload = jnp.concatenate(
        [
            stiff_blocks[0, 0].reshape(slots * edge, edge),
            mass_blocks[0, 0].reshape(slots * edge, edge),
            tag,
        ],
        axis=0,
    )
    first = jnp.dot(current, coeffs[0][:, :modes], preferred_element_type=f32).astype(bf16)
    x_parts = gather(first, nz)
    km_parts = gather(payload, nz)
    later = jnp.dot(current, coeffs[0][:, modes:], preferred_element_type=f32).astype(bf16)
    h_parts = gather(later, nz)

    meta = jnp.stack([z, g % 2, g // 2]).astype(jnp.int32)
    own_cols = block_cols[0]
    stats = call(
        functools.partial(stats_kernel, nz, slots, edge, modes, 1),
        [meta, own_cols, *x_parts, payload],
        2,
        jax.ShapeDtypeStruct((3, modes), f32),
        [
            pltpu.VMEM((rows, modes), bf16),
            pltpu.VMEM((edge, modes), f32),
            pltpu.VMEM((edge, modes), f32),
        ],
        4 * edge * slots * edge * modes,
    )
    stats = merge_over("blk", nz, stats)
    stats = merge_over("grp", ng, stats)

    cols = jnp.stack([p[2 * slots * edge, :slots] for p in km_parts]).astype(jnp.int32)
    turned, stiff_x, mass_x, stats = call(
        functools.partial(sweep_kernel, nz, slots, edge, modes, total_rows),
        [meta, cols, *x_parts, *h_parts, *km_parts, stats, coeffs[1]],
        2,
        (
            jax.ShapeDtypeStruct((rows, 2 * modes), bf16),
            jax.ShapeDtypeStruct((rows, modes), f32),
            jax.ShapeDtypeStruct((rows, modes), f32),
            jax.ShapeDtypeStruct((3, modes), f32),
        ),
        [pltpu.VMEM((rows, columns), bf16)],
        2 * rows * columns * 2 * modes,
    )
    stats = merge_over("grp", ng, stats)

    split = (columns // ng) % 16 == 0
    chips = ng // 2
    block = columns // ng
    gram_shape = (2, chips, block, 2 * width) if split else (columns, 2 * width)
    window = -(-(width + max(i * width % 128 for i in range(nz))) // 128) * 128
    basis_out, ritz, gram = call(
        functools.partial(gram_kernel, nz, ng, slots, edge, modes, total_rows, split),
        [meta, cols, *km_parts, turned, stiff_x, mass_x, stats],
        2,
        (
            jax.ShapeDtypeStruct((edge, columns), bf16),
            jax.ShapeDtypeStruct((1, modes), f32),
            jax.ShapeDtypeStruct(gram_shape, bf16),
        ),
        [
            pltpu.VMEM((rows, columns), bf16),
            pltpu.VMEM((rows, window), bf16),
            pltpu.VMEM((rows, 2 * width), bf16),
        ],
        2 * rows * columns * 2 * width,
    )
    if split:
        keep, send = gram[0], gram[1]
        got = lax.ppermute(send, "grp", by_xor(ng, 1))
        mine = (keep.astype(f32) + got.astype(f32)).astype(bf16)
        total = mine[0].astype(f32)
        for k in range(1, chips):
            total = total + lax.ppermute(mine[k], "grp", by_xor(ng, 2 * k)).astype(f32)
    else:
        total = lax.psum_scatter(gram, "grp", scatter_dimension=0, tiled=True).astype(f32)
    return (basis_out[None], ritz[0], total.reshape(block, 2, width))


def solution(mesh):
    in_specs = (
        P("grp", "blk", None),
        P(),
        P("grp", "blk", None, None, None),
        P("grp", "blk", None, None, None),
        P("grp", "blk", None),
    )
    out_specs = (P("grp", "blk", None), P(), P("grp", None, "blk"))
    return jax.shard_map(body, mesh=mesh, in_specs=in_specs, out_specs=out_specs, check_vma=False)
```

time: 330 us -> 106 us (0.32)
  blocking collectives: 211 us -> 0 us
  waiting for transfers between devices: 81.6 us -> 41.9 us
  starting transfers between devices: 0.08 us -> 34.2 us
  Pallas kernels: 0 us -> 14.8 us
  between operations: 14.3 us -> 0.9 us
  matrix products: 8.84 us -> 0.62 us
    psum x4 -> x0, blocking collectives: 161 us -> none  [the longest x2 80.8 us: body(): lax.psum((jnp.sum(stiff_x * mass_x, axis=0), jnp.sum(mass_x * mass_x, axi...]
    reduce_scatter x1 -> x0, waiting for transfers between devices: 57.6 us -> none  [body(): lax.psum_scatter(jnp.stack([gram_stiff, gram_mass], axis=1).astype(jnp.bf...]
    all_gather x3 -> x0, blocking collectives: 49.4 us -> none  [apply_pair(): lax.all_gather(own_blocks, 'blk', axis=0, tiled=True)]
    ppermute x0 -> x23, waiting for transfers between devices: none -> 41.9 us  [the longest x9 18.7 us: gather(): return [x] + [lax.ppermute(x, 'blk', by_xor(nz, k)) for k in range(1, nz)]]
    ppermute x0 -> x23, starting transfers between devices: none -> 34.2 us  [the longest x9 21.8 us: gather(): return [x] + [lax.ppermute(x, 'blk', by_xor(nz, k)) for k in range(1, nz)]]
    unnamed x3 -> x0, waiting for transfers between devices: 24 us -> none
    pallas_call x0 -> x3, Pallas kernels: none -> 14.8 us  [call(): pl.pallas_call(kernel, out_shape=out_shape, in_specs=[smem()] * n_smem +...]
    dot_general x13 -> x2, matrix products: 8.84 us -> 0.62 us  [the longest x1 0.31 us: body(): jnp.dot(current, coeffs[0][:, :modes], preferred_element_type=f32)]
  transfers between devices with their start and end apart: 2 -> 23, of which waited for: 2 -> 15; matrix products, arithmetic and copies ran while one was open for 0% -> 3% of each run, Pallas kernels for 0% -> 0%
where the time goes in v1:
time: 106 us
  waiting for transfers between devices  41.9 us (40%)
  starting transfers between devices  34.2 us (32%)
  Pallas kernels  14.8 us (14%)
  local copies, waits for them, and re-layouts  7.32 us (7%)
  other arithmetic  5.95 us (6%)
    ppermute x9, starting transfers between devices, gather(): return [x] + [lax.ppermute(x, 'blk', by_xor(nz, k)) for k in range(1, nz)]  21.8 us
    ppermute x9, waiting for transfers between devices, gather(): return [x] + [lax.ppermute(x, 'blk', by_xor(nz, k)) for k in range(1, nz)]  18.7 us
    pallas_call x3, Pallas kernels, call(): pl.pallas_call(kernel, out_shape=out_shape, in_specs=[smem()] * n_smem +...  14.8 us
    ppermute x3, waiting for transfers between devices, body(): total = total + lax.ppermute(mine[k], 'grp', by_xor(ng, 2 * k)).astype(f32)  8.96 us
    ppermute x6, starting transfers between devices, merge_over(): got = [lax.ppermute(stats, axis, by_xor(size, 2 * k)) for k in (1, 2, 3)]  7.11 us
    ppermute x2, waiting for transfers between devices, merge_over(): stats = merge(stats, lax.ppermute(stats, axis, by_xor(size, step)))  6.83 us
    ppermute x6, waiting for transfers between devices, merge_over(): got = [lax.ppermute(stats, axis, by_xor(size, 2 * k)) for k in (1, 2, 3)]  3.81 us
    ppermute x3, starting transfers between devices, body(): total = total + lax.ppermute(mine[k], 'grp', by_xor(ng, 2 * k)).astype(f32)  3.55 us
  transfers between devices with their start and end apart: 23, of which 15 were waited for; matrix products, arithmetic and copies ran while one was open for 3% of the time, Pallas kernels for 0%

profile of v1, /device:TPU:0, one launch (start us, length us, event | category | flops | bytes accessed | tf_op | source)
XLA Modules:
  0.0 105.7 jit_solution(14637434309877049551)
XLA Ops:
  0.6 0.0 copy-start
  0.6 0.0 copy-start.17
  0.7 3.5 %slice_bitcast_fusion = (bf16[1152,768]{1,0:T(8,128)(2,1)}, bf16[1152,768]{1,0:T(8,128)(2,1)S(1)}) fusion(bf16[2,1152,768]{2,1,0:T(8,128)(2,1)} %param.6), kind=kLoop, calls=%fused_computation | loop fusion | bytes 7077888 | tf_op jit(solution)/shard_map/squeeze | solution.py:215
  4.2 0.3 convolution_convert_fusion.1.refs_0_
  4.5 0.0 copy-start.6
  4.6 5.1 %collective-permute-start.5 = (bf16[128,384]{1,0:T(8,128)(2,1)S(1)}, bf16[128,384]{1,0:T(8,128)(2,1)S(1)}, u32[]{:S(2)}, u32[]{:S(2)}) collective-permute-start(bf16[128,384]{1,0:T(8,128)(2,1)S(1)} %convolution_convert_fusion.1.refs_0_), channel_id=1, source_target_pairs={{0,24},{8,16},{16,8},{24,0},{1,25},{9,17},{17,9},{25,1},{2,26},{10... | collective-permute-start | bytes 294920 | tf_op jit(solution)/shard_map/ppermute | solution.py:166
  9.7 0.6 collective-permute-start.3
  10.3 0.7 fusion.8.refs_4_.refs_8_.refs_0_
  11.1 0.7 pad_add_fusion.meta
  11.7 1.6 %collective-permute-done.5.refs_3_ = bf16[128,384]{1,0:T(8,128)(2,1)S(1)} collective-permute-done((bf16[128,384]{1,0:T(8,128)(2,1)S(1)}, bf16[128,384]{1,0:T(8,128)(2,1)S(1)}, u32[]{:S(2)}, u32[]{:S(2)}) %collective-permute-start.5) | collective-permute-done | bytes 98336 | tf_op jit(solution)/shard_map/ppermute | solution.py:166
  13.4 4.6 %collective-permute-done.4.refs_2_ = bf16[128,384]{1,0:T(8,128)(2,1)S(1)} collective-permute-done((bf16[128,384]{1,0:T(8,128)(2,1)S(1)}, bf16[128,384]{1,0:T(8,128)(2,1)S(1)}, u32[]{:S(2)}, u32[]{:S(2)}) %collective-permute-start.4) | collective-permute-done | bytes 98336 | tf_op jit(solution)/shard_map/ppermute | solution.py:166
  18.0 0.6 copy-done.8
  18.6 0.0 copy-done.9
  18.6 2.1 %shard_map.76 = f32[3,384]{1,0:T(4,128)} custom-call(s32[3]{0:T(128)} %pad_add_fusion.meta, s32[1,4]{1,0:T(1,128)} %bitcast.35, bf16[128,384]{1,0:T(8,128)(2,1)} %copy-done.6, bf16[128,384]{1,0:T(8,128)(2,1)} %copy-done.9, bf16[128,384]{1,0:T(8,128)(2,1)} %copy-done.8, bf16[128,384]{1,0:T(8,128)(2,1)} %copy-done.7, ...), custom_call_target="tpu_custom_call" | custom-call | flops 100663296 | bytes 4000000 | tf_op jit(solution)/shard_map/pallas_call | solution.py:128
  20.8 0.5 collective-permute-start.9
  21.2 3.4 %collective-permute-done.9 = f32[3,384]{1,0:T(4,128)S(1)} collective-permute-done((f32[3,384]{1,0:T(4,128)}, f32[3,384]{1,0:T(4,128)S(1)}, u32[]{:S(2)}, u32[]{:S(2)}) %collective-permute-start.9) | collective-permute-done | bytes 4640 | tf_op jit(solution)/shard_map/ppermute | solution.py:160
  24.6 0.8 fusion.18
  25.4 1.1 %collective-permute-start.10 = (f32[3,384]{1,0:T(4,128)S(1)}, f32[3,384]{1,0:T(4,128)S(1)}, u32[]{:S(2)}, u32[]{:S(2)}) collective-permute-start(f32[3,384]{1,0:T(4,128)S(1)} %pad_maximum_fusion), channel_id=1, source_target_pairs={{0,16},{8,24},{16,0},{24,8},{1,17},{9,25},{17,1},{25,9},{2,18},{10... | collective-permute-start | bytes 13832 | tf_op jit(solution)/shard_map/ppermute | solution.py:160
  26.6 3.5 %collective-permute-done.10 = f32[3,384]{1,0:T(4,128)S(1)} collective-permute-done((f32[3,384]{1,0:T(4,128)S(1)}, f32[3,384]{1,0:T(4,128)S(1)}, u32[]{:S(2)}, u32[]{:S(2)}) %collective-permute-start.10) | collective-permute-done | bytes 4640 | tf_op jit(solution)/shard_map/ppermute | solution.py:160
  30.1 0.1 collective-permute-start.11
  30.2 2.6 %collective-permute-start.2 = (bf16[1040,128]{1,0:T(8,128)(2,1)}, bf16[1040,128]{1,0:T(8,128)(2,1)S(1)}, u32[]{:S(2)}, u32[]{:S(2)}) collective-permute-start(bf16[1040,128]{1,0:T(8,128)(2,1)} %fusion.8.refs_4_.refs_8_.refs_0_), channel_id=1, source_target_pairs={{0,24},{8,16},{16,8},{24,0},{1,25},{9,17},{17,9},{25,1},{2,26},{10... | collective-permute-start | bytes 798728 | tf_op jit(solution)/shard_map/ppermute | solution.py:166
  32.7 0.0 collective-permute-start.1
  32.8 2.5 %collective-permute-start.14 = (f32[3,384]{1,0:T(4,128)S(1)}, f32[3,384]{1,0:T(4,128)S(1)}, u32[]{:S(2)}, u32[]{:S(2)}) collective-permute-start(f32[3,384]{1,0:T(4,128)S(1)} %pad_maximum_fusion.2), channel_id=1, source_target_pairs={{0,6},{1,7},{2,4},{3,5},{4,2},{5,3},{6,0},{7,1},{8,14},{9,15},{10,... | collective-permute-start | bytes 13832 | tf_op jit(solution)/shard_map/ppermute | solution.py:157
  35.3 0.5 collective-permute-start.13
  35.8 0.5 collective-permute-start.12
  36.3 0.3 convolution_convert_fusion.refs_4_
  36.7 0.7 collective-permute-done.14
  37.4 1.9 %collective-permute-start = (bf16[1040,128]{1,0:T(8,128)(2,1)S(1)}, bf16[1040,128]{1,0:T(8,128)(2,1)S(1)}, u32[]{:S(2)}, u32[]{:S(2)}) collective-permute-start(bf16[1040,128]{1,0:T(8,128)(2,1)S(1)} %copy-done.1), channel_id=1, source_target_pairs={{0,8},{8,0},{16,24},{24,16},{1,9},{9,1},{17,25},{25,17},{2,10},{10... | collective-permute-start | bytes 798728 | tf_op jit(solution)/shard_map/ppermute | solution.py:166
  39.3 0.0 collective-permute-done.13
  39.3 2.5 %collective-permute-start.8 = (bf16[128,384]{1,0:T(8,128)(2,1)S(1)}, bf16[128,384]{1,0:T(8,128)(2,1)S(1)}, u32[]{:S(2)}, u32[]{:S(2)}) collective-permute-start(bf16[128,384]{1,0:T(8,128)(2,1)S(1)} %convolution_convert_fusion.refs_4_), channel_id=1, source_target_pairs={{0,24},{8,16},{16,8},{24,0},{1,25},{9,17},{17,9},{25,1},{2,26},{10... | collective-permute-start | bytes 294920 | tf_op jit(solution)/shard_map/ppermute | solution.py:166
  41.8 0.0 collective-permute-done.12
  41.8 0.6 collective-permute-start.7
  42.4 0.6 pad_maximum_fusion.3.refs_12_
  43.0 8.5 %collective-permute-start.6 = (bf16[128,384]{1,0:T(8,128)(2,1)S(1)}, bf16[128,384]{1,0:T(8,128)(2,1)S(1)}, u32[]{:S(2)}, u32[]{:S(2)}) collective-permute-start(bf16[128,384]{1,0:T(8,128)(2,1)S(1)} %convolution_convert_fusion.refs_4_), channel_id=1, source_target_pairs={{0,8},{8,0},{16,24},{24,16},{1,9},{9,1},{17,25},{25,17},{2,10},{10... | collective-permute-start | bytes 294920 | tf_op jit(solution)/shard_map/ppermute | solution.py:166
  51.5 9.4 %collective-permute-done.1.refs_10_.refs_2_ = bf16[1040,128]{1,0:T(8,128)(2,1)S(1)} collective-permute-done((bf16[1040,128]{1,0:T(8,128)(2,1)}, bf16[1040,128]{1,0:T(8,128)(2,1)S(1)}, u32[]{:S(2)}, u32[]{:S(2)}) %collective-permute-start.1) | collective-permute-done | bytes 266272 | tf_op jit(solution)/shard_map/ppermute | solution.py:166
  60.9 0.7 maximum_convert_fusion.cols
  61.6 3.1 %collective-permute-done.7.refs_6_ = bf16[128,384]{1,0:T(8,128)(2,1)S(1)} collective-permute-done((bf16[128,384]{1,0:T(8,128)(2,1)S(1)}, bf16[128,384]{1,0:T(8,128)(2,1)S(1)}, u32[]{:S(2)}, u32[]{:S(2)}) %collective-permute-start.7) | collective-permute-done | bytes 98336 | tf_op jit(solution)/shard_map/ppermute | solution.py:166
  64.7 0.6 copy-done.14
  65.3 0.0 copy-done.15
  65.4 7.1 %shard_map.77 = (bf16[512,768]{1,0:T(8,128)(2,1)}, f32[512,384]{1,0:T(8,128)}, f32[512,384]{1,0:T(8,128)}, f32[3,384]{1,0:T(4,128)}) custom-call(s32[3]{0:T(128)} %pad_add_fusion.meta, s32[4,4]{1,0:T(4,128)} %maximum_convert_fusion.cols, bf16[128,384]{1,0:T(8,128)(2,1)} %copy-done.6, bf16[128,384]{1,0:T(8,128)(2,1)} %copy-done.9, ...), custom_call_target="tpu_custom_call" | custom-call | flops 905969664 | bytes 4000000 | tf_op jit(solution)/shard_map/pallas_call | solution.py:128
  72.4 1.4 %collective-permute-done.15 = f32[3,384]{1,0:T(4,128)S(1)} collective-permute-done((f32[3,384]{1,0:T(4,128)}, f32[3,384]{1,0:T(4,128)S(1)}, u32[]{:S(2)}, u32[]{:S(2)}) %collective-permute-start.15) | collective-permute-done | bytes 4640 | tf_op jit(solution)/shard_map/ppermute | solution.py:154
  73.8 0.8 fusion.12
  74.7 2.5 %collective-permute-start.18 = (f32[3,384]{1,0:T(4,128)S(1)}, f32[3,384]{1,0:T(4,128)S(1)}, u32[]{:S(2)}, u32[]{:S(2)}) collective-permute-start(f32[3,384]{1,0:T(4,128)S(1)} %pad_maximum_fusion.4), channel_id=1, source_target_pairs={{0,6},{1,7},{2,4},{3,5},{4,2},{5,3},{6,0},{7,1},{8,14},{9,15},{10,... | collective-permute-start | bytes 13832 | tf_op jit(solution)/shard_map/ppermute | solution.py:157
  77.2 0.5 collective-permute-start.17
  77.7 0.5 collective-permute-start.16
  78.2 1.0 collective-permute-done.18
  79.3 1.5 %collective-permute-done.17 = f32[3,384]{1,0:T(4,128)S(1)} collective-permute-done((f32[3,384]{1,0:T(4,128)S(1)}, f32[3,384]{1,0:T(4,128)S(1)}, u32[]{:S(2)}, u32[]{:S(2)}) %collective-permute-start.17) | collective-permute-done | bytes 4640 | tf_op jit(solution)/shard_map/ppermute | solution.py:157
  80.8 0.5 collective-permute-done.16
  81.4 0.6 pad_maximum_fusion.5.refs_7_
  82.0 5.6 %shard_map.78 = (bf16[128,1152]{1,0:T(8,128)(2,1)}, f32[1,384]{1,0:T(1,128)}, bf16[2,4,144,576]{3,2,1,0:T(8,128)(2,1)}) custom-call(s32[3]{0:T(128)} %pad_add_fusion.meta, s32[4,4]{1,0:T(4,128)} %maximum_convert_fusion.cols, bf16[1040,128]{1,0:T(8,128)(2,1)} %fusion.8.refs_4_.refs_8_.refs_0_, bf16[1040,128]{1,0:T(8,128)(2,1)} %copy-done.5, ...), custom_call_target="tpu_custom_call" | custom-call | flops 679477248 | bytes 4000000 | tf_op jit(solution)/shard_map/pallas_call | solution.py:128
  87.6 1.3 %slice_bitcast_fusion.2 = bf16[4,144,576]{2,1,0:T(8,128)(2,1)S(1)} fusion(bf16[2,4,144,576]{3,2,1,0:T(8,128)(2,1)} %get-tuple-element.16), kind=kLoop, calls=%fused_computation.8 | loop fusion | bytes 1327104 | tf_op jit(solution)/shard_map/squeeze | solution.py:250
  88.9 0.1 collective-permute-start.19
  89.0 2.2 %collective-permute-done.19 = bf16[4,144,576]{2,1,0:T(8,128)(2,1)S(1)} collective-permute-done((bf16[4,144,576]{2,1,0:T(8,128)(2,1)S(1)}, bf16[4,144,576]{2,1,0:T(8,128)(2,1)S(1)}, u32[]{:S(2)}, u32[]{:S(2)}) %collective-permute-start.19) | collective-permute-done | bytes 663584 | tf_op jit(solution)/shard_map/ppermute | solution.py:251
  91.2 0.2 fusion
  91.4 0.1 slice_bitcast_fusion.5
  91.4 0.6 collective-permute-start.20
  92.0 2.4 %collective-permute-start.22 = (bf16[144,576]{1,0:T(8,128)(2,1)S(1)}, bf16[144,576]{1,0:T(8,128)(2,1)S(1)}, u32[]{:S(2)}, u32[]{:S(2)}) collective-permute-start(bf16[144,576]{1,0:T(8,128)(2,1)S(1)} %get-tuple-element.32), channel_id=1, source_target_pairs={{0,6},{1,7},{2,4},{3,5},{4,2},{5,3},{6,0},{7,1},{8,14},{9,15},{10,... | collective-permute-start | bytes 497672 | tf_op jit(solution)/shard_map/ppermute | solution.py:255
  94.5 0.5 collective-permute-start.21
  95.0 0.6 reduce
  95.6 3.4 %collective-permute-done.20 = bf16[144,576]{1,0:T(8,128)(2,1)S(1)} collective-permute-done((bf16[144,576]{1,0:T(8,128)(2,1)S(1)}, bf16[144,576]{1,0:T(8,128)(2,1)S(1)}, u32[]{:S(2)}, u32[]{:S(2)}) %collective-permute-start.20) | collective-permute-done | bytes 165920 | tf_op jit(solution)/shard_map/ppermute | solution.py:255
  99.0 4.2 %collective-permute-done.22 = bf16[144,576]{1,0:T(8,128)(2,1)S(1)} collective-permute-done((bf16[144,576]{1,0:T(8,128)(2,1)S(1)}, bf16[144,576]{1,0:T(8,128)(2,1)S(1)}, u32[]{:S(2)}, u32[]{:S(2)}) %collective-permute-start.22) | collective-permute-done | bytes 165920 | tf_op jit(solution)/shard_map/ppermute | solution.py:255
  103.2 1.4 %collective-permute-done.21 = bf16[144,576]{1,0:T(8,128)(2,1)S(1)} collective-permute-done((bf16[144,576]{1,0:T(8,128)(2,1)S(1)}, bf16[144,576]{1,0:T(8,128)(2,1)S(1)}, u32[]{:S(2)}, u32[]{:S(2)}) %collective-permute-start.21) | collective-permute-done | bytes 165920 | tf_op jit(solution)/shard_map/ppermute | solution.py:255
  104.5 0.1 fusion.5
  104.6 1.1 %reshape.23 = f32[144,2,288]{2,1,0:T(2,128)} reshape(f32[144,576]{1,0:T(8,128)S(1)} %fusion.5) | data formatting | bytes 663552 | tf_op jit(solution)/shard_map/reshape | solution.py:258
  (49 shorter events, 0.3 us)
Async XLA Ops:
  0.6 3.6 %copy-start = (bf16[1,128,1152]{2,1,0:T(8,128)(2,1)S(1)}, bf16[1,128,1152]{2,1,0:T(8,128)(2,1)}, u32[]{:S(2)}) copy-start(bf16[1,128,1152]{2,1,0:T(8,128)(2,1)} %param.5) | copy-start | bytes 884740
  0.6 9.7 %copy-start.17 = (s32[1,1,4]{2,1,0:T(1,128)S(1)}, s32[1,1,4]{2,1,0:T(1,128)}, u32[]{:S(2)}) copy-start(s32[1,1,4]{2,1,0:T(1,128)} %param.9) | copy-start | bytes 52
  0.7 9.7 %copy-start.10 = (bf16[1,1,4,128,128]{4,3,2,1,0:T(8,128)(2,1)S(1)}, bf16[1,1,4,128,128]{4,3,2,1,0:T(8,128)(2,1)}, u32[]{:S(2)}) copy-start(bf16[1,1,4,128,128]{4,3,2,1,0:T(8,128)(2,1)} %param.8) | copy-start | bytes 393220
  0.7 9.7 %copy-start.11 = (bf16[1,1,4,128,128]{4,3,2,1,0:T(8,128)(2,1)S(1)}, bf16[1,1,4,128,128]{4,3,2,1,0:T(8,128)(2,1)}, u32[]{:S(2)}) copy-start(bf16[1,1,4,128,128]{4,3,2,1,0:T(8,128)(2,1)} %param.7) | copy-start | bytes 393220
  4.5 13.4 %copy-start.6 = (bf16[128,384]{1,0:T(8,128)(2,1)}, bf16[128,384]{1,0:T(8,128)(2,1)S(1)}, u32[]{:S(2)}) copy-start(bf16[128,384]{1,0:T(8,128)(2,1)S(1)} %convolution_convert_fusion.1.refs_0_) | copy-start | bytes 294916
  4.6 8.8 %collective-permute-start.5 = (bf16[128,384]{1,0:T(8,128)(2,1)S(1)}, bf16[128,384]{1,0:T(8,128)(2,1)S(1)}, u32[]{:S(2)}, u32[]{:S(2)}) collective-permute-start(bf16[128,384]{1,0:T(8,128)(2,1)S(1)} %convolution_convert_fusion.1.refs_0_), channel_id=1, source_target_pairs={{0,24},{8,16},{16,8},{24,0},{1,25},{9,17},{17,9},{25,1},{2,26},{10... | collective-permute-start | bytes 294920 | tf_op jit(solution)/shard_map/ppermute | solution.py:166
  9.7 8.3 %collective-permute-start.4 = (bf16[128,384]{1,0:T(8,128)(2,1)S(1)}, bf16[128,384]{1,0:T(8,128)(2,1)S(1)}, u32[]{:S(2)}, u32[]{:S(2)}) collective-permute-start(bf16[128,384]{1,0:T(8,128)(2,1)S(1)} %convolution_convert_fusion.1.refs_0_), channel_id=1, source_target_pairs={{0,16},{8,24},{16,0},{24,8},{1,17},{9,25},{17,1},{25,9},{2,18},{10... | collective-permute-start | bytes 294920 | tf_op jit(solution)/shard_map/ppermute | solution.py:166
  9.7 8.3 %collective-permute-start.3 = (bf16[128,384]{1,0:T(8,128)(2,1)S(1)}, bf16[128,384]{1,0:T(8,128)(2,1)S(1)}, u32[]{:S(2)}, u32[]{:S(2)}) collective-permute-start(bf16[128,384]{1,0:T(8,128)(2,1)S(1)} %convolution_convert_fusion.1.refs_0_), channel_id=1, source_target_pairs={{0,8},{8,0},{16,24},{24,16},{1,9},{9,1},{17,25},{25,17},{2,10},{10... | collective-permute-start | bytes 294920 | tf_op jit(solution)/shard_map/ppermute | solution.py:166
  11.1 26.3 %copy-start.1 = (bf16[1040,128]{1,0:T(8,128)(2,1)S(1)}, bf16[1040,128]{1,0:T(8,128)(2,1)}, u32[]{:S(2)}) copy-start(bf16[1040,128]{1,0:T(8,128)(2,1)} %fusion.8.refs_4_.refs_8_.refs_0_) | copy-start | bytes 798724
  13.4 4.6 %copy-start.7 = (bf16[128,384]{1,0:T(8,128)(2,1)}, bf16[128,384]{1,0:T(8,128)(2,1)S(1)}, u32[]{:S(2)}) copy-start(bf16[128,384]{1,0:T(8,128)(2,1)S(1)} %collective-permute-done.5.refs_3_) | copy-start | bytes 294916
  17.9 0.6 copy-start.8
  17.9 0.7 copy-start.9
  20.8 3.8 %collective-permute-start.9 = (f32[3,384]{1,0:T(4,128)}, f32[3,384]{1,0:T(4,128)S(1)}, u32[]{:S(2)}, u32[]{:S(2)}) collective-permute-start(f32[3,384]{1,0:T(4,128)} %shard_map.76), channel_id=1, source_target_pairs={{0,8},{8,0},{16,24},{24,16},{1,9},{9,1},{17,25},{25,17},{2,10},{10... | collective-permute-start | bytes 13832 | tf_op jit(solution)/shard_map/ppermute | solution.py:160
  25.4 4.6 %collective-permute-start.10 = (f32[3,384]{1,0:T(4,128)S(1)}, f32[3,384]{1,0:T(4,128)S(1)}, u32[]{:S(2)}, u32[]{:S(2)}) collective-permute-start(f32[3,384]{1,0:T(4,128)S(1)} %pad_maximum_fusion), channel_id=1, source_target_pairs={{0,16},{8,24},{16,0},{24,8},{1,17},{9,25},{17,1},{25,9},{2,18},{10... | collective-permute-start | bytes 13832 | tf_op jit(solution)/shard_map/ppermute | solution.py:160
  30.1 2.7 %collective-permute-start.11 = (f32[3,384]{1,0:T(4,128)S(1)}, f32[3,384]{1,0:T(4,128)S(1)}, u32[]{:S(2)}, u32[]{:S(2)}) collective-permute-start(f32[3,384]{1,0:T(4,128)S(1)} %pad_maximum_fusion.1), channel_id=1, source_target_pairs={{0,1},{1,0},{2,3},{3,2},{4,5},{5,4},{6,7},{7,6},{8,9},{9,8},{10,11... | collective-permute-start | bytes 13832 | tf_op jit(solution)/shard_map/ppermute | solution.py:154
  30.2 12.8 %collective-permute-start.2 = (bf16[1040,128]{1,0:T(8,128)(2,1)}, bf16[1040,128]{1,0:T(8,128)(2,1)S(1)}, u32[]{:S(2)}, u32[]{:S(2)}) collective-permute-start(bf16[1040,128]{1,0:T(8,128)(2,1)} %fusion.8.refs_4_.refs_8_.refs_0_), channel_id=1, source_target_pairs={{0,24},{8,16},{16,8},{24,0},{1,25},{9,17},{17,9},{25,1},{2,26},{10... | collective-permute-start | bytes 798728 | tf_op jit(solution)/shard_map/ppermute | solution.py:166
  32.7 28.2 %collective-permute-start.1 = (bf16[1040,128]{1,0:T(8,128)(2,1)}, bf16[1040,128]{1,0:T(8,128)(2,1)S(1)}, u32[]{:S(2)}, u32[]{:S(2)}) collective-permute-start(bf16[1040,128]{1,0:T(8,128)(2,1)} %fusion.8.refs_4_.refs_8_.refs_0_), channel_id=1, source_target_pairs={{0,16},{8,24},{16,0},{24,8},{1,17},{9,25},{17,1},{25,9},{2,18},{10... | collective-permute-start | bytes 798728 | tf_op jit(solution)/shard_map/ppermute | solution.py:166
  32.8 4.6 %collective-permute-start.14 = (f32[3,384]{1,0:T(4,128)S(1)}, f32[3,384]{1,0:T(4,128)S(1)}, u32[]{:S(2)}, u32[]{:S(2)}) collective-permute-start(f32[3,384]{1,0:T(4,128)S(1)} %pad_maximum_fusion.2), channel_id=1, source_target_pairs={{0,6},{1,7},{2,4},{3,5},{4,2},{5,3},{6,0},{7,1},{8,14},{9,15},{10,... | collective-permute-start | bytes 13832 | tf_op jit(solution)/shard_map/ppermute | solution.py:157
  35.3 4.0 %collective-permute-start.13 = (f32[3,384]{1,0:T(4,128)S(1)}, f32[3,384]{1,0:T(4,128)S(1)}, u32[]{:S(2)}, u32[]{:S(2)}) collective-permute-start(f32[3,384]{1,0:T(4,128)S(1)} %pad_maximum_fusion.2), channel_id=1, source_target_pairs={{0,4},{1,5},{2,6},{3,7},{4,0},{5,1},{6,2},{7,3},{8,12},{9,13},{10,... | collective-permute-start | bytes 13832 | tf_op jit(solution)/shard_map/ppermute | solution.py:157
  35.8 6.0 %collective-permute-start.12 = (f32[3,384]{1,0:T(4,128)S(1)}, f32[3,384]{1,0:T(4,128)S(1)}, u32[]{:S(2)}, u32[]{:S(2)}) collective-permute-start(f32[3,384]{1,0:T(4,128)S(1)} %pad_maximum_fusion.2), channel_id=1, source_target_pairs={{0,2},{1,3},{2,0},{3,1},{4,6},{5,7},{6,4},{7,5},{8,10},{9,11},{10,... | collective-permute-start | bytes 13832 | tf_op jit(solution)/shard_map/ppermute | solution.py:157
  36.7 28.0 %copy-start.12 = (bf16[128,384]{1,0:T(8,128)(2,1)}, bf16[128,384]{1,0:T(8,128)(2,1)S(1)}, u32[]{:S(2)}) copy-start(bf16[128,384]{1,0:T(8,128)(2,1)S(1)} %convolution_convert_fusion.refs_4_) | copy-start | bytes 294916
  37.4 23.6 %collective-permute-start = (bf16[1040,128]{1,0:T(8,128)(2,1)S(1)}, bf16[1040,128]{1,0:T(8,128)(2,1)S(1)}, u32[]{:S(2)}, u32[]{:S(2)}) collective-permute-start(bf16[1040,128]{1,0:T(8,128)(2,1)S(1)} %copy-done.1), channel_id=1, source_target_pairs={{0,8},{8,0},{16,24},{24,16},{1,9},{9,1},{17,25},{25,17},{2,10},{10... | collective-permute-start | bytes 798728 | tf_op jit(solution)/shard_map/ppermute | solution.py:166
  39.3 22.3 %collective-permute-start.8 = (bf16[128,384]{1,0:T(8,128)(2,1)S(1)}, bf16[128,384]{1,0:T(8,128)(2,1)S(1)}, u32[]{:S(2)}, u32[]{:S(2)}) collective-permute-start(bf16[128,384]{1,0:T(8,128)(2,1)S(1)} %convolution_convert_fusion.refs_4_), channel_id=1, source_target_pairs={{0,24},{8,16},{16,8},{24,0},{1,25},{9,17},{17,9},{25,1},{2,26},{10... | collective-permute-start | bytes 294920 | tf_op jit(solution)/shard_map/ppermute | solution.py:166
  41.8 22.9 %collective-permute-start.7 = (bf16[128,384]{1,0:T(8,128)(2,1)S(1)}, bf16[128,384]{1,0:T(8,128)(2,1)S(1)}, u32[]{:S(2)}, u32[]{:S(2)}) collective-permute-start(bf16[128,384]{1,0:T(8,128)(2,1)S(1)} %convolution_convert_fusion.refs_4_), channel_id=1, source_target_pairs={{0,16},{8,24},{16,0},{24,8},{1,17},{9,25},{17,1},{25,9},{2,18},{10... | collective-permute-start | bytes 294920 | tf_op jit(solution)/shard_map/ppermute | solution.py:166
  43.0 21.7 %copy-start.3 = (bf16[1040,128]{1,0:T(8,128)(2,1)}, bf16[1040,128]{1,0:T(8,128)(2,1)S(1)}, u32[]{:S(2)}) copy-start(bf16[1040,128]{1,0:T(8,128)(2,1)S(1)} %collective-permute-done.2.refs_11_.refs_3_) | copy-start | bytes 798724
  43.0 21.7 %collective-permute-start.6 = (bf16[128,384]{1,0:T(8,128)(2,1)S(1)}, bf16[128,384]{1,0:T(8,128)(2,1)S(1)}, u32[]{:S(2)}, u32[]{:S(2)}) collective-permute-start(bf16[128,384]{1,0:T(8,128)(2,1)S(1)} %convolution_convert_fusion.refs_4_), channel_id=1, source_target_pairs={{0,8},{8,0},{16,24},{24,16},{1,9},{9,1},{17,25},{25,17},{2,10},{10... | collective-permute-start | bytes 294920 | tf_op jit(solution)/shard_map/ppermute | solution.py:166
  60.9 3.8 %copy-start.4 = (bf16[1040,128]{1,0:T(8,128)(2,1)}, bf16[1040,128]{1,0:T(8,128)(2,1)S(1)}, u32[]{:S(2)}) copy-start(bf16[1040,128]{1,0:T(8,128)(2,1)S(1)} %collective-permute-done.1.refs_10_.refs_2_) | copy-start | bytes 798724
  60.9 3.8 %copy-start.5 = (bf16[1040,128]{1,0:T(8,128)(2,1)}, bf16[1040,128]{1,0:T(8,128)(2,1)S(1)}, u32[]{:S(2)}) copy-start(bf16[1040,128]{1,0:T(8,128)(2,1)S(1)} %collective-permute-done.refs_9_.refs_1_) | copy-start | bytes 798724
  61.6 3.1 %copy-start.13 = (bf16[128,384]{1,0:T(8,128)(2,1)}, bf16[128,384]{1,0:T(8,128)(2,1)S(1)}, u32[]{:S(2)}) copy-start(bf16[128,384]{1,0:T(8,128)(2,1)S(1)} %collective-permute-done.8.refs_7_) | copy-start | bytes 294916
  64.7 0.6 copy-start.14
  64.7 0.7 copy-start.15
  72.4 1.4 %collective-permute-start.15 = (f32[3,384]{1,0:T(4,128)}, f32[3,384]{1,0:T(4,128)S(1)}, u32[]{:S(2)}, u32[]{:S(2)}) collective-permute-start(f32[3,384]{1,0:T(4,128)} %get-tuple-element.13), channel_id=1, source_target_pairs={{0,1},{1,0},{2,3},{3,2},{4,5},{5,4},{6,7},{7,6},{8,9},{9,8},{10,11... | collective-permute-start | bytes 13832 | tf_op jit(solution)/shard_map/ppermute | solution.py:154
  74.7 4.6 %collective-permute-start.18 = (f32[3,384]{1,0:T(4,128)S(1)}, f32[3,384]{1,0:T(4,128)S(1)}, u32[]{:S(2)}, u32[]{:S(2)}) collective-permute-start(f32[3,384]{1,0:T(4,128)S(1)} %pad_maximum_fusion.4), channel_id=1, source_target_pairs={{0,6},{1,7},{2,4},{3,5},{4,2},{5,3},{6,0},{7,1},{8,14},{9,15},{10,... | collective-permute-start | bytes 13832 | tf_op jit(solution)/shard_map/ppermute | solution.py:157
  77.2 3.6 %collective-permute-start.17 = (f32[3,384]{1,0:T(4,128)S(1)}, f32[3,384]{1,0:T(4,128)S(1)}, u32[]{:S(2)}, u32[]{:S(2)}) collective-permute-start(f32[3,384]{1,0:T(4,128)S(1)} %pad_maximum_fusion.4), channel_id=1, source_target_pairs={{0,4},{1,5},{2,6},{3,7},{4,0},{5,1},{6,2},{7,3},{8,12},{9,13},{10,... | collective-permute-start | bytes 13832 | tf_op jit(solution)/shard_map/ppermute | solution.py:157
  77.7 3.6 %collective-permute-start.16 = (f32[3,384]{1,0:T(4,128)S(1)}, f32[3,384]{1,0:T(4,128)S(1)}, u32[]{:S(2)}, u32[]{:S(2)}) collective-permute-start(f32[3,384]{1,0:T(4,128)S(1)} %pad_maximum_fusion.4), channel_id=1, source_target_pairs={{0,2},{1,3},{2,0},{3,1},{4,6},{5,7},{6,4},{7,5},{8,10},{9,11},{10,... | collective-permute-start | bytes 13832 | tf_op jit(solution)/shard_map/ppermute | solution.py:157
  87.6 3.6 %copy-start.2 = (bf16[2,4,144,576]{3,2,1,0:T(8,128)(2,1)S(1)}, bf16[2,4,144,576]{3,2,1,0:T(8,128)(2,1)}, u32[]{:S(2)}) copy-start(bf16[2,4,144,576]{3,2,1,0:T(8,128)(2,1)} %get-tuple-element.16) | copy-start | bytes 3981316
  88.9 6.1 %copy-start.16 = (f32[1,384]{1,0:T(1,128)S(1)}, f32[1,384]{1,0:T(1,128)}, u32[]{:S(2)}) copy-start(f32[1,384]{1,0:T(1,128)} %get-tuple-element.15) | copy-start | bytes 4612
  88.9 2.3 %collective-permute-start.19 = (bf16[4,144,576]{2,1,0:T(8,128)(2,1)S(1)}, bf16[4,144,576]{2,1,0:T(8,128)(2,1)S(1)}, u32[]{:S(2)}, u32[]{:S(2)}) collective-permute-start(bf16[4,144,576]{2,1,0:T(8,128)(2,1)S(1)} %slice_bitcast_fusion.2), channel_id=1, source_target_pairs={{0,1},{1,0},{2,3},{3,2},{4,5},{5,4},{6,7},{7,6},{8,9},{9,8},{10,11... | collective-permute-start | bytes 1990664 | tf_op jit(solution)/shard_map/ppermute | solution.py:251
  91.4 7.5 %collective-permute-start.20 = (bf16[144,576]{1,0:T(8,128)(2,1)S(1)}, bf16[144,576]{1,0:T(8,128)(2,1)S(1)}, u32[]{:S(2)}, u32[]{:S(2)}) collective-permute-start(bf16[144,576]{1,0:T(8,128)(2,1)S(1)} %get-tuple-element.31), channel_id=1, source_target_pairs={{0,2},{1,3},{2,0},{3,1},{4,6},{5,7},{6,4},{7,5},{8,10},{9,11},{10,... | collective-permute-start | bytes 497672 | tf_op jit(solution)/shard_map/ppermute | solution.py:255
  92.0 11.2 %collective-permute-start.22 = (bf16[144,576]{1,0:T(8,128)(2,1)S(1)}, bf16[144,576]{1,0:T(8,128)(2,1)S(1)}, u32[]{:S(2)}, u32[]{:S(2)}) collective-permute-start(bf16[144,576]{1,0:T(8,128)(2,1)S(1)} %get-tuple-element.32), channel_id=1, source_target_pairs={{0,6},{1,7},{2,4},{3,5},{4,2},{5,3},{6,0},{7,1},{8,14},{9,15},{10,... | collective-permute-start | bytes 497672 | tf_op jit(solution)/shard_map/ppermute | solution.py:255
  94.5 10.1 %collective-permute-start.21 = (bf16[144,576]{1,0:T(8,128)(2,1)S(1)}, bf16[144,576]{1,0:T(8,128)(2,1)S(1)}, u32[]{:S(2)}, u32[]{:S(2)}) collective-permute-start(bf16[144,576]{1,0:T(8,128)(2,1)S(1)} %get-tuple-element.33), channel_id=1, source_target_pairs={{0,4},{1,5},{2,6},{3,7},{4,0},{5,1},{6,2},{7,3},{8,12},{9,13},{10,... | collective-permute-start | bytes 497672 | tf_op jit(solution)/shard_map/ppermute | solution.py:255

commit v2 on v1

--- a/solution.py
+++ b/solution.py
@@ -11,7 +11,7 @@
 tiny = 1e-30
 f32 = jnp.float32
 bf16 = jnp.bfloat16
-VMEM_BYTES = 56 * 1024 * 1024
+VMEM_BYTES = 24 * 1024 * 1024
 
 
 def vmem():
@@ -53,10 +53,32 @@
     return shift, scale
 
 
-def stats_kernel(nz, slots, edge, modes, rows_of, meta, cols, *refs):
+def turn_kernel(current, coeffs, out_ref):
+    out_ref[...] = jnp.dot(current[...], coeffs[0], preferred_element_type=f32).astype(bf16)
+
+
+def turn_part(current, coeffs, sweep, part, modes):
+    rows, columns = current.shape
+    return pl.pallas_call(
+        turn_kernel,
+        grid=(1,),
+        out_shape=jax.ShapeDtypeStruct((rows, modes), bf16),
+        in_specs=[
+            pl.BlockSpec((rows, columns), lambda i: (0, 0)),
+            pl.BlockSpec((1, columns, modes), lambda i: (sweep, 0, part)),
+        ],
+        out_specs=pl.BlockSpec((rows, modes), lambda i: (0, 0)),
+        compiler_params=pltpu.CompilerParams(vmem_limit_bytes=VMEM_BYTES),
+        cost_estimate=pl.CostEstimate(
+            flops=2 * rows * columns * modes, bytes_accessed=2 * columns * modes, transcendentals=0
+        ),
+    )(current, coeffs)
+
+
+def stats_kernel(nz, slots, edge, modes, rows_of, cols, *refs):
     x_refs, km_refs = refs[:nz], refs[nz : nz + rows_of]
     stats_ref, field, stiff, mass = refs[nz + rows_of :]
-    z = meta[0]
+    z = lax.axis_index("blk")
     for k in range(nz):
         field[pl.ds(pl.multiple_of((z ^ k) * edge, edge), edge), :] = x_refs[k][...]
     for k in range(rows_of):
@@ -70,10 +92,10 @@
     stats_ref[2:3, :] = about
 
 
-def sweep_kernel(nz, slots, edge, modes, total_rows, meta, cols, *refs):
+def sweep_kernel(nz, slots, edge, modes, total_rows, cols, *refs):
     x_refs, h_refs, km_refs = refs[:nz], refs[nz : 2 * nz], refs[2 * nz : 3 * nz]
     stats, coeffs, turned_ref, stiff_ref, mass_ref, stats_ref, full = refs[3 * nz :]
-    z = meta[0]
+    z = lax.axis_index("blk")
     at = [pl.ds(pl.multiple_of((z ^ k) * edge, edge), edge) for k in range(nz)]
     for k in range(nz):
         full[at[k], 0:modes] = x_refs[k][...]
@@ -93,10 +115,11 @@
     stats_ref[2:3, :] = about
 
 
-def gram_kernel(nz, ng, slots, edge, modes, total_rows, split, meta, cols, *refs):
+def gram_kernel(nz, ng, slots, edge, modes, total_rows, split, cols, *refs):
     km_refs = refs[:nz]
-    turned, stiff, mass, stats, basis_ref, ritz_ref, gram_ref, full, chosen, applied = refs[nz:]
-    z, core, chip = meta[0], meta[1], meta[2]
+    turned, stiff, mass, stats, basis_ref, ritz_ref, gram_ref, send_ref, full, chosen, applied = refs[nz:]
+    z, g = lax.axis_index("blk"), lax.axis_index("grp")
+    core, chip = lax.rem(g, 2), lax.div(g, 2)
     at = [pl.ds(pl.multiple_of((z ^ k) * edge, edge), edge) for k in range(nz)]
     width = 3 * modes // nz
     shift, scale = shift_and_scale(stats, total_rows)
@@ -119,7 +142,15 @@
     if split:
         rows = 3 * modes // ng
         for q in range(ng):
-            gram_ref[(q % 2) ^ core, (q // 2) ^ chip] = gram[q * rows : (q + 1) * rows]
+            piece = gram[q * rows : (q + 1) * rows]
+
+            @pl.when(core == q % 2)
+            def _():
+                gram_ref[(q // 2) ^ chip] = piece
+
+            @pl.when(core != q % 2)
+            def _():
+                send_ref[(q // 2) ^ chip] = piece
     else:
         gram_ref[...] = gram
 
@@ -168,7 +199,6 @@
 
 def body(basis, coeffs, stiff_blocks, mass_blocks, block_cols):
     nz, ng = lax.axis_size("blk"), lax.axis_size("grp")
-    z, g = lax.axis_index("blk"), lax.axis_index("grp")
     current = basis[0]
     edge, columns = current.shape
     slots = block_cols.shape[-1]
@@ -177,43 +207,38 @@
     total_rows = rows * ng
     width = columns // nz
 
-    tag = jnp.pad(block_cols[0, 0].astype(bf16)[None, :], ((0, 15), (0, edge - slots)))
     payload = jnp.concatenate(
         [
             stiff_blocks[0, 0].reshape(slots * edge, edge),
             mass_blocks[0, 0].reshape(slots * edge, edge),
-            tag,
         ],
         axis=0,
     )
-    first = jnp.dot(current, coeffs[0][:, :modes], preferred_element_type=f32).astype(bf16)
+    first = turn_part(current, coeffs, 0, 0, modes)
     x_parts = gather(first, nz)
     km_parts = gather(payload, nz)
-    later = jnp.dot(current, coeffs[0][:, modes:], preferred_element_type=f32).astype(bf16)
+    later = turn_part(current, coeffs, 0, 1, modes)
     h_parts = gather(later, nz)
 
-    meta = jnp.stack([z, g % 2, g // 2]).astype(jnp.int32)
-    own_cols = block_cols[0]
+    cols = jnp.concatenate(gather(block_cols[0], nz))
     stats = call(
-        functools.partial(stats_kernel, nz, slots, edge, modes, 1),
-        [meta, own_cols, *x_parts, payload],
-        2,
+        functools.partial(stats_kernel, nz, slots, edge, modes, nz),
+        [cols, *x_parts, *km_parts],
+        1,
         jax.ShapeDtypeStruct((3, modes), f32),
         [
             pltpu.VMEM((rows, modes), bf16),
-            pltpu.VMEM((edge, modes), f32),
-            pltpu.VMEM((edge, modes), f32),
+            pltpu.VMEM((rows, modes), f32),
+            pltpu.VMEM((rows, modes), f32),
         ],
         4 * edge * slots * edge * modes,
     )
-    stats = merge_over("blk", nz, stats)
     stats = merge_over("grp", ng, stats)
 
-    cols = jnp.stack([p[2 * slots * edge, :slots] for p in km_parts]).astype(jnp.int32)
     turned, stiff_x, mass_x, stats = call(
         functools.partial(sweep_kernel, nz, slots, edge, modes, total_rows),
-        [meta, cols, *x_parts, *h_parts, *km_parts, stats, coeffs[1]],
-        2,
+        [cols, *x_parts, *h_parts, *km_parts, stats, coeffs[1]],
+        1,
         (
             jax.ShapeDtypeStruct((rows, 2 * modes), bf16),
             jax.ShapeDtypeStruct((rows, modes), f32),
@@ -228,15 +253,16 @@
     split = (columns // ng) % 16 == 0
     chips = ng // 2
     block = columns // ng
-    gram_shape = (2, chips, block, 2 * width) if split else (columns, 2 * width)
+    gram_shape = (chips, block, 2 * width) if split else (columns, 2 * width)
     window = -(-(width + max(i * width % 128 for i in range(nz))) // 128) * 128
-    basis_out, ritz, gram = call(
+    basis_out, ritz, gram, send = call(
         functools.partial(gram_kernel, nz, ng, slots, edge, modes, total_rows, split),
-        [meta, cols, *km_parts, turned, stiff_x, mass_x, stats],
-        2,
+        [cols, *km_parts, turned, stiff_x, mass_x, stats],
+        1,
         (
             jax.ShapeDtypeStruct((edge, columns), bf16),
             jax.ShapeDtypeStruct((1, modes), f32),
+            jax.ShapeDtypeStruct(gram_shape, bf16),
             jax.ShapeDtypeStruct(gram_shape, bf16),
         ),
         [
@@ -247,9 +273,8 @@
         2 * rows * columns * 2 * width,
     )
     if split:
-        keep, send = gram[0], gram[1]
         got = lax.ppermute(send, "grp", by_xor(ng, 1))
-        mine = (keep.astype(f32) + got.astype(f32)).astype(bf16)
+        mine = (gram.astype(f32) + got.astype(f32)).astype(bf16)
         total = mine[0].astype(f32)
         for k in range(1, chips):
             total = total + lax.ppermute(mine[k], "grp", by_xor(ng, 2 * k)).astype(f32)

time: 106 us -> 96.3 us (0.908)
  Pallas kernels: 14.8 us -> 10.8 us
  starting transfers between devices: 34.2 us -> 38.2 us
  other arithmetic: 5.95 us -> 2.06 us
  local copies, waits for them, and re-layouts: 7.32 us -> 4.23 us
  waiting for transfers between devices: 41.9 us -> 39.9 us
    ppermute x2 -> x0, waiting for transfers between devices: 6.83 us -> none  [merge_over(): stats = merge(stats, lax.ppermute(stats, axis, by_xor(size, step)))]
    ppermute x9 -> x12, starting transfers between devices: 21.8 us -> 27.4 us  [gather(): return [x] + [lax.ppermute(x, 'blk', by_xor(nz, k)) for k in range(1, nz)]]
    ppermute x9 -> x12, waiting for transfers between devices: 18.7 us -> 23.4 us  [gather(): return [x] + [lax.ppermute(x, 'blk', by_xor(nz, k)) for k in range(1, nz)]]
    pallas_call x3, Pallas kernels: 14.8 us -> 10.2 us  [call(): pl.pallas_call(kernel, out_shape=out_shape, in_specs=[smem()] * n_smem +...]
    squeeze x1, local copies, waits for them, and re-layouts: 3.54 us -> 0.11 us  [body(): coeffs[1]]
    add x6 -> x4, other arithmetic: 1.79 us -> 0.15 us  [merge(): return jnp.stack([num, den, one[2] + two[2] + gap * gap])]
    unnamed x36 -> x10, local copies, waits for them, and re-layouts: 1.34 us -> 2.97 us
    ppermute x2 -> x0, starting transfers between devices: 1.6 us -> none  [merge_over(): stats = merge(stats, lax.ppermute(stats, axis, by_xor(size, step)))]
  transfers between devices with their start and end apart: 23 -> 24, of which waited for: 15 -> 17; matrix products, arithmetic and copies ran while one was open for 3% -> 1% of each run, Pallas kernels for 0% -> 1%
where the time goes in v2:
time: 96.3 us; the launch traced here: 96.1 us
  waiting for transfers between devices  39.9 us (41%)
  starting transfers between devices  38.2 us (40%)
  Pallas kernels  10.8 us (11%)
  local copies, waits for them, and re-layouts  4.23 us (4%)
  other arithmetic  2.06 us (2%)
    ppermute x12, starting transfers between devices, gather(): return [x] + [lax.ppermute(x, 'blk', by_xor(nz, k)) for k in range(1, nz)]  27.4 us
    ppermute x12, waiting for transfers between devices, gather(): return [x] + [lax.ppermute(x, 'blk', by_xor(nz, k)) for k in range(1, nz)]  23.4 us
    pallas_call x3, Pallas kernels, call(): pl.pallas_call(kernel, out_shape=out_shape, in_specs=[smem()] * n_smem +...  10.2 us
    ppermute x3, waiting for transfers between devices, body(): total = total + lax.ppermute(mine[k], 'grp', by_xor(ng, 2 * k)).astype(f32)  8.96 us
    ppermute x6, starting transfers between devices, merge_over(): got = [lax.ppermute(stats, axis, by_xor(size, 2 * k)) for k in (1, 2, 3)]  7.11 us
    ppermute x6, waiting for transfers between devices, merge_over(): got = [lax.ppermute(stats, axis, by_xor(size, 2 * k)) for k in (1, 2, 3)]  4.2 us
    ppermute x3, starting transfers between devices, body(): total = total + lax.ppermute(mine[k], 'grp', by_xor(ng, 2 * k)).astype(f32)  3.55 us
    unnamed x10, local copies, waits for them, and re-layouts  2.97 us
  transfers between devices with their start and end apart: 24, of which 17 were waited for; matrix products, arithmetic and copies ran while one was open for 1% of the time, Pallas kernels for 1%

profile of v2, /device:TPU:0, one launch (start us, length us, event | category | flops | bytes accessed | tf_op | source)
XLA Modules:
  0.0 96.1 jit_solution(5058358935360307511)
XLA Ops:
  0.6 1.0 %pad_maximum_fusion.refs_4_.refs_8_.refs_0_ = bf16[1024,128]{1,0:T(8,128)(2,1)S(1)} fusion(bf16[512,128]{1,0:T(8,128)(2,1)} %bitcast.20, bf16[512,128]{1,0:T(8,128)(2,1)} %bitcast.21), kind=kLoop, calls=%fused_computation.5 | loop fusion | flops 524288 | bytes 524288 | tf_op jit(solution)/shard_map/concatenate | solution.py:210
  1.6 5.1 %collective-permute-start.5 = (bf16[1024,128]{1,0:T(8,128)(2,1)S(1)}, bf16[1024,128]{1,0:T(8,128)(2,1)S(1)}, u32[]{:S(2)}, u32[]{:S(2)}) collective-permute-start(bf16[1024,128]{1,0:T(8,128)(2,1)S(1)} %pad_maximum_fusion.refs_4_.refs_8_.refs_0_), channel_id=1, source_target_pairs={{0,24},{8,16},{16,8},{24,0},{1,25},{9,17},{17,9},{25,1},{2,26},{10... | collective-permute-start | bytes 786440 | tf_op jit(solution)/shard_map/ppermute | solution.py:197
  6.7 0.0 collective-permute-start.4
  6.7 0.6 collective-permute-start.3
  7.4 2.0 %copy-done = bf16[2,1152,768]{2,1,0:T(8,128)(2,1)S(1)} copy-done((bf16[2,1152,768]{2,1,0:T(8,128)(2,1)S(1)}, bf16[2,1152,768]{2,1,0:T(8,128)(2,1)}, u32[]{:S(2)}) %copy-start) | copy-done | bytes 3538968
  9.4 1.0 copy-done.2
  10.3 0.3 shard_map.76.refs_0_
  10.7 3.8 %collective-permute-start.8 = (bf16[128,384]{1,0:T(8,128)(2,1)S(1)}, bf16[128,384]{1,0:T(8,128)(2,1)S(1)}, u32[]{:S(2)}, u32[]{:S(2)}) collective-permute-start(bf16[128,384]{1,0:T(8,128)(2,1)S(1)} %shard_map.76.refs_0_), channel_id=1, source_target_pairs={{0,24},{8,16},{16,8},{24,0},{1,25},{9,17},{17,9},{25,1},{2,26},{10... | collective-permute-start | bytes 294920 | tf_op jit(solution)/shard_map/ppermute | solution.py:197
  14.5 0.3 collective-permute-start.2
  14.7 11.9 %collective-permute-done.2 = s32[1,4]{1,0:T(1,128)S(1)} collective-permute-done((s32[1,4]{1,0:T(1,128)S(1)}, s32[1,4]{1,0:T(1,128)S(1)}, u32[]{:S(2)}, u32[]{:S(2)}) %collective-permute-start.2) | collective-permute-done | bytes 48 | tf_op jit(solution)/shard_map/ppermute | solution.py:197
  26.6 8.3 %collective-permute-start.1 = (s32[1,4]{1,0:T(1,128)S(1)}, s32[1,4]{1,0:T(1,128)S(1)}, u32[]{:S(2)}, u32[]{:S(2)}) collective-permute-start(s32[1,4]{1,0:T(1,128)S(1)} %bitcast.23), channel_id=1, source_target_pairs={{0,16},{8,24},{16,0},{24,8},{1,17},{9,25},{17,1},{25,9},{2,18},{10... | collective-permute-start | bytes 56 | tf_op jit(solution)/shard_map/ppermute | solution.py:197
  34.9 1.5 %collective-permute-done.1 = s32[1,4]{1,0:T(1,128)S(1)} collective-permute-done((s32[1,4]{1,0:T(1,128)S(1)}, s32[1,4]{1,0:T(1,128)S(1)}, u32[]{:S(2)}, u32[]{:S(2)}) %collective-permute-start.1) | collective-permute-done | bytes 48 | tf_op jit(solution)/shard_map/ppermute | solution.py:197
  36.4 1.9 %collective-permute-start = (s32[1,4]{1,0:T(1,128)S(1)}, s32[1,4]{1,0:T(1,128)S(1)}, u32[]{:S(2)}, u32[]{:S(2)}) collective-permute-start(s32[1,4]{1,0:T(1,128)S(1)} %bitcast.24), channel_id=1, source_target_pairs={{0,8},{8,0},{16,24},{24,16},{1,9},{9,1},{17,25},{25,17},{2,10},{10... | collective-permute-start | bytes 56 | tf_op jit(solution)/shard_map/ppermute | solution.py:197
  38.3 1.6 %collective-permute-done = s32[1,4]{1,0:T(1,128)S(1)} collective-permute-done((s32[1,4]{1,0:T(1,128)S(1)}, s32[1,4]{1,0:T(1,128)S(1)}, u32[]{:S(2)}, u32[]{:S(2)}) %collective-permute-start) | collective-permute-done | bytes 48 | tf_op jit(solution)/shard_map/ppermute | solution.py:197
  40.0 2.9 %collective-permute-start.7 = (bf16[128,384]{1,0:T(8,128)(2,1)S(1)}, bf16[128,384]{1,0:T(8,128)(2,1)S(1)}, u32[]{:S(2)}, u32[]{:S(2)}) collective-permute-start(bf16[128,384]{1,0:T(8,128)(2,1)S(1)} %shard_map.76.refs_0_), channel_id=1, source_target_pairs={{0,16},{8,24},{16,0},{24,8},{1,17},{9,25},{17,1},{25,9},{2,18},{10... | collective-permute-start | bytes 294920 | tf_op jit(solution)/shard_map/ppermute | solution.py:197
  42.9 0.0 collective-permute-done.8.refs_3_
  42.9 0.0 collective-permute-start.6
  42.9 2.6 %collective-permute-done.7.refs_2_ = bf16[128,384]{1,0:T(8,128)(2,1)S(1)} collective-permute-done((bf16[128,384]{1,0:T(8,128)(2,1)S(1)}, bf16[128,384]{1,0:T(8,128)(2,1)S(1)}, u32[]{:S(2)}, u32[]{:S(2)}) %collective-permute-start.7) | collective-permute-done | bytes 98336 | tf_op jit(solution)/shard_map/ppermute | solution.py:197
  45.5 2.0 %collective-permute-done.6.refs_1_ = bf16[128,384]{1,0:T(8,128)(2,1)S(1)} collective-permute-done((bf16[128,384]{1,0:T(8,128)(2,1)S(1)}, bf16[128,384]{1,0:T(8,128)(2,1)S(1)}, u32[]{:S(2)}, u32[]{:S(2)}) %collective-permute-start.6) | collective-permute-done | bytes 98336 | tf_op jit(solution)/shard_map/ppermute | solution.py:197
  47.5 0.0 collective-permute-done.5.refs_7_.refs_11_.refs_3_
  47.5 0.0 collective-permute-done.4.refs_6_.refs_10_.refs_2_
  47.5 0.0 collective-permute-done.3.refs_5_.refs_9_.refs_1_
  47.5 1.6 %shard_map.78 = f32[3,384]{1,0:T(4,128)S(1)} custom-call(s32[4,4]{1,0:T(4,128)S(1)} %pad_add_fusion.cols, bf16[128,384]{1,0:T(8,128)(2,1)S(1)} %shard_map.76.refs_0_, bf16[128,384]{1,0:T(8,128)(2,1)S(1)} %collective-permute-done.6.refs_1_, bf16[128,384]{1,0:T(8,128)(2,1)S(1)} %collective-permute-done.7.refs_2_, ...), custom_call_target="tpu_custom_call" | custom-call | flops 100663296 | bytes 4000000 | tf_op jit(solution)/shard_map/pallas_call | solution.py:159
  49.1 0.1 collective-permute-start.12
  49.2 0.0 copy-done.1
  49.2 0.0 copy-done.3
  49.2 0.3 shard_map.77.refs_4_
  49.5 1.5 %collective-permute-start.11 = (bf16[128,384]{1,0:T(8,128)(2,1)S(1)}, bf16[128,384]{1,0:T(8,128)(2,1)S(1)}, u32[]{:S(2)}, u32[]{:S(2)}) collective-permute-start(bf16[128,384]{1,0:T(8,128)(2,1)S(1)} %shard_map.77.refs_4_), channel_id=1, source_target_pairs={{0,24},{8,16},{16,8},{24,0},{1,25},{9,17},{17,9},{25,1},{2,26},{10... | collective-permute-start | bytes 294920 | tf_op jit(solution)/shard_map/ppermute | solution.py:197
  51.0 1.1 %collective-permute-start.10 = (bf16[128,384]{1,0:T(8,128)(2,1)S(1)}, bf16[128,384]{1,0:T(8,128)(2,1)S(1)}, u32[]{:S(2)}, u32[]{:S(2)}) collective-permute-start(bf16[128,384]{1,0:T(8,128)(2,1)S(1)} %shard_map.77.refs_4_), channel_id=1, source_target_pairs={{0,16},{8,24},{16,0},{24,8},{1,17},{9,25},{17,1},{25,9},{2,18},{10... | collective-permute-start | bytes 294920 | tf_op jit(solution)/shard_map/ppermute | solution.py:197
  52.1 0.0 collective-permute-done.12
  52.2 2.5 %collective-permute-start.15 = (f32[3,384]{1,0:T(4,128)S(1)}, f32[3,384]{1,0:T(4,128)S(1)}, u32[]{:S(2)}, u32[]{:S(2)}) collective-permute-start(f32[3,384]{1,0:T(4,128)S(1)} %pad_maximum_fusion.1), channel_id=1, source_target_pairs={{0,6},{1,7},{2,4},{3,5},{4,2},{5,3},{6,0},{7,1},{8,14},{9,15},{10,... | collective-permute-start | bytes 13832 | tf_op jit(solution)/shard_map/ppermute | solution.py:188
  54.7 0.5 collective-permute-start.14
  55.2 0.5 collective-permute-start.13
  55.7 0.1 slice_bitcast_fusion.refs_13_
  55.8 0.9 collective-permute-done.15
  56.8 1.9 %collective-permute-start.9 = (bf16[128,384]{1,0:T(8,128)(2,1)S(1)}, bf16[128,384]{1,0:T(8,128)(2,1)S(1)}, u32[]{:S(2)}, u32[]{:S(2)}) collective-permute-start(bf16[128,384]{1,0:T(8,128)(2,1)S(1)} %shard_map.77.refs_4_), channel_id=1, source_target_pairs={{0,8},{8,0},{16,24},{24,16},{1,9},{9,1},{17,25},{25,17},{2,10},{10... | collective-permute-start | bytes 294920 | tf_op jit(solution)/shard_map/ppermute | solution.py:197
  58.6 0.0 collective-permute-done.14
  58.6 0.2 collective-permute-done.13
  58.9 0.0 collective-permute-done.11.refs_7_
  58.9 2.8 %collective-permute-done.10.refs_6_ = bf16[128,384]{1,0:T(8,128)(2,1)S(1)} collective-permute-done((bf16[128,384]{1,0:T(8,128)(2,1)S(1)}, bf16[128,384]{1,0:T(8,128)(2,1)S(1)}, u32[]{:S(2)}, u32[]{:S(2)}) %collective-permute-start.10) | collective-permute-done | bytes 98336 | tf_op jit(solution)/shard_map/ppermute | solution.py:197
  61.7 0.9 collective-permute-done.9.refs_5_
  62.6 4.7 %shard_map.79 = (bf16[512,768]{1,0:T(8,128)(2,1)S(1)}, f32[512,384]{1,0:T(8,128)S(1)}, f32[512,384]{1,0:T(8,128)S(1)}, f32[3,384]{1,0:T(4,128)S(1)}) custom-call(s32[4,4]{1,0:T(4,128)S(1)} %pad_add_fusion.cols, bf16[128,384]{1,0:T(8,128)(2,1)S(1)} %shard_map.76.refs_0_, bf16[128,384]{1,0:T(8,128)(2,1)S(1)} %collective-permute-done.6.refs_1_, ...), custom_call_target="tpu_custom_call" | custom-call | flops 905969664 | bytes 4000000 | tf_op jit(solution)/shard_map/pallas_call | solution.py:159
  67.4 0.1 collective-permute-start.16
  67.4 1.2 %collective-permute-done.16 = f32[3,384]{1,0:T(4,128)S(1)} collective-permute-done((f32[3,384]{1,0:T(4,128)S(1)}, f32[3,384]{1,0:T(4,128)S(1)}, u32[]{:S(2)}, u32[]{:S(2)}) %collective-permute-start.16) | collective-permute-done | bytes 4640 | tf_op jit(solution)/shard_map/ppermute | solution.py:185
  68.6 2.5 %collective-permute-start.19 = (f32[3,384]{1,0:T(4,128)S(1)}, f32[3,384]{1,0:T(4,128)S(1)}, u32[]{:S(2)}, u32[]{:S(2)}) collective-permute-start(f32[3,384]{1,0:T(4,128)S(1)} %pad_maximum_fusion.3), channel_id=1, source_target_pairs={{0,6},{1,7},{2,4},{3,5},{4,2},{5,3},{6,0},{7,1},{8,14},{9,15},{10,... | collective-permute-start | bytes 13832 | tf_op jit(solution)/shard_map/ppermute | solution.py:188
  71.2 0.5 collective-permute-start.18
  71.7 0.5 collective-permute-start.17
  72.2 1.0 %collective-permute-done.19 = f32[3,384]{1,0:T(4,128)S(1)} collective-permute-done((f32[3,384]{1,0:T(4,128)S(1)}, f32[3,384]{1,0:T(4,128)S(1)}, u32[]{:S(2)}, u32[]{:S(2)}) %collective-permute-start.19) | collective-permute-done | bytes 4640 | tf_op jit(solution)/shard_map/ppermute | solution.py:188
  73.2 1.6 %collective-permute-done.18 = f32[3,384]{1,0:T(4,128)S(1)} collective-permute-done((f32[3,384]{1,0:T(4,128)S(1)}, f32[3,384]{1,0:T(4,128)S(1)}, u32[]{:S(2)}, u32[]{:S(2)}) %collective-permute-start.18) | collective-permute-done | bytes 4640 | tf_op jit(solution)/shard_map/ppermute | solution.py:188
  74.8 0.5 collective-permute-done.17
  75.4 3.9 %shard_map.80 = (bf16[128,1152]{1,0:T(8,128)(2,1)}, f32[1,384]{1,0:T(1,128)S(1)}, bf16[4,144,576]{2,1,0:T(8,128)(2,1)S(1)}, bf16[4,144,576]{2,1,0:T(8,128)(2,1)S(1)}) custom-call(s32[4,4]{1,0:T(4,128)S(1)} %pad_add_fusion.cols, bf16[1024,128]{1,0:T(8,128)(2,1)S(1)} %pad_maximum_fusion.refs_4_.refs_8_.refs_0_, ...), custom_call_target="tpu_custom_call" | custom-call | flops 679477248 | bytes 4000000 | tf_op jit(solution)/shard_map/pallas_call | solution.py:159
  79.3 0.0 collective-permute-start.20
  79.3 2.2 %collective-permute-done.20 = bf16[4,144,576]{2,1,0:T(8,128)(2,1)S(1)} collective-permute-done((bf16[4,144,576]{2,1,0:T(8,128)(2,1)S(1)}, bf16[4,144,576]{2,1,0:T(8,128)(2,1)S(1)}, u32[]{:S(2)}, u32[]{:S(2)}) %collective-permute-start.20) | collective-permute-done | bytes 663584 | tf_op jit(solution)/shard_map/ppermute | solution.py:276
  81.5 0.2 add_convert_fusion
  81.7 0.1 slice_bitcast_fusion.3
  81.8 0.6 collective-permute-start.21
  82.3 2.4 %collective-permute-start.23 = (bf16[144,576]{1,0:T(8,128)(2,1)S(1)}, bf16[144,576]{1,0:T(8,128)(2,1)S(1)}, u32[]{:S(2)}, u32[]{:S(2)}) collective-permute-start(bf16[144,576]{1,0:T(8,128)(2,1)S(1)} %get-tuple-element.28), channel_id=1, source_target_pairs={{0,6},{1,7},{2,4},{3,5},{4,2},{5,3},{6,0},{7,1},{8,14},{9,15},{10,... | collective-permute-start | bytes 497672 | tf_op jit(solution)/shard_map/ppermute | solution.py:280
  84.8 0.5 collective-permute-start.22
  85.3 0.6 reduce
  85.9 3.4 %collective-permute-done.21 = bf16[144,576]{1,0:T(8,128)(2,1)S(1)} collective-permute-done((bf16[144,576]{1,0:T(8,128)(2,1)S(1)}, bf16[144,576]{1,0:T(8,128)(2,1)S(1)}, u32[]{:S(2)}, u32[]{:S(2)}) %collective-permute-start.21) | collective-permute-done | bytes 165920 | tf_op jit(solution)/shard_map/ppermute | solution.py:280
  89.3 4.2 %collective-permute-done.23 = bf16[144,576]{1,0:T(8,128)(2,1)S(1)} collective-permute-done((bf16[144,576]{1,0:T(8,128)(2,1)S(1)}, bf16[144,576]{1,0:T(8,128)(2,1)S(1)}, u32[]{:S(2)}, u32[]{:S(2)}) %collective-permute-start.23) | collective-permute-done | bytes 165920 | tf_op jit(solution)/shard_map/ppermute | solution.py:280
  93.5 1.4 %collective-permute-done.22 = bf16[144,576]{1,0:T(8,128)(2,1)S(1)} collective-permute-done((bf16[144,576]{1,0:T(8,128)(2,1)S(1)}, bf16[144,576]{1,0:T(8,128)(2,1)S(1)}, u32[]{:S(2)}, u32[]{:S(2)}) %collective-permute-start.22) | collective-permute-done | bytes 165920 | tf_op jit(solution)/shard_map/ppermute | solution.py:280
  94.9 0.1 fusion.1
  95.0 1.1 %reshape.11 = f32[144,2,288]{2,1,0:T(2,128)} reshape(f32[144,576]{1,0:T(8,128)S(1)} %fusion.1) | data formatting | bytes 663552 | tf_op jit(solution)/shard_map/reshape | solution.py:283
  (15 shorter events, 0.2 us)
Async XLA Ops:
  1.6 45.9 %collective-permute-start.5 = (bf16[1024,128]{1,0:T(8,128)(2,1)S(1)}, bf16[1024,128]{1,0:T(8,128)(2,1)S(1)}, u32[]{:S(2)}, u32[]{:S(2)}) collective-permute-start(bf16[1024,128]{1,0:T(8,128)(2,1)S(1)} %pad_maximum_fusion.refs_4_.refs_8_.refs_0_), channel_id=1, source_target_pairs={{0,24},{8,16},{16,8},{24,0},{1,25},{9,17},{17,9},{25,1},{2,26},{10... | collective-permute-start | bytes 786440 | tf_op jit(solution)/shard_map/ppermute | solution.py:197
  6.7 40.8 %collective-permute-start.4 = (bf16[1024,128]{1,0:T(8,128)(2,1)S(1)}, bf16[1024,128]{1,0:T(8,128)(2,1)S(1)}, u32[]{:S(2)}, u32[]{:S(2)}) collective-permute-start(bf16[1024,128]{1,0:T(8,128)(2,1)S(1)} %pad_maximum_fusion.refs_4_.refs_8_.refs_0_), channel_id=1, source_target_pairs={{0,16},{8,24},{16,0},{24,8},{1,17},{9,25},{17,1},{25,9},{2,18},{10... | collective-permute-start | bytes 786440 | tf_op jit(solution)/shard_map/ppermute | solution.py:197
  6.7 40.8 %collective-permute-start.3 = (bf16[1024,128]{1,0:T(8,128)(2,1)S(1)}, bf16[1024,128]{1,0:T(8,128)(2,1)S(1)}, u32[]{:S(2)}, u32[]{:S(2)}) collective-permute-start(bf16[1024,128]{1,0:T(8,128)(2,1)S(1)} %pad_maximum_fusion.refs_4_.refs_8_.refs_0_), channel_id=1, source_target_pairs={{0,8},{8,0},{16,24},{24,16},{1,9},{9,1},{17,25},{25,17},{2,10},{10... | collective-permute-start | bytes 786440 | tf_op jit(solution)/shard_map/ppermute | solution.py:197
  7.4 2.0 %copy-start = (bf16[2,1152,768]{2,1,0:T(8,128)(2,1)S(1)}, bf16[2,1152,768]{2,1,0:T(8,128)(2,1)}, u32[]{:S(2)}) copy-start(bf16[2,1152,768]{2,1,0:T(8,128)(2,1)} %coeffs.3) | copy-start | bytes 10616836
  9.4 1.0 %copy-start.2 = (bf16[1,128,1152]{2,1,0:T(8,128)(2,1)S(1)}, bf16[1,128,1152]{2,1,0:T(8,128)(2,1)}, u32[]{:S(2)}) copy-start(bf16[1,128,1152]{2,1,0:T(8,128)(2,1)} %param.5) | copy-start | bytes 884740
  10.3 4.1 %copy-start.4 = (s32[1,1,4]{2,1,0:T(1,128)S(1)}, s32[1,1,4]{2,1,0:T(1,128)}, u32[]{:S(2)}) copy-start(s32[1,1,4]{2,1,0:T(1,128)} %param.9) | copy-start | bytes 52
  10.3 38.9 %copy-start.1 = (bf16[2,1152,768]{2,1,0:T(8,128)(2,1)S(1)}, bf16[2,1152,768]{2,1,0:T(8,128)(2,1)}, u32[]{:S(2)}) copy-start(bf16[2,1152,768]{2,1,0:T(8,128)(2,1)} %coeffs.3) | copy-start | bytes 10616836
  10.3 38.9 %copy-start.3 = (bf16[1,128,1152]{2,1,0:T(8,128)(2,1)S(1)}, bf16[1,128,1152]{2,1,0:T(8,128)(2,1)}, u32[]{:S(2)}) copy-start(bf16[1,128,1152]{2,1,0:T(8,128)(2,1)} %param.5) | copy-start | bytes 884740
  10.7 32.2 %collective-permute-start.8 = (bf16[128,384]{1,0:T(8,128)(2,1)S(1)}, bf16[128,384]{1,0:T(8,128)(2,1)S(1)}, u32[]{:S(2)}, u32[]{:S(2)}) collective-permute-start(bf16[128,384]{1,0:T(8,128)(2,1)S(1)} %shard_map.76.refs_0_), channel_id=1, source_target_pairs={{0,24},{8,16},{16,8},{24,0},{1,25},{9,17},{17,9},{25,1},{2,26},{10... | collective-permute-start | bytes 294920 | tf_op jit(solution)/shard_map/ppermute | solution.py:197
  14.5 12.2 %collective-permute-start.2 = (s32[1,4]{1,0:T(1,128)S(1)}, s32[1,4]{1,0:T(1,128)S(1)}, u32[]{:S(2)}, u32[]{:S(2)}) collective-permute-start(s32[1,4]{1,0:T(1,128)S(1)} %bitcast.22), channel_id=1, source_target_pairs={{0,24},{8,16},{16,8},{24,0},{1,25},{9,17},{17,9},{25,1},{2,26},{10... | collective-permute-start | bytes 56 | tf_op jit(solution)/shard_map/ppermute | solution.py:197
  26.6 9.8 %collective-permute-start.1 = (s32[1,4]{1,0:T(1,128)S(1)}, s32[1,4]{1,0:T(1,128)S(1)}, u32[]{:S(2)}, u32[]{:S(2)}) collective-permute-start(s32[1,4]{1,0:T(1,128)S(1)} %bitcast.23), channel_id=1, source_target_pairs={{0,16},{8,24},{16,0},{24,8},{1,17},{9,25},{17,1},{25,9},{2,18},{10... | collective-permute-start | bytes 56 | tf_op jit(solution)/shard_map/ppermute | solution.py:197
  36.4 3.5 %collective-permute-start = (s32[1,4]{1,0:T(1,128)S(1)}, s32[1,4]{1,0:T(1,128)S(1)}, u32[]{:S(2)}, u32[]{:S(2)}) collective-permute-start(s32[1,4]{1,0:T(1,128)S(1)} %bitcast.24), channel_id=1, source_target_pairs={{0,8},{8,0},{16,24},{24,16},{1,9},{9,1},{17,25},{25,17},{2,10},{10... | collective-permute-start | bytes 56 | tf_op jit(solution)/shard_map/ppermute | solution.py:197
  40.0 5.5 %collective-permute-start.7 = (bf16[128,384]{1,0:T(8,128)(2,1)S(1)}, bf16[128,384]{1,0:T(8,128)(2,1)S(1)}, u32[]{:S(2)}, u32[]{:S(2)}) collective-permute-start(bf16[128,384]{1,0:T(8,128)(2,1)S(1)} %shard_map.76.refs_0_), channel_id=1, source_target_pairs={{0,16},{8,24},{16,0},{24,8},{1,17},{9,25},{17,1},{25,9},{2,18},{10... | collective-permute-start | bytes 294920 | tf_op jit(solution)/shard_map/ppermute | solution.py:197
  42.9 4.6 %collective-permute-start.6 = (bf16[128,384]{1,0:T(8,128)(2,1)S(1)}, bf16[128,384]{1,0:T(8,128)(2,1)S(1)}, u32[]{:S(2)}, u32[]{:S(2)}) collective-permute-start(bf16[128,384]{1,0:T(8,128)(2,1)S(1)} %shard_map.76.refs_0_), channel_id=1, source_target_pairs={{0,8},{8,0},{16,24},{24,16},{1,9},{9,1},{17,25},{25,17},{2,10},{10... | collective-permute-start | bytes 294920 | tf_op jit(solution)/shard_map/ppermute | solution.py:197
  49.1 3.0 %collective-permute-start.12 = (f32[3,384]{1,0:T(4,128)S(1)}, f32[3,384]{1,0:T(4,128)S(1)}, u32[]{:S(2)}, u32[]{:S(2)}) collective-permute-start(f32[3,384]{1,0:T(4,128)S(1)} %shard_map.78), channel_id=1, source_target_pairs={{0,1},{1,0},{2,3},{3,2},{4,5},{5,4},{6,7},{7,6},{8,9},{9,8},{10,11... | collective-permute-start | bytes 13832 | tf_op jit(solution)/shard_map/ppermute | solution.py:185
  49.5 9.3 %collective-permute-start.11 = (bf16[128,384]{1,0:T(8,128)(2,1)S(1)}, bf16[128,384]{1,0:T(8,128)(2,1)S(1)}, u32[]{:S(2)}, u32[]{:S(2)}) collective-permute-start(bf16[128,384]{1,0:T(8,128)(2,1)S(1)} %shard_map.77.refs_4_), channel_id=1, source_target_pairs={{0,24},{8,16},{16,8},{24,0},{1,25},{9,17},{17,9},{25,1},{2,26},{10... | collective-permute-start | bytes 294920 | tf_op jit(solution)/shard_map/ppermute | solution.py:197
  51.0 10.7 %collective-permute-start.10 = (bf16[128,384]{1,0:T(8,128)(2,1)S(1)}, bf16[128,384]{1,0:T(8,128)(2,1)S(1)}, u32[]{:S(2)}, u32[]{:S(2)}) collective-permute-start(bf16[128,384]{1,0:T(8,128)(2,1)S(1)} %shard_map.77.refs_4_), channel_id=1, source_target_pairs={{0,16},{8,24},{16,0},{24,8},{1,17},{9,25},{17,1},{25,9},{2,18},{10... | collective-permute-start | bytes 294920 | tf_op jit(solution)/shard_map/ppermute | solution.py:197
  52.2 4.6 %collective-permute-start.15 = (f32[3,384]{1,0:T(4,128)S(1)}, f32[3,384]{1,0:T(4,128)S(1)}, u32[]{:S(2)}, u32[]{:S(2)}) collective-permute-start(f32[3,384]{1,0:T(4,128)S(1)} %pad_maximum_fusion.1), channel_id=1, source_target_pairs={{0,6},{1,7},{2,4},{3,5},{4,2},{5,3},{6,0},{7,1},{8,14},{9,15},{10,... | collective-permute-start | bytes 13832 | tf_op jit(solution)/shard_map/ppermute | solution.py:188
  54.7 4.0 %collective-permute-start.14 = (f32[3,384]{1,0:T(4,128)S(1)}, f32[3,384]{1,0:T(4,128)S(1)}, u32[]{:S(2)}, u32[]{:S(2)}) collective-permute-start(f32[3,384]{1,0:T(4,128)S(1)} %pad_maximum_fusion.1), channel_id=1, source_target_pairs={{0,4},{1,5},{2,6},{3,7},{4,0},{5,1},{6,2},{7,3},{8,12},{9,13},{10,... | collective-permute-start | bytes 13832 | tf_op jit(solution)/shard_map/ppermute | solution.py:188
  55.2 3.6 %collective-permute-start.13 = (f32[3,384]{1,0:T(4,128)S(1)}, f32[3,384]{1,0:T(4,128)S(1)}, u32[]{:S(2)}, u32[]{:S(2)}) collective-permute-start(f32[3,384]{1,0:T(4,128)S(1)} %pad_maximum_fusion.1), channel_id=1, source_target_pairs={{0,2},{1,3},{2,0},{3,1},{4,6},{5,7},{6,4},{7,5},{8,10},{9,11},{10,... | collective-permute-start | bytes 13832 | tf_op jit(solution)/shard_map/ppermute | solution.py:188
  56.8 5.9 %collective-permute-start.9 = (bf16[128,384]{1,0:T(8,128)(2,1)S(1)}, bf16[128,384]{1,0:T(8,128)(2,1)S(1)}, u32[]{:S(2)}, u32[]{:S(2)}) collective-permute-start(bf16[128,384]{1,0:T(8,128)(2,1)S(1)} %shard_map.77.refs_4_), channel_id=1, source_target_pairs={{0,8},{8,0},{16,24},{24,16},{1,9},{9,1},{17,25},{25,17},{2,10},{10... | collective-permute-start | bytes 294920 | tf_op jit(solution)/shard_map/ppermute | solution.py:197
  67.4 1.2 %collective-permute-start.16 = (f32[3,384]{1,0:T(4,128)S(1)}, f32[3,384]{1,0:T(4,128)S(1)}, u32[]{:S(2)}, u32[]{:S(2)}) collective-permute-start(f32[3,384]{1,0:T(4,128)S(1)} %get-tuple-element.14), channel_id=1, source_target_pairs={{0,1},{1,0},{2,3},{3,2},{4,5},{5,4},{6,7},{7,6},{8,9},{9,8},{10,11... | collective-permute-start | bytes 13832 | tf_op jit(solution)/shard_map/ppermute | solution.py:185
  68.6 4.6 %collective-permute-start.19 = (f32[3,384]{1,0:T(4,128)S(1)}, f32[3,384]{1,0:T(4,128)S(1)}, u32[]{:S(2)}, u32[]{:S(2)}) collective-permute-start(f32[3,384]{1,0:T(4,128)S(1)} %pad_maximum_fusion.3), channel_id=1, source_target_pairs={{0,6},{1,7},{2,4},{3,5},{4,2},{5,3},{6,0},{7,1},{8,14},{9,15},{10,... | collective-permute-start | bytes 13832 | tf_op jit(solution)/shard_map/ppermute | solution.py:188
  71.2 3.6 %collective-permute-start.18 = (f32[3,384]{1,0:T(4,128)S(1)}, f32[3,384]{1,0:T(4,128)S(1)}, u32[]{:S(2)}, u32[]{:S(2)}) collective-permute-start(f32[3,384]{1,0:T(4,128)S(1)} %pad_maximum_fusion.3), channel_id=1, source_target_pairs={{0,4},{1,5},{2,6},{3,7},{4,0},{5,1},{6,2},{7,3},{8,12},{9,13},{10,... | collective-permute-start | bytes 13832 | tf_op jit(solution)/shard_map/ppermute | solution.py:188
  71.7 3.6 %collective-permute-start.17 = (f32[3,384]{1,0:T(4,128)S(1)}, f32[3,384]{1,0:T(4,128)S(1)}, u32[]{:S(2)}, u32[]{:S(2)}) collective-permute-start(f32[3,384]{1,0:T(4,128)S(1)} %pad_maximum_fusion.3), channel_id=1, source_target_pairs={{0,2},{1,3},{2,0},{3,1},{4,6},{5,7},{6,4},{7,5},{8,10},{9,11},{10,... | collective-permute-start | bytes 13832 | tf_op jit(solution)/shard_map/ppermute | solution.py:188
  79.3 2.2 %collective-permute-start.20 = (bf16[4,144,576]{2,1,0:T(8,128)(2,1)S(1)}, bf16[4,144,576]{2,1,0:T(8,128)(2,1)S(1)}, u32[]{:S(2)}, u32[]{:S(2)}) collective-permute-start(bf16[4,144,576]{2,1,0:T(8,128)(2,1)S(1)} %get-tuple-element.18), channel_id=1, source_target_pairs={{0,1},{1,0},{2,3},{3,2},{4,5},{5,4},{6,7},{7,6},{8,9},{9,8},{10,11... | collective-permute-start | bytes 1990664 | tf_op jit(solution)/shard_map/ppermute | solution.py:276
  81.8 7.5 %collective-permute-start.21 = (bf16[144,576]{1,0:T(8,128)(2,1)S(1)}, bf16[144,576]{1,0:T(8,128)(2,1)S(1)}, u32[]{:S(2)}, u32[]{:S(2)}) collective-permute-start(bf16[144,576]{1,0:T(8,128)(2,1)S(1)} %get-tuple-element.27), channel_id=1, source_target_pairs={{0,2},{1,3},{2,0},{3,1},{4,6},{5,7},{6,4},{7,5},{8,10},{9,11},{10,... | collective-permute-start | bytes 497672 | tf_op jit(solution)/shard_map/ppermute | solution.py:280
  82.3 11.2 %collective-permute-start.23 = (bf16[144,576]{1,0:T(8,128)(2,1)S(1)}, bf16[144,576]{1,0:T(8,128)(2,1)S(1)}, u32[]{:S(2)}, u32[]{:S(2)}) collective-permute-start(bf16[144,576]{1,0:T(8,128)(2,1)S(1)} %get-tuple-element.28), channel_id=1, source_target_pairs={{0,6},{1,7},{2,4},{3,5},{4,2},{5,3},{6,0},{7,1},{8,14},{9,15},{10,... | collective-permute-start | bytes 497672 | tf_op jit(solution)/shard_map/ppermute | solution.py:280
  84.8 10.1 %collective-permute-start.22 = (bf16[144,576]{1,0:T(8,128)(2,1)S(1)}, bf16[144,576]{1,0:T(8,128)(2,1)S(1)}, u32[]{:S(2)}, u32[]{:S(2)}) collective-permute-start(bf16[144,576]{1,0:T(8,128)(2,1)S(1)} %get-tuple-element.29), channel_id=1, source_target_pairs={{0,4},{1,5},{2,6},{3,7},{4,0},{5,1},{6,2},{7,3},{8,12},{9,13},{10,... | collective-permute-start | bytes 497672 | tf_op jit(solution)/shard_map/ppermute | solution.py:280

commit v3 on v2

--- a/solution.py
+++ b/solution.py
@@ -53,37 +53,40 @@
     return shift, scale
 
 
-def turn_kernel(current, coeffs, out_ref):
-    out_ref[...] = jnp.dot(current[...], coeffs[0], preferred_element_type=f32).astype(bf16)
-
-
-def turn_part(current, coeffs, sweep, part, modes):
+def turn_kernel(modes, current, coeffs, first_ref, later_ref):
+    turned = jnp.dot(current[...], coeffs[0], preferred_element_type=f32).astype(bf16)
+    first_ref[...] = turned[:, :modes]
+    later_ref[...] = turned[:, modes:]
+
+
+def turn_first(current, coeffs, modes):
     rows, columns = current.shape
+    half = jax.ShapeDtypeStruct((rows, modes), bf16)
     return pl.pallas_call(
-        turn_kernel,
+        functools.partial(turn_kernel, modes),
         grid=(1,),
-        out_shape=jax.ShapeDtypeStruct((rows, modes), bf16),
+        out_shape=(half, half),
         in_specs=[
             pl.BlockSpec((rows, columns), lambda i: (0, 0)),
-            pl.BlockSpec((1, columns, modes), lambda i: (sweep, 0, part)),
-        ],
-        out_specs=pl.BlockSpec((rows, modes), lambda i: (0, 0)),
+            pl.BlockSpec((1, columns, 2 * modes), lambda i: (0, 0, 0)),
+        ],
+        out_specs=(pl.BlockSpec((rows, modes), lambda i: (0, 0)),) * 2,
         compiler_params=pltpu.CompilerParams(vmem_limit_bytes=VMEM_BYTES),
         cost_estimate=pl.CostEstimate(
-            flops=2 * rows * columns * modes, bytes_accessed=2 * columns * modes, transcendentals=0
+            flops=4 * rows * columns * modes, bytes_accessed=4 * columns * modes, transcendentals=0
         ),
     )(current, coeffs)
 
 
-def stats_kernel(nz, slots, edge, modes, rows_of, cols, *refs):
-    x_refs, km_refs = refs[:nz], refs[nz : nz + rows_of]
-    stats_ref, field, stiff, mass = refs[nz + rows_of :]
+def stats_kernel(nz, slots, edge, cols, *refs):
+    x_refs, km_refs = refs[:nz], refs[nz : 2 * nz]
+    _, stats_ref, field, stiff, mass = refs[2 * nz :]
     z = lax.axis_index("blk")
     for k in range(nz):
         field[pl.ds(pl.multiple_of((z ^ k) * edge, edge), edge), :] = x_refs[k][...]
-    for k in range(rows_of):
+    for k in range(nz):
         both = block_dot(km_refs[k], slots, edge, cols, k, field, slice(None))
-        at = pl.ds(pl.multiple_of((z ^ k) * edge, edge), edge) if rows_of > 1 else slice(None)
+        at = pl.ds(pl.multiple_of((z ^ k) * edge, edge), edge)
         stiff[at, :] = both[:edge]
         mass[at, :] = both[edge:]
     num, den, about = column_stats(stiff[...], mass[...])
@@ -207,23 +210,24 @@
     total_rows = rows * ng
     width = columns // nz
 
+    tag = jnp.pad(block_cols[0, 0].astype(bf16)[None, :], ((0, 15), (0, edge - slots)))
     payload = jnp.concatenate(
         [
             stiff_blocks[0, 0].reshape(slots * edge, edge),
             mass_blocks[0, 0].reshape(slots * edge, edge),
+            tag,
         ],
         axis=0,
     )
-    first = turn_part(current, coeffs, 0, 0, modes)
+    first, later = turn_first(current, coeffs, modes)
     x_parts = gather(first, nz)
     km_parts = gather(payload, nz)
-    later = turn_part(current, coeffs, 0, 1, modes)
     h_parts = gather(later, nz)
 
-    cols = jnp.concatenate(gather(block_cols[0], nz))
+    cols = jnp.stack([p[2 * slots * edge, :slots] for p in km_parts]).astype(jnp.int32)
     stats = call(
-        functools.partial(stats_kernel, nz, slots, edge, modes, nz),
-        [cols, *x_parts, *km_parts],
+        functools.partial(stats_kernel, nz, slots, edge),
+        [cols, *x_parts, *km_parts, h_parts[1]],
         1,
         jax.ShapeDtypeStruct((3, modes), f32),
         [

time: 96.3 us -> 86.5 us (0.90)
  waiting for transfers between devices: 39.9 us -> 33.4 us
  starting transfers between devices: 38.2 us -> 34.5 us
    ppermute x12 -> x9, waiting for transfers between devices: 23.4 us -> 15 us  [gather(): return [x] + [lax.ppermute(x, 'blk', by_xor(nz, k)) for k in range(1, nz)]]
    ppermute x12 -> x9, starting transfers between devices: 27.4 us -> 23.7 us  [gather(): return [x] + [lax.ppermute(x, 'blk', by_xor(nz, k)) for k in range(1, nz)]]
    ppermute x6, waiting for transfers between devices: 4.2 us -> 6.06 us  [merge_over(): got = [lax.ppermute(stats, axis, by_xor(size, 2 * k)) for k in (1, 2, 3)]]
    unnamed x10 -> x6, local copies, waits for them, and re-layouts: 2.97 us -> 2.97 us
  transfers between devices with their start and end apart: 24 -> 21, of which waited for: 17 -> 14; matrix products, arithmetic and copies ran while one was open for 1% -> 1% of each run, Pallas kernels for 1% -> 0%
where the time goes in v3:
time: 86.5 us; the launch traced here: 86.3 us
  starting transfers between devices  34.5 us (40%)
  waiting for transfers between devices  33.4 us (39%)
  Pallas kernels  10.7 us (12%)
  local copies, waits for them, and re-layouts  4.23 us (5%)
  other arithmetic  2.72 us (3%)
    ppermute x9, starting transfers between devices, gather(): return [x] + [lax.ppermute(x, 'blk', by_xor(nz, k)) for k in range(1, nz)]  23.7 us
    ppermute x9, waiting for transfers between devices, gather(): return [x] + [lax.ppermute(x, 'blk', by_xor(nz, k)) for k in range(1, nz)]  15 us
    pallas_call x3, Pallas kernels, call(): pl.pallas_call(kernel, out_shape=out_shape, in_specs=[smem()] * n_smem +...  10.2 us
    ppermute x3, waiting for transfers between devices, body(): total = total + lax.ppermute(mine[k], 'grp', by_xor(ng, 2 * k)).astype(f32)  8.97 us
    ppermute x6, starting transfers between devices, merge_over(): got = [lax.ppermute(stats, axis, by_xor(size, 2 * k)) for k in (1, 2, 3)]  7.11 us
    ppermute x6, waiting for transfers between devices, merge_over(): got = [lax.ppermute(stats, axis, by_xor(size, 2 * k)) for k in (1, 2, 3)]  6.06 us
    ppermute x3, starting transfers between devices, body(): total = total + lax.ppermute(mine[k], 'grp', by_xor(ng, 2 * k)).astype(f32)  3.55 us
    unnamed x6, local copies, waits for them, and re-layouts  2.97 us
  transfers between devices with their start and end apart: 21, of which 14 were waited for; matrix products, arithmetic and copies ran while one was open for 1% of the time, Pallas kernels for 0%

profile of v3, /device:TPU:0, one launch (start us, length us, event | category | flops | bytes accessed | tf_op | source)
XLA Modules:
  0.0 86.3 jit_solution(9096178366134462169)
XLA Ops:
  0.6 0.7 convert_bitcast_fusion
  1.3 1.0 %fusion.3.refs_4_.refs_8_.refs_0_ = bf16[1040,128]{1,0:T(8,128)(2,1)S(1)} fusion(bf16[1,4]{1,0:T(2,128)(2,1)S(1)} %convert_bitcast_fusion, bf16[512,128]{1,0:T(8,128)(2,1)} %bitcast.20, bf16[512,128]{1,0:T(8,128)(2,1)} %bitcast.21), kind=kLoop, calls=%fused_computation.7 | loop fusion | flops 1064960 | bytes 528392 | tf_op jit(solution)/shard_map/concatenate | solution.py:214
  2.3 5.1 %collective-permute-start.2 = (bf16[1040,128]{1,0:T(8,128)(2,1)S(1)}, bf16[1040,128]{1,0:T(8,128)(2,1)S(1)}, u32[]{:S(2)}, u32[]{:S(2)}) collective-permute-start(bf16[1040,128]{1,0:T(8,128)(2,1)S(1)} %fusion.3.refs_4_.refs_8_.refs_0_), channel_id=1, source_target_pairs={{0,24},{8,16},{16,8},{24,0},{1,25},{9,17},{17,9},{25,1},{2,26},{10... | collective-permute-start | bytes 798728 | tf_op jit(solution)/shard_map/ppermute | solution.py:200
  7.4 0.0 collective-permute-start.1
  7.4 0.6 collective-permute-start
  8.0 0.0 copy-start
  8.0 2.0 %copy-done = bf16[2,1152,768]{2,1,0:T(8,128)(2,1)S(1)} copy-done((bf16[2,1152,768]{2,1,0:T(8,128)(2,1)S(1)}, bf16[2,1152,768]{2,1,0:T(8,128)(2,1)}, u32[]{:S(2)}) %copy-start) | copy-done | bytes 3538968
  10.0 0.0 copy-start.2
  10.0 1.0 %copy-done.2 = bf16[1,128,1152]{2,1,0:T(8,128)(2,1)S(1)} copy-done((bf16[1,128,1152]{2,1,0:T(8,128)(2,1)S(1)}, bf16[1,128,1152]{2,1,0:T(8,128)(2,1)}, u32[]{:S(2)}) %copy-start.2) | copy-done | bytes 294936
  11.0 0.0 copy-start.1
  11.0 0.4 shard_map.76
  11.4 3.8 %collective-permute-start.5 = (bf16[128,384]{1,0:T(8,128)(2,1)S(1)}, bf16[128,384]{1,0:T(8,128)(2,1)S(1)}, u32[]{:S(2)}, u32[]{:S(2)}) collective-permute-start(bf16[128,384]{1,0:T(8,128)(2,1)S(1)} %get-tuple-element.13.refs_0_), channel_id=1, source_target_pairs={{0,24},{8,16},{16,8},{24,0},{1,25},{9,17},{17,9},{25,1},{2,26},{10... | collective-permute-start | bytes 294920 | tf_op jit(solution)/shard_map/ppermute | solution.py:200
  15.2 0.0 collective-permute-start.4
  15.2 0.0 collective-permute-done.2.refs_7_.refs_11_.refs_3_
  15.3 11.5 %collective-permute-start.3 = (bf16[128,384]{1,0:T(8,128)(2,1)S(1)}, bf16[128,384]{1,0:T(8,128)(2,1)S(1)}, u32[]{:S(2)}, u32[]{:S(2)}) collective-permute-start(bf16[128,384]{1,0:T(8,128)(2,1)S(1)} %get-tuple-element.13.refs_0_), channel_id=1, source_target_pairs={{0,8},{8,0},{16,24},{24,16},{1,9},{9,1},{17,25},{25,17},{2,10},{10... | collective-permute-start | bytes 294920 | tf_op jit(solution)/shard_map/ppermute | solution.py:200
  26.7 8.5 %collective-permute-done.1.refs_6_.refs_10_.refs_2_ = bf16[1040,128]{1,0:T(8,128)(2,1)S(1)} collective-permute-done((bf16[1040,128]{1,0:T(8,128)(2,1)S(1)}, bf16[1040,128]{1,0:T(8,128)(2,1)S(1)}, u32[]{:S(2)}, u32[]{:S(2)}) %collective-permute-start.1) | collective-permute-done | bytes 266272 | tf_op jit(solution)/shard_map/ppermute | solution.py:200
  35.2 0.0 collective-permute-start.6
  35.2 0.0 collective-permute-done.refs_5_.refs_9_.refs_1_
  35.3 4.7 %collective-permute-done.6.refs_8_.refs_5_ = bf16[128,384]{1,0:T(8,128)(2,1)S(1)} collective-permute-done((bf16[128,384]{1,0:T(8,128)(2,1)S(1)}, bf16[128,384]{1,0:T(8,128)(2,1)S(1)}, u32[]{:S(2)}, u32[]{:S(2)}) %collective-permute-start.6) | collective-permute-done | bytes 98336 | tf_op jit(solution)/shard_map/ppermute | solution.py:200
  39.9 0.0 collective-permute-done.5.refs_3_
  39.9 0.0 collective-permute-done.4.refs_2_
  39.9 0.0 collective-permute-done.3.refs_1_
  39.9 1.6 %shard_map.77 = f32[3,384]{1,0:T(4,128)S(1)} custom-call(s32[4,4]{1,0:T(4,128)S(1)} %maximum_convert_fusion.cols, bf16[128,384]{1,0:T(8,128)(2,1)S(1)} %get-tuple-element.13.refs_0_, bf16[128,384]{1,0:T(8,128)(2,1)S(1)} %collective-permute-done.3.refs_1_, bf16[128,384]{1,0:T(8,128)(2,1)S(1)} %collective-permute-done.4.refs_2_, ...), custom_call_target="tpu_custom_call" | custom-call | flops 100663296 | bytes 4000000 | tf_op jit(solution)/shard_map/pallas_call | solution.py:162
  41.5 0.1 collective-permute-start.9
  41.6 2.6 %collective-permute-start.8 = (bf16[128,384]{1,0:T(8,128)(2,1)S(1)}, bf16[128,384]{1,0:T(8,128)(2,1)S(1)}, u32[]{:S(2)}, u32[]{:S(2)}) collective-permute-start(bf16[128,384]{1,0:T(8,128)(2,1)S(1)} %get-tuple-element.14.refs_4_), channel_id=1, source_target_pairs={{0,24},{8,16},{16,8},{24,0},{1,25},{9,17},{17,9},{25,1},{2,26},{10... | collective-permute-start | bytes 294920 | tf_op jit(solution)/shard_map/ppermute | solution.py:200
  44.3 0.0 collective-permute-start.7
  44.3 0.0 collective-permute-done.9
  44.3 2.5 %collective-permute-start.12 = (f32[3,384]{1,0:T(4,128)S(1)}, f32[3,384]{1,0:T(4,128)S(1)}, u32[]{:S(2)}, u32[]{:S(2)}) collective-permute-start(f32[3,384]{1,0:T(4,128)S(1)} %pad_maximum_fusion), channel_id=1, source_target_pairs={{0,6},{1,7},{2,4},{3,5},{4,2},{5,3},{6,0},{7,1},{8,14},{9,15},{10,... | collective-permute-start | bytes 13832 | tf_op jit(solution)/shard_map/ppermute | solution.py:191
  46.8 0.5 collective-permute-start.11
  47.3 0.5 collective-permute-start.10
  47.9 0.0 copy-done.1
  47.9 0.1 slice_bitcast_fusion.refs_13_
  48.0 0.9 %collective-permute-done.12 = f32[3,384]{1,0:T(4,128)S(1)} collective-permute-done((f32[3,384]{1,0:T(4,128)S(1)}, f32[3,384]{1,0:T(4,128)S(1)}, u32[]{:S(2)}, u32[]{:S(2)}) %collective-permute-start.12) | collective-permute-done | bytes 4640 | tf_op jit(solution)/shard_map/ppermute | solution.py:191
  48.9 1.5 %collective-permute-done.11 = f32[3,384]{1,0:T(4,128)S(1)} collective-permute-done((f32[3,384]{1,0:T(4,128)S(1)}, f32[3,384]{1,0:T(4,128)S(1)}, u32[]{:S(2)}, u32[]{:S(2)}) %collective-permute-start.11) | collective-permute-done | bytes 4640 | tf_op jit(solution)/shard_map/ppermute | solution.py:191
  50.4 0.5 collective-permute-done.10
  51.0 0.0 collective-permute-done.8.refs_7_
  51.0 1.8 %collective-permute-done.7.refs_6_ = bf16[128,384]{1,0:T(8,128)(2,1)S(1)} collective-permute-done((bf16[128,384]{1,0:T(8,128)(2,1)S(1)}, bf16[128,384]{1,0:T(8,128)(2,1)S(1)}, u32[]{:S(2)}, u32[]{:S(2)}) %collective-permute-start.7) | collective-permute-done | bytes 98336 | tf_op jit(solution)/shard_map/ppermute | solution.py:200
  52.8 4.7 %shard_map.78 = (bf16[512,768]{1,0:T(8,128)(2,1)S(1)}, f32[512,384]{1,0:T(8,128)S(1)}, f32[512,384]{1,0:T(8,128)S(1)}, f32[3,384]{1,0:T(4,128)S(1)}) custom-call(s32[4,4]{1,0:T(4,128)S(1)} %maximum_convert_fusion.cols, bf16[128,384]{1,0:T(8,128)(2,1)S(1)} %get-tuple-element.13.refs_0_, bf16[128,384]{1,0:T(8,128)(2,1)S(1)} %collective-permute-done.3.refs_1_, ...), custom_call_target="tpu_custom_call" | custom-call | flops 905969664 | bytes 4000000 | tf_op jit(solution)/shard_map/pallas_call | solution.py:162
  57.5 0.1 collective-permute-start.13
  57.7 1.1 %collective-permute-done.13 = f32[3,384]{1,0:T(4,128)S(1)} collective-permute-done((f32[3,384]{1,0:T(4,128)S(1)}, f32[3,384]{1,0:T(4,128)S(1)}, u32[]{:S(2)}, u32[]{:S(2)}) %collective-permute-start.13) | collective-permute-done | bytes 4640 | tf_op jit(solution)/shard_map/ppermute | solution.py:188
  58.8 2.5 %collective-permute-start.16 = (f32[3,384]{1,0:T(4,128)S(1)}, f32[3,384]{1,0:T(4,128)S(1)}, u32[]{:S(2)}, u32[]{:S(2)}) collective-permute-start(f32[3,384]{1,0:T(4,128)S(1)} %pad_maximum_fusion.2), channel_id=1, source_target_pairs={{0,6},{1,7},{2,4},{3,5},{4,2},{5,3},{6,0},{7,1},{8,14},{9,15},{10,... | collective-permute-start | bytes 13832 | tf_op jit(solution)/shard_map/ppermute | solution.py:191
  61.3 0.5 collective-permute-start.15
  61.8 0.5 collective-permute-start.14
  62.4 1.0 %collective-permute-done.16 = f32[3,384]{1,0:T(4,128)S(1)} collective-permute-done((f32[3,384]{1,0:T(4,128)S(1)}, f32[3,384]{1,0:T(4,128)S(1)}, u32[]{:S(2)}, u32[]{:S(2)}) %collective-permute-start.16) | collective-permute-done | bytes 4640 | tf_op jit(solution)/shard_map/ppermute | solution.py:191
  63.4 1.5 %collective-permute-done.15 = f32[3,384]{1,0:T(4,128)S(1)} collective-permute-done((f32[3,384]{1,0:T(4,128)S(1)}, f32[3,384]{1,0:T(4,128)S(1)}, u32[]{:S(2)}, u32[]{:S(2)}) %collective-permute-start.15) | collective-permute-done | bytes 4640 | tf_op jit(solution)/shard_map/ppermute | solution.py:191
  65.0 0.5 collective-permute-done.14
  65.5 3.9 %shard_map.79 = (bf16[128,1152]{1,0:T(8,128)(2,1)}, f32[1,384]{1,0:T(1,128)S(1)}, bf16[4,144,576]{2,1,0:T(8,128)(2,1)S(1)}, bf16[4,144,576]{2,1,0:T(8,128)(2,1)S(1)}) custom-call(s32[4,4]{1,0:T(4,128)S(1)} %maximum_convert_fusion.cols, bf16[1040,128]{1,0:T(8,128)(2,1)S(1)} %fusion.3.refs_4_.refs_8_.refs_0_, ...), custom_call_target="tpu_custom_call" | custom-call | flops 679477248 | bytes 4000000 | tf_op jit(solution)/shard_map/pallas_call | solution.py:162
  69.5 0.0 collective-permute-start.17
  69.5 2.2 %collective-permute-done.17 = bf16[4,144,576]{2,1,0:T(8,128)(2,1)S(1)} collective-permute-done((bf16[4,144,576]{2,1,0:T(8,128)(2,1)S(1)}, bf16[4,144,576]{2,1,0:T(8,128)(2,1)S(1)}, u32[]{:S(2)}, u32[]{:S(2)}) %collective-permute-start.17) | collective-permute-done | bytes 663584 | tf_op jit(solution)/shard_map/ppermute | solution.py:280
  71.7 0.2 add_convert_fusion
  71.9 0.1 slice_bitcast_fusion.3
  71.9 0.6 collective-permute-start.18
  72.5 2.5 %collective-permute-start.20 = (bf16[144,576]{1,0:T(8,128)(2,1)S(1)}, bf16[144,576]{1,0:T(8,128)(2,1)S(1)}, u32[]{:S(2)}, u32[]{:S(2)}) collective-permute-start(bf16[144,576]{1,0:T(8,128)(2,1)S(1)} %get-tuple-element.32), channel_id=1, source_target_pairs={{0,6},{1,7},{2,4},{3,5},{4,2},{5,3},{6,0},{7,1},{8,14},{9,15},{10,... | collective-permute-start | bytes 497672 | tf_op jit(solution)/shard_map/ppermute | solution.py:284
  75.0 0.5 collective-permute-start.19
  75.5 0.6 reduce
  76.1 3.4 %collective-permute-done.18 = bf16[144,576]{1,0:T(8,128)(2,1)S(1)} collective-permute-done((bf16[144,576]{1,0:T(8,128)(2,1)S(1)}, bf16[144,576]{1,0:T(8,128)(2,1)S(1)}, u32[]{:S(2)}, u32[]{:S(2)}) %collective-permute-start.18) | collective-permute-done | bytes 165920 | tf_op jit(solution)/shard_map/ppermute | solution.py:284
  79.5 4.2 %collective-permute-done.20 = bf16[144,576]{1,0:T(8,128)(2,1)S(1)} collective-permute-done((bf16[144,576]{1,0:T(8,128)(2,1)S(1)}, bf16[144,576]{1,0:T(8,128)(2,1)S(1)}, u32[]{:S(2)}, u32[]{:S(2)}) %collective-permute-start.20) | collective-permute-done | bytes 165920 | tf_op jit(solution)/shard_map/ppermute | solution.py:284
  83.7 1.4 %collective-permute-done.19 = bf16[144,576]{1,0:T(8,128)(2,1)S(1)} collective-permute-done((bf16[144,576]{1,0:T(8,128)(2,1)S(1)}, bf16[144,576]{1,0:T(8,128)(2,1)S(1)}, u32[]{:S(2)}, u32[]{:S(2)}) %collective-permute-start.19) | collective-permute-done | bytes 165920 | tf_op jit(solution)/shard_map/ppermute | solution.py:284
  85.1 0.1 fusion.2
  85.2 1.1 %reshape.22 = f32[144,2,288]{2,1,0:T(2,128)} reshape(f32[144,576]{1,0:T(8,128)S(1)} %fusion.2) | data formatting | bytes 663552 | tf_op jit(solution)/shard_map/reshape | solution.py:287
  (12 shorter events, 0.2 us)
Async XLA Ops:
  2.3 13.0 %collective-permute-start.2 = (bf16[1040,128]{1,0:T(8,128)(2,1)S(1)}, bf16[1040,128]{1,0:T(8,128)(2,1)S(1)}, u32[]{:S(2)}, u32[]{:S(2)}) collective-permute-start(bf16[1040,128]{1,0:T(8,128)(2,1)S(1)} %fusion.3.refs_4_.refs_8_.refs_0_), channel_id=1, source_target_pairs={{0,24},{8,16},{16,8},{24,0},{1,25},{9,17},{17,9},{25,1},{2,26},{10... | collective-permute-start | bytes 798728 | tf_op jit(solution)/shard_map/ppermute | solution.py:200
  7.4 27.8 %collective-permute-start.1 = (bf16[1040,128]{1,0:T(8,128)(2,1)S(1)}, bf16[1040,128]{1,0:T(8,128)(2,1)S(1)}, u32[]{:S(2)}, u32[]{:S(2)}) collective-permute-start(bf16[1040,128]{1,0:T(8,128)(2,1)S(1)} %fusion.3.refs_4_.refs_8_.refs_0_), channel_id=1, source_target_pairs={{0,16},{8,24},{16,0},{24,8},{1,17},{9,25},{17,1},{25,9},{2,18},{10... | collective-permute-start | bytes 798728 | tf_op jit(solution)/shard_map/ppermute | solution.py:200
  7.4 27.8 %collective-permute-start = (bf16[1040,128]{1,0:T(8,128)(2,1)S(1)}, bf16[1040,128]{1,0:T(8,128)(2,1)S(1)}, u32[]{:S(2)}, u32[]{:S(2)}) collective-permute-start(bf16[1040,128]{1,0:T(8,128)(2,1)S(1)} %fusion.3.refs_4_.refs_8_.refs_0_), channel_id=1, source_target_pairs={{0,8},{8,0},{16,24},{24,16},{1,9},{9,1},{17,25},{25,17},{2,10},{10... | collective-permute-start | bytes 798728 | tf_op jit(solution)/shard_map/ppermute | solution.py:200
  8.0 2.0 %copy-start = (bf16[2,1152,768]{2,1,0:T(8,128)(2,1)S(1)}, bf16[2,1152,768]{2,1,0:T(8,128)(2,1)}, u32[]{:S(2)}) copy-start(bf16[2,1152,768]{2,1,0:T(8,128)(2,1)} %coeffs.1) | copy-start | bytes 10616836
  10.0 1.0 %copy-start.2 = (bf16[1,128,1152]{2,1,0:T(8,128)(2,1)S(1)}, bf16[1,128,1152]{2,1,0:T(8,128)(2,1)}, u32[]{:S(2)}) copy-start(bf16[1,128,1152]{2,1,0:T(8,128)(2,1)} %param.5) | copy-start | bytes 884740
  11.0 36.9 %copy-start.1 = (bf16[2,1152,768]{2,1,0:T(8,128)(2,1)S(1)}, bf16[2,1152,768]{2,1,0:T(8,128)(2,1)}, u32[]{:S(2)}) copy-start(bf16[2,1152,768]{2,1,0:T(8,128)(2,1)} %coeffs.1) | copy-start | bytes 10616836
  11.4 28.5 %collective-permute-start.5 = (bf16[128,384]{1,0:T(8,128)(2,1)S(1)}, bf16[128,384]{1,0:T(8,128)(2,1)S(1)}, u32[]{:S(2)}, u32[]{:S(2)}) collective-permute-start(bf16[128,384]{1,0:T(8,128)(2,1)S(1)} %get-tuple-element.13.refs_0_), channel_id=1, source_target_pairs={{0,24},{8,16},{16,8},{24,0},{1,25},{9,17},{17,9},{25,1},{2,26},{10... | collective-permute-start | bytes 294920 | tf_op jit(solution)/shard_map/ppermute | solution.py:200
  15.2 24.7 %collective-permute-start.4 = (bf16[128,384]{1,0:T(8,128)(2,1)S(1)}, bf16[128,384]{1,0:T(8,128)(2,1)S(1)}, u32[]{:S(2)}, u32[]{:S(2)}) collective-permute-start(bf16[128,384]{1,0:T(8,128)(2,1)S(1)} %get-tuple-element.13.refs_0_), channel_id=1, source_target_pairs={{0,16},{8,24},{16,0},{24,8},{1,17},{9,25},{17,1},{25,9},{2,18},{10... | collective-permute-start | bytes 294920 | tf_op jit(solution)/shard_map/ppermute | solution.py:200
  15.3 24.7 %collective-permute-start.3 = (bf16[128,384]{1,0:T(8,128)(2,1)S(1)}, bf16[128,384]{1,0:T(8,128)(2,1)S(1)}, u32[]{:S(2)}, u32[]{:S(2)}) collective-permute-start(bf16[128,384]{1,0:T(8,128)(2,1)S(1)} %get-tuple-element.13.refs_0_), channel_id=1, source_target_pairs={{0,8},{8,0},{16,24},{24,16},{1,9},{9,1},{17,25},{25,17},{2,10},{10... | collective-permute-start | bytes 294920 | tf_op jit(solution)/shard_map/ppermute | solution.py:200
  35.2 4.7 %collective-permute-start.6 = (bf16[128,384]{1,0:T(8,128)(2,1)S(1)}, bf16[128,384]{1,0:T(8,128)(2,1)S(1)}, u32[]{:S(2)}, u32[]{:S(2)}) collective-permute-start(bf16[128,384]{1,0:T(8,128)(2,1)S(1)} %get-tuple-element.14.refs_4_), channel_id=1, source_target_pairs={{0,8},{8,0},{16,24},{24,16},{1,9},{9,1},{17,25},{25,17},{2,10},{10... | collective-permute-start | bytes 294920 | tf_op jit(solution)/shard_map/ppermute | solution.py:200
  41.5 2.7 %collective-permute-start.9 = (f32[3,384]{1,0:T(4,128)S(1)}, f32[3,384]{1,0:T(4,128)S(1)}, u32[]{:S(2)}, u32[]{:S(2)}) collective-permute-start(f32[3,384]{1,0:T(4,128)S(1)} %shard_map.77), channel_id=1, source_target_pairs={{0,1},{1,0},{2,3},{3,2},{4,5},{5,4},{6,7},{7,6},{8,9},{9,8},{10,11... | collective-permute-start | bytes 13832 | tf_op jit(solution)/shard_map/ppermute | solution.py:188
  41.6 9.4 %collective-permute-start.8 = (bf16[128,384]{1,0:T(8,128)(2,1)S(1)}, bf16[128,384]{1,0:T(8,128)(2,1)S(1)}, u32[]{:S(2)}, u32[]{:S(2)}) collective-permute-start(bf16[128,384]{1,0:T(8,128)(2,1)S(1)} %get-tuple-element.14.refs_4_), channel_id=1, source_target_pairs={{0,24},{8,16},{16,8},{24,0},{1,25},{9,17},{17,9},{25,1},{2,26},{10... | collective-permute-start | bytes 294920 | tf_op jit(solution)/shard_map/ppermute | solution.py:200
  44.3 8.6 %collective-permute-start.7 = (bf16[128,384]{1,0:T(8,128)(2,1)S(1)}, bf16[128,384]{1,0:T(8,128)(2,1)S(1)}, u32[]{:S(2)}, u32[]{:S(2)}) collective-permute-start(bf16[128,384]{1,0:T(8,128)(2,1)S(1)} %get-tuple-element.14.refs_4_), channel_id=1, source_target_pairs={{0,16},{8,24},{16,0},{24,8},{1,17},{9,25},{17,1},{25,9},{2,18},{10... | collective-permute-start | bytes 294920 | tf_op jit(solution)/shard_map/ppermute | solution.py:200
  44.3 4.6 %collective-permute-start.12 = (f32[3,384]{1,0:T(4,128)S(1)}, f32[3,384]{1,0:T(4,128)S(1)}, u32[]{:S(2)}, u32[]{:S(2)}) collective-permute-start(f32[3,384]{1,0:T(4,128)S(1)} %pad_maximum_fusion), channel_id=1, source_target_pairs={{0,6},{1,7},{2,4},{3,5},{4,2},{5,3},{6,0},{7,1},{8,14},{9,15},{10,... | collective-permute-start | bytes 13832 | tf_op jit(solution)/shard_map/ppermute | solution.py:191
  46.8 3.6 %collective-permute-start.11 = (f32[3,384]{1,0:T(4,128)S(1)}, f32[3,384]{1,0:T(4,128)S(1)}, u32[]{:S(2)}, u32[]{:S(2)}) collective-permute-start(f32[3,384]{1,0:T(4,128)S(1)} %pad_maximum_fusion), channel_id=1, source_target_pairs={{0,4},{1,5},{2,6},{3,7},{4,0},{5,1},{6,2},{7,3},{8,12},{9,13},{10,... | collective-permute-start | bytes 13832 | tf_op jit(solution)/shard_map/ppermute | solution.py:191
  47.3 3.6 %collective-permute-start.10 = (f32[3,384]{1,0:T(4,128)S(1)}, f32[3,384]{1,0:T(4,128)S(1)}, u32[]{:S(2)}, u32[]{:S(2)}) collective-permute-start(f32[3,384]{1,0:T(4,128)S(1)} %pad_maximum_fusion), channel_id=1, source_target_pairs={{0,2},{1,3},{2,0},{3,1},{4,6},{5,7},{6,4},{7,5},{8,10},{9,11},{10,... | collective-permute-start | bytes 13832 | tf_op jit(solution)/shard_map/ppermute | solution.py:191
  57.5 1.2 %collective-permute-start.13 = (f32[3,384]{1,0:T(4,128)S(1)}, f32[3,384]{1,0:T(4,128)S(1)}, u32[]{:S(2)}, u32[]{:S(2)}) collective-permute-start(f32[3,384]{1,0:T(4,128)S(1)} %get-tuple-element.18), channel_id=1, source_target_pairs={{0,1},{1,0},{2,3},{3,2},{4,5},{5,4},{6,7},{7,6},{8,9},{9,8},{10,11... | collective-permute-start | bytes 13832 | tf_op jit(solution)/shard_map/ppermute | solution.py:188
  58.8 4.6 %collective-permute-start.16 = (f32[3,384]{1,0:T(4,128)S(1)}, f32[3,384]{1,0:T(4,128)S(1)}, u32[]{:S(2)}, u32[]{:S(2)}) collective-permute-start(f32[3,384]{1,0:T(4,128)S(1)} %pad_maximum_fusion.2), channel_id=1, source_target_pairs={{0,6},{1,7},{2,4},{3,5},{4,2},{5,3},{6,0},{7,1},{8,14},{9,15},{10,... | collective-permute-start | bytes 13832 | tf_op jit(solution)/shard_map/ppermute | solution.py:191
  61.3 3.6 %collective-permute-start.15 = (f32[3,384]{1,0:T(4,128)S(1)}, f32[3,384]{1,0:T(4,128)S(1)}, u32[]{:S(2)}, u32[]{:S(2)}) collective-permute-start(f32[3,384]{1,0:T(4,128)S(1)} %pad_maximum_fusion.2), channel_id=1, source_target_pairs={{0,4},{1,5},{2,6},{3,7},{4,0},{5,1},{6,2},{7,3},{8,12},{9,13},{10,... | collective-permute-start | bytes 13832 | tf_op jit(solution)/shard_map/ppermute | solution.py:191
  61.8 3.6 %collective-permute-start.14 = (f32[3,384]{1,0:T(4,128)S(1)}, f32[3,384]{1,0:T(4,128)S(1)}, u32[]{:S(2)}, u32[]{:S(2)}) collective-permute-start(f32[3,384]{1,0:T(4,128)S(1)} %pad_maximum_fusion.2), channel_id=1, source_target_pairs={{0,2},{1,3},{2,0},{3,1},{4,6},{5,7},{6,4},{7,5},{8,10},{9,11},{10,... | collective-permute-start | bytes 13832 | tf_op jit(solution)/shard_map/ppermute | solution.py:191
  69.5 2.2 %collective-permute-start.17 = (bf16[4,144,576]{2,1,0:T(8,128)(2,1)S(1)}, bf16[4,144,576]{2,1,0:T(8,128)(2,1)S(1)}, u32[]{:S(2)}, u32[]{:S(2)}) collective-permute-start(bf16[4,144,576]{2,1,0:T(8,128)(2,1)S(1)} %get-tuple-element.22), channel_id=1, source_target_pairs={{0,1},{1,0},{2,3},{3,2},{4,5},{5,4},{6,7},{7,6},{8,9},{9,8},{10,11... | collective-permute-start | bytes 1990664 | tf_op jit(solution)/shard_map/ppermute | solution.py:280
  71.9 7.5 %collective-permute-start.18 = (bf16[144,576]{1,0:T(8,128)(2,1)S(1)}, bf16[144,576]{1,0:T(8,128)(2,1)S(1)}, u32[]{:S(2)}, u32[]{:S(2)}) collective-permute-start(bf16[144,576]{1,0:T(8,128)(2,1)S(1)} %get-tuple-element.31), channel_id=1, source_target_pairs={{0,2},{1,3},{2,0},{3,1},{4,6},{5,7},{6,4},{7,5},{8,10},{9,11},{10,... | collective-permute-start | bytes 497672 | tf_op jit(solution)/shard_map/ppermute | solution.py:284
  72.5 11.2 %collective-permute-start.20 = (bf16[144,576]{1,0:T(8,128)(2,1)S(1)}, bf16[144,576]{1,0:T(8,128)(2,1)S(1)}, u32[]{:S(2)}, u32[]{:S(2)}) collective-permute-start(bf16[144,576]{1,0:T(8,128)(2,1)S(1)} %get-tuple-element.32), channel_id=1, source_target_pairs={{0,6},{1,7},{2,4},{3,5},{4,2},{5,3},{6,0},{7,1},{8,14},{9,15},{10,... | collective-permute-start | bytes 497672 | tf_op jit(solution)/shard_map/ppermute | solution.py:284
  75.0 10.1 %collective-permute-start.19 = (bf16[144,576]{1,0:T(8,128)(2,1)S(1)}, bf16[144,576]{1,0:T(8,128)(2,1)S(1)}, u32[]{:S(2)}, u32[]{:S(2)}) collective-permute-start(bf16[144,576]{1,0:T(8,128)(2,1)S(1)} %get-tuple-element.33), channel_id=1, source_target_pairs={{0,4},{1,5},{2,6},{3,7},{4,0},{5,1},{6,2},{7,3},{8,12},{9,13},{10,... | collective-permute-start | bytes 497672 | tf_op jit(solution)/shard_map/ppermute | solution.py:284

commit v4 on v3

--- a/solution.py
+++ b/solution.py
@@ -12,6 +12,7 @@
 f32 = jnp.float32
 bf16 = jnp.bfloat16
 VMEM_BYTES = 24 * 1024 * 1024
+FIRST_VMEM_BYTES = 61 * 1024 * 1024
 
 
 def vmem():
@@ -53,37 +54,83 @@
     return shift, scale
 
 
-def turn_kernel(modes, current, coeffs, first_ref, later_ref):
-    turned = jnp.dot(current[...], coeffs[0], preferred_element_type=f32).astype(bf16)
-    first_ref[...] = turned[:, :modes]
+def hbm():
+    return pl.BlockSpec(memory_space=pltpu.HBM)
+
+
+def first_kernel(
+    chunks, modes, cols, stiff_hbm, mass_hbm, current_hbm, coeffs_hbm,
+    packed_ref, later_ref, current, coeffs, sems,
+):
+    kept, edge = stiff_hbm.shape
+    rows = current.shape[1] // chunks
+    copies = [pltpu.make_async_copy(current_hbm, current, sems.at[0])]
+    for c in range(chunks):
+        part = pl.ds(c * rows, rows)
+        copies.append(pltpu.make_async_copy(coeffs_hbm.at[0, part], coeffs.at[part], sems.at[c + 1]))
+    for i, operator in enumerate((stiff_hbm, mass_hbm)):
+        target = packed_ref.at[pl.ds(i * kept, kept)]
+        copies.append(pltpu.make_async_copy(operator, target, sems.at[chunks + 1 + i]))
+    for copy in copies:
+        copy.start()
+    lane = lax.broadcasted_iota(jnp.int32, (16, edge), 1)
+    tag = jnp.zeros((16, edge), jnp.int32)
+    for s in range(kept // edge):
+        tag = jnp.where(lane == s, cols[0, s], tag)
+    packed_ref[2 * kept : 2 * kept + 16, :] = tag.astype(f32).astype(bf16)
+    copies[0].wait()
+    turned = None
+    for c in range(chunks):
+        copies[c + 1].wait()
+        part = slice(c * rows, (c + 1) * rows)
+        more = jnp.dot(current[:, part], coeffs[part, :], preferred_element_type=f32)
+        turned = more if turned is None else turned + more
+    turned = turned.astype(bf16)
+    for b in range(modes // edge):
+        packed_ref[pl.ds(2 * kept + 16 + b * current.shape[0], current.shape[0]), :] = turned[
+            :, b * edge : (b + 1) * edge
+        ]
     later_ref[...] = turned[:, modes:]
-
-
-def turn_first(current, coeffs, modes):
+    copies[chunks + 1].wait()
+    copies[chunks + 2].wait()
+
+
+def first_step(cols, stiff, mass, current, coeffs, modes):
     rows, columns = current.shape
+    kept, edge = stiff.shape
     half = jax.ShapeDtypeStruct((rows, modes), bf16)
+    chunks = 3
     return pl.pallas_call(
-        functools.partial(turn_kernel, modes),
-        grid=(1,),
-        out_shape=(half, half),
-        in_specs=[
-            pl.BlockSpec((rows, columns), lambda i: (0, 0)),
-            pl.BlockSpec((1, columns, 2 * modes), lambda i: (0, 0, 0)),
+        functools.partial(first_kernel, chunks, modes),
+        out_shape=(jax.ShapeDtypeStruct((2 * kept + 16 + modes, edge), bf16), half),
+        in_specs=[smem(), hbm(), hbm(), hbm(), hbm()],
+        out_specs=(vmem(),) * 2,
+        scratch_shapes=[
+            pltpu.VMEM((rows, columns), bf16),
+            pltpu.VMEM((columns, 2 * modes), bf16),
+            pltpu.SemaphoreType.DMA((chunks + 3,)),
         ],
-        out_specs=(pl.BlockSpec((rows, modes), lambda i: (0, 0)),) * 2,
-        compiler_params=pltpu.CompilerParams(vmem_limit_bytes=VMEM_BYTES),
+        compiler_params=pltpu.CompilerParams(vmem_limit_bytes=FIRST_VMEM_BYTES),
         cost_estimate=pl.CostEstimate(
             flops=4 * rows * columns * modes, bytes_accessed=4 * columns * modes, transcendentals=0
         ),
-    )(current, coeffs)
+    )(cols, stiff, mass, current, coeffs)
+
+
+def unpack_modes(z, slots, edge, km_refs, field):
+    base = 2 * slots * edge + 16
+    for k, packed in enumerate(km_refs):
+        at = pl.ds(pl.multiple_of((z ^ k) * edge, edge), edge)
+        for b in range((packed.shape[0] - base) // edge):
+            part = packed[base + b * edge : base + (b + 1) * edge, :]
+            field[at, b * edge : (b + 1) * edge] = part
 
 
 def stats_kernel(nz, slots, edge, cols, *refs):
-    x_refs, km_refs = refs[:nz], refs[nz : 2 * nz]
-    _, stats_ref, field, stiff, mass = refs[2 * nz :]
+    km_refs = refs[:nz]
+    stats_ref, field, stiff, mass = refs[nz:]
     z = lax.axis_index("blk")
-    for k in range(nz):
-        field[pl.ds(pl.multiple_of((z ^ k) * edge, edge), edge), :] = x_refs[k][...]
+    unpack_modes(z, slots, edge, km_refs, field)
     for k in range(nz):
         both = block_dot(km_refs[k], slots, edge, cols, k, field, slice(None))
         at = pl.ds(pl.multiple_of((z ^ k) * edge, edge), edge)
@@ -96,12 +143,12 @@
 
 
 def sweep_kernel(nz, slots, edge, modes, total_rows, cols, *refs):
-    x_refs, h_refs, km_refs = refs[:nz], refs[nz : 2 * nz], refs[2 * nz : 3 * nz]
-    stats, coeffs, turned_ref, stiff_ref, mass_ref, stats_ref, full = refs[3 * nz :]
+    h_refs, km_refs = refs[:nz], refs[nz : 2 * nz]
+    stats, coeffs, turned_ref, stiff_ref, mass_ref, stats_ref, full = refs[2 * nz :]
     z = lax.axis_index("blk")
     at = [pl.ds(pl.multiple_of((z ^ k) * edge, edge), edge) for k in range(nz)]
-    for k in range(nz):
-        full[at[k], 0:modes] = x_refs[k][...]
+    unpack_modes(z, slots, edge, km_refs, full)
+    for k in range(nz):
         full[at[k], 2 * modes : 3 * modes] = h_refs[k][...]
     shift, scale = shift_and_scale(stats, total_rows)
     for k in range(nz):
@@ -197,7 +244,12 @@
 
 
 def gather(x, nz):
-    return [x] + [lax.ppermute(x, "blk", by_xor(nz, k)) for k in range(1, nz)]
+    parts = {0: x}
+    step = nz // 2
+    while step:
+        parts |= {k ^ step: lax.ppermute(p, "blk", by_xor(nz, step)) for k, p in parts.items()}
+        step //= 2
+    return [parts[k] for k in range(nz)]
 
 
 def body(basis, coeffs, stiff_blocks, mass_blocks, block_cols):
@@ -210,24 +262,21 @@
     total_rows = rows * ng
     width = columns // nz
 
-    tag = jnp.pad(block_cols[0, 0].astype(bf16)[None, :], ((0, 15), (0, edge - slots)))
-    payload = jnp.concatenate(
-        [
-            stiff_blocks[0, 0].reshape(slots * edge, edge),
-            mass_blocks[0, 0].reshape(slots * edge, edge),
-            tag,
-        ],
-        axis=0,
-    )
-    first, later = turn_first(current, coeffs, modes)
-    x_parts = gather(first, nz)
+    payload, later = first_step(
+        block_cols[0],
+        stiff_blocks[0, 0].reshape(slots * edge, edge),
+        mass_blocks[0, 0].reshape(slots * edge, edge),
+        current,
+        coeffs,
+        modes,
+    )
     km_parts = gather(payload, nz)
     h_parts = gather(later, nz)
 
     cols = jnp.stack([p[2 * slots * edge, :slots] for p in km_parts]).astype(jnp.int32)
     stats = call(
         functools.partial(stats_kernel, nz, slots, edge),
-        [cols, *x_parts, *km_parts, h_parts[1]],
+        [cols, *km_parts],
         1,
         jax.ShapeDtypeStruct((3, modes), f32),
         [
@@ -241,7 +290,7 @@
 
     turned, stiff_x, mass_x, stats = call(
         functools.partial(sweep_kernel, nz, slots, edge, modes, total_rows),
-        [cols, *x_parts, *h_parts, *km_parts, stats, coeffs[1]],
+        [cols, *h_parts, *km_parts, stats, coeffs[1]],
         1,
         (
             jax.ShapeDtypeStruct((rows, 2 * modes), bf16),

time: 86.5 us -> 85.5 us (0.988)
  starting transfers between devices: 34.5 us -> 22.4 us
  waiting for transfers between devices: 33.4 us -> 42.9 us
  Pallas kernels: 10.7 us -> 13.7 us
  other arithmetic: 2.72 us -> 1.09 us
    ppermute x9 -> x6, starting transfers between devices: 23.7 us -> 11.6 us  [gather(): lax.ppermute(p, 'blk', by_xor(nz, step))]
    ppermute x9 -> x6, waiting for transfers between devices: 15 us -> 26.4 us  [gather(): lax.ppermute(p, 'blk', by_xor(nz, step))]
    pallas_call x1, Pallas kernels: 0.43 us -> 3.4 us  [first_step(): pl.pallas_call(functools.partial(first_kernel, chunks, modes), out_shape=...]
    unnamed x6 -> x4, local copies, waits for them, and re-layouts: 2.97 us -> 0.99 us
    ppermute x6, waiting for transfers between devices: 6.06 us -> 4.23 us  [merge_over(): got = [lax.ppermute(stats, axis, by_xor(size, 2 * k)) for k in (1, 2, 3)]]
    squeeze x1, local copies, waits for them, and re-layouts: 0.11 us -> 1.59 us  [body(): coeffs[1]]
    concatenate x1 -> x0, other arithmetic: 0.99 us -> none  [body(): jnp.concatenate([stiff_blocks[0, 0].reshape(slots * edge, edge), mass_blo...]
  transfers between devices with their start and end apart: 21 -> 18, of which waited for: 14 -> 13; matrix products, arithmetic and copies ran while one was open for 1% -> 3% of each run, Pallas kernels for 0% -> 0%
where the time goes in v4:
time: 85.5 us; the launch traced here: 85.3 us
  waiting for transfers between devices  42.9 us (50%)
  starting transfers between devices  22.4 us (26%)
  Pallas kernels  13.7 us (16%)
  local copies, waits for them, and re-layouts  4.41 us (5%)
  other arithmetic  1.09 us (1%)
    ppermute x6, waiting for transfers between devices, gather(): lax.ppermute(p, 'blk', by_xor(nz, step))  26.4 us
    ppermute x6, starting transfers between devices, gather(): lax.ppermute(p, 'blk', by_xor(nz, step))  11.6 us
    pallas_call x3, Pallas kernels, call(): pl.pallas_call(kernel, out_shape=out_shape, in_specs=[smem()] * n_smem +...  10.3 us
    ppermute x3, waiting for transfers between devices, body(): total = total + lax.ppermute(mine[k], 'grp', by_xor(ng, 2 * k)).astype(f32)  8.96 us
    ppermute x6, starting transfers between devices, merge_over(): got = [lax.ppermute(stats, axis, by_xor(size, 2 * k)) for k in (1, 2, 3)]  7.11 us
    ppermute x6, waiting for transfers between devices, merge_over(): got = [lax.ppermute(stats, axis, by_xor(size, 2 * k)) for k in (1, 2, 3)]  4.23 us
    ppermute x3, starting transfers between devices, body(): total = total + lax.ppermute(mine[k], 'grp', by_xor(ng, 2 * k)).astype(f32)  3.55 us
    pallas_call x1, Pallas kernels, first_step(): pl.pallas_call(functools.partial(first_kernel, chunks, modes), out_shape=...  3.4 us
  transfers between devices with their start and end apart: 18, of which 13 were waited for; matrix products, arithmetic and copies ran while one was open for 3% of the time, Pallas kernels for 0%

profile of v4, /device:TPU:0, one launch (start us, length us, event | category | flops | bytes accessed | tf_op | source)
XLA Modules:
  0.0 85.3 jit_solution(12472541168833004510)
XLA Ops:
  0.6 3.4 %shard_map.76 = (bf16[1424,128]{1,0:T(8,128)(2,1)}, bf16[128,384]{1,0:T(8,128)(2,1)}) custom-call(s32[1,4]{1,0:T(1,128)} %bitcast.21, bf16[512,128]{1,0:T(8,128)(2,1)} %bitcast.19, bf16[512,128]{1,0:T(8,128)(2,1)} %bitcast.20, bf16[128,1152]{1,0:T(8,128)(2,1)} %bitcast.18, bf16[2,1152,768]{2,1,0:T(8,128)(2,1)} %coeffs_hbm.1), custom_call_target="tpu_custom_call" | custom-call | flops 226492416 | bytes 1769472 | tf_op jit(solution)/shard_map/pallas_call | solution.py:103
  4.0 4.1 %collective-permute-start.1 = (bf16[1424,128]{1,0:T(8,128)(2,1)}, bf16[1424,128]{1,0:T(8,128)(2,1)S(1)}, u32[]{:S(2)}, u32[]{:S(2)}) collective-permute-start(bf16[1424,128]{1,0:T(8,128)(2,1)} %get-tuple-element.13.refs_0_.refs_4_), channel_id=1, source_target_pairs={{0,16},{8,24},{16,0},{24,8},{1,17},{9,25},{17,1},{25,9},{2,18},{10... | collective-permute-start | bytes 1093640 | tf_op jit(solution)/shard_map/ppermute | solution.py:250
  8.1 1.6 %collective-permute-start = (bf16[1424,128]{1,0:T(8,128)(2,1)}, bf16[1424,128]{1,0:T(8,128)(2,1)S(1)}, u32[]{:S(2)}, u32[]{:S(2)}) collective-permute-start(bf16[1424,128]{1,0:T(8,128)(2,1)} %get-tuple-element.13.refs_0_.refs_4_), channel_id=1, source_target_pairs={{0,8},{8,0},{16,24},{24,16},{1,9},{9,1},{17,25},{25,17},{2,10},{10... | collective-permute-start | bytes 1093640 | tf_op jit(solution)/shard_map/ppermute | solution.py:250
  9.7 15.1 %collective-permute-done.1.refs_2_.refs_6_ = bf16[1424,128]{1,0:T(8,128)(2,1)S(1)} collective-permute-done((bf16[1424,128]{1,0:T(8,128)(2,1)}, bf16[1424,128]{1,0:T(8,128)(2,1)S(1)}, u32[]{:S(2)}, u32[]{:S(2)}) %collective-permute-start.1) | collective-permute-done | bytes 364576 | tf_op jit(solution)/shard_map/ppermute | solution.py:250
  24.8 0.7 collective-permute-start.2
  25.5 0.7 slice.147
  26.2 0.0 collective-permute-done.refs_1_.refs_5_
  26.2 8.2 %collective-permute-done.2.refs_3_.refs_7_ = bf16[1424,128]{1,0:T(8,128)(2,1)S(1)} collective-permute-done((bf16[1424,128]{1,0:T(8,128)(2,1)S(1)}, bf16[1424,128]{1,0:T(8,128)(2,1)S(1)}, u32[]{:S(2)}, u32[]{:S(2)}) %collective-permute-start.2) | collective-permute-done | bytes 364576 | tf_op jit(solution)/shard_map/ppermute | solution.py:250
  34.4 0.0 copy-start
  34.4 1.0 %copy-done = bf16[1424,128]{1,0:T(8,128)(2,1)S(1)} copy-done((bf16[1424,128]{1,0:T(8,128)(2,1)S(1)}, bf16[1424,128]{1,0:T(8,128)(2,1)}, u32[]{:S(2)}) %copy-start) | copy-done | bytes 364568
  35.4 1.6 %shard_map.77 = f32[3,384]{1,0:T(4,128)S(1)} custom-call(s32[4,4]{1,0:T(4,128)S(1)} %maximum_convert_fusion.cols, bf16[1424,128]{1,0:T(8,128)(2,1)S(1)} %copy-done, bf16[1424,128]{1,0:T(8,128)(2,1)S(1)} %collective-permute-done.refs_1_.refs_5_, bf16[1424,128]{1,0:T(8,128)(2,1)S(1)} %collective-permute-done.1.refs_2_.refs_6_, ...), custom_call_target="tpu_custom_call" | custom-call | flops 100663296 | bytes 4000000 | tf_op jit(solution)/shard_map/pallas_call | solution.py:209
  37.0 0.1 collective-permute-start.6
  37.1 3.1 %collective-permute-start.4 = (bf16[128,384]{1,0:T(8,128)(2,1)}, bf16[128,384]{1,0:T(8,128)(2,1)S(1)}, u32[]{:S(2)}, u32[]{:S(2)}) collective-permute-start(bf16[128,384]{1,0:T(8,128)(2,1)} %get-tuple-element.14.refs_0_), channel_id=1, source_target_pairs={{0,16},{8,24},{16,0},{24,8},{1,17},{9,25},{17,1},{25,9},{2,18},{10... | collective-permute-start | bytes 294920 | tf_op jit(solution)/shard_map/ppermute | solution.py:250
  40.2 1.7 %collective-permute-start.3 = (bf16[128,384]{1,0:T(8,128)(2,1)}, bf16[128,384]{1,0:T(8,128)(2,1)S(1)}, u32[]{:S(2)}, u32[]{:S(2)}) collective-permute-start(bf16[128,384]{1,0:T(8,128)(2,1)} %get-tuple-element.14.refs_0_), channel_id=1, source_target_pairs={{0,8},{8,0},{16,24},{24,16},{1,9},{9,1},{17,25},{25,17},{2,10},{10... | collective-permute-start | bytes 294920 | tf_op jit(solution)/shard_map/ppermute | solution.py:250
  41.9 0.0 collective-permute-done.6
  42.0 0.0 copy-start.1
  42.0 2.5 %collective-permute-start.9 = (f32[3,384]{1,0:T(4,128)S(1)}, f32[3,384]{1,0:T(4,128)S(1)}, u32[]{:S(2)}, u32[]{:S(2)}) collective-permute-start(f32[3,384]{1,0:T(4,128)S(1)} %pad_maximum_fusion), channel_id=1, source_target_pairs={{0,6},{1,7},{2,4},{3,5},{4,2},{5,3},{6,0},{7,1},{8,14},{9,15},{10,... | collective-permute-start | bytes 13832 | tf_op jit(solution)/shard_map/ppermute | solution.py:238
  44.5 0.5 collective-permute-start.8
  45.0 0.5 collective-permute-start.7
  45.6 1.6 %slice_bitcast_fusion.refs_9_ = bf16[1152,768]{1,0:T(8,128)(2,1)S(1)} fusion(bf16[2,1152,768]{2,1,0:T(8,128)(2,1)} %coeffs_hbm.1), kind=kLoop, calls=%fused_computation | loop fusion | bytes 3538944 | tf_op jit(solution)/shard_map/squeeze | solution.py:293
  47.2 0.0 collective-permute-done.4.refs_2_
  47.2 0.3 collective-permute-start.5
  47.5 0.0 collective-permute-done.9
  47.5 0.6 collective-permute-done.8
  48.1 0.5 collective-permute-done.7
  48.7 0.0 collective-permute-done.3.refs_1_
  48.7 3.1 %collective-permute-done.5.refs_3_ = bf16[128,384]{1,0:T(8,128)(2,1)S(1)} collective-permute-done((bf16[128,384]{1,0:T(8,128)(2,1)S(1)}, bf16[128,384]{1,0:T(8,128)(2,1)S(1)}, u32[]{:S(2)}, u32[]{:S(2)}) %collective-permute-start.5) | collective-permute-done | bytes 98336 | tf_op jit(solution)/shard_map/ppermute | solution.py:250
  51.8 0.0 copy-done.1
  51.9 4.7 %shard_map.78 = (bf16[512,768]{1,0:T(8,128)(2,1)S(1)}, f32[512,384]{1,0:T(8,128)S(1)}, f32[512,384]{1,0:T(8,128)S(1)}, f32[3,384]{1,0:T(4,128)S(1)}) custom-call(s32[4,4]{1,0:T(4,128)S(1)} %maximum_convert_fusion.cols, bf16[128,384]{1,0:T(8,128)(2,1)S(1)} %copy-done.1, bf16[128,384]{1,0:T(8,128)(2,1)S(1)} %collective-permute-done.3.refs_1_, ...), custom_call_target="tpu_custom_call" | custom-call | flops 905969664 | bytes 4000000 | tf_op jit(solution)/shard_map/pallas_call | solution.py:209
  56.6 0.1 collective-permute-start.10
  56.7 1.2 %collective-permute-done.10 = f32[3,384]{1,0:T(4,128)S(1)} collective-permute-done((f32[3,384]{1,0:T(4,128)S(1)}, f32[3,384]{1,0:T(4,128)S(1)}, u32[]{:S(2)}, u32[]{:S(2)}) %collective-permute-start.10) | collective-permute-done | bytes 4640 | tf_op jit(solution)/shard_map/ppermute | solution.py:235
  57.9 2.5 %collective-permute-start.13 = (f32[3,384]{1,0:T(4,128)S(1)}, f32[3,384]{1,0:T(4,128)S(1)}, u32[]{:S(2)}, u32[]{:S(2)}) collective-permute-start(f32[3,384]{1,0:T(4,128)S(1)} %pad_maximum_fusion.2), channel_id=1, source_target_pairs={{0,6},{1,7},{2,4},{3,5},{4,2},{5,3},{6,0},{7,1},{8,14},{9,15},{10,... | collective-permute-start | bytes 13832 | tf_op jit(solution)/shard_map/ppermute | solution.py:238
  60.4 0.5 collective-permute-start.12
  60.9 0.5 collective-permute-start.11
  61.4 1.0 %collective-permute-done.13 = f32[3,384]{1,0:T(4,128)S(1)} collective-permute-done((f32[3,384]{1,0:T(4,128)S(1)}, f32[3,384]{1,0:T(4,128)S(1)}, u32[]{:S(2)}, u32[]{:S(2)}) %collective-permute-start.13) | collective-permute-done | bytes 4640 | tf_op jit(solution)/shard_map/ppermute | solution.py:238
  62.4 1.5 %collective-permute-done.12 = f32[3,384]{1,0:T(4,128)S(1)} collective-permute-done((f32[3,384]{1,0:T(4,128)S(1)}, f32[3,384]{1,0:T(4,128)S(1)}, u32[]{:S(2)}, u32[]{:S(2)}) %collective-permute-start.12) | collective-permute-done | bytes 4640 | tf_op jit(solution)/shard_map/ppermute | solution.py:238
  64.0 0.5 collective-permute-done.11
  64.6 3.9 %shard_map.79 = (bf16[128,1152]{1,0:T(8,128)(2,1)}, f32[1,384]{1,0:T(1,128)S(1)}, bf16[4,144,576]{2,1,0:T(8,128)(2,1)S(1)}, bf16[4,144,576]{2,1,0:T(8,128)(2,1)S(1)}) custom-call(s32[4,4]{1,0:T(4,128)S(1)} %maximum_convert_fusion.cols, bf16[1424,128]{1,0:T(8,128)(2,1)S(1)} %copy-done, bf16[1424,128]{1,0:T(8,128)(2,1)S(1)} %collective-permute-done.refs_1_.refs_5_, ...), custom_call_target="tpu_custom_call" | custom-call | flops 679477248 | bytes 4000000 | tf_op jit(solution)/shard_map/pallas_call | solution.py:209
  68.5 0.0 collective-permute-start.14
  68.5 2.2 %collective-permute-done.14 = bf16[4,144,576]{2,1,0:T(8,128)(2,1)S(1)} collective-permute-done((bf16[4,144,576]{2,1,0:T(8,128)(2,1)S(1)}, bf16[4,144,576]{2,1,0:T(8,128)(2,1)S(1)}, u32[]{:S(2)}, u32[]{:S(2)}) %collective-permute-start.14) | collective-permute-done | bytes 663584 | tf_op jit(solution)/shard_map/ppermute | solution.py:329
  70.7 0.2 add_convert_fusion
  70.9 0.1 slice_bitcast_fusion.3
  71.0 0.6 collective-permute-start.15
  71.6 2.4 %collective-permute-start.17 = (bf16[144,576]{1,0:T(8,128)(2,1)S(1)}, bf16[144,576]{1,0:T(8,128)(2,1)S(1)}, u32[]{:S(2)}, u32[]{:S(2)}) collective-permute-start(bf16[144,576]{1,0:T(8,128)(2,1)S(1)} %get-tuple-element.32), channel_id=1, source_target_pairs={{0,6},{1,7},{2,4},{3,5},{4,2},{5,3},{6,0},{7,1},{8,14},{9,15},{10,... | collective-permute-start | bytes 497672 | tf_op jit(solution)/shard_map/ppermute | solution.py:333
  74.0 0.5 collective-permute-start.16
  74.5 0.6 reduce
  75.1 3.4 %collective-permute-done.15 = bf16[144,576]{1,0:T(8,128)(2,1)S(1)} collective-permute-done((bf16[144,576]{1,0:T(8,128)(2,1)S(1)}, bf16[144,576]{1,0:T(8,128)(2,1)S(1)}, u32[]{:S(2)}, u32[]{:S(2)}) %collective-permute-start.15) | collective-permute-done | bytes 165920 | tf_op jit(solution)/shard_map/ppermute | solution.py:333
  78.5 4.2 %collective-permute-done.17 = bf16[144,576]{1,0:T(8,128)(2,1)S(1)} collective-permute-done((bf16[144,576]{1,0:T(8,128)(2,1)S(1)}, bf16[144,576]{1,0:T(8,128)(2,1)S(1)}, u32[]{:S(2)}, u32[]{:S(2)}) %collective-permute-start.17) | collective-permute-done | bytes 165920 | tf_op jit(solution)/shard_map/ppermute | solution.py:333
  82.7 1.4 %collective-permute-done.16 = bf16[144,576]{1,0:T(8,128)(2,1)S(1)} collective-permute-done((bf16[144,576]{1,0:T(8,128)(2,1)S(1)}, bf16[144,576]{1,0:T(8,128)(2,1)S(1)}, u32[]{:S(2)}, u32[]{:S(2)}) %collective-permute-start.16) | collective-permute-done | bytes 165920 | tf_op jit(solution)/shard_map/ppermute | solution.py:333
  84.1 0.1 fusion.1
  84.2 1.1 %reshape.11 = f32[144,2,288]{2,1,0:T(2,128)} reshape(f32[144,576]{1,0:T(8,128)S(1)} %fusion.1) | data formatting | bytes 663552 | tf_op jit(solution)/shard_map/reshape | solution.py:336
  (12 shorter events, 0.2 us)
Async XLA Ops:
  4.0 20.7 %collective-permute-start.1 = (bf16[1424,128]{1,0:T(8,128)(2,1)}, bf16[1424,128]{1,0:T(8,128)(2,1)S(1)}, u32[]{:S(2)}, u32[]{:S(2)}) collective-permute-start(bf16[1424,128]{1,0:T(8,128)(2,1)} %get-tuple-element.13.refs_0_.refs_4_), channel_id=1, source_target_pairs={{0,16},{8,24},{16,0},{24,8},{1,17},{9,25},{17,1},{25,9},{2,18},{10... | collective-permute-start | bytes 1093640 | tf_op jit(solution)/shard_map/ppermute | solution.py:250
  8.1 18.0 %collective-permute-start = (bf16[1424,128]{1,0:T(8,128)(2,1)}, bf16[1424,128]{1,0:T(8,128)(2,1)S(1)}, u32[]{:S(2)}, u32[]{:S(2)}) collective-permute-start(bf16[1424,128]{1,0:T(8,128)(2,1)} %get-tuple-element.13.refs_0_.refs_4_), channel_id=1, source_target_pairs={{0,8},{8,0},{16,24},{24,16},{1,9},{9,1},{17,25},{25,17},{2,10},{10... | collective-permute-start | bytes 1093640 | tf_op jit(solution)/shard_map/ppermute | solution.py:250
  24.8 9.6 %collective-permute-start.2 = (bf16[1424,128]{1,0:T(8,128)(2,1)S(1)}, bf16[1424,128]{1,0:T(8,128)(2,1)S(1)}, u32[]{:S(2)}, u32[]{:S(2)}) collective-permute-start(bf16[1424,128]{1,0:T(8,128)(2,1)S(1)} %collective-permute-done.1.refs_2_.refs_6_), channel_id=1, source_target_pairs={{0,8},{8,0},{16,24},{24,16},{1,9},{9,1},{17,25},{25,17},{2,10},{10... | collective-permute-start | bytes 1093640 | tf_op jit(solution)/shard_map/ppermute | solution.py:250
  34.4 1.0 %copy-start = (bf16[1424,128]{1,0:T(8,128)(2,1)S(1)}, bf16[1424,128]{1,0:T(8,128)(2,1)}, u32[]{:S(2)}) copy-start(bf16[1424,128]{1,0:T(8,128)(2,1)} %get-tuple-element.13.refs_0_.refs_4_) | copy-start | bytes 1093636
  37.0 4.9 %collective-permute-start.6 = (f32[3,384]{1,0:T(4,128)S(1)}, f32[3,384]{1,0:T(4,128)S(1)}, u32[]{:S(2)}, u32[]{:S(2)}) collective-permute-start(f32[3,384]{1,0:T(4,128)S(1)} %shard_map.77), channel_id=1, source_target_pairs={{0,1},{1,0},{2,3},{3,2},{4,5},{5,4},{6,7},{7,6},{8,9},{9,8},{10,11... | collective-permute-start | bytes 13832 | tf_op jit(solution)/shard_map/ppermute | solution.py:235
  37.1 10.1 %collective-permute-start.4 = (bf16[128,384]{1,0:T(8,128)(2,1)}, bf16[128,384]{1,0:T(8,128)(2,1)S(1)}, u32[]{:S(2)}, u32[]{:S(2)}) collective-permute-start(bf16[128,384]{1,0:T(8,128)(2,1)} %get-tuple-element.14.refs_0_), channel_id=1, source_target_pairs={{0,16},{8,24},{16,0},{24,8},{1,17},{9,25},{17,1},{25,9},{2,18},{10... | collective-permute-start | bytes 294920 | tf_op jit(solution)/shard_map/ppermute | solution.py:250
  40.2 8.5 %collective-permute-start.3 = (bf16[128,384]{1,0:T(8,128)(2,1)}, bf16[128,384]{1,0:T(8,128)(2,1)S(1)}, u32[]{:S(2)}, u32[]{:S(2)}) collective-permute-start(bf16[128,384]{1,0:T(8,128)(2,1)} %get-tuple-element.14.refs_0_), channel_id=1, source_target_pairs={{0,8},{8,0},{16,24},{24,16},{1,9},{9,1},{17,25},{25,17},{2,10},{10... | collective-permute-start | bytes 294920 | tf_op jit(solution)/shard_map/ppermute | solution.py:250
  42.0 9.9 %copy-start.1 = (bf16[128,384]{1,0:T(8,128)(2,1)S(1)}, bf16[128,384]{1,0:T(8,128)(2,1)}, u32[]{:S(2)}) copy-start(bf16[128,384]{1,0:T(8,128)(2,1)} %get-tuple-element.14.refs_0_) | copy-start | bytes 294916
  42.0 5.5 %collective-permute-start.9 = (f32[3,384]{1,0:T(4,128)S(1)}, f32[3,384]{1,0:T(4,128)S(1)}, u32[]{:S(2)}, u32[]{:S(2)}) collective-permute-start(f32[3,384]{1,0:T(4,128)S(1)} %pad_maximum_fusion), channel_id=1, source_target_pairs={{0,6},{1,7},{2,4},{3,5},{4,2},{5,3},{6,0},{7,1},{8,14},{9,15},{10,... | collective-permute-start | bytes 13832 | tf_op jit(solution)/shard_map/ppermute | solution.py:238
  44.5 3.6 %collective-permute-start.8 = (f32[3,384]{1,0:T(4,128)S(1)}, f32[3,384]{1,0:T(4,128)S(1)}, u32[]{:S(2)}, u32[]{:S(2)}) collective-permute-start(f32[3,384]{1,0:T(4,128)S(1)} %pad_maximum_fusion), channel_id=1, source_target_pairs={{0,4},{1,5},{2,6},{3,7},{4,0},{5,1},{6,2},{7,3},{8,12},{9,13},{10,... | collective-permute-start | bytes 13832 | tf_op jit(solution)/shard_map/ppermute | solution.py:238
  45.0 3.6 %collective-permute-start.7 = (f32[3,384]{1,0:T(4,128)S(1)}, f32[3,384]{1,0:T(4,128)S(1)}, u32[]{:S(2)}, u32[]{:S(2)}) collective-permute-start(f32[3,384]{1,0:T(4,128)S(1)} %pad_maximum_fusion), channel_id=1, source_target_pairs={{0,2},{1,3},{2,0},{3,1},{4,6},{5,7},{6,4},{7,5},{8,10},{9,11},{10,... | collective-permute-start | bytes 13832 | tf_op jit(solution)/shard_map/ppermute | solution.py:238
  47.2 4.7 %collective-permute-start.5 = (bf16[128,384]{1,0:T(8,128)(2,1)S(1)}, bf16[128,384]{1,0:T(8,128)(2,1)S(1)}, u32[]{:S(2)}, u32[]{:S(2)}) collective-permute-start(bf16[128,384]{1,0:T(8,128)(2,1)S(1)} %collective-permute-done.4.refs_2_), channel_id=1, source_target_pairs={{0,8},{8,0},{16,24},{24,16},{1,9},{9,1},{17,25},{25,17},{2,10},{10... | collective-permute-start | bytes 294920 | tf_op jit(solution)/shard_map/ppermute | solution.py:250
  56.6 1.2 %collective-permute-start.10 = (f32[3,384]{1,0:T(4,128)S(1)}, f32[3,384]{1,0:T(4,128)S(1)}, u32[]{:S(2)}, u32[]{:S(2)}) collective-permute-start(f32[3,384]{1,0:T(4,128)S(1)} %get-tuple-element.18), channel_id=1, source_target_pairs={{0,1},{1,0},{2,3},{3,2},{4,5},{5,4},{6,7},{7,6},{8,9},{9,8},{10,11... | collective-permute-start | bytes 13832 | tf_op jit(solution)/shard_map/ppermute | solution.py:235
  57.9 4.6 %collective-permute-start.13 = (f32[3,384]{1,0:T(4,128)S(1)}, f32[3,384]{1,0:T(4,128)S(1)}, u32[]{:S(2)}, u32[]{:S(2)}) collective-permute-start(f32[3,384]{1,0:T(4,128)S(1)} %pad_maximum_fusion.2), channel_id=1, source_target_pairs={{0,6},{1,7},{2,4},{3,5},{4,2},{5,3},{6,0},{7,1},{8,14},{9,15},{10,... | collective-permute-start | bytes 13832 | tf_op jit(solution)/shard_map/ppermute | solution.py:238
  60.4 3.6 %collective-permute-start.12 = (f32[3,384]{1,0:T(4,128)S(1)}, f32[3,384]{1,0:T(4,128)S(1)}, u32[]{:S(2)}, u32[]{:S(2)}) collective-permute-start(f32[3,384]{1,0:T(4,128)S(1)} %pad_maximum_fusion.2), channel_id=1, source_target_pairs={{0,4},{1,5},{2,6},{3,7},{4,0},{5,1},{6,2},{7,3},{8,12},{9,13},{10,... | collective-permute-start | bytes 13832 | tf_op jit(solution)/shard_map/ppermute | solution.py:238
  60.9 3.6 %collective-permute-start.11 = (f32[3,384]{1,0:T(4,128)S(1)}, f32[3,384]{1,0:T(4,128)S(1)}, u32[]{:S(2)}, u32[]{:S(2)}) collective-permute-start(f32[3,384]{1,0:T(4,128)S(1)} %pad_maximum_fusion.2), channel_id=1, source_target_pairs={{0,2},{1,3},{2,0},{3,1},{4,6},{5,7},{6,4},{7,5},{8,10},{9,11},{10,... | collective-permute-start | bytes 13832 | tf_op jit(solution)/shard_map/ppermute | solution.py:238
  68.5 2.2 %collective-permute-start.14 = (bf16[4,144,576]{2,1,0:T(8,128)(2,1)S(1)}, bf16[4,144,576]{2,1,0:T(8,128)(2,1)S(1)}, u32[]{:S(2)}, u32[]{:S(2)}) collective-permute-start(bf16[4,144,576]{2,1,0:T(8,128)(2,1)S(1)} %get-tuple-element.22), channel_id=1, source_target_pairs={{0,1},{1,0},{2,3},{3,2},{4,5},{5,4},{6,7},{7,6},{8,9},{9,8},{10,11... | collective-permute-start | bytes 1990664 | tf_op jit(solution)/shard_map/ppermute | solution.py:329
  71.0 7.5 %collective-permute-start.15 = (bf16[144,576]{1,0:T(8,128)(2,1)S(1)}, bf16[144,576]{1,0:T(8,128)(2,1)S(1)}, u32[]{:S(2)}, u32[]{:S(2)}) collective-permute-start(bf16[144,576]{1,0:T(8,128)(2,1)S(1)} %get-tuple-element.31), channel_id=1, source_target_pairs={{0,2},{1,3},{2,0},{3,1},{4,6},{5,7},{6,4},{7,5},{8,10},{9,11},{10,... | collective-permute-start | bytes 497672 | tf_op jit(solution)/shard_map/ppermute | solution.py:333
  71.6 11.2 %collective-permute-start.17 = (bf16[144,576]{1,0:T(8,128)(2,1)S(1)}, bf16[144,576]{1,0:T(8,128)(2,1)S(1)}, u32[]{:S(2)}, u32[]{:S(2)}) collective-permute-start(bf16[144,576]{1,0:T(8,128)(2,1)S(1)} %get-tuple-element.32), channel_id=1, source_target_pairs={{0,6},{1,7},{2,4},{3,5},{4,2},{5,3},{6,0},{7,1},{8,14},{9,15},{10,... | collective-permute-start | bytes 497672 | tf_op jit(solution)/shard_map/ppermute | solution.py:333
  74.0 10.1 %collective-permute-start.16 = (bf16[144,576]{1,0:T(8,128)(2,1)S(1)}, bf16[144,576]{1,0:T(8,128)(2,1)S(1)}, u32[]{:S(2)}, u32[]{:S(2)}) collective-permute-start(bf16[144,576]{1,0:T(8,128)(2,1)S(1)} %get-tuple-element.33), channel_id=1, source_target_pairs={{0,4},{1,5},{2,6},{3,7},{4,0},{5,1},{6,2},{7,3},{8,12},{9,13},{10,... | collective-permute-start | bytes 497672 | tf_op jit(solution)/shard_map/ppermute | solution.py:333

commit v5 on v3

--- a/solution.py
+++ b/solution.py
@@ -53,37 +53,63 @@
     return shift, scale
 
 
-def turn_kernel(modes, current, coeffs, first_ref, later_ref):
-    turned = jnp.dot(current[...], coeffs[0], preferred_element_type=f32).astype(bf16)
-    first_ref[...] = turned[:, :modes]
-    later_ref[...] = turned[:, modes:]
-
-
-def turn_first(current, coeffs, modes):
-    rows, columns = current.shape
-    half = jax.ShapeDtypeStruct((rows, modes), bf16)
-    return pl.pallas_call(
-        functools.partial(turn_kernel, modes),
-        grid=(1,),
-        out_shape=(half, half),
-        in_specs=[
-            pl.BlockSpec((rows, columns), lambda i: (0, 0)),
-            pl.BlockSpec((1, columns, 2 * modes), lambda i: (0, 0, 0)),
-        ],
-        out_specs=(pl.BlockSpec((rows, modes), lambda i: (0, 0)),) * 2,
-        compiler_params=pltpu.CompilerParams(vmem_limit_bytes=VMEM_BYTES),
-        cost_estimate=pl.CostEstimate(
-            flops=4 * rows * columns * modes, bytes_accessed=4 * columns * modes, transcendentals=0
-        ),
-    )(current, coeffs)
+def block_dot(pieces_k, slots, edge, cols, k, field, lanes):
+    half = slots * edge
+    top = jnp.concatenate([pieces_k[s * edge : (s + 1) * edge, :] for s in range(slots)], axis=1)
+    low = jnp.concatenate(
+        [pieces_k[half + s * edge : half + (s + 1) * edge, :] for s in range(slots)], axis=1
+    )
+    rows = [
+        field[pl.ds(pl.multiple_of(cols[k, s] * edge, edge), edge), lanes] for s in range(slots)
+    ]
+    return jnp.dot(
+        jnp.concatenate([top, low], axis=0),
+        jnp.concatenate(rows, axis=0),
+        preferred_element_type=f32,
+    )
+
+
+def column_stats(stiff_x, mass_x):
+    num = jnp.sum(stiff_x * mass_x, axis=0, keepdims=True)
+    den = jnp.sum(mass_x * mass_x, axis=0, keepdims=True)
+    rest = stiff_x - (num / jnp.maximum(den, tiny)) * mass_x
+    return num, den, jnp.sum(rest * rest, axis=0, keepdims=True)
+
+
+def shift_and_scale(stats, total_rows):
+    num, den, about = stats[0:1, :], stats[1:2, :], stats[2:3, :]
+    shift = num / (den + epsilon)
+    off = shift - num / jnp.maximum(den, tiny)
+    scale = lax.rsqrt((about + off * off * den) / total_rows + epsilon)
+    return shift, scale
+
+
+def hbm():
+    return pl.BlockSpec(memory_space=pltpu.HBM)
+
+
+def pack_kernel(cols, stiff, mass, out_ref):
+    rows, edge = stiff.shape
+    out_ref[0:rows, :] = stiff[...]
+    out_ref[rows : 2 * rows, :] = mass[...]
+    lane = lax.broadcasted_iota(jnp.int32, (16, edge), 1)
+    tag = jnp.zeros((16, edge), jnp.int32)
+    for s in range(rows // edge):
+        tag = jnp.where(lane == s, cols[0, s], tag)
+    out_ref[2 * rows : 2 * rows + 16, :] = tag.astype(f32).astype(bf16)
+
+
+def turn_kernel(current, coeffs, out_ref):
+    out_ref[...] = jnp.dot(current[...], coeffs[0], preferred_element_type=f32).astype(bf16)
 
 
 def stats_kernel(nz, slots, edge, cols, *refs):
-    x_refs, km_refs = refs[:nz], refs[nz : 2 * nz]
-    _, stats_ref, field, stiff, mass = refs[2 * nz :]
+    t_refs, km_refs = refs[:nz], refs[nz : 2 * nz]
+    stats_ref, field, stiff, mass = refs[2 * nz :]
     z = lax.axis_index("blk")
     for k in range(nz):
-        field[pl.ds(pl.multiple_of((z ^ k) * edge, edge), edge), :] = x_refs[k][...]
+        at = pl.ds(pl.multiple_of((z ^ k) * edge, edge), edge)
+        field[at, :] = t_refs[k][:, : field.shape[1]]
     for k in range(nz):
         both = block_dot(km_refs[k], slots, edge, cols, k, field, slice(None))
         at = pl.ds(pl.multiple_of((z ^ k) * edge, edge), edge)
@@ -96,18 +122,18 @@
 
 
 def sweep_kernel(nz, slots, edge, modes, total_rows, cols, *refs):
-    x_refs, h_refs, km_refs = refs[:nz], refs[nz : 2 * nz], refs[2 * nz : 3 * nz]
-    stats, coeffs, turned_ref, stiff_ref, mass_ref, stats_ref, full = refs[3 * nz :]
+    t_refs, km_refs = refs[:nz], refs[nz : 2 * nz]
+    stats, coeffs, turned_ref, stiff_ref, mass_ref, stats_ref, full = refs[2 * nz :]
     z = lax.axis_index("blk")
     at = [pl.ds(pl.multiple_of((z ^ k) * edge, edge), edge) for k in range(nz)]
     for k in range(nz):
-        full[at[k], 0:modes] = x_refs[k][...]
-        full[at[k], 2 * modes : 3 * modes] = h_refs[k][...]
+        full[at[k], 0:modes] = t_refs[k][:, :modes]
+        full[at[k], 2 * modes : 3 * modes] = t_refs[k][:, modes:]
     shift, scale = shift_and_scale(stats, total_rows)
     for k in range(nz):
         both = block_dot(km_refs[k], slots, edge, cols, k, full, slice(0, modes))
         full[at[k], modes : 2 * modes] = ((both[:edge] - shift * both[edge:]) * scale).astype(bf16)
-    turned_ref[...] = jnp.dot(full[...], coeffs[...], preferred_element_type=f32).astype(bf16)
+    turned_ref[...] = jnp.dot(full[...], coeffs[1], preferred_element_type=f32).astype(bf16)
     for k in range(nz):
         both = block_dot(km_refs[k], slots, edge, cols, k, turned_ref, slice(0, modes))
         stiff_ref[at[k], :] = both[:edge]
@@ -196,8 +222,39 @@
     return stats
 
 
-def gather(x, nz):
-    return [x] + [lax.ppermute(x, "blk", by_xor(nz, k)) for k in range(1, nz)]
+def hold_kernel(*refs):
+    pass
+
+
+def hold(arrays, until):
+    anywhere = pl.BlockSpec(memory_space=pl.ANY)
+    return pl.pallas_call(
+        hold_kernel,
+        out_shape=tuple(jax.ShapeDtypeStruct(a.shape, a.dtype) for a in arrays),
+        in_specs=[anywhere] * (len(arrays) + len(until)),
+        out_specs=(anywhere,) * len(arrays),
+        input_output_aliases={i: i for i in range(len(arrays))},
+        compiler_params=pltpu.CompilerParams(vmem_limit_bytes=1024 * 1024),
+        cost_estimate=pl.CostEstimate(flops=0, bytes_accessed=0, transcendentals=0),
+    )(*arrays, *until)
+
+
+def gather(arrays, nz):
+    far = nz // 2
+
+    def send(held, step):
+        return tuple(lax.ppermute(a, "blk", by_xor(nz, step)) for a in held)
+
+    parts = {0: tuple(arrays)}
+    if nz == 4:
+        parts[2], parts[1] = send(arrays, 2), send(arrays, 1)
+        parts[2] = hold(parts[2], parts[1])
+        parts[3] = send(parts[2], 1)
+    else:
+        while far:
+            parts |= {k ^ far: send(held, far) for k, held in parts.items()}
+            far //= 2
+    return [[parts[k][i] for k in range(nz)] for i in range(len(arrays))]
 
 
 def body(basis, coeffs, stiff_blocks, mass_blocks, block_cols):
@@ -210,24 +267,32 @@
     total_rows = rows * ng
     width = columns // nz
 
-    tag = jnp.pad(block_cols[0, 0].astype(bf16)[None, :], ((0, 15), (0, edge - slots)))
-    payload = jnp.concatenate(
+    payload = call(
+        pack_kernel,
         [
+            block_cols[0],
             stiff_blocks[0, 0].reshape(slots * edge, edge),
             mass_blocks[0, 0].reshape(slots * edge, edge),
-            tag,
         ],
-        axis=0,
-    )
-    first, later = turn_first(current, coeffs, modes)
-    x_parts = gather(first, nz)
-    km_parts = gather(payload, nz)
-    h_parts = gather(later, nz)
+        1,
+        jax.ShapeDtypeStruct((2 * slots * edge + 16, edge), bf16),
+        [],
+        0,
+    )
+    turned = call(
+        turn_kernel,
+        [current, coeffs],
+        0,
+        jax.ShapeDtypeStruct((edge, 2 * modes), bf16),
+        [],
+        2 * edge * columns * 2 * modes,
+    )
+    km_parts, t_parts = gather((payload, turned), nz)
 
     cols = jnp.stack([p[2 * slots * edge, :slots] for p in km_parts]).astype(jnp.int32)
     stats = call(
         functools.partial(stats_kernel, nz, slots, edge),
-        [cols, *x_parts, *km_parts, h_parts[1]],
+        [cols, *t_parts, *km_parts],
         1,
         jax.ShapeDtypeStruct((3, modes), f32),
         [
@@ -241,7 +306,7 @@
 
     turned, stiff_x, mass_x, stats = call(
         functools.partial(sweep_kernel, nz, slots, edge, modes, total_rows),
-        [cols, *x_parts, *h_parts, *km_parts, stats, coeffs[1]],
+        [cols, *t_parts, *km_parts, stats, coeffs],
         1,
         (
             jax.ShapeDtypeStruct((rows, 2 * modes), bf16),

time: 86.5 us -> 82.5 us (0.954)
  starting transfers between devices: 34.5 us -> 19.2 us
  waiting for transfers between devices: 33.4 us -> 43.5 us
  local copies, waits for them, and re-layouts: 4.23 us -> 6.57 us
  other arithmetic: 2.72 us -> 1.08 us
    ppermute x9 -> x6, starting transfers between devices: 23.7 us -> 8.36 us  [send(): return tuple((lax.ppermute(a, 'blk', by_xor(nz, step)) for a in held))]
    ppermute x9 -> x6, waiting for transfers between devices: 15 us -> 24.8 us  [send(): return tuple((lax.ppermute(a, 'blk', by_xor(nz, step)) for a in held))]
    unnamed x6 -> x12, local copies, waits for them, and re-layouts: 2.97 us -> 5.42 us
    ppermute x2, waiting for transfers between devices: 1.13 us -> 2.31 us  [merge_over(): stats = merge(stats, lax.ppermute(stats, axis, by_xor(size, 1)))]
    concatenate x1 -> x0, other arithmetic: 0.99 us -> none  [body(): jnp.concatenate([stiff_blocks[0, 0].reshape(slots * edge, edge), mass_blo...]
    pallas_call x3 -> x5, Pallas kernels: 10.2 us -> 11.2 us  [call(): pl.pallas_call(kernel, out_shape=out_shape, in_specs=[smem()] * n_smem +...]
  transfers between devices with their start and end apart: 21 -> 18, of which waited for: 14 -> 15; matrix products, arithmetic and copies ran while one was open for 1% -> 1% of each run, Pallas kernels for 0% -> 1%
where the time goes in v5:
time: 82.5 us; the launch traced here: 82.3 us
  waiting for transfers between devices  43.5 us (53%)
  starting transfers between devices  19.2 us (23%)
  Pallas kernels  11.2 us (14%)
  local copies, waits for them, and re-layouts  6.57 us (8%)
  other arithmetic  1.08 us (1%)
    ppermute x6, waiting for transfers between devices, send(): return tuple((lax.ppermute(a, 'blk', by_xor(nz, step)) for a in held))  24.8 us
    pallas_call x5, Pallas kernels, call(): pl.pallas_call(kernel, out_shape=out_shape, in_specs=[smem()] * n_smem +...  11.2 us
    ppermute x3, waiting for transfers between devices, body(): total = total + lax.ppermute(mine[k], 'grp', by_xor(ng, 2 * k)).astype(f32)  9.02 us
    ppermute x6, starting transfers between devices, send(): return tuple((lax.ppermute(a, 'blk', by_xor(nz, step)) for a in held))  8.36 us
    ppermute x6, starting transfers between devices, merge_over(): got = [lax.ppermute(stats, axis, by_xor(size, 2 * k)) for k in (1, 2, 3)]  7.11 us
    unnamed x12, local copies, waits for them, and re-layouts  5.42 us
    ppermute x6, waiting for transfers between devices, merge_over(): got = [lax.ppermute(stats, axis, by_xor(size, 2 * k)) for k in (1, 2, 3)]  5.23 us
    ppermute x3, starting transfers between devices, body(): total = total + lax.ppermute(mine[k], 'grp', by_xor(ng, 2 * k)).astype(f32)  3.55 us
  transfers between devices with their start and end apart: 18, of which 15 were waited for; matrix products, arithmetic and copies ran while one was open for 1% of the time, Pallas kernels for 1%

profile of v5, /device:TPU:0, one launch (start us, length us, event | category | flops | bytes accessed | tf_op | source)
XLA Modules:
  0.0 82.3 jit_solution(15917036851322816228)
XLA Ops:
  0.6 0.0 copy-start.3
  0.6 0.9 %copy-done.3 = bf16[1,1,4,128,128]{4,3,2,1,0:T(8,128)(2,1)S(1)} copy-done((bf16[1,1,4,128,128]{4,3,2,1,0:T(8,128)(2,1)S(1)}, bf16[1,1,4,128,128]{4,3,2,1,0:T(8,128)(2,1)}, u32[]{:S(2)}) %copy-start.3) | copy-done | bytes 131096
  1.5 0.0 copy-start.4
  1.5 0.9 %copy-done.4 = bf16[1,1,4,128,128]{4,3,2,1,0:T(8,128)(2,1)S(1)} copy-done((bf16[1,1,4,128,128]{4,3,2,1,0:T(8,128)(2,1)S(1)}, bf16[1,1,4,128,128]{4,3,2,1,0:T(8,128)(2,1)}, u32[]{:S(2)}) %copy-start.4) | copy-done | bytes 131096
  2.4 0.0 copy-start.5
  2.4 0.7 copy-done.5
  3.1 0.6 shard_map.76.refs_4_.refs_0_
  3.7 4.1 %collective-permute-start.1 = (bf16[1040,128]{1,0:T(8,128)(2,1)S(1)}, bf16[1040,128]{1,0:T(8,128)(2,1)S(1)}, u32[]{:S(2)}, u32[]{:S(2)}) collective-permute-start(bf16[1040,128]{1,0:T(8,128)(2,1)S(1)} %shard_map.76.refs_4_.refs_0_), channel_id=1, source_target_pairs={{0,16},{8,24},{16,0},{24,8},{1,17},{9,25},{17,1},{25,9},{2,18},{10... | collective-permute-start | bytes 798728 | tf_op jit(solution)/shard_map/ppermute | solution.py:246
  7.8 1.6 %collective-permute-start = (bf16[1040,128]{1,0:T(8,128)(2,1)S(1)}, bf16[1040,128]{1,0:T(8,128)(2,1)S(1)}, u32[]{:S(2)}, u32[]{:S(2)}) collective-permute-start(bf16[1040,128]{1,0:T(8,128)(2,1)S(1)} %shard_map.76.refs_4_.refs_0_), channel_id=1, source_target_pairs={{0,8},{8,0},{16,24},{24,16},{1,9},{9,1},{17,25},{25,17},{2,10},{10... | collective-permute-start | bytes 798728 | tf_op jit(solution)/shard_map/ppermute | solution.py:246
  9.3 0.0 copy-start
  9.3 2.0 %copy-done = bf16[2,1152,768]{2,1,0:T(8,128)(2,1)S(1)} copy-done((bf16[2,1152,768]{2,1,0:T(8,128)(2,1)S(1)}, bf16[2,1152,768]{2,1,0:T(8,128)(2,1)}, u32[]{:S(2)}) %copy-start) | copy-done | bytes 3538968
  11.3 0.0 copy-start.2
  11.3 1.0 %copy-done.2 = bf16[1,128,1152]{2,1,0:T(8,128)(2,1)S(1)} copy-done((bf16[1,128,1152]{2,1,0:T(8,128)(2,1)S(1)}, bf16[1,128,1152]{2,1,0:T(8,128)(2,1)}, u32[]{:S(2)}) %copy-start.2) | copy-done | bytes 294936
  12.3 0.0 copy-start.1
  12.3 0.4 shard_map.77.refs_0_
  12.7 0.5 collective-permute-start.3
  13.3 0.1 collective-permute-start.2
  13.3 15.3 %collective-permute-done.3.refs_3_.refs_1_ = bf16[128,768]{1,0:T(8,128)(2,1)S(1)} collective-permute-done((bf16[128,768]{1,0:T(8,128)(2,1)S(1)}, bf16[128,768]{1,0:T(8,128)(2,1)S(1)}, u32[]{:S(2)}, u32[]{:S(2)}) %collective-permute-start.3) | collective-permute-done | bytes 196640 | tf_op jit(solution)/shard_map/ppermute | solution.py:246
  28.6 0.0 collective-permute-done.2.refs_1_
  28.6 0.0 collective-permute-done.1.refs_0_
  28.6 0.0 collective-permute-done.refs_2_.refs_5_.refs_1_
  28.6 1.4 %collective-permute-start.4 = (bf16[1040,128]{1,0:T(8,128)(2,1)S(1)}, bf16[1040,128]{1,0:T(8,128)(2,1)S(1)}, u32[]{:S(2)}, u32[]{:S(2)}) collective-permute-start(bf16[1040,128]{1,0:T(8,128)(2,1)S(1)} %get-tuple-element.13.refs_6_.refs_2_), channel_id=1, source_target_pairs={{0,8},{8,0},{16,24},{24,16},{1,9},{9,1},{17,25},{25,17},{2,10},{10... | collective-permute-start | bytes 798728 | tf_op jit(solution)/shard_map/ppermute | solution.py:246
  30.0 0.7 collective-permute-start.5
  30.7 7.3 %collective-permute-done.4.refs_7_.refs_3_ = bf16[1040,128]{1,0:T(8,128)(2,1)S(1)} collective-permute-done((bf16[1040,128]{1,0:T(8,128)(2,1)S(1)}, bf16[1040,128]{1,0:T(8,128)(2,1)S(1)}, u32[]{:S(2)}, u32[]{:S(2)}) %collective-permute-start.4) | collective-permute-done | bytes 266272 | tf_op jit(solution)/shard_map/ppermute | solution.py:246
  38.0 2.2 %collective-permute-done.5.refs_3_ = bf16[128,768]{1,0:T(8,128)(2,1)S(1)} collective-permute-done((bf16[128,768]{1,0:T(8,128)(2,1)S(1)}, bf16[128,768]{1,0:T(8,128)(2,1)S(1)}, u32[]{:S(2)}, u32[]{:S(2)}) %collective-permute-start.5) | collective-permute-done | bytes 196640 | tf_op jit(solution)/shard_map/ppermute | solution.py:246
  40.2 1.6 %shard_map.79 = f32[3,384]{1,0:T(4,128)S(1)} custom-call(s32[4,4]{1,0:T(4,128)S(1)} %maximum_convert_fusion.cols, bf16[128,768]{1,0:T(8,128)(2,1)S(1)} %shard_map.77.refs_0_, bf16[128,768]{1,0:T(8,128)(2,1)S(1)} %collective-permute-done.3.refs_3_.refs_1_, bf16[128,768]{1,0:T(8,128)(2,1)S(1)} %get-tuple-element.14.refs_2_, ...), custom_call_target="tpu_custom_call" | custom-call | flops 100663296 | bytes 4000000 | tf_op jit(solution)/shard_map/pallas_call | solution.py:188
  41.8 0.1 collective-permute-start.6
  41.9 1.2 %collective-permute-done.6 = f32[3,384]{1,0:T(4,128)S(1)} collective-permute-done((f32[3,384]{1,0:T(4,128)S(1)}, f32[3,384]{1,0:T(4,128)S(1)}, u32[]{:S(2)}, u32[]{:S(2)}) %collective-permute-start.6) | collective-permute-done | bytes 4640 | tf_op jit(solution)/shard_map/ppermute | solution.py:214
  43.1 2.6 %collective-permute-start.9 = (f32[3,384]{1,0:T(4,128)S(1)}, f32[3,384]{1,0:T(4,128)S(1)}, u32[]{:S(2)}, u32[]{:S(2)}) collective-permute-start(f32[3,384]{1,0:T(4,128)S(1)} %pad_maximum_fusion), channel_id=1, source_target_pairs={{0,6},{1,7},{2,4},{3,5},{4,2},{5,3},{6,0},{7,1},{8,14},{9,15},{10,... | collective-permute-start | bytes 13832 | tf_op jit(solution)/shard_map/ppermute | solution.py:217
  45.6 0.5 collective-permute-start.8
  46.2 0.5 collective-permute-start.7
  46.6 1.0 %collective-permute-done.9 = f32[3,384]{1,0:T(4,128)S(1)} collective-permute-done((f32[3,384]{1,0:T(4,128)S(1)}, f32[3,384]{1,0:T(4,128)S(1)}, u32[]{:S(2)}, u32[]{:S(2)}) %collective-permute-start.9) | collective-permute-done | bytes 4640 | tf_op jit(solution)/shard_map/ppermute | solution.py:217
  47.7 1.6 %collective-permute-done.8 = f32[3,384]{1,0:T(4,128)S(1)} collective-permute-done((f32[3,384]{1,0:T(4,128)S(1)}, f32[3,384]{1,0:T(4,128)S(1)}, u32[]{:S(2)}, u32[]{:S(2)}) %collective-permute-start.8) | collective-permute-done | bytes 4640 | tf_op jit(solution)/shard_map/ppermute | solution.py:217
  49.3 0.5 collective-permute-done.7
  49.9 0.0 copy-done.1
  49.9 4.7 %shard_map.80 = (bf16[512,768]{1,0:T(8,128)(2,1)S(1)}, f32[512,384]{1,0:T(8,128)S(1)}, f32[512,384]{1,0:T(8,128)S(1)}, f32[3,384]{1,0:T(4,128)S(1)}) custom-call(s32[4,4]{1,0:T(4,128)S(1)} %maximum_convert_fusion.cols, bf16[128,768]{1,0:T(8,128)(2,1)S(1)} %shard_map.77.refs_0_, bf16[128,768]{1,0:T(8,128)(2,1)S(1)} %collective-permute-done.3.refs_3_.refs_1_, ...), custom_call_target="tpu_custom_call" | custom-call | flops 905969664 | bytes 4000000 | tf_op jit(solution)/shard_map/pallas_call | solution.py:188
  54.6 0.1 collective-permute-start.10
  54.6 1.2 %collective-permute-done.10 = f32[3,384]{1,0:T(4,128)S(1)} collective-permute-done((f32[3,384]{1,0:T(4,128)S(1)}, f32[3,384]{1,0:T(4,128)S(1)}, u32[]{:S(2)}, u32[]{:S(2)}) %collective-permute-start.10) | collective-permute-done | bytes 4640 | tf_op jit(solution)/shard_map/ppermute | solution.py:214
  55.8 1.6 %collective-permute-start.13 = (f32[3,384]{1,0:T(4,128)S(1)}, f32[3,384]{1,0:T(4,128)S(1)}, u32[]{:S(2)}, u32[]{:S(2)}) collective-permute-start(f32[3,384]{1,0:T(4,128)S(1)} %pad_maximum_fusion.2), channel_id=1, source_target_pairs={{0,6},{1,7},{2,4},{3,5},{4,2},{5,3},{6,0},{7,1},{8,14},{9,15},{10,... | collective-permute-start | bytes 13832 | tf_op jit(solution)/shard_map/ppermute | solution.py:217
  57.4 0.5 collective-permute-start.12
  57.9 1.5 %collective-permute-start.11 = (f32[3,384]{1,0:T(4,128)S(1)}, f32[3,384]{1,0:T(4,128)S(1)}, u32[]{:S(2)}, u32[]{:S(2)}) collective-permute-start(f32[3,384]{1,0:T(4,128)S(1)} %pad_maximum_fusion.2), channel_id=1, source_target_pairs={{0,2},{1,3},{2,0},{3,1},{4,6},{5,7},{6,4},{7,5},{8,10},{9,11},{10,... | collective-permute-start | bytes 13832 | tf_op jit(solution)/shard_map/ppermute | solution.py:217
  59.4 1.0 %collective-permute-done.13 = f32[3,384]{1,0:T(4,128)S(1)} collective-permute-done((f32[3,384]{1,0:T(4,128)S(1)}, f32[3,384]{1,0:T(4,128)S(1)}, u32[]{:S(2)}, u32[]{:S(2)}) %collective-permute-start.13) | collective-permute-done | bytes 4640 | tf_op jit(solution)/shard_map/ppermute | solution.py:217
  60.4 0.6 collective-permute-done.12
  61.0 0.5 collective-permute-done.11
  61.6 3.9 %shard_map.81 = (bf16[128,1152]{1,0:T(8,128)(2,1)}, f32[1,384]{1,0:T(1,128)S(1)}, bf16[4,144,576]{2,1,0:T(8,128)(2,1)S(1)}, bf16[4,144,576]{2,1,0:T(8,128)(2,1)S(1)}) custom-call(s32[4,4]{1,0:T(4,128)S(1)} %maximum_convert_fusion.cols, bf16[1040,128]{1,0:T(8,128)(2,1)S(1)} %shard_map.76.refs_4_.refs_0_, ...), custom_call_target="tpu_custom_call" | custom-call | flops 679477248 | bytes 4000000 | tf_op jit(solution)/shard_map/pallas_call | solution.py:188
  65.5 0.0 collective-permute-start.14
  65.5 2.2 %collective-permute-done.14 = bf16[4,144,576]{2,1,0:T(8,128)(2,1)S(1)} collective-permute-done((bf16[4,144,576]{2,1,0:T(8,128)(2,1)S(1)}, bf16[4,144,576]{2,1,0:T(8,128)(2,1)S(1)}, u32[]{:S(2)}, u32[]{:S(2)}) %collective-permute-start.14) | collective-permute-done | bytes 663584 | tf_op jit(solution)/shard_map/ppermute | solution.py:345
  67.7 0.2 add_convert_fusion
  67.9 0.1 slice_bitcast_fusion.2
  67.9 1.6 %collective-permute-start.15 = (bf16[144,576]{1,0:T(8,128)(2,1)S(1)}, bf16[144,576]{1,0:T(8,128)(2,1)S(1)}, u32[]{:S(2)}, u32[]{:S(2)}) collective-permute-start(bf16[144,576]{1,0:T(8,128)(2,1)S(1)} %get-tuple-element.31), channel_id=1, source_target_pairs={{0,2},{1,3},{2,0},{3,1},{4,6},{5,7},{6,4},{7,5},{8,10},{9,11},{10,... | collective-permute-start | bytes 497672 | tf_op jit(solution)/shard_map/ppermute | solution.py:349
  69.5 1.5 %collective-permute-start.17 = (bf16[144,576]{1,0:T(8,128)(2,1)S(1)}, bf16[144,576]{1,0:T(8,128)(2,1)S(1)}, u32[]{:S(2)}, u32[]{:S(2)}) collective-permute-start(bf16[144,576]{1,0:T(8,128)(2,1)S(1)} %get-tuple-element.32), channel_id=1, source_target_pairs={{0,6},{1,7},{2,4},{3,5},{4,2},{5,3},{6,0},{7,1},{8,14},{9,15},{10,... | collective-permute-start | bytes 497672 | tf_op jit(solution)/shard_map/ppermute | solution.py:349
  71.0 0.5 collective-permute-start.16
  71.5 0.6 reduce
  72.1 3.4 %collective-permute-done.15 = bf16[144,576]{1,0:T(8,128)(2,1)S(1)} collective-permute-done((bf16[144,576]{1,0:T(8,128)(2,1)S(1)}, bf16[144,576]{1,0:T(8,128)(2,1)S(1)}, u32[]{:S(2)}, u32[]{:S(2)}) %collective-permute-start.15) | collective-permute-done | bytes 165920 | tf_op jit(solution)/shard_map/ppermute | solution.py:349
  75.5 4.3 %collective-permute-done.17 = bf16[144,576]{1,0:T(8,128)(2,1)S(1)} collective-permute-done((bf16[144,576]{1,0:T(8,128)(2,1)S(1)}, bf16[144,576]{1,0:T(8,128)(2,1)S(1)}, u32[]{:S(2)}, u32[]{:S(2)}) %collective-permute-start.17) | collective-permute-done | bytes 165920 | tf_op jit(solution)/shard_map/ppermute | solution.py:349
  79.8 1.4 %collective-permute-done.16 = bf16[144,576]{1,0:T(8,128)(2,1)S(1)} collective-permute-done((bf16[144,576]{1,0:T(8,128)(2,1)S(1)}, bf16[144,576]{1,0:T(8,128)(2,1)S(1)}, u32[]{:S(2)}, u32[]{:S(2)}) %collective-permute-start.16) | collective-permute-done | bytes 165920 | tf_op jit(solution)/shard_map/ppermute | solution.py:349
  81.1 0.1 fusion.1
  81.2 1.1 %reshape.11 = f32[144,2,288]{2,1,0:T(2,128)} reshape(f32[144,576]{1,0:T(8,128)S(1)} %fusion.1) | data formatting | bytes 663552 | tf_op jit(solution)/shard_map/reshape | solution.py:352
  (14 shorter events, 0.2 us)
Async XLA Ops:
  0.6 0.9 %copy-start.3 = (bf16[1,1,4,128,128]{4,3,2,1,0:T(8,128)(2,1)S(1)}, bf16[1,1,4,128,128]{4,3,2,1,0:T(8,128)(2,1)}, u32[]{:S(2)}) copy-start(bf16[1,1,4,128,128]{4,3,2,1,0:T(8,128)(2,1)} %param.7) | copy-start | bytes 393220
  1.5 0.9 %copy-start.4 = (bf16[1,1,4,128,128]{4,3,2,1,0:T(8,128)(2,1)S(1)}, bf16[1,1,4,128,128]{4,3,2,1,0:T(8,128)(2,1)}, u32[]{:S(2)}) copy-start(bf16[1,1,4,128,128]{4,3,2,1,0:T(8,128)(2,1)} %param.8) | copy-start | bytes 393220
  2.4 0.7 copy-start.5
  3.7 24.9 %collective-permute-start.1 = (bf16[1040,128]{1,0:T(8,128)(2,1)S(1)}, bf16[1040,128]{1,0:T(8,128)(2,1)S(1)}, u32[]{:S(2)}, u32[]{:S(2)}) collective-permute-start(bf16[1040,128]{1,0:T(8,128)(2,1)S(1)} %shard_map.76.refs_4_.refs_0_), channel_id=1, source_target_pairs={{0,16},{8,24},{16,0},{24,8},{1,17},{9,25},{17,1},{25,9},{2,18},{10... | collective-permute-start | bytes 798728 | tf_op jit(solution)/shard_map/ppermute | solution.py:246
  7.8 20.8 %collective-permute-start = (bf16[1040,128]{1,0:T(8,128)(2,1)S(1)}, bf16[1040,128]{1,0:T(8,128)(2,1)S(1)}, u32[]{:S(2)}, u32[]{:S(2)}) collective-permute-start(bf16[1040,128]{1,0:T(8,128)(2,1)S(1)} %shard_map.76.refs_4_.refs_0_), channel_id=1, source_target_pairs={{0,8},{8,0},{16,24},{24,16},{1,9},{9,1},{17,25},{25,17},{2,10},{10... | collective-permute-start | bytes 798728 | tf_op jit(solution)/shard_map/ppermute | solution.py:246
  9.3 2.0 %copy-start = (bf16[2,1152,768]{2,1,0:T(8,128)(2,1)S(1)}, bf16[2,1152,768]{2,1,0:T(8,128)(2,1)}, u32[]{:S(2)}) copy-start(bf16[2,1152,768]{2,1,0:T(8,128)(2,1)} %refs_9_.1) | copy-start | bytes 10616836
  11.3 1.0 %copy-start.2 = (bf16[1,128,1152]{2,1,0:T(8,128)(2,1)S(1)}, bf16[1,128,1152]{2,1,0:T(8,128)(2,1)}, u32[]{:S(2)}) copy-start(bf16[1,128,1152]{2,1,0:T(8,128)(2,1)} %param.5) | copy-start | bytes 884740
  12.3 37.6 %copy-start.1 = (bf16[2,1152,768]{2,1,0:T(8,128)(2,1)S(1)}, bf16[2,1152,768]{2,1,0:T(8,128)(2,1)}, u32[]{:S(2)}) copy-start(bf16[2,1152,768]{2,1,0:T(8,128)(2,1)} %refs_9_.1) | copy-start | bytes 10616836
  12.7 15.8 %collective-permute-start.3 = (bf16[128,768]{1,0:T(8,128)(2,1)S(1)}, bf16[128,768]{1,0:T(8,128)(2,1)S(1)}, u32[]{:S(2)}, u32[]{:S(2)}) collective-permute-start(bf16[128,768]{1,0:T(8,128)(2,1)S(1)} %shard_map.77.refs_0_), channel_id=1, source_target_pairs={{0,8},{8,0},{16,24},{24,16},{1,9},{9,1},{17,25},{25,17},{2,10},{10... | collective-permute-start | bytes 589832 | tf_op jit(solution)/shard_map/ppermute | solution.py:246
  13.3 15.3 %collective-permute-start.2 = (bf16[128,768]{1,0:T(8,128)(2,1)S(1)}, bf16[128,768]{1,0:T(8,128)(2,1)S(1)}, u32[]{:S(2)}, u32[]{:S(2)}) collective-permute-start(bf16[128,768]{1,0:T(8,128)(2,1)S(1)} %shard_map.77.refs_0_), channel_id=1, source_target_pairs={{0,16},{8,24},{16,0},{24,8},{1,17},{9,25},{17,1},{25,9},{2,18},{10... | collective-permute-start | bytes 589832 | tf_op jit(solution)/shard_map/ppermute | solution.py:246
  28.6 9.4 %collective-permute-start.4 = (bf16[1040,128]{1,0:T(8,128)(2,1)S(1)}, bf16[1040,128]{1,0:T(8,128)(2,1)S(1)}, u32[]{:S(2)}, u32[]{:S(2)}) collective-permute-start(bf16[1040,128]{1,0:T(8,128)(2,1)S(1)} %get-tuple-element.13.refs_6_.refs_2_), channel_id=1, source_target_pairs={{0,8},{8,0},{16,24},{24,16},{1,9},{9,1},{17,25},{25,17},{2,10},{10... | collective-permute-start | bytes 798728 | tf_op jit(solution)/shard_map/ppermute | solution.py:246
  30.0 10.2 %collective-permute-start.5 = (bf16[128,768]{1,0:T(8,128)(2,1)S(1)}, bf16[128,768]{1,0:T(8,128)(2,1)S(1)}, u32[]{:S(2)}, u32[]{:S(2)}) collective-permute-start(bf16[128,768]{1,0:T(8,128)(2,1)S(1)} %get-tuple-element.14.refs_2_), channel_id=1, source_target_pairs={{0,8},{8,0},{16,24},{24,16},{1,9},{9,1},{17,25},{25,17},{2,10},{10... | collective-permute-start | bytes 589832 | tf_op jit(solution)/shard_map/ppermute | solution.py:246
  41.8 1.2 %collective-permute-start.6 = (f32[3,384]{1,0:T(4,128)S(1)}, f32[3,384]{1,0:T(4,128)S(1)}, u32[]{:S(2)}, u32[]{:S(2)}) collective-permute-start(f32[3,384]{1,0:T(4,128)S(1)} %shard_map.79), channel_id=1, source_target_pairs={{0,1},{1,0},{2,3},{3,2},{4,5},{5,4},{6,7},{7,6},{8,9},{9,8},{10,11... | collective-permute-start | bytes 13832 | tf_op jit(solution)/shard_map/ppermute | solution.py:214
  43.1 4.6 %collective-permute-start.9 = (f32[3,384]{1,0:T(4,128)S(1)}, f32[3,384]{1,0:T(4,128)S(1)}, u32[]{:S(2)}, u32[]{:S(2)}) collective-permute-start(f32[3,384]{1,0:T(4,128)S(1)} %pad_maximum_fusion), channel_id=1, source_target_pairs={{0,6},{1,7},{2,4},{3,5},{4,2},{5,3},{6,0},{7,1},{8,14},{9,15},{10,... | collective-permute-start | bytes 13832 | tf_op jit(solution)/shard_map/ppermute | solution.py:217
  45.6 3.6 %collective-permute-start.8 = (f32[3,384]{1,0:T(4,128)S(1)}, f32[3,384]{1,0:T(4,128)S(1)}, u32[]{:S(2)}, u32[]{:S(2)}) collective-permute-start(f32[3,384]{1,0:T(4,128)S(1)} %pad_maximum_fusion), channel_id=1, source_target_pairs={{0,4},{1,5},{2,6},{3,7},{4,0},{5,1},{6,2},{7,3},{8,12},{9,13},{10,... | collective-permute-start | bytes 13832 | tf_op jit(solution)/shard_map/ppermute | solution.py:217
  46.2 3.6 %collective-permute-start.7 = (f32[3,384]{1,0:T(4,128)S(1)}, f32[3,384]{1,0:T(4,128)S(1)}, u32[]{:S(2)}, u32[]{:S(2)}) collective-permute-start(f32[3,384]{1,0:T(4,128)S(1)} %pad_maximum_fusion), channel_id=1, source_target_pairs={{0,2},{1,3},{2,0},{3,1},{4,6},{5,7},{6,4},{7,5},{8,10},{9,11},{10,... | collective-permute-start | bytes 13832 | tf_op jit(solution)/shard_map/ppermute | solution.py:217
  54.6 1.2 %collective-permute-start.10 = (f32[3,384]{1,0:T(4,128)S(1)}, f32[3,384]{1,0:T(4,128)S(1)}, u32[]{:S(2)}, u32[]{:S(2)}) collective-permute-start(f32[3,384]{1,0:T(4,128)S(1)} %get-tuple-element.18), channel_id=1, source_target_pairs={{0,1},{1,0},{2,3},{3,2},{4,5},{5,4},{6,7},{7,6},{8,9},{9,8},{10,11... | collective-permute-start | bytes 13832 | tf_op jit(solution)/shard_map/ppermute | solution.py:214
  55.8 4.6 %collective-permute-start.13 = (f32[3,384]{1,0:T(4,128)S(1)}, f32[3,384]{1,0:T(4,128)S(1)}, u32[]{:S(2)}, u32[]{:S(2)}) collective-permute-start(f32[3,384]{1,0:T(4,128)S(1)} %pad_maximum_fusion.2), channel_id=1, source_target_pairs={{0,6},{1,7},{2,4},{3,5},{4,2},{5,3},{6,0},{7,1},{8,14},{9,15},{10,... | collective-permute-start | bytes 13832 | tf_op jit(solution)/shard_map/ppermute | solution.py:217
  57.4 3.6 %collective-permute-start.12 = (f32[3,384]{1,0:T(4,128)S(1)}, f32[3,384]{1,0:T(4,128)S(1)}, u32[]{:S(2)}, u32[]{:S(2)}) collective-permute-start(f32[3,384]{1,0:T(4,128)S(1)} %pad_maximum_fusion.2), channel_id=1, source_target_pairs={{0,4},{1,5},{2,6},{3,7},{4,0},{5,1},{6,2},{7,3},{8,12},{9,13},{10,... | collective-permute-start | bytes 13832 | tf_op jit(solution)/shard_map/ppermute | solution.py:217
  57.9 3.6 %collective-permute-start.11 = (f32[3,384]{1,0:T(4,128)S(1)}, f32[3,384]{1,0:T(4,128)S(1)}, u32[]{:S(2)}, u32[]{:S(2)}) collective-permute-start(f32[3,384]{1,0:T(4,128)S(1)} %pad_maximum_fusion.2), channel_id=1, source_target_pairs={{0,2},{1,3},{2,0},{3,1},{4,6},{5,7},{6,4},{7,5},{8,10},{9,11},{10,... | collective-permute-start | bytes 13832 | tf_op jit(solution)/shard_map/ppermute | solution.py:217
  65.5 2.2 %collective-permute-start.14 = (bf16[4,144,576]{2,1,0:T(8,128)(2,1)S(1)}, bf16[4,144,576]{2,1,0:T(8,128)(2,1)S(1)}, u32[]{:S(2)}, u32[]{:S(2)}) collective-permute-start(bf16[4,144,576]{2,1,0:T(8,128)(2,1)S(1)} %get-tuple-element.22), channel_id=1, source_target_pairs={{0,1},{1,0},{2,3},{3,2},{4,5},{5,4},{6,7},{7,6},{8,9},{9,8},{10,11... | collective-permute-start | bytes 1990664 | tf_op jit(solution)/shard_map/ppermute | solution.py:345
  67.9 7.5 %collective-permute-start.15 = (bf16[144,576]{1,0:T(8,128)(2,1)S(1)}, bf16[144,576]{1,0:T(8,128)(2,1)S(1)}, u32[]{:S(2)}, u32[]{:S(2)}) collective-permute-start(bf16[144,576]{1,0:T(8,128)(2,1)S(1)} %get-tuple-element.31), channel_id=1, source_target_pairs={{0,2},{1,3},{2,0},{3,1},{4,6},{5,7},{6,4},{7,5},{8,10},{9,11},{10,... | collective-permute-start | bytes 497672 | tf_op jit(solution)/shard_map/ppermute | solution.py:349
  69.5 10.2 %collective-permute-start.17 = (bf16[144,576]{1,0:T(8,128)(2,1)S(1)}, bf16[144,576]{1,0:T(8,128)(2,1)S(1)}, u32[]{:S(2)}, u32[]{:S(2)}) collective-permute-start(bf16[144,576]{1,0:T(8,128)(2,1)S(1)} %get-tuple-element.32), channel_id=1, source_target_pairs={{0,6},{1,7},{2,4},{3,5},{4,2},{5,3},{6,0},{7,1},{8,14},{9,15},{10,... | collective-permute-start | bytes 497672 | tf_op jit(solution)/shard_map/ppermute | solution.py:349
  71.0 10.1 %collective-permute-start.16 = (bf16[144,576]{1,0:T(8,128)(2,1)S(1)}, bf16[144,576]{1,0:T(8,128)(2,1)S(1)}, u32[]{:S(2)}, u32[]{:S(2)}) collective-permute-start(bf16[144,576]{1,0:T(8,128)(2,1)S(1)} %get-tuple-element.33), channel_id=1, source_target_pairs={{0,4},{1,5},{2,6},{3,7},{4,0},{5,1},{6,2},{7,3},{8,12},{9,13},{10,... | collective-permute-start | bytes 497672 | tf_op jit(solution)/shard_map/ppermute | solution.py:349

commit v6 on v5

--- a/solution.py
+++ b/solution.py
@@ -88,19 +88,14 @@
     return pl.BlockSpec(memory_space=pltpu.HBM)
 
 
-def pack_kernel(cols, stiff, mass, out_ref):
-    rows, edge = stiff.shape
-    out_ref[0:rows, :] = stiff[...]
-    out_ref[rows : 2 * rows, :] = mass[...]
-    lane = lax.broadcasted_iota(jnp.int32, (16, edge), 1)
-    tag = jnp.zeros((16, edge), jnp.int32)
-    for s in range(rows // edge):
+def turn_kernel(modes, cols, current, coeffs, out_ref):
+    rows, columns = out_ref.shape[0] - 16, out_ref.shape[1]
+    lane = lax.broadcasted_iota(jnp.int32, (16, columns), 1)
+    tag = jnp.zeros((16, columns), jnp.int32)
+    for s in range(cols.shape[1]):
         tag = jnp.where(lane == s, cols[0, s], tag)
-    out_ref[2 * rows : 2 * rows + 16, :] = tag.astype(f32).astype(bf16)
-
-
-def turn_kernel(current, coeffs, out_ref):
-    out_ref[...] = jnp.dot(current[...], coeffs[0], preferred_element_type=f32).astype(bf16)
+    out_ref[rows : rows + 16, :] = tag.astype(f32).astype(bf16)
+    out_ref[0:rows, :] = jnp.dot(current[...], coeffs[0], preferred_element_type=f32).astype(bf16)
 
 
 def stats_kernel(nz, slots, edge, cols, *refs):
@@ -109,7 +104,7 @@
     z = lax.axis_index("blk")
     for k in range(nz):
         at = pl.ds(pl.multiple_of((z ^ k) * edge, edge), edge)
-        field[at, :] = t_refs[k][:, : field.shape[1]]
+        field[at, :] = t_refs[k][:edge, : field.shape[1]]
     for k in range(nz):
         both = block_dot(km_refs[k], slots, edge, cols, k, field, slice(None))
         at = pl.ds(pl.multiple_of((z ^ k) * edge, edge), edge)
@@ -127,8 +122,8 @@
     z = lax.axis_index("blk")
     at = [pl.ds(pl.multiple_of((z ^ k) * edge, edge), edge) for k in range(nz)]
     for k in range(nz):
-        full[at[k], 0:modes] = t_refs[k][:, :modes]
-        full[at[k], 2 * modes : 3 * modes] = t_refs[k][:, modes:]
+        full[at[k], 0:modes] = t_refs[k][:edge, :modes]
+        full[at[k], 2 * modes : 3 * modes] = t_refs[k][:edge, modes:]
     shift, scale = shift_and_scale(stats, total_rows)
     for k in range(nz):
         both = block_dot(km_refs[k], slots, edge, cols, k, full, slice(0, modes))
@@ -267,29 +262,24 @@
     total_rows = rows * ng
     width = columns // nz
 
-    payload = call(
-        pack_kernel,
+    payload = jnp.concatenate(
         [
-            block_cols[0],
             stiff_blocks[0, 0].reshape(slots * edge, edge),
             mass_blocks[0, 0].reshape(slots * edge, edge),
         ],
+        axis=0,
+    )
+    turned = call(
+        functools.partial(turn_kernel, modes),
+        [block_cols[0], current, coeffs],
         1,
-        jax.ShapeDtypeStruct((2 * slots * edge + 16, edge), bf16),
-        [],
-        0,
-    )
-    turned = call(
-        turn_kernel,
-        [current, coeffs],
-        0,
-        jax.ShapeDtypeStruct((edge, 2 * modes), bf16),
+        jax.ShapeDtypeStruct((edge + 16, 2 * modes), bf16),
         [],
         2 * edge * columns * 2 * modes,
     )
     km_parts, t_parts = gather((payload, turned), nz)
 
-    cols = jnp.stack([p[2 * slots * edge, :slots] for p in km_parts]).astype(jnp.int32)
+    cols = jnp.stack([p[edge, :slots] for p in t_parts]).astype(jnp.int32)
     stats = call(
         functools.partial(stats_kernel, nz, slots, edge),
         [cols, *t_parts, *km_parts],

time: 82.5 us -> 83.9 us (1.017)
  waiting for transfers between devices: 43.5 us -> 45.7 us
  local copies, waits for them, and re-layouts: 6.57 us -> 4.77 us
  other arithmetic: 1.08 us -> 2.06 us
    ppermute x6, waiting for transfers between devices: 24.8 us -> 27 us  [send(): return tuple((lax.ppermute(a, 'blk', by_xor(nz, step)) for a in held))]
    unnamed x12 -> x8, local copies, waits for them, and re-layouts: 5.42 us -> 3.62 us
    concatenate x0 -> x1, other arithmetic: none -> 0.99 us  [body(): jnp.concatenate([stiff_blocks[0, 0].reshape(slots * edge, edge), mass_blo...]
    pallas_call x5 -> x4, Pallas kernels: 11.2 us -> 11.2 us  [call(): pl.pallas_call(kernel, out_shape=out_shape, in_specs=[smem()] * n_smem +...]
where the time goes in v6:
time: 83.9 us; the launch traced here: 83.7 us
  waiting for transfers between devices  45.7 us (54%)
  starting transfers between devices  19.2 us (23%)
  Pallas kernels  11.2 us (13%)
  local copies, waits for them, and re-layouts  4.77 us (6%)
  other arithmetic  2.06 us (2%)
    ppermute x6, waiting for transfers between devices, send(): return tuple((lax.ppermute(a, 'blk', by_xor(nz, step)) for a in held))  27 us
    pallas_call x4, Pallas kernels, call(): pl.pallas_call(kernel, out_shape=out_shape, in_specs=[smem()] * n_smem +...  11.2 us
    ppermute x3, waiting for transfers between devices, body(): total = total + lax.ppermute(mine[k], 'grp', by_xor(ng, 2 * k)).astype(f32)  8.96 us
    ppermute x6, starting transfers between devices, send(): return tuple((lax.ppermute(a, 'blk', by_xor(nz, step)) for a in held))  8.35 us
    ppermute x6, starting transfers between devices, merge_over(): got = [lax.ppermute(stats, axis, by_xor(size, 2 * k)) for k in (1, 2, 3)]  7.11 us
    ppermute x6, waiting for transfers between devices, merge_over(): got = [lax.ppermute(stats, axis, by_xor(size, 2 * k)) for k in (1, 2, 3)]  5.23 us
    unnamed x8, local copies, waits for them, and re-layouts  3.62 us
    ppermute x3, starting transfers between devices, body(): total = total + lax.ppermute(mine[k], 'grp', by_xor(ng, 2 * k)).astype(f32)  3.55 us
  transfers between devices with their start and end apart: 18, of which 15 were waited for; matrix products, arithmetic and copies ran while one was open for 1% of the time, Pallas kernels for 1%

profile of v6, /device:TPU:0, one launch (start us, length us, event | category | flops | bytes accessed | tf_op | source)
XLA Modules:
  0.0 83.7 jit_solution(16981044576846423163)
XLA Ops:
  0.6 1.0 %pad_maximum_fusion.refs_4_.refs_0_ = bf16[1024,128]{1,0:T(8,128)(2,1)S(1)} fusion(bf16[512,128]{1,0:T(8,128)(2,1)} %bitcast.18, bf16[512,128]{1,0:T(8,128)(2,1)} %bitcast.19), kind=kLoop, calls=%fused_computation.4 | loop fusion | flops 524288 | bytes 524288 | tf_op jit(solution)/shard_map/concatenate | solution.py:265
  1.6 3.1 %collective-permute-start.3 = (bf16[1024,128]{1,0:T(8,128)(2,1)S(1)}, bf16[1024,128]{1,0:T(8,128)(2,1)S(1)}, u32[]{:S(2)}, u32[]{:S(2)}) collective-permute-start(bf16[1024,128]{1,0:T(8,128)(2,1)S(1)} %pad_maximum_fusion.refs_4_.refs_0_), channel_id=1, source_target_pairs={{0,8},{8,0},{16,24},{24,16},{1,9},{9,1},{17,25},{25,17},{2,10},{10... | collective-permute-start | bytes 786440 | tf_op jit(solution)/shard_map/ppermute | solution.py:241
  4.7 2.6 %collective-permute-start.1 = (bf16[1024,128]{1,0:T(8,128)(2,1)S(1)}, bf16[1024,128]{1,0:T(8,128)(2,1)S(1)}, u32[]{:S(2)}, u32[]{:S(2)}) collective-permute-start(bf16[1024,128]{1,0:T(8,128)(2,1)S(1)} %pad_maximum_fusion.refs_4_.refs_0_), channel_id=1, source_target_pairs={{0,16},{8,24},{16,0},{24,8},{1,17},{9,25},{17,1},{25,9},{2,18},{10... | collective-permute-start | bytes 786440 | tf_op jit(solution)/shard_map/ppermute | solution.py:241
  7.3 0.0 copy-start
  7.3 2.0 %copy-done = bf16[2,1152,768]{2,1,0:T(8,128)(2,1)S(1)} copy-done((bf16[2,1152,768]{2,1,0:T(8,128)(2,1)S(1)}, bf16[2,1152,768]{2,1,0:T(8,128)(2,1)}, u32[]{:S(2)}) %copy-start) | copy-done | bytes 3538968
  9.3 0.0 copy-start.2
  9.3 1.0 %copy-done.2 = bf16[1,128,1152]{2,1,0:T(8,128)(2,1)S(1)} copy-done((bf16[1,128,1152]{2,1,0:T(8,128)(2,1)S(1)}, bf16[1,128,1152]{2,1,0:T(8,128)(2,1)}, u32[]{:S(2)}) %copy-start.2) | copy-done | bytes 294936
  10.3 0.0 copy-start.3
  10.3 0.7 copy-done.3
  10.9 0.0 copy-start.1
  10.9 1.0 %shard_map.76.refs_0_ = bf16[144,768]{1,0:T(8,128)(2,1)S(1)} custom-call(s32[1,4]{1,0:T(1,128)S(1)} %bitcast.17, bf16[128,1152]{1,0:T(8,128)(2,1)S(1)} %bitcast.16, bf16[2,1152,768]{2,1,0:T(8,128)(2,1)S(1)} %copy-done), custom_call_target="tpu_custom_call" | custom-call | flops 226492416 | bytes 4000000 | tf_op jit(solution)/shard_map/pallas_call | solution.py:183
  11.9 0.4 collective-permute-start.2
  12.3 0.2 collective-permute-start
  12.5 16.0 %collective-permute-done.2.refs_1_ = bf16[144,768]{1,0:T(8,128)(2,1)S(1)} collective-permute-done((bf16[144,768]{1,0:T(8,128)(2,1)S(1)}, bf16[144,768]{1,0:T(8,128)(2,1)S(1)}, u32[]{:S(2)}, u32[]{:S(2)}) %collective-permute-start.2) | collective-permute-done | bytes 221216 | tf_op jit(solution)/shard_map/ppermute | solution.py:241
  28.5 0.0 collective-permute-done.refs_3_.refs_1_
  28.5 0.0 collective-permute-done.3.refs_2_.refs_5_.refs_1_
  28.5 0.0 collective-permute-done.1.refs_0_
  28.5 0.1 collective-permute-start.4
  28.6 2.0 %collective-permute-start.5 = (bf16[1024,128]{1,0:T(8,128)(2,1)S(1)}, bf16[1024,128]{1,0:T(8,128)(2,1)S(1)}, u32[]{:S(2)}, u32[]{:S(2)}) collective-permute-start(bf16[1024,128]{1,0:T(8,128)(2,1)S(1)} %get-tuple-element.14.refs_6_.refs_2_), channel_id=1, source_target_pairs={{0,8},{8,0},{16,24},{24,16},{1,9},{9,1},{17,25},{25,17},{2,10},{10... | collective-permute-start | bytes 786440 | tf_op jit(solution)/shard_map/ppermute | solution.py:241
  30.6 6.2 %collective-permute-done.4.refs_3_ = bf16[144,768]{1,0:T(8,128)(2,1)S(1)} collective-permute-done((bf16[144,768]{1,0:T(8,128)(2,1)S(1)}, bf16[144,768]{1,0:T(8,128)(2,1)S(1)}, u32[]{:S(2)}, u32[]{:S(2)}) %collective-permute-start.4) | collective-permute-done | bytes 221216 | tf_op jit(solution)/shard_map/ppermute | solution.py:241
  36.9 4.7 %collective-permute-done.5.refs_7_.refs_3_ = bf16[1024,128]{1,0:T(8,128)(2,1)S(1)} collective-permute-done((bf16[1024,128]{1,0:T(8,128)(2,1)S(1)}, bf16[1024,128]{1,0:T(8,128)(2,1)S(1)}, u32[]{:S(2)}, u32[]{:S(2)}) %collective-permute-start.5) | collective-permute-done | bytes 262176 | tf_op jit(solution)/shard_map/ppermute | solution.py:241
  41.6 1.6 %shard_map.78 = f32[3,384]{1,0:T(4,128)S(1)} custom-call(s32[4,4]{1,0:T(4,128)S(1)} %maximum_convert_fusion.cols, bf16[144,768]{1,0:T(8,128)(2,1)S(1)} %shard_map.76.refs_0_, bf16[144,768]{1,0:T(8,128)(2,1)S(1)} %collective-permute-done.refs_3_.refs_1_, bf16[144,768]{1,0:T(8,128)(2,1)S(1)} %get-tuple-element.13.refs_2_, ...), custom_call_target="tpu_custom_call" | custom-call | flops 100663296 | bytes 4000000 | tf_op jit(solution)/shard_map/pallas_call | solution.py:183
  43.2 0.1 collective-permute-start.6
  43.3 1.2 %collective-permute-done.6 = f32[3,384]{1,0:T(4,128)S(1)} collective-permute-done((f32[3,384]{1,0:T(4,128)S(1)}, f32[3,384]{1,0:T(4,128)S(1)}, u32[]{:S(2)}, u32[]{:S(2)}) %collective-permute-start.6) | collective-permute-done | bytes 4640 | tf_op jit(solution)/shard_map/ppermute | solution.py:209
  44.5 2.5 %collective-permute-start.9 = (f32[3,384]{1,0:T(4,128)S(1)}, f32[3,384]{1,0:T(4,128)S(1)}, u32[]{:S(2)}, u32[]{:S(2)}) collective-permute-start(f32[3,384]{1,0:T(4,128)S(1)} %pad_maximum_fusion.1), channel_id=1, source_target_pairs={{0,6},{1,7},{2,4},{3,5},{4,2},{5,3},{6,0},{7,1},{8,14},{9,15},{10,... | collective-permute-start | bytes 13832 | tf_op jit(solution)/shard_map/ppermute | solution.py:212
  47.0 0.5 collective-permute-start.8
  47.5 0.5 collective-permute-start.7
  48.0 1.0 %collective-permute-done.9 = f32[3,384]{1,0:T(4,128)S(1)} collective-permute-done((f32[3,384]{1,0:T(4,128)S(1)}, f32[3,384]{1,0:T(4,128)S(1)}, u32[]{:S(2)}, u32[]{:S(2)}) %collective-permute-start.9) | collective-permute-done | bytes 4640 | tf_op jit(solution)/shard_map/ppermute | solution.py:212
  49.1 1.5 %collective-permute-done.8 = f32[3,384]{1,0:T(4,128)S(1)} collective-permute-done((f32[3,384]{1,0:T(4,128)S(1)}, f32[3,384]{1,0:T(4,128)S(1)}, u32[]{:S(2)}, u32[]{:S(2)}) %collective-permute-start.8) | collective-permute-done | bytes 4640 | tf_op jit(solution)/shard_map/ppermute | solution.py:212
  50.6 0.5 collective-permute-done.7
  51.2 0.0 copy-done.1
  51.2 4.7 %shard_map.79 = (bf16[512,768]{1,0:T(8,128)(2,1)S(1)}, f32[512,384]{1,0:T(8,128)S(1)}, f32[512,384]{1,0:T(8,128)S(1)}, f32[3,384]{1,0:T(4,128)S(1)}) custom-call(s32[4,4]{1,0:T(4,128)S(1)} %maximum_convert_fusion.cols, bf16[144,768]{1,0:T(8,128)(2,1)S(1)} %shard_map.76.refs_0_, bf16[144,768]{1,0:T(8,128)(2,1)S(1)} %collective-permute-done.refs_3_.refs_1_, ...), custom_call_target="tpu_custom_call" | custom-call | flops 905969664 | bytes 4000000 | tf_op jit(solution)/shard_map/pallas_call | solution.py:183
  55.9 0.1 collective-permute-start.10
  56.0 1.2 %collective-permute-done.10 = f32[3,384]{1,0:T(4,128)S(1)} collective-permute-done((f32[3,384]{1,0:T(4,128)S(1)}, f32[3,384]{1,0:T(4,128)S(1)}, u32[]{:S(2)}, u32[]{:S(2)}) %collective-permute-start.10) | collective-permute-done | bytes 4640 | tf_op jit(solution)/shard_map/ppermute | solution.py:209
  57.2 1.6 %collective-permute-start.13 = (f32[3,384]{1,0:T(4,128)S(1)}, f32[3,384]{1,0:T(4,128)S(1)}, u32[]{:S(2)}, u32[]{:S(2)}) collective-permute-start(f32[3,384]{1,0:T(4,128)S(1)} %pad_maximum_fusion.3), channel_id=1, source_target_pairs={{0,6},{1,7},{2,4},{3,5},{4,2},{5,3},{6,0},{7,1},{8,14},{9,15},{10,... | collective-permute-start | bytes 13832 | tf_op jit(solution)/shard_map/ppermute | solution.py:212
  58.8 0.5 collective-permute-start.12
  59.3 1.5 %collective-permute-start.11 = (f32[3,384]{1,0:T(4,128)S(1)}, f32[3,384]{1,0:T(4,128)S(1)}, u32[]{:S(2)}, u32[]{:S(2)}) collective-permute-start(f32[3,384]{1,0:T(4,128)S(1)} %pad_maximum_fusion.3), channel_id=1, source_target_pairs={{0,2},{1,3},{2,0},{3,1},{4,6},{5,7},{6,4},{7,5},{8,10},{9,11},{10,... | collective-permute-start | bytes 13832 | tf_op jit(solution)/shard_map/ppermute | solution.py:212
  60.8 1.0 %collective-permute-done.13 = f32[3,384]{1,0:T(4,128)S(1)} collective-permute-done((f32[3,384]{1,0:T(4,128)S(1)}, f32[3,384]{1,0:T(4,128)S(1)}, u32[]{:S(2)}, u32[]{:S(2)}) %collective-permute-start.13) | collective-permute-done | bytes 4640 | tf_op jit(solution)/shard_map/ppermute | solution.py:212
  61.8 0.6 collective-permute-done.12
  62.4 0.5 collective-permute-done.11
  63.0 3.9 %shard_map.80 = (bf16[128,1152]{1,0:T(8,128)(2,1)}, f32[1,384]{1,0:T(1,128)S(1)}, bf16[4,144,576]{2,1,0:T(8,128)(2,1)S(1)}, bf16[4,144,576]{2,1,0:T(8,128)(2,1)S(1)}) custom-call(s32[4,4]{1,0:T(4,128)S(1)} %maximum_convert_fusion.cols, bf16[1024,128]{1,0:T(8,128)(2,1)S(1)} %pad_maximum_fusion.refs_4_.refs_0_, ...), custom_call_target="tpu_custom_call" | custom-call | flops 679477248 | bytes 4000000 | tf_op jit(solution)/shard_map/pallas_call | solution.py:183
  66.9 0.0 collective-permute-start.14
  66.9 2.2 %collective-permute-done.14 = bf16[4,144,576]{2,1,0:T(8,128)(2,1)S(1)} collective-permute-done((bf16[4,144,576]{2,1,0:T(8,128)(2,1)S(1)}, bf16[4,144,576]{2,1,0:T(8,128)(2,1)S(1)}, u32[]{:S(2)}, u32[]{:S(2)}) %collective-permute-start.14) | collective-permute-done | bytes 663584 | tf_op jit(solution)/shard_map/ppermute | solution.py:335
  69.1 0.2 add_convert_fusion
  69.3 0.1 slice_bitcast_fusion.2
  69.4 1.6 %collective-permute-start.15 = (bf16[144,576]{1,0:T(8,128)(2,1)S(1)}, bf16[144,576]{1,0:T(8,128)(2,1)S(1)}, u32[]{:S(2)}, u32[]{:S(2)}) collective-permute-start(bf16[144,576]{1,0:T(8,128)(2,1)S(1)} %get-tuple-element.31), channel_id=1, source_target_pairs={{0,2},{1,3},{2,0},{3,1},{4,6},{5,7},{6,4},{7,5},{8,10},{9,11},{10,... | collective-permute-start | bytes 497672 | tf_op jit(solution)/shard_map/ppermute | solution.py:339
  70.9 1.5 %collective-permute-start.17 = (bf16[144,576]{1,0:T(8,128)(2,1)S(1)}, bf16[144,576]{1,0:T(8,128)(2,1)S(1)}, u32[]{:S(2)}, u32[]{:S(2)}) collective-permute-start(bf16[144,576]{1,0:T(8,128)(2,1)S(1)} %get-tuple-element.32), channel_id=1, source_target_pairs={{0,6},{1,7},{2,4},{3,5},{4,2},{5,3},{6,0},{7,1},{8,14},{9,15},{10,... | collective-permute-start | bytes 497672 | tf_op jit(solution)/shard_map/ppermute | solution.py:339
  72.4 0.5 collective-permute-start.16
  72.9 0.6 reduce
  73.5 3.4 %collective-permute-done.15 = bf16[144,576]{1,0:T(8,128)(2,1)S(1)} collective-permute-done((bf16[144,576]{1,0:T(8,128)(2,1)S(1)}, bf16[144,576]{1,0:T(8,128)(2,1)S(1)}, u32[]{:S(2)}, u32[]{:S(2)}) %collective-permute-start.15) | collective-permute-done | bytes 165920 | tf_op jit(solution)/shard_map/ppermute | solution.py:339
  76.9 4.2 %collective-permute-done.17 = bf16[144,576]{1,0:T(8,128)(2,1)S(1)} collective-permute-done((bf16[144,576]{1,0:T(8,128)(2,1)S(1)}, bf16[144,576]{1,0:T(8,128)(2,1)S(1)}, u32[]{:S(2)}, u32[]{:S(2)}) %collective-permute-start.17) | collective-permute-done | bytes 165920 | tf_op jit(solution)/shard_map/ppermute | solution.py:339
  81.1 1.4 %collective-permute-done.16 = bf16[144,576]{1,0:T(8,128)(2,1)S(1)} collective-permute-done((bf16[144,576]{1,0:T(8,128)(2,1)S(1)}, bf16[144,576]{1,0:T(8,128)(2,1)S(1)}, u32[]{:S(2)}, u32[]{:S(2)}) %collective-permute-start.16) | collective-permute-done | bytes 165920 | tf_op jit(solution)/shard_map/ppermute | solution.py:339
  82.5 0.1 fusion.1
  82.6 1.1 %reshape.11 = f32[144,2,288]{2,1,0:T(2,128)} reshape(f32[144,576]{1,0:T(8,128)S(1)} %fusion.1) | data formatting | bytes 663552 | tf_op jit(solution)/shard_map/reshape | solution.py:342
  (14 shorter events, 0.2 us)
Async XLA Ops:
  1.6 26.9 %collective-permute-start.3 = (bf16[1024,128]{1,0:T(8,128)(2,1)S(1)}, bf16[1024,128]{1,0:T(8,128)(2,1)S(1)}, u32[]{:S(2)}, u32[]{:S(2)}) collective-permute-start(bf16[1024,128]{1,0:T(8,128)(2,1)S(1)} %pad_maximum_fusion.refs_4_.refs_0_), channel_id=1, source_target_pairs={{0,8},{8,0},{16,24},{24,16},{1,9},{9,1},{17,25},{25,17},{2,10},{10... | collective-permute-start | bytes 786440 | tf_op jit(solution)/shard_map/ppermute | solution.py:241
  4.7 23.8 %collective-permute-start.1 = (bf16[1024,128]{1,0:T(8,128)(2,1)S(1)}, bf16[1024,128]{1,0:T(8,128)(2,1)S(1)}, u32[]{:S(2)}, u32[]{:S(2)}) collective-permute-start(bf16[1024,128]{1,0:T(8,128)(2,1)S(1)} %pad_maximum_fusion.refs_4_.refs_0_), channel_id=1, source_target_pairs={{0,16},{8,24},{16,0},{24,8},{1,17},{9,25},{17,1},{25,9},{2,18},{10... | collective-permute-start | bytes 786440 | tf_op jit(solution)/shard_map/ppermute | solution.py:241
  7.3 2.0 %copy-start = (bf16[2,1152,768]{2,1,0:T(8,128)(2,1)S(1)}, bf16[2,1152,768]{2,1,0:T(8,128)(2,1)}, u32[]{:S(2)}) copy-start(bf16[2,1152,768]{2,1,0:T(8,128)(2,1)} %refs_9_.1) | copy-start | bytes 10616836
  9.3 1.0 %copy-start.2 = (bf16[1,128,1152]{2,1,0:T(8,128)(2,1)S(1)}, bf16[1,128,1152]{2,1,0:T(8,128)(2,1)}, u32[]{:S(2)}) copy-start(bf16[1,128,1152]{2,1,0:T(8,128)(2,1)} %param.5) | copy-start | bytes 884740
  10.3 0.7 copy-start.3
  10.9 40.3 %copy-start.1 = (bf16[2,1152,768]{2,1,0:T(8,128)(2,1)S(1)}, bf16[2,1152,768]{2,1,0:T(8,128)(2,1)}, u32[]{:S(2)}) copy-start(bf16[2,1152,768]{2,1,0:T(8,128)(2,1)} %refs_9_.1) | copy-start | bytes 10616836
  11.9 16.6 %collective-permute-start.2 = (bf16[144,768]{1,0:T(8,128)(2,1)S(1)}, bf16[144,768]{1,0:T(8,128)(2,1)S(1)}, u32[]{:S(2)}, u32[]{:S(2)}) collective-permute-start(bf16[144,768]{1,0:T(8,128)(2,1)S(1)} %shard_map.76.refs_0_), channel_id=1, source_target_pairs={{0,16},{8,24},{16,0},{24,8},{1,17},{9,25},{17,1},{25,9},{2,18},{10... | collective-permute-start | bytes 663560 | tf_op jit(solution)/shard_map/ppermute | solution.py:241
  12.3 16.2 %collective-permute-start = (bf16[144,768]{1,0:T(8,128)(2,1)S(1)}, bf16[144,768]{1,0:T(8,128)(2,1)S(1)}, u32[]{:S(2)}, u32[]{:S(2)}) collective-permute-start(bf16[144,768]{1,0:T(8,128)(2,1)S(1)} %shard_map.76.refs_0_), channel_id=1, source_target_pairs={{0,8},{8,0},{16,24},{24,16},{1,9},{9,1},{17,25},{25,17},{2,10},{10... | collective-permute-start | bytes 663560 | tf_op jit(solution)/shard_map/ppermute | solution.py:241
  28.5 8.3 %collective-permute-start.4 = (bf16[144,768]{1,0:T(8,128)(2,1)S(1)}, bf16[144,768]{1,0:T(8,128)(2,1)S(1)}, u32[]{:S(2)}, u32[]{:S(2)}) collective-permute-start(bf16[144,768]{1,0:T(8,128)(2,1)S(1)} %get-tuple-element.13.refs_2_), channel_id=1, source_target_pairs={{0,8},{8,0},{16,24},{24,16},{1,9},{9,1},{17,25},{25,17},{2,10},{10... | collective-permute-start | bytes 663560 | tf_op jit(solution)/shard_map/ppermute | solution.py:241
  28.6 13.0 %collective-permute-start.5 = (bf16[1024,128]{1,0:T(8,128)(2,1)S(1)}, bf16[1024,128]{1,0:T(8,128)(2,1)S(1)}, u32[]{:S(2)}, u32[]{:S(2)}) collective-permute-start(bf16[1024,128]{1,0:T(8,128)(2,1)S(1)} %get-tuple-element.14.refs_6_.refs_2_), channel_id=1, source_target_pairs={{0,8},{8,0},{16,24},{24,16},{1,9},{9,1},{17,25},{25,17},{2,10},{10... | collective-permute-start | bytes 786440 | tf_op jit(solution)/shard_map/ppermute | solution.py:241
  43.2 1.2 %collective-permute-start.6 = (f32[3,384]{1,0:T(4,128)S(1)}, f32[3,384]{1,0:T(4,128)S(1)}, u32[]{:S(2)}, u32[]{:S(2)}) collective-permute-start(f32[3,384]{1,0:T(4,128)S(1)} %shard_map.78), channel_id=1, source_target_pairs={{0,1},{1,0},{2,3},{3,2},{4,5},{5,4},{6,7},{7,6},{8,9},{9,8},{10,11... | collective-permute-start | bytes 13832 | tf_op jit(solution)/shard_map/ppermute | solution.py:209
  44.5 4.6 %collective-permute-start.9 = (f32[3,384]{1,0:T(4,128)S(1)}, f32[3,384]{1,0:T(4,128)S(1)}, u32[]{:S(2)}, u32[]{:S(2)}) collective-permute-start(f32[3,384]{1,0:T(4,128)S(1)} %pad_maximum_fusion.1), channel_id=1, source_target_pairs={{0,6},{1,7},{2,4},{3,5},{4,2},{5,3},{6,0},{7,1},{8,14},{9,15},{10,... | collective-permute-start | bytes 13832 | tf_op jit(solution)/shard_map/ppermute | solution.py:212
  47.0 3.6 %collective-permute-start.8 = (f32[3,384]{1,0:T(4,128)S(1)}, f32[3,384]{1,0:T(4,128)S(1)}, u32[]{:S(2)}, u32[]{:S(2)}) collective-permute-start(f32[3,384]{1,0:T(4,128)S(1)} %pad_maximum_fusion.1), channel_id=1, source_target_pairs={{0,4},{1,5},{2,6},{3,7},{4,0},{5,1},{6,2},{7,3},{8,12},{9,13},{10,... | collective-permute-start | bytes 13832 | tf_op jit(solution)/shard_map/ppermute | solution.py:212
  47.5 3.6 %collective-permute-start.7 = (f32[3,384]{1,0:T(4,128)S(1)}, f32[3,384]{1,0:T(4,128)S(1)}, u32[]{:S(2)}, u32[]{:S(2)}) collective-permute-start(f32[3,384]{1,0:T(4,128)S(1)} %pad_maximum_fusion.1), channel_id=1, source_target_pairs={{0,2},{1,3},{2,0},{3,1},{4,6},{5,7},{6,4},{7,5},{8,10},{9,11},{10,... | collective-permute-start | bytes 13832 | tf_op jit(solution)/shard_map/ppermute | solution.py:212
  55.9 1.2 %collective-permute-start.10 = (f32[3,384]{1,0:T(4,128)S(1)}, f32[3,384]{1,0:T(4,128)S(1)}, u32[]{:S(2)}, u32[]{:S(2)}) collective-permute-start(f32[3,384]{1,0:T(4,128)S(1)} %get-tuple-element.18), channel_id=1, source_target_pairs={{0,1},{1,0},{2,3},{3,2},{4,5},{5,4},{6,7},{7,6},{8,9},{9,8},{10,11... | collective-permute-start | bytes 13832 | tf_op jit(solution)/shard_map/ppermute | solution.py:209
  57.2 4.6 %collective-permute-start.13 = (f32[3,384]{1,0:T(4,128)S(1)}, f32[3,384]{1,0:T(4,128)S(1)}, u32[]{:S(2)}, u32[]{:S(2)}) collective-permute-start(f32[3,384]{1,0:T(4,128)S(1)} %pad_maximum_fusion.3), channel_id=1, source_target_pairs={{0,6},{1,7},{2,4},{3,5},{4,2},{5,3},{6,0},{7,1},{8,14},{9,15},{10,... | collective-permute-start | bytes 13832 | tf_op jit(solution)/shard_map/ppermute | solution.py:212
  58.8 3.6 %collective-permute-start.12 = (f32[3,384]{1,0:T(4,128)S(1)}, f32[3,384]{1,0:T(4,128)S(1)}, u32[]{:S(2)}, u32[]{:S(2)}) collective-permute-start(f32[3,384]{1,0:T(4,128)S(1)} %pad_maximum_fusion.3), channel_id=1, source_target_pairs={{0,4},{1,5},{2,6},{3,7},{4,0},{5,1},{6,2},{7,3},{8,12},{9,13},{10,... | collective-permute-start | bytes 13832 | tf_op jit(solution)/shard_map/ppermute | solution.py:212
  59.3 3.6 %collective-permute-start.11 = (f32[3,384]{1,0:T(4,128)S(1)}, f32[3,384]{1,0:T(4,128)S(1)}, u32[]{:S(2)}, u32[]{:S(2)}) collective-permute-start(f32[3,384]{1,0:T(4,128)S(1)} %pad_maximum_fusion.3), channel_id=1, source_target_pairs={{0,2},{1,3},{2,0},{3,1},{4,6},{5,7},{6,4},{7,5},{8,10},{9,11},{10,... | collective-permute-start | bytes 13832 | tf_op jit(solution)/shard_map/ppermute | solution.py:212
  66.9 2.2 %collective-permute-start.14 = (bf16[4,144,576]{2,1,0:T(8,128)(2,1)S(1)}, bf16[4,144,576]{2,1,0:T(8,128)(2,1)S(1)}, u32[]{:S(2)}, u32[]{:S(2)}) collective-permute-start(bf16[4,144,576]{2,1,0:T(8,128)(2,1)S(1)} %get-tuple-element.22), channel_id=1, source_target_pairs={{0,1},{1,0},{2,3},{3,2},{4,5},{5,4},{6,7},{7,6},{8,9},{9,8},{10,11... | collective-permute-start | bytes 1990664 | tf_op jit(solution)/shard_map/ppermute | solution.py:335
  69.4 7.5 %collective-permute-start.15 = (bf16[144,576]{1,0:T(8,128)(2,1)S(1)}, bf16[144,576]{1,0:T(8,128)(2,1)S(1)}, u32[]{:S(2)}, u32[]{:S(2)}) collective-permute-start(bf16[144,576]{1,0:T(8,128)(2,1)S(1)} %get-tuple-element.31), channel_id=1, source_target_pairs={{0,2},{1,3},{2,0},{3,1},{4,6},{5,7},{6,4},{7,5},{8,10},{9,11},{10,... | collective-permute-start | bytes 497672 | tf_op jit(solution)/shard_map/ppermute | solution.py:339
  70.9 10.2 %collective-permute-start.17 = (bf16[144,576]{1,0:T(8,128)(2,1)S(1)}, bf16[144,576]{1,0:T(8,128)(2,1)S(1)}, u32[]{:S(2)}, u32[]{:S(2)}) collective-permute-start(bf16[144,576]{1,0:T(8,128)(2,1)S(1)} %get-tuple-element.32), channel_id=1, source_target_pairs={{0,6},{1,7},{2,4},{3,5},{4,2},{5,3},{6,0},{7,1},{8,14},{9,15},{10,... | collective-permute-start | bytes 497672 | tf_op jit(solution)/shard_map/ppermute | solution.py:339
  72.4 10.1 %collective-permute-start.16 = (bf16[144,576]{1,0:T(8,128)(2,1)S(1)}, bf16[144,576]{1,0:T(8,128)(2,1)S(1)}, u32[]{:S(2)}, u32[]{:S(2)}) collective-permute-start(bf16[144,576]{1,0:T(8,128)(2,1)S(1)} %get-tuple-element.33), channel_id=1, source_target_pairs={{0,4},{1,5},{2,6},{3,7},{4,0},{5,1},{6,2},{7,3},{8,12},{9,13},{10,... | collective-permute-start | bytes 497672 | tf_op jit(solution)/shard_map/ppermute | solution.py:339

commit v7 on v6

--- a/solution.py
+++ b/solution.py
@@ -36,13 +36,6 @@
         jnp.concatenate(rows, axis=0),
         preferred_element_type=f32,
     )
-
-
-def column_stats(stiff_x, mass_x):
-    num = jnp.sum(stiff_x * mass_x, axis=0, keepdims=True)
-    den = jnp.sum(mass_x * mass_x, axis=0, keepdims=True)
-    rest = stiff_x - (num / jnp.maximum(den, tiny)) * mass_x
-    return num, den, jnp.sum(rest * rest, axis=0, keepdims=True)
 
 
 def shift_and_scale(stats, total_rows):
@@ -98,52 +91,92 @@
     out_ref[0:rows, :] = jnp.dot(current[...], coeffs[0], preferred_element_type=f32).astype(bf16)
 
 
-def stats_kernel(nz, slots, edge, cols, *refs):
-    t_refs, km_refs = refs[:nz], refs[nz : 2 * nz]
-    stats_ref, field, stiff, mass = refs[2 * nz :]
+def rows_kernel(nz, slots, edge, modes, cols, *refs):
+    t_refs, km_refs = refs[:nz], refs[nz : 2 * nz - 1]
+    placed, stiff_ref, mass_ref = refs[2 * nz - 1 :]
     z = lax.axis_index("blk")
     for k in range(nz):
-        at = pl.ds(pl.multiple_of((z ^ k) * edge, edge), edge)
-        field[at, :] = t_refs[k][:edge, : field.shape[1]]
-    for k in range(nz):
-        both = block_dot(km_refs[k], slots, edge, cols, k, field, slice(None))
-        at = pl.ds(pl.multiple_of((z ^ k) * edge, edge), edge)
-        stiff[at, :] = both[:edge]
-        mass[at, :] = both[edge:]
-    num, den, about = column_stats(stiff[...], mass[...])
-    stats_ref[0:1, :] = num
-    stats_ref[1:2, :] = den
+        placed[pl.ds(pl.multiple_of((z ^ k) * edge, edge), edge), :] = t_refs[k][:edge, :]
+    for k in range(nz - 1):
+        both = block_dot(km_refs[k], slots, edge, cols, k, placed, slice(0, modes))
+        stiff_ref[k] = both[:edge]
+        mass_ref[k] = both[edge:]
+
+
+def block_stats(z, pairs, sums, stats_ref):
+    for k, (stiff_x, mass_x) in enumerate(pairs):
+        sums[z ^ k, 0:1, :] = jnp.sum(stiff_x * mass_x, axis=0, keepdims=True)
+        sums[z ^ k, 1:2, :] = jnp.sum(mass_x * mass_x, axis=0, keepdims=True)
+    total = sums[0]
+    for r in range(1, len(pairs)):
+        total = total + sums[r]
+    own_shift = total[0:1, :] / jnp.maximum(total[1:2, :], tiny)
+    for k, (stiff_x, mass_x) in enumerate(pairs):
+        rest = stiff_x - own_shift * mass_x
+        sums[z ^ k, 2:3, :] = jnp.sum(rest * rest, axis=0, keepdims=True)
+    about = sums[0, 2:3, :]
+    for r in range(1, len(pairs)):
+        about = about + sums[r, 2:3, :]
+    stats_ref[0:2, :] = total[0:2, :]
     stats_ref[2:3, :] = about
 
 
+def stats_kernel(nz, slots, edge, modes, cols, km_last, placed, stiff, mass, stiff_ref, mass_ref, stats_ref, sums):
+    z = lax.axis_index("blk")
+    both = block_dot(km_last, slots, edge, cols, nz - 1, placed, slice(0, modes))
+    stiff_ref[...] = both[:edge]
+    mass_ref[...] = both[edge:]
+    pairs = [(stiff[k], mass[k]) for k in range(nz - 1)] + [(both[:edge], both[edge:])]
+    sums[...] = jnp.zeros_like(sums)
+    block_stats(z, pairs, sums, stats_ref)
+
+
+def early_turn_kernel(modes, placed, coeffs, out_ref):
+    out_ref[...] = jnp.dot(
+        placed[:, :modes], coeffs[1, :modes, :], preferred_element_type=f32
+    ) + jnp.dot(placed[:, modes:], coeffs[1, 2 * modes :, :], preferred_element_type=f32)
+
+
 def sweep_kernel(nz, slots, edge, modes, total_rows, cols, *refs):
-    t_refs, km_refs = refs[:nz], refs[nz : 2 * nz]
-    stats, coeffs, turned_ref, stiff_ref, mass_ref, stats_ref, full = refs[2 * nz :]
+    km_refs = refs[:nz]
+    early, stiff, mass, stiff_last, mass_last, stats, coeffs = refs[nz : nz + 7]
+    turned_ref, stiff_ref, mass_ref, stats_ref, search, sums = refs[nz + 7 :]
     z = lax.axis_index("blk")
     at = [pl.ds(pl.multiple_of((z ^ k) * edge, edge), edge) for k in range(nz)]
-    for k in range(nz):
-        full[at[k], 0:modes] = t_refs[k][:edge, :modes]
-        full[at[k], 2 * modes : 3 * modes] = t_refs[k][:edge, modes:]
     shift, scale = shift_and_scale(stats, total_rows)
     for k in range(nz):
-        both = block_dot(km_refs[k], slots, edge, cols, k, full, slice(0, modes))
-        full[at[k], modes : 2 * modes] = ((both[:edge] - shift * both[edge:]) * scale).astype(bf16)
-    turned_ref[...] = jnp.dot(full[...], coeffs[1], preferred_element_type=f32).astype(bf16)
+        stiff_x = stiff[k] if k < nz - 1 else stiff_last[...]
+        mass_x = mass[k] if k < nz - 1 else mass_last[...]
+        search[at[k], :] = ((stiff_x - shift * mass_x) * scale).astype(bf16)
+    late = jnp.dot(search[...], coeffs[1, modes : 2 * modes, :], preferred_element_type=f32)
+    turned_ref[...] = (early[...] + late).astype(bf16)
+    pairs = []
     for k in range(nz):
         both = block_dot(km_refs[k], slots, edge, cols, k, turned_ref, slice(0, modes))
         stiff_ref[at[k], :] = both[:edge]
         mass_ref[at[k], :] = both[edge:]
-    num, den, about = column_stats(stiff_ref[...], mass_ref[...])
-    stats_ref[0:1, :] = num
-    stats_ref[1:2, :] = den
-    stats_ref[2:3, :] = about
-
-
-def gram_kernel(nz, ng, slots, edge, modes, total_rows, split, cols, *refs):
+        pairs.append((both[:edge], both[edge:]))
+    sums[...] = jnp.zeros_like(sums)
+    block_stats(z, pairs, sums, stats_ref)
+
+
+def gram_rows(full_t, applied, chips, core, out_ref):
+    chip = lax.div(lax.axis_index("grp"), 2)
+    block = full_t.shape[0] // (2 * chips)
+    rows = [
+        full_t[pl.ds(pl.multiple_of((2 * j + core) * block, 16), block), :] for j in range(chips)
+    ]
+    gram = jnp.dot(jnp.concatenate(rows, axis=0), applied[...], preferred_element_type=f32)
+    gram = gram.astype(bf16)
+    for j in range(chips):
+        out_ref[j ^ chip] = gram[j * block : (j + 1) * block]
+
+
+def gram_kernel(nz, chips, slots, edge, modes, total_rows, split, cols, *refs):
     km_refs = refs[:nz]
-    turned, stiff, mass, stats, basis_ref, ritz_ref, gram_ref, send_ref, full, chosen, applied = refs[nz:]
-    z, g = lax.axis_index("blk"), lax.axis_index("grp")
-    core, chip = lax.rem(g, 2), lax.div(g, 2)
+    turned, stiff, mass, stats = refs[nz : nz + 4]
+    basis_ref, ritz_ref, gram_ref, full_t, applied, full, chosen = refs[nz + 4 :]
+    z = lax.axis_index("blk")
     at = [pl.ds(pl.multiple_of((z ^ k) * edge, edge), edge) for k in range(nz)]
     width = 3 * modes // nz
     shift, scale = shift_and_scale(stats, total_rows)
@@ -160,23 +193,15 @@
         both = block_dot(km_refs[k], slots, edge, cols, k, chosen, slice(0, width)).astype(bf16)
         applied[at[k], 0:width] = both[:edge]
         applied[at[k], width : 2 * width] = both[edge:]
-    gram = lax.dot_general(
-        full[...], applied[...], (((0,), (0,)), ((), ())), preferred_element_type=f32
-    ).astype(bf16)
+    full_t[...] = full[...].T
     if split:
-        rows = 3 * modes // ng
-        for q in range(ng):
-            piece = gram[q * rows : (q + 1) * rows]
-
-            @pl.when(core == q % 2)
-            def _():
-                gram_ref[(q // 2) ^ chip] = piece
-
-            @pl.when(core != q % 2)
-            def _():
-                send_ref[(q // 2) ^ chip] = piece
+        gram_rows(full_t, applied, chips, 1 - lax.rem(lax.axis_index("grp"), 2), gram_ref)
     else:
-        gram_ref[...] = gram
+        gram_ref[...] = jnp.dot(full_t[...], applied[...], preferred_element_type=f32).astype(bf16)
+
+
+def gram_rest_kernel(chips, full_t, applied, gram_ref):
+    gram_rows(full_t, applied, chips, lax.rem(lax.axis_index("grp"), 2), gram_ref)
 
 
 def call(kernel, inputs, n_smem, out_shape, scratch, flops):
@@ -280,60 +305,82 @@
     km_parts, t_parts = gather((payload, turned), nz)
 
     cols = jnp.stack([p[edge, :slots] for p in t_parts]).astype(jnp.int32)
-    stats = call(
-        functools.partial(stats_kernel, nz, slots, edge),
-        [cols, *t_parts, *km_parts],
+    some = jax.ShapeDtypeStruct((nz - 1, edge, modes), f32)
+    last = jax.ShapeDtypeStruct((edge, modes), f32)
+    stats_shape = jax.ShapeDtypeStruct((3, modes), f32)
+    work = 4 * edge * slots * edge * modes
+    placed, stiff_some, mass_some = call(
+        functools.partial(rows_kernel, nz, slots, edge, modes),
+        [cols, *t_parts, *km_parts[:-1]],
         1,
-        jax.ShapeDtypeStruct((3, modes), f32),
-        [
-            pltpu.VMEM((rows, modes), bf16),
-            pltpu.VMEM((rows, modes), f32),
-            pltpu.VMEM((rows, modes), f32),
-        ],
-        4 * edge * slots * edge * modes,
+        (jax.ShapeDtypeStruct((rows, 2 * modes), bf16), some, some),
+        [],
+        (nz - 1) * work,
+    )
+    stiff_last, mass_last, stats = call(
+        functools.partial(stats_kernel, nz, slots, edge, modes),
+        [cols, km_parts[-1], placed, stiff_some, mass_some],
+        1,
+        (last, last, stats_shape),
+        [pltpu.VMEM((nz, 8, modes), f32)],
+        work,
     )
     stats = merge_over("grp", ng, stats)
-
+    early = call(
+        functools.partial(early_turn_kernel, modes),
+        [placed, coeffs],
+        0,
+        jax.ShapeDtypeStruct((rows, 2 * modes), f32),
+        [],
+        8 * rows * modes * modes,
+    )
     turned, stiff_x, mass_x, stats = call(
         functools.partial(sweep_kernel, nz, slots, edge, modes, total_rows),
-        [cols, *t_parts, *km_parts, stats, coeffs],
+        [cols, *km_parts, early, stiff_some, mass_some, stiff_last, mass_last, stats, coeffs],
         1,
         (
             jax.ShapeDtypeStruct((rows, 2 * modes), bf16),
             jax.ShapeDtypeStruct((rows, modes), f32),
             jax.ShapeDtypeStruct((rows, modes), f32),
-            jax.ShapeDtypeStruct((3, modes), f32),
+            stats_shape,
         ),
-        [pltpu.VMEM((rows, columns), bf16)],
-        2 * rows * columns * 2 * modes,
+        [pltpu.VMEM((rows, modes), bf16), pltpu.VMEM((nz, 8, modes), f32)],
+        4 * rows * modes * modes + nz * work,
     )
     stats = merge_over("grp", ng, stats)
 
-    split = (columns // ng) % 16 == 0
     chips = ng // 2
     block = columns // ng
-    gram_shape = (chips, block, 2 * width) if split else (columns, 2 * width)
+    split = block % 16 == 0
+    gram_shape = jax.ShapeDtypeStruct(
+        (chips, block, 2 * width) if split else (columns, 2 * width), bf16
+    )
     window = -(-(width + max(i * width % 128 for i in range(nz))) // 128) * 128
-    basis_out, ritz, gram, send = call(
-        functools.partial(gram_kernel, nz, ng, slots, edge, modes, total_rows, split),
+    basis_out, ritz, gram, full_t, applied = call(
+        functools.partial(gram_kernel, nz, chips, slots, edge, modes, total_rows, split),
         [cols, *km_parts, turned, stiff_x, mass_x, stats],
         1,
         (
             jax.ShapeDtypeStruct((edge, columns), bf16),
             jax.ShapeDtypeStruct((1, modes), f32),
-            jax.ShapeDtypeStruct(gram_shape, bf16),
-            jax.ShapeDtypeStruct(gram_shape, bf16),
+            gram_shape,
+            jax.ShapeDtypeStruct((columns, rows), bf16),
+            jax.ShapeDtypeStruct((rows, 2 * width), bf16),
         ),
-        [
-            pltpu.VMEM((rows, columns), bf16),
-            pltpu.VMEM((rows, window), bf16),
-            pltpu.VMEM((rows, 2 * width), bf16),
-        ],
-        2 * rows * columns * 2 * width,
+        [pltpu.VMEM((rows, columns), bf16), pltpu.VMEM((rows, window), bf16)],
+        2 * rows * columns * width,
     )
     if split:
-        got = lax.ppermute(send, "grp", by_xor(ng, 1))
-        mine = (gram.astype(f32) + got.astype(f32)).astype(bf16)
+        got = lax.ppermute(gram, "grp", by_xor(ng, 1))
+        keep = call(
+            functools.partial(gram_rest_kernel, chips),
+            [full_t, applied],
+            0,
+            gram_shape,
+            [],
+            2 * rows * columns * width,
+        )
+        mine = (keep.astype(f32) + got.astype(f32)).astype(bf16)
         total = mine[0].astype(f32)
         for k in range(1, chips):
             total = total + lax.ppermute(mine[k], "grp", by_xor(ng, 2 * k)).astype(f32)

time: 83.9 us -> 80.6 us (0.961)
  waiting for transfers between devices: 45.7 us -> 42.9 us
    ppermute x6, waiting for transfers between devices: 27 us -> 25.8 us  [send(): return tuple((lax.ppermute(a, 'blk', by_xor(nz, step)) for a in held))]
    ppermute x6, waiting for transfers between devices: 5.23 us -> 4.25 us  [merge_over(): got = [lax.ppermute(stats, axis, by_xor(size, 2 * k)) for k in (1, 2, 3)]]
    pallas_call x4 -> x7, Pallas kernels: 11.2 us -> 10.7 us  [call(): pl.pallas_call(kernel, out_shape=out_shape, in_specs=[smem()] * n_smem +...]
  transfers between devices with their start and end apart: 18 -> 18, of which waited for: 15 -> 15; matrix products, arithmetic and copies ran while one was open for 1% -> 1% of each run, Pallas kernels for 1% -> 5%
where the time goes in v7:
time: 80.6 us; the launch traced here: 80.4 us
  waiting for transfers between devices  42.9 us (53%)
  starting transfers between devices  19.2 us (24%)
  Pallas kernels  10.7 us (13%)
  local copies, waits for them, and re-layouts  4.77 us (6%)
  other arithmetic  2.06 us (3%)
    ppermute x6, waiting for transfers between devices, send(): return tuple((lax.ppermute(a, 'blk', by_xor(nz, step)) for a in held))  25.8 us
    pallas_call x7, Pallas kernels, call(): pl.pallas_call(kernel, out_shape=out_shape, in_specs=[smem()] * n_smem +...  10.7 us
    ppermute x3, waiting for transfers between devices, body(): total = total + lax.ppermute(mine[k], 'grp', by_xor(ng, 2 * k)).astype(f32)  8.96 us
    ppermute x6, starting transfers between devices, send(): return tuple((lax.ppermute(a, 'blk', by_xor(nz, step)) for a in held))  8.35 us
    ppermute x6, starting transfers between devices, merge_over(): got = [lax.ppermute(stats, axis, by_xor(size, 2 * k)) for k in (1, 2, 3)]  7.11 us
    ppermute x6, waiting for transfers between devices, merge_over(): got = [lax.ppermute(stats, axis, by_xor(size, 2 * k)) for k in (1, 2, 3)]  4.25 us
    unnamed x8, local copies, waits for them, and re-layouts  3.62 us
    ppermute x3, starting transfers between devices, body(): total = total + lax.ppermute(mine[k], 'grp', by_xor(ng, 2 * k)).astype(f32)  3.55 us
  transfers between devices with their start and end apart: 18, of which 15 were waited for; matrix products, arithmetic and copies ran while one was open for 1% of the time, Pallas kernels for 5%

profile of v7, /device:TPU:0, one launch (start us, length us, event | category | flops | bytes accessed | tf_op | source)
XLA Modules:
  0.0 80.4 jit_solution(7412007295269538047)
XLA Ops:
  0.6 1.0 %pad_maximum_fusion.refs_4_.refs_0_ = bf16[1024,128]{1,0:T(8,128)(2,1)S(1)} fusion(bf16[512,128]{1,0:T(8,128)(2,1)} %bitcast.18, bf16[512,128]{1,0:T(8,128)(2,1)} %bitcast.19), kind=kLoop, calls=%fused_computation.4 | loop fusion | flops 524288 | bytes 524288 | tf_op jit(solution)/shard_map/concatenate | solution.py:290
  1.6 3.1 %collective-permute-start.3 = (bf16[1024,128]{1,0:T(8,128)(2,1)S(1)}, bf16[1024,128]{1,0:T(8,128)(2,1)S(1)}, u32[]{:S(2)}, u32[]{:S(2)}) collective-permute-start(bf16[1024,128]{1,0:T(8,128)(2,1)S(1)} %pad_maximum_fusion.refs_4_.refs_0_), channel_id=1, source_target_pairs={{0,8},{8,0},{16,24},{24,16},{1,9},{9,1},{17,25},{25,17},{2,10},{10... | collective-permute-start | bytes 786440 | tf_op jit(solution)/shard_map/ppermute | solution.py:266
  4.7 2.6 %collective-permute-start.1 = (bf16[1024,128]{1,0:T(8,128)(2,1)S(1)}, bf16[1024,128]{1,0:T(8,128)(2,1)S(1)}, u32[]{:S(2)}, u32[]{:S(2)}) collective-permute-start(bf16[1024,128]{1,0:T(8,128)(2,1)S(1)} %pad_maximum_fusion.refs_4_.refs_0_), channel_id=1, source_target_pairs={{0,16},{8,24},{16,0},{24,8},{1,17},{9,25},{17,1},{25,9},{2,18},{10... | collective-permute-start | bytes 786440 | tf_op jit(solution)/shard_map/ppermute | solution.py:266
  7.3 0.0 copy-start
  7.3 2.0 %copy-done = bf16[2,1152,768]{2,1,0:T(8,128)(2,1)S(1)} copy-done((bf16[2,1152,768]{2,1,0:T(8,128)(2,1)S(1)}, bf16[2,1152,768]{2,1,0:T(8,128)(2,1)}, u32[]{:S(2)}) %copy-start) | copy-done | bytes 3538968
  9.3 0.0 copy-start.2
  9.3 1.0 %copy-done.2 = bf16[1,128,1152]{2,1,0:T(8,128)(2,1)S(1)} copy-done((bf16[1,128,1152]{2,1,0:T(8,128)(2,1)S(1)}, bf16[1,128,1152]{2,1,0:T(8,128)(2,1)}, u32[]{:S(2)}) %copy-start.2) | copy-done | bytes 294936
  10.3 0.0 copy-start.3
  10.3 0.7 copy-done.3
  10.9 1.0 %shard_map.76.refs_0_ = bf16[144,768]{1,0:T(8,128)(2,1)S(1)} custom-call(s32[1,4]{1,0:T(1,128)S(1)} %bitcast.17, bf16[128,1152]{1,0:T(8,128)(2,1)S(1)} %bitcast.16, bf16[2,1152,768]{2,1,0:T(8,128)(2,1)S(1)} %copy-done), custom_call_target="tpu_custom_call" | custom-call | flops 226492416 | bytes 4000000 | tf_op jit(solution)/shard_map/pallas_call | solution.py:208
  11.9 0.4 collective-permute-start.2
  12.3 0.2 collective-permute-start
  12.5 16.0 %collective-permute-done.2.refs_1_ = bf16[144,768]{1,0:T(8,128)(2,1)S(1)} collective-permute-done((bf16[144,768]{1,0:T(8,128)(2,1)S(1)}, bf16[144,768]{1,0:T(8,128)(2,1)S(1)}, u32[]{:S(2)}, u32[]{:S(2)}) %collective-permute-start.2) | collective-permute-done | bytes 221216 | tf_op jit(solution)/shard_map/ppermute | solution.py:266
  28.5 0.0 collective-permute-done.refs_3_.refs_1_
  28.5 0.0 collective-permute-done.3.refs_2_.refs_5_.refs_1_
  28.5 0.0 collective-permute-done.1.refs_0_
  28.5 0.1 collective-permute-start.4
  28.6 2.0 %collective-permute-start.5 = (bf16[1024,128]{1,0:T(8,128)(2,1)S(1)}, bf16[1024,128]{1,0:T(8,128)(2,1)S(1)}, u32[]{:S(2)}, u32[]{:S(2)}) collective-permute-start(bf16[1024,128]{1,0:T(8,128)(2,1)S(1)} %get-tuple-element.21.refs_6_.refs_2_), channel_id=1, source_target_pairs={{0,8},{8,0},{16,24},{24,16},{1,9},{9,1},{17,25},{25,17},{2,10},{10... | collective-permute-start | bytes 786440 | tf_op jit(solution)/shard_map/ppermute | solution.py:266
  30.6 6.2 %collective-permute-done.4.refs_3_ = bf16[144,768]{1,0:T(8,128)(2,1)S(1)} collective-permute-done((bf16[144,768]{1,0:T(8,128)(2,1)S(1)}, bf16[144,768]{1,0:T(8,128)(2,1)S(1)}, u32[]{:S(2)}, u32[]{:S(2)}) %collective-permute-start.4) | collective-permute-done | bytes 221216 | tf_op jit(solution)/shard_map/ppermute | solution.py:266
  36.9 0.0 copy-start.1
  36.9 1.2 %shard_map.78 = (bf16[512,768]{1,0:T(8,128)(2,1)S(1)}, f32[3,128,384]{2,1,0:T(8,128)S(1)}, f32[3,128,384]{2,1,0:T(8,128)S(1)}) custom-call(s32[4,4]{1,0:T(4,128)S(1)} %maximum_convert_fusion.cols, bf16[144,768]{1,0:T(8,128)(2,1)S(1)} %shard_map.76.refs_0_, bf16[144,768]{1,0:T(8,128)(2,1)S(1)} %collective-permute-done.refs_3_.refs_1_, ...), custom_call_target="tpu_custom_call" | custom-call | flops 301989888 | bytes 4000000 | tf_op jit(solution)/shard_map/pallas_call | solution.py:208
  38.1 3.5 %collective-permute-done.5.km_last.refs_3_ = bf16[1024,128]{1,0:T(8,128)(2,1)S(1)} collective-permute-done((bf16[1024,128]{1,0:T(8,128)(2,1)S(1)}, bf16[1024,128]{1,0:T(8,128)(2,1)S(1)}, u32[]{:S(2)}, u32[]{:S(2)}) %collective-permute-start.5) | collective-permute-done | bytes 262176 | tf_op jit(solution)/shard_map/ppermute | solution.py:266
  41.6 1.1 %shard_map.80 = (f32[128,384]{1,0:T(8,128)S(1)}, f32[128,384]{1,0:T(8,128)S(1)}, f32[3,384]{1,0:T(4,128)S(1)}) custom-call(s32[4,4]{1,0:T(4,128)S(1)} %maximum_convert_fusion.cols, bf16[1024,128]{1,0:T(8,128)(2,1)S(1)} %collective-permute-done.5.km_last.refs_3_, bf16[512,768]{1,0:T(8,128)(2,1)S(1)} %get-tuple-element.22.placed, ...), custom_call_target="tpu_custom_call" | custom-call | flops 100663296 | bytes 4000000 | tf_op jit(solution)/shard_map/pallas_call | solution.py:208
  42.7 0.1 collective-permute-start.6
  42.8 1.2 %collective-permute-done.6 = f32[3,384]{1,0:T(4,128)S(1)} collective-permute-done((f32[3,384]{1,0:T(4,128)S(1)}, f32[3,384]{1,0:T(4,128)S(1)}, u32[]{:S(2)}, u32[]{:S(2)}) %collective-permute-start.6) | collective-permute-done | bytes 4640 | tf_op jit(solution)/shard_map/ppermute | solution.py:234
  44.0 2.5 %collective-permute-start.9 = (f32[3,384]{1,0:T(4,128)S(1)}, f32[3,384]{1,0:T(4,128)S(1)}, u32[]{:S(2)}, u32[]{:S(2)}) collective-permute-start(f32[3,384]{1,0:T(4,128)S(1)} %pad_maximum_fusion.1), channel_id=1, source_target_pairs={{0,6},{1,7},{2,4},{3,5},{4,2},{5,3},{6,0},{7,1},{8,14},{9,15},{10,... | collective-permute-start | bytes 13832 | tf_op jit(solution)/shard_map/ppermute | solution.py:237
  46.5 0.5 collective-permute-start.8
  47.0 0.5 collective-permute-start.7
  47.6 0.0 copy-done.1
  47.6 1.0 %shard_map.79.refs_4_ = f32[512,768]{1,0:T(8,128)S(1)} custom-call(bf16[512,768]{1,0:T(8,128)(2,1)S(1)} %get-tuple-element.22.placed, bf16[2,1152,768]{2,1,0:T(8,128)(2,1)S(1)} %copy-done.1), custom_call_target="tpu_custom_call" | custom-call | flops 603979776 | bytes 4000000 | tf_op jit(solution)/shard_map/pallas_call | solution.py:208
  48.5 0.1 collective-permute-done.9
  48.6 1.5 %collective-permute-done.8 = f32[3,384]{1,0:T(4,128)S(1)} collective-permute-done((f32[3,384]{1,0:T(4,128)S(1)}, f32[3,384]{1,0:T(4,128)S(1)}, u32[]{:S(2)}, u32[]{:S(2)}) %collective-permute-start.8) | collective-permute-done | bytes 4640 | tf_op jit(solution)/shard_map/ppermute | solution.py:237
  50.2 0.5 collective-permute-done.7
  50.7 2.4 %shard_map.81 = (bf16[512,768]{1,0:T(8,128)(2,1)S(1)}, f32[512,384]{1,0:T(8,128)S(1)}, f32[512,384]{1,0:T(8,128)S(1)}, f32[3,384]{1,0:T(4,128)S(1)}) custom-call(s32[4,4]{1,0:T(4,128)S(1)} %maximum_convert_fusion.cols, bf16[1024,128]{1,0:T(8,128)(2,1)S(1)} %pad_maximum_fusion.refs_4_.refs_0_, ...), custom_call_target="tpu_custom_call" | custom-call | flops 704643072 | bytes 4000000 | tf_op jit(solution)/shard_map/pallas_call | solution.py:208
  53.2 0.1 collective-permute-start.10
  53.3 1.2 %collective-permute-done.10 = f32[3,384]{1,0:T(4,128)S(1)} collective-permute-done((f32[3,384]{1,0:T(4,128)S(1)}, f32[3,384]{1,0:T(4,128)S(1)}, u32[]{:S(2)}, u32[]{:S(2)}) %collective-permute-start.10) | collective-permute-done | bytes 4640 | tf_op jit(solution)/shard_map/ppermute | solution.py:234
  54.5 1.6 %collective-permute-start.13 = (f32[3,384]{1,0:T(4,128)S(1)}, f32[3,384]{1,0:T(4,128)S(1)}, u32[]{:S(2)}, u32[]{:S(2)}) collective-permute-start(f32[3,384]{1,0:T(4,128)S(1)} %pad_maximum_fusion.3), channel_id=1, source_target_pairs={{0,6},{1,7},{2,4},{3,5},{4,2},{5,3},{6,0},{7,1},{8,14},{9,15},{10,... | collective-permute-start | bytes 13832 | tf_op jit(solution)/shard_map/ppermute | solution.py:237
  56.0 0.5 collective-permute-start.12
  56.5 1.5 %collective-permute-start.11 = (f32[3,384]{1,0:T(4,128)S(1)}, f32[3,384]{1,0:T(4,128)S(1)}, u32[]{:S(2)}, u32[]{:S(2)}) collective-permute-start(f32[3,384]{1,0:T(4,128)S(1)} %pad_maximum_fusion.3), channel_id=1, source_target_pairs={{0,2},{1,3},{2,0},{3,1},{4,6},{5,7},{6,4},{7,5},{8,10},{9,11},{10,... | collective-permute-start | bytes 13832 | tf_op jit(solution)/shard_map/ppermute | solution.py:237
  58.0 1.0 %collective-permute-done.13 = f32[3,384]{1,0:T(4,128)S(1)} collective-permute-done((f32[3,384]{1,0:T(4,128)S(1)}, f32[3,384]{1,0:T(4,128)S(1)}, u32[]{:S(2)}, u32[]{:S(2)}) %collective-permute-start.13) | collective-permute-done | bytes 4640 | tf_op jit(solution)/shard_map/ppermute | solution.py:237
  59.1 0.6 collective-permute-done.12
  59.6 0.5 collective-permute-done.11
  60.2 3.4 %shard_map.82 = (bf16[128,1152]{1,0:T(8,128)(2,1)}, f32[1,384]{1,0:T(1,128)S(1)}, bf16[4,144,576]{2,1,0:T(8,128)(2,1)S(1)}, bf16[1152,512]{1,0:T(8,128)(2,1)S(1)}, bf16[512,576]{1,0:T(8,128)(2,1)S(1)}) custom-call(s32[4,4]{1,0:T(4,128)S(1)} %maximum_convert_fusion.cols, bf16[1024,128]{1,0:T(8,128)(2,1)S(1)} %pad_maximum_fusion.refs_4_.refs_0_, ...), custom_call_target="tpu_custom_call" | custom-call | flops 339738624 | bytes 4000000 | tf_op jit(solution)/shard_map/pallas_call | solution.py:208
  63.6 0.0 collective-permute-start.14
  63.6 0.6 shard_map.83
  64.2 1.6 %collective-permute-done.14 = bf16[4,144,576]{2,1,0:T(8,128)(2,1)S(1)} collective-permute-done((bf16[4,144,576]{2,1,0:T(8,128)(2,1)S(1)}, bf16[4,144,576]{2,1,0:T(8,128)(2,1)S(1)}, u32[]{:S(2)}, u32[]{:S(2)}) %collective-permute-start.14) | collective-permute-done | bytes 663584 | tf_op jit(solution)/shard_map/ppermute | solution.py:374
  65.8 0.2 add_convert_fusion
  66.0 0.1 slice_bitcast_fusion.2
  66.1 1.6 %collective-permute-start.15 = (bf16[144,576]{1,0:T(8,128)(2,1)S(1)}, bf16[144,576]{1,0:T(8,128)(2,1)S(1)}, u32[]{:S(2)}, u32[]{:S(2)}) collective-permute-start(bf16[144,576]{1,0:T(8,128)(2,1)S(1)} %get-tuple-element.45), channel_id=1, source_target_pairs={{0,2},{1,3},{2,0},{3,1},{4,6},{5,7},{6,4},{7,5},{8,10},{9,11},{10,... | collective-permute-start | bytes 497672 | tf_op jit(solution)/shard_map/ppermute | solution.py:386
  67.6 1.5 %collective-permute-start.17 = (bf16[144,576]{1,0:T(8,128)(2,1)S(1)}, bf16[144,576]{1,0:T(8,128)(2,1)S(1)}, u32[]{:S(2)}, u32[]{:S(2)}) collective-permute-start(bf16[144,576]{1,0:T(8,128)(2,1)S(1)} %get-tuple-element.46), channel_id=1, source_target_pairs={{0,6},{1,7},{2,4},{3,5},{4,2},{5,3},{6,0},{7,1},{8,14},{9,15},{10,... | collective-permute-start | bytes 497672 | tf_op jit(solution)/shard_map/ppermute | solution.py:386
  69.1 0.5 collective-permute-start.16
  69.6 0.6 reduce
  70.2 3.4 %collective-permute-done.15 = bf16[144,576]{1,0:T(8,128)(2,1)S(1)} collective-permute-done((bf16[144,576]{1,0:T(8,128)(2,1)S(1)}, bf16[144,576]{1,0:T(8,128)(2,1)S(1)}, u32[]{:S(2)}, u32[]{:S(2)}) %collective-permute-start.15) | collective-permute-done | bytes 165920 | tf_op jit(solution)/shard_map/ppermute | solution.py:386
  73.6 4.2 %collective-permute-done.17 = bf16[144,576]{1,0:T(8,128)(2,1)S(1)} collective-permute-done((bf16[144,576]{1,0:T(8,128)(2,1)S(1)}, bf16[144,576]{1,0:T(8,128)(2,1)S(1)}, u32[]{:S(2)}, u32[]{:S(2)}) %collective-permute-start.17) | collective-permute-done | bytes 165920 | tf_op jit(solution)/shard_map/ppermute | solution.py:386
  77.8 1.4 %collective-permute-done.16 = bf16[144,576]{1,0:T(8,128)(2,1)S(1)} collective-permute-done((bf16[144,576]{1,0:T(8,128)(2,1)S(1)}, bf16[144,576]{1,0:T(8,128)(2,1)S(1)}, u32[]{:S(2)}, u32[]{:S(2)}) %collective-permute-start.16) | collective-permute-done | bytes 165920 | tf_op jit(solution)/shard_map/ppermute | solution.py:386
  79.2 0.1 fusion.1
  79.3 1.1 %reshape.11 = f32[144,2,288]{2,1,0:T(2,128)} reshape(f32[144,576]{1,0:T(8,128)S(1)} %fusion.1) | data formatting | bytes 663552 | tf_op jit(solution)/shard_map/reshape | solution.py:389
  (14 shorter events, 0.2 us)
Async XLA Ops:
  1.6 26.9 %collective-permute-start.3 = (bf16[1024,128]{1,0:T(8,128)(2,1)S(1)}, bf16[1024,128]{1,0:T(8,128)(2,1)S(1)}, u32[]{:S(2)}, u32[]{:S(2)}) collective-permute-start(bf16[1024,128]{1,0:T(8,128)(2,1)S(1)} %pad_maximum_fusion.refs_4_.refs_0_), channel_id=1, source_target_pairs={{0,8},{8,0},{16,24},{24,16},{1,9},{9,1},{17,25},{25,17},{2,10},{10... | collective-permute-start | bytes 786440 | tf_op jit(solution)/shard_map/ppermute | solution.py:266
  4.7 23.8 %collective-permute-start.1 = (bf16[1024,128]{1,0:T(8,128)(2,1)S(1)}, bf16[1024,128]{1,0:T(8,128)(2,1)S(1)}, u32[]{:S(2)}, u32[]{:S(2)}) collective-permute-start(bf16[1024,128]{1,0:T(8,128)(2,1)S(1)} %pad_maximum_fusion.refs_4_.refs_0_), channel_id=1, source_target_pairs={{0,16},{8,24},{16,0},{24,8},{1,17},{9,25},{17,1},{25,9},{2,18},{10... | collective-permute-start | bytes 786440 | tf_op jit(solution)/shard_map/ppermute | solution.py:266
  7.3 2.0 %copy-start = (bf16[2,1152,768]{2,1,0:T(8,128)(2,1)S(1)}, bf16[2,1152,768]{2,1,0:T(8,128)(2,1)}, u32[]{:S(2)}) copy-start(bf16[2,1152,768]{2,1,0:T(8,128)(2,1)} %refs_10_.1) | copy-start | bytes 10616836
  9.3 1.0 %copy-start.2 = (bf16[1,128,1152]{2,1,0:T(8,128)(2,1)S(1)}, bf16[1,128,1152]{2,1,0:T(8,128)(2,1)}, u32[]{:S(2)}) copy-start(bf16[1,128,1152]{2,1,0:T(8,128)(2,1)} %param.5) | copy-start | bytes 884740
  10.3 0.7 copy-start.3
  11.9 16.6 %collective-permute-start.2 = (bf16[144,768]{1,0:T(8,128)(2,1)S(1)}, bf16[144,768]{1,0:T(8,128)(2,1)S(1)}, u32[]{:S(2)}, u32[]{:S(2)}) collective-permute-start(bf16[144,768]{1,0:T(8,128)(2,1)S(1)} %shard_map.76.refs_0_), channel_id=1, source_target_pairs={{0,16},{8,24},{16,0},{24,8},{1,17},{9,25},{17,1},{25,9},{2,18},{10... | collective-permute-start | bytes 663560 | tf_op jit(solution)/shard_map/ppermute | solution.py:266
  12.3 16.2 %collective-permute-start = (bf16[144,768]{1,0:T(8,128)(2,1)S(1)}, bf16[144,768]{1,0:T(8,128)(2,1)S(1)}, u32[]{:S(2)}, u32[]{:S(2)}) collective-permute-start(bf16[144,768]{1,0:T(8,128)(2,1)S(1)} %shard_map.76.refs_0_), channel_id=1, source_target_pairs={{0,8},{8,0},{16,24},{24,16},{1,9},{9,1},{17,25},{25,17},{2,10},{10... | collective-permute-start | bytes 663560 | tf_op jit(solution)/shard_map/ppermute | solution.py:266
  28.5 8.3 %collective-permute-start.4 = (bf16[144,768]{1,0:T(8,128)(2,1)S(1)}, bf16[144,768]{1,0:T(8,128)(2,1)S(1)}, u32[]{:S(2)}, u32[]{:S(2)}) collective-permute-start(bf16[144,768]{1,0:T(8,128)(2,1)S(1)} %get-tuple-element.20.refs_2_), channel_id=1, source_target_pairs={{0,8},{8,0},{16,24},{24,16},{1,9},{9,1},{17,25},{25,17},{2,10},{10... | collective-permute-start | bytes 663560 | tf_op jit(solution)/shard_map/ppermute | solution.py:266
  28.6 13.0 %collective-permute-start.5 = (bf16[1024,128]{1,0:T(8,128)(2,1)S(1)}, bf16[1024,128]{1,0:T(8,128)(2,1)S(1)}, u32[]{:S(2)}, u32[]{:S(2)}) collective-permute-start(bf16[1024,128]{1,0:T(8,128)(2,1)S(1)} %get-tuple-element.21.refs_6_.refs_2_), channel_id=1, source_target_pairs={{0,8},{8,0},{16,24},{24,16},{1,9},{9,1},{17,25},{25,17},{2,10},{10... | collective-permute-start | bytes 786440 | tf_op jit(solution)/shard_map/ppermute | solution.py:266
  36.9 10.7 %copy-start.1 = (bf16[2,1152,768]{2,1,0:T(8,128)(2,1)S(1)}, bf16[2,1152,768]{2,1,0:T(8,128)(2,1)}, u32[]{:S(2)}) copy-start(bf16[2,1152,768]{2,1,0:T(8,128)(2,1)} %refs_10_.1) | copy-start | bytes 10616836
  42.7 1.2 %collective-permute-start.6 = (f32[3,384]{1,0:T(4,128)S(1)}, f32[3,384]{1,0:T(4,128)S(1)}, u32[]{:S(2)}, u32[]{:S(2)}) collective-permute-start(f32[3,384]{1,0:T(4,128)S(1)} %get-tuple-element.27), channel_id=1, source_target_pairs={{0,1},{1,0},{2,3},{3,2},{4,5},{5,4},{6,7},{7,6},{8,9},{9,8},{10,11... | collective-permute-start | bytes 13832 | tf_op jit(solution)/shard_map/ppermute | solution.py:234
  44.0 4.6 %collective-permute-start.9 = (f32[3,384]{1,0:T(4,128)S(1)}, f32[3,384]{1,0:T(4,128)S(1)}, u32[]{:S(2)}, u32[]{:S(2)}) collective-permute-start(f32[3,384]{1,0:T(4,128)S(1)} %pad_maximum_fusion.1), channel_id=1, source_target_pairs={{0,6},{1,7},{2,4},{3,5},{4,2},{5,3},{6,0},{7,1},{8,14},{9,15},{10,... | collective-permute-start | bytes 13832 | tf_op jit(solution)/shard_map/ppermute | solution.py:237
  46.5 3.6 %collective-permute-start.8 = (f32[3,384]{1,0:T(4,128)S(1)}, f32[3,384]{1,0:T(4,128)S(1)}, u32[]{:S(2)}, u32[]{:S(2)}) collective-permute-start(f32[3,384]{1,0:T(4,128)S(1)} %pad_maximum_fusion.1), channel_id=1, source_target_pairs={{0,4},{1,5},{2,6},{3,7},{4,0},{5,1},{6,2},{7,3},{8,12},{9,13},{10,... | collective-permute-start | bytes 13832 | tf_op jit(solution)/shard_map/ppermute | solution.py:237
  47.0 3.6 %collective-permute-start.7 = (f32[3,384]{1,0:T(4,128)S(1)}, f32[3,384]{1,0:T(4,128)S(1)}, u32[]{:S(2)}, u32[]{:S(2)}) collective-permute-start(f32[3,384]{1,0:T(4,128)S(1)} %pad_maximum_fusion.1), channel_id=1, source_target_pairs={{0,2},{1,3},{2,0},{3,1},{4,6},{5,7},{6,4},{7,5},{8,10},{9,11},{10,... | collective-permute-start | bytes 13832 | tf_op jit(solution)/shard_map/ppermute | solution.py:237
  53.2 1.2 %collective-permute-start.10 = (f32[3,384]{1,0:T(4,128)S(1)}, f32[3,384]{1,0:T(4,128)S(1)}, u32[]{:S(2)}, u32[]{:S(2)}) collective-permute-start(f32[3,384]{1,0:T(4,128)S(1)} %get-tuple-element.31), channel_id=1, source_target_pairs={{0,1},{1,0},{2,3},{3,2},{4,5},{5,4},{6,7},{7,6},{8,9},{9,8},{10,11... | collective-permute-start | bytes 13832 | tf_op jit(solution)/shard_map/ppermute | solution.py:234
  54.5 4.6 %collective-permute-start.13 = (f32[3,384]{1,0:T(4,128)S(1)}, f32[3,384]{1,0:T(4,128)S(1)}, u32[]{:S(2)}, u32[]{:S(2)}) collective-permute-start(f32[3,384]{1,0:T(4,128)S(1)} %pad_maximum_fusion.3), channel_id=1, source_target_pairs={{0,6},{1,7},{2,4},{3,5},{4,2},{5,3},{6,0},{7,1},{8,14},{9,15},{10,... | collective-permute-start | bytes 13832 | tf_op jit(solution)/shard_map/ppermute | solution.py:237
  56.0 3.6 %collective-permute-start.12 = (f32[3,384]{1,0:T(4,128)S(1)}, f32[3,384]{1,0:T(4,128)S(1)}, u32[]{:S(2)}, u32[]{:S(2)}) collective-permute-start(f32[3,384]{1,0:T(4,128)S(1)} %pad_maximum_fusion.3), channel_id=1, source_target_pairs={{0,4},{1,5},{2,6},{3,7},{4,0},{5,1},{6,2},{7,3},{8,12},{9,13},{10,... | collective-permute-start | bytes 13832 | tf_op jit(solution)/shard_map/ppermute | solution.py:237
  56.5 3.6 %collective-permute-start.11 = (f32[3,384]{1,0:T(4,128)S(1)}, f32[3,384]{1,0:T(4,128)S(1)}, u32[]{:S(2)}, u32[]{:S(2)}) collective-permute-start(f32[3,384]{1,0:T(4,128)S(1)} %pad_maximum_fusion.3), channel_id=1, source_target_pairs={{0,2},{1,3},{2,0},{3,1},{4,6},{5,7},{6,4},{7,5},{8,10},{9,11},{10,... | collective-permute-start | bytes 13832 | tf_op jit(solution)/shard_map/ppermute | solution.py:237
  63.6 2.2 %collective-permute-start.14 = (bf16[4,144,576]{2,1,0:T(8,128)(2,1)S(1)}, bf16[4,144,576]{2,1,0:T(8,128)(2,1)S(1)}, u32[]{:S(2)}, u32[]{:S(2)}) collective-permute-start(bf16[4,144,576]{2,1,0:T(8,128)(2,1)S(1)} %get-tuple-element.36), channel_id=1, source_target_pairs={{0,1},{1,0},{2,3},{3,2},{4,5},{5,4},{6,7},{7,6},{8,9},{9,8},{10,11... | collective-permute-start | bytes 1990664 | tf_op jit(solution)/shard_map/ppermute | solution.py:374
  66.1 7.5 %collective-permute-start.15 = (bf16[144,576]{1,0:T(8,128)(2,1)S(1)}, bf16[144,576]{1,0:T(8,128)(2,1)S(1)}, u32[]{:S(2)}, u32[]{:S(2)}) collective-permute-start(bf16[144,576]{1,0:T(8,128)(2,1)S(1)} %get-tuple-element.45), channel_id=1, source_target_pairs={{0,2},{1,3},{2,0},{3,1},{4,6},{5,7},{6,4},{7,5},{8,10},{9,11},{10,... | collective-permute-start | bytes 497672 | tf_op jit(solution)/shard_map/ppermute | solution.py:386
  67.6 10.2 %collective-permute-start.17 = (bf16[144,576]{1,0:T(8,128)(2,1)S(1)}, bf16[144,576]{1,0:T(8,128)(2,1)S(1)}, u32[]{:S(2)}, u32[]{:S(2)}) collective-permute-start(bf16[144,576]{1,0:T(8,128)(2,1)S(1)} %get-tuple-element.46), channel_id=1, source_target_pairs={{0,6},{1,7},{2,4},{3,5},{4,2},{5,3},{6,0},{7,1},{8,14},{9,15},{10,... | collective-permute-start | bytes 497672 | tf_op jit(solution)/shard_map/ppermute | solution.py:386
  69.1 10.1 %collective-permute-start.16 = (bf16[144,576]{1,0:T(8,128)(2,1)S(1)}, bf16[144,576]{1,0:T(8,128)(2,1)S(1)}, u32[]{:S(2)}, u32[]{:S(2)}) collective-permute-start(bf16[144,576]{1,0:T(8,128)(2,1)S(1)} %get-tuple-element.47), channel_id=1, source_target_pairs={{0,4},{1,5},{2,6},{3,7},{4,0},{5,1},{6,2},{7,3},{8,12},{9,13},{10,... | collective-permute-start | bytes 497672 | tf_op jit(solution)/shard_map/ppermute | solution.py:386

commit v8 on v7

--- a/solution.py
+++ b/solution.py
@@ -175,16 +175,14 @@
 def gram_kernel(nz, chips, slots, edge, modes, total_rows, split, cols, *refs):
     km_refs = refs[:nz]
     turned, stiff, mass, stats = refs[nz : nz + 4]
-    basis_ref, ritz_ref, gram_ref, full_t, applied, full, chosen = refs[nz + 4 :]
+    gram_ref, full, full_t, applied, chosen = refs[nz + 4 :]
     z = lax.axis_index("blk")
     at = [pl.ds(pl.multiple_of((z ^ k) * edge, edge), edge) for k in range(nz)]
     width = 3 * modes // nz
     shift, scale = shift_and_scale(stats, total_rows)
-    ritz_ref[...] = shift
     full[:, 0:modes] = turned[:, 0:modes]
     full[:, modes : 2 * modes] = ((stiff[...] - shift * mass[...]) * scale).astype(bf16)
     full[:, 2 * modes : 3 * modes] = turned[:, modes : 2 * modes]
-    basis_ref[...] = full[at[0], :]
     window = chosen.shape[1]
     start = z * width // 128 * 128
     picked = full[:, pl.ds(pl.multiple_of(start, 128), window)].astype(f32)
@@ -200,6 +198,12 @@
         gram_ref[...] = jnp.dot(full_t[...], applied[...], preferred_element_type=f32).astype(bf16)
 
 
+def results_kernel(edge, total_rows, stats, full, basis_ref, ritz_ref):
+    z = lax.axis_index("blk")
+    basis_ref[...] = full[pl.ds(pl.multiple_of(z * edge, edge), edge), :]
+    ritz_ref[...] = shift_and_scale(stats, total_rows)[0]
+
+
 def gram_rest_kernel(chips, full_t, applied, gram_ref):
     gram_rows(full_t, applied, chips, lax.rem(lax.axis_index("grp"), 2), gram_ref)
 
@@ -242,39 +246,19 @@
     return stats
 
 
-def hold_kernel(*refs):
-    pass
-
-
-def hold(arrays, until):
-    anywhere = pl.BlockSpec(memory_space=pl.ANY)
-    return pl.pallas_call(
-        hold_kernel,
-        out_shape=tuple(jax.ShapeDtypeStruct(a.shape, a.dtype) for a in arrays),
-        in_specs=[anywhere] * (len(arrays) + len(until)),
-        out_specs=(anywhere,) * len(arrays),
-        input_output_aliases={i: i for i in range(len(arrays))},
-        compiler_params=pltpu.CompilerParams(vmem_limit_bytes=1024 * 1024),
-        cost_estimate=pl.CostEstimate(flops=0, bytes_accessed=0, transcendentals=0),
-    )(*arrays, *until)
-
-
-def gather(arrays, nz):
-    far = nz // 2
-
-    def send(held, step):
-        return tuple(lax.ppermute(a, "blk", by_xor(nz, step)) for a in held)
-
-    parts = {0: tuple(arrays)}
+def gather(operators, turned, nz):
+    def send(x, step):
+        return lax.ppermute(x, "blk", by_xor(nz, step))
+
     if nz == 4:
-        parts[2], parts[1] = send(arrays, 2), send(arrays, 1)
-        parts[2] = hold(parts[2], parts[1])
-        parts[3] = send(parts[2], 1)
-    else:
-        while far:
-            parts |= {k ^ far: send(held, far) for k, held in parts.items()}
-            far //= 2
-    return [[parts[k][i] for k in range(nz)] for i in range(len(arrays))]
+        km_2, km_1 = send(operators, 2), send(operators, 1)
+        t_3, t_2, t_1 = send(turned, 3), send(turned, 2), send(turned, 1)
+        return [operators, km_1, km_2, send(km_2, 1)], [turned, t_1, t_2, t_3]
+    parts, far = {0: (operators, turned)}, nz // 2
+    while far:
+        parts |= {k ^ far: tuple(send(x, far) for x in held) for k, held in parts.items()}
+        far //= 2
+    return [[parts[k][i] for k in range(nz)] for i in range(2)]
 
 
 def body(basis, coeffs, stiff_blocks, mass_blocks, block_cols):
@@ -302,7 +286,7 @@
         [],
         2 * edge * columns * 2 * modes,
     )
-    km_parts, t_parts = gather((payload, turned), nz)
+    km_parts, t_parts = gather(payload, turned, nz)
 
     cols = jnp.stack([p[edge, :slots] for p in t_parts]).astype(jnp.int32)
     some = jax.ShapeDtypeStruct((nz - 1, edge, modes), f32)
@@ -356,19 +340,26 @@
         (chips, block, 2 * width) if split else (columns, 2 * width), bf16
     )
     window = -(-(width + max(i * width % 128 for i in range(nz))) // 128) * 128
-    basis_out, ritz, gram, full_t, applied = call(
+    gram, full, full_t, applied = call(
         functools.partial(gram_kernel, nz, chips, slots, edge, modes, total_rows, split),
         [cols, *km_parts, turned, stiff_x, mass_x, stats],
         1,
         (
-            jax.ShapeDtypeStruct((edge, columns), bf16),
-            jax.ShapeDtypeStruct((1, modes), f32),
             gram_shape,
+            jax.ShapeDtypeStruct((rows, columns), bf16),
             jax.ShapeDtypeStruct((columns, rows), bf16),
             jax.ShapeDtypeStruct((rows, 2 * width), bf16),
         ),
-        [pltpu.VMEM((rows, columns), bf16), pltpu.VMEM((rows, window), bf16)],
+        [pltpu.VMEM((rows, window), bf16)],
         2 * rows * columns * width,
+    )
+    basis_out, ritz = call(
+        functools.partial(results_kernel, edge, total_rows),
+        [stats, full],
+        0,
+        (jax.ShapeDtypeStruct((edge, columns), bf16), jax.ShapeDtypeStruct((1, modes), f32)),
+        [],
+        0,
     )
     if split:
         got = lax.ppermute(gram, "grp", by_xor(ng, 1))

time: 80.6 us -> 81.5 us (1.011)
  starting transfers between devices: 19.2 us -> 20.1 us
    ppermute x6, starting transfers between devices: 8.35 us -> 9.23 us  [send(): return lax.ppermute(x, 'blk', by_xor(nz, step))]
    pallas_call x7 -> x8, Pallas kernels: 10.7 us -> 10.8 us  [call(): pl.pallas_call(kernel, out_shape=out_shape, in_specs=[smem()] * n_smem +...]
  transfers between devices with their start and end apart: 18 -> 18, of which waited for: 15 -> 16; matrix products, arithmetic and copies ran while one was open for 1% -> 1% of each run, Pallas kernels for 5% -> 6%
where the time goes in v8:
time: 81.5 us; the launch traced here: 81.3 us
  waiting for transfers between devices  42.8 us (53%)
  starting transfers between devices  20.1 us (25%)
  Pallas kernels  10.8 us (13%)
  local copies, waits for them, and re-layouts  4.77 us (6%)
  other arithmetic  2.07 us (3%)
    ppermute x6, waiting for transfers between devices, send(): return lax.ppermute(x, 'blk', by_xor(nz, step))  26.4 us
    pallas_call x8, Pallas kernels, call(): pl.pallas_call(kernel, out_shape=out_shape, in_specs=[smem()] * n_smem +...  10.8 us
    ppermute x6, starting transfers between devices, send(): return lax.ppermute(x, 'blk', by_xor(nz, step))  9.23 us
    ppermute x3, waiting for transfers between devices, body(): total = total + lax.ppermute(mine[k], 'grp', by_xor(ng, 2 * k)).astype(f32)  8.27 us
    ppermute x6, starting transfers between devices, merge_over(): got = [lax.ppermute(stats, axis, by_xor(size, 2 * k)) for k in (1, 2, 3)]  7.11 us
    ppermute x6, waiting for transfers between devices, merge_over(): got = [lax.ppermute(stats, axis, by_xor(size, 2 * k)) for k in (1, 2, 3)]  4.25 us
    unnamed x8, local copies, waits for them, and re-layouts  3.62 us
    ppermute x3, starting transfers between devices, body(): total = total + lax.ppermute(mine[k], 'grp', by_xor(ng, 2 * k)).astype(f32)  3.55 us
  transfers between devices with their start and end apart: 18, of which 16 were waited for; matrix products, arithmetic and copies ran while one was open for 1% of the time, Pallas kernels for 6%

profile of v8, /device:TPU:0, one launch (start us, length us, event | category | flops | bytes accessed | tf_op | source)
XLA Modules:
  0.0 81.3 jit_solution(5317649975691439984)
XLA Ops:
  0.6 1.0 %pad_maximum_fusion.refs_4_.refs_0_ = bf16[1024,128]{1,0:T(8,128)(2,1)S(1)} fusion(bf16[512,128]{1,0:T(8,128)(2,1)} %bitcast.18, bf16[512,128]{1,0:T(8,128)(2,1)} %bitcast.19), kind=kLoop, calls=%fused_computation.4 | loop fusion | flops 524288 | bytes 524288 | tf_op jit(solution)/shard_map/concatenate | solution.py:274
  1.6 4.1 %collective-permute-start.4 = (bf16[1024,128]{1,0:T(8,128)(2,1)S(1)}, bf16[1024,128]{1,0:T(8,128)(2,1)S(1)}, u32[]{:S(2)}, u32[]{:S(2)}) collective-permute-start(bf16[1024,128]{1,0:T(8,128)(2,1)S(1)} %pad_maximum_fusion.refs_4_.refs_0_), channel_id=1, source_target_pairs={{0,16},{8,24},{16,0},{24,8},{1,17},{9,25},{17,1},{25,9},{2,18},{10... | collective-permute-start | bytes 786440 | tf_op jit(solution)/shard_map/ppermute | solution.py:251
  5.7 0.0 copy-start
  5.7 2.0 %copy-done = bf16[2,1152,768]{2,1,0:T(8,128)(2,1)S(1)} copy-done((bf16[2,1152,768]{2,1,0:T(8,128)(2,1)S(1)}, bf16[2,1152,768]{2,1,0:T(8,128)(2,1)}, u32[]{:S(2)}) %copy-start) | copy-done | bytes 3538968
  7.7 0.0 copy-start.2
  7.7 1.0 %copy-done.2 = bf16[1,128,1152]{2,1,0:T(8,128)(2,1)S(1)} copy-done((bf16[1,128,1152]{2,1,0:T(8,128)(2,1)S(1)}, bf16[1,128,1152]{2,1,0:T(8,128)(2,1)}, u32[]{:S(2)}) %copy-start.2) | copy-done | bytes 294936
  8.7 0.0 copy-start.3
  8.7 0.7 copy-done.3
  9.3 1.0 %shard_map.76.refs_0_ = bf16[144,768]{1,0:T(8,128)(2,1)S(1)} custom-call(s32[1,4]{1,0:T(1,128)S(1)} %bitcast.17, bf16[128,1152]{1,0:T(8,128)(2,1)S(1)} %bitcast.16, bf16[2,1152,768]{2,1,0:T(8,128)(2,1)S(1)} %copy-done), custom_call_target="tpu_custom_call" | custom-call | flops 226492416 | bytes 4000000 | tf_op jit(solution)/shard_map/pallas_call | solution.py:212
  10.3 1.4 %collective-permute-start.2 = (bf16[144,768]{1,0:T(8,128)(2,1)S(1)}, bf16[144,768]{1,0:T(8,128)(2,1)S(1)}, u32[]{:S(2)}, u32[]{:S(2)}) collective-permute-start(bf16[144,768]{1,0:T(8,128)(2,1)S(1)} %shard_map.76.refs_0_), channel_id=1, source_target_pairs={{0,24},{8,16},{16,8},{24,0},{1,25},{9,17},{17,9},{25,1},{2,26},{10... | collective-permute-start | bytes 663560 | tf_op jit(solution)/shard_map/ppermute | solution.py:251
  11.7 1.7 %collective-permute-start.1 = (bf16[144,768]{1,0:T(8,128)(2,1)S(1)}, bf16[144,768]{1,0:T(8,128)(2,1)S(1)}, u32[]{:S(2)}, u32[]{:S(2)}) collective-permute-start(bf16[144,768]{1,0:T(8,128)(2,1)S(1)} %shard_map.76.refs_0_), channel_id=1, source_target_pairs={{0,16},{8,24},{16,0},{24,8},{1,17},{9,25},{17,1},{25,9},{2,18},{10... | collective-permute-start | bytes 663560 | tf_op jit(solution)/shard_map/ppermute | solution.py:251
  13.4 1.3 %collective-permute-start = (bf16[144,768]{1,0:T(8,128)(2,1)S(1)}, bf16[144,768]{1,0:T(8,128)(2,1)S(1)}, u32[]{:S(2)}, u32[]{:S(2)}) collective-permute-start(bf16[144,768]{1,0:T(8,128)(2,1)S(1)} %shard_map.76.refs_0_), channel_id=1, source_target_pairs={{0,8},{8,0},{16,24},{24,16},{1,9},{9,1},{17,25},{25,17},{2,10},{10... | collective-permute-start | bytes 663560 | tf_op jit(solution)/shard_map/ppermute | solution.py:251
  14.8 0.7 collective-permute-start.3
  15.4 12.6 %collective-permute-done.4.refs_6_.refs_2_ = bf16[1024,128]{1,0:T(8,128)(2,1)S(1)} collective-permute-done((bf16[1024,128]{1,0:T(8,128)(2,1)S(1)}, bf16[1024,128]{1,0:T(8,128)(2,1)S(1)}, u32[]{:S(2)}, u32[]{:S(2)}) %collective-permute-start.4) | collective-permute-done | bytes 262176 | tf_op jit(solution)/shard_map/ppermute | solution.py:251
  28.0 0.0 collective-permute-start.5
  28.0 0.0 collective-permute-done.2.refs_3_
  28.1 8.7 %collective-permute-done.1.refs_2_ = bf16[144,768]{1,0:T(8,128)(2,1)S(1)} collective-permute-done((bf16[144,768]{1,0:T(8,128)(2,1)S(1)}, bf16[144,768]{1,0:T(8,128)(2,1)S(1)}, u32[]{:S(2)}, u32[]{:S(2)}) %collective-permute-start.1) | collective-permute-done | bytes 221216 | tf_op jit(solution)/shard_map/ppermute | solution.py:251
  36.8 0.0 collective-permute-done.refs_1_
  36.8 0.8 collective-permute-done.3.refs_5_.refs_1_
  37.6 0.0 copy-start.1
  37.6 1.2 %shard_map.77 = (bf16[512,768]{1,0:T(8,128)(2,1)S(1)}, f32[3,128,384]{2,1,0:T(8,128)S(1)}, f32[3,128,384]{2,1,0:T(8,128)S(1)}) custom-call(s32[4,4]{1,0:T(4,128)S(1)} %maximum_convert_fusion.cols, bf16[144,768]{1,0:T(8,128)(2,1)S(1)} %shard_map.76.refs_0_, bf16[144,768]{1,0:T(8,128)(2,1)S(1)} %collective-permute-done.refs_1_, ...), custom_call_target="tpu_custom_call" | custom-call | flops 301989888 | bytes 4000000 | tf_op jit(solution)/shard_map/pallas_call | solution.py:212
  38.8 4.3 %collective-permute-done.5.km_last.refs_3_ = bf16[1024,128]{1,0:T(8,128)(2,1)S(1)} collective-permute-done((bf16[1024,128]{1,0:T(8,128)(2,1)S(1)}, bf16[1024,128]{1,0:T(8,128)(2,1)S(1)}, u32[]{:S(2)}, u32[]{:S(2)}) %collective-permute-start.5) | collective-permute-done | bytes 262176 | tf_op jit(solution)/shard_map/ppermute | solution.py:251
  43.1 1.1 %shard_map.79 = (f32[128,384]{1,0:T(8,128)S(1)}, f32[128,384]{1,0:T(8,128)S(1)}, f32[3,384]{1,0:T(4,128)S(1)}) custom-call(s32[4,4]{1,0:T(4,128)S(1)} %maximum_convert_fusion.cols, bf16[1024,128]{1,0:T(8,128)(2,1)S(1)} %collective-permute-done.5.km_last.refs_3_, bf16[512,768]{1,0:T(8,128)(2,1)S(1)} %get-tuple-element.19.placed, ...), custom_call_target="tpu_custom_call" | custom-call | flops 100663296 | bytes 4000000 | tf_op jit(solution)/shard_map/pallas_call | solution.py:212
  44.2 0.1 collective-permute-start.6
  44.3 1.2 %collective-permute-done.6 = f32[3,384]{1,0:T(4,128)S(1)} collective-permute-done((f32[3,384]{1,0:T(4,128)S(1)}, f32[3,384]{1,0:T(4,128)S(1)}, u32[]{:S(2)}, u32[]{:S(2)}) %collective-permute-start.6) | collective-permute-done | bytes 4640 | tf_op jit(solution)/shard_map/ppermute | solution.py:238
  45.5 2.6 %collective-permute-start.9 = (f32[3,384]{1,0:T(4,128)S(1)}, f32[3,384]{1,0:T(4,128)S(1)}, u32[]{:S(2)}, u32[]{:S(2)}) collective-permute-start(f32[3,384]{1,0:T(4,128)S(1)} %pad_maximum_fusion.1), channel_id=1, source_target_pairs={{0,6},{1,7},{2,4},{3,5},{4,2},{5,3},{6,0},{7,1},{8,14},{9,15},{10,... | collective-permute-start | bytes 13832 | tf_op jit(solution)/shard_map/ppermute | solution.py:241
  48.1 0.5 collective-permute-start.8
  48.6 0.5 collective-permute-start.7
  49.0 0.0 copy-done.1
  49.1 1.0 %shard_map.78.refs_4_ = f32[512,768]{1,0:T(8,128)S(1)} custom-call(bf16[512,768]{1,0:T(8,128)(2,1)S(1)} %get-tuple-element.19.placed, bf16[2,1152,768]{2,1,0:T(8,128)(2,1)S(1)} %copy-done.1), custom_call_target="tpu_custom_call" | custom-call | flops 603979776 | bytes 4000000 | tf_op jit(solution)/shard_map/pallas_call | solution.py:212
  50.0 0.1 collective-permute-done.9
  50.1 1.6 %collective-permute-done.8 = f32[3,384]{1,0:T(4,128)S(1)} collective-permute-done((f32[3,384]{1,0:T(4,128)S(1)}, f32[3,384]{1,0:T(4,128)S(1)}, u32[]{:S(2)}, u32[]{:S(2)}) %collective-permute-start.8) | collective-permute-done | bytes 4640 | tf_op jit(solution)/shard_map/ppermute | solution.py:241
  51.7 0.5 collective-permute-done.7
  52.3 2.4 %shard_map.80 = (bf16[512,768]{1,0:T(8,128)(2,1)S(1)}, f32[512,384]{1,0:T(8,128)S(1)}, f32[512,384]{1,0:T(8,128)S(1)}, f32[3,384]{1,0:T(4,128)S(1)}) custom-call(s32[4,4]{1,0:T(4,128)S(1)} %maximum_convert_fusion.cols, bf16[1024,128]{1,0:T(8,128)(2,1)S(1)} %pad_maximum_fusion.refs_4_.refs_0_, bf16[1024,128]{1,0:T(8,128)(2,1)S(1)} %collective-permute-done.3.refs_5_.refs_1_, ...), custom_call_target="tpu_custom_call" | custom-call | flops 704643072 | bytes 4000000 | tf_op jit(solution)/shard_map/pallas_call | solution.py:212
  54.7 0.1 collective-permute-start.10
  54.8 1.2 %collective-permute-done.10 = f32[3,384]{1,0:T(4,128)S(1)} collective-permute-done((f32[3,384]{1,0:T(4,128)S(1)}, f32[3,384]{1,0:T(4,128)S(1)}, u32[]{:S(2)}, u32[]{:S(2)}) %collective-permute-start.10) | collective-permute-done | bytes 4640 | tf_op jit(solution)/shard_map/ppermute | solution.py:238
  56.0 1.6 %collective-permute-start.13 = (f32[3,384]{1,0:T(4,128)S(1)}, f32[3,384]{1,0:T(4,128)S(1)}, u32[]{:S(2)}, u32[]{:S(2)}) collective-permute-start(f32[3,384]{1,0:T(4,128)S(1)} %pad_maximum_fusion.3), channel_id=1, source_target_pairs={{0,6},{1,7},{2,4},{3,5},{4,2},{5,3},{6,0},{7,1},{8,14},{9,15},{10,... | collective-permute-start | bytes 13832 | tf_op jit(solution)/shard_map/ppermute | solution.py:241
  57.5 0.5 collective-permute-start.12
  58.0 1.5 %collective-permute-start.11 = (f32[3,384]{1,0:T(4,128)S(1)}, f32[3,384]{1,0:T(4,128)S(1)}, u32[]{:S(2)}, u32[]{:S(2)}) collective-permute-start(f32[3,384]{1,0:T(4,128)S(1)} %pad_maximum_fusion.3), channel_id=1, source_target_pairs={{0,2},{1,3},{2,0},{3,1},{4,6},{5,7},{6,4},{7,5},{8,10},{9,11},{10,... | collective-permute-start | bytes 13832 | tf_op jit(solution)/shard_map/ppermute | solution.py:241
  59.5 1.0 %collective-permute-done.13 = f32[3,384]{1,0:T(4,128)S(1)} collective-permute-done((f32[3,384]{1,0:T(4,128)S(1)}, f32[3,384]{1,0:T(4,128)S(1)}, u32[]{:S(2)}, u32[]{:S(2)}) %collective-permute-start.13) | collective-permute-done | bytes 4640 | tf_op jit(solution)/shard_map/ppermute | solution.py:241
  60.6 0.6 collective-permute-done.12
  61.2 0.5 collective-permute-done.11
  61.7 2.7 %shard_map.81 = (bf16[4,144,576]{2,1,0:T(8,128)(2,1)S(1)}, bf16[512,1152]{1,0:T(8,128)(2,1)S(1)}, bf16[1152,512]{1,0:T(8,128)(2,1)S(1)}, bf16[512,576]{1,0:T(8,128)(2,1)S(1)}) custom-call(s32[4,4]{1,0:T(4,128)S(1)} %maximum_convert_fusion.cols, bf16[1024,128]{1,0:T(8,128)(2,1)S(1)} %pad_maximum_fusion.refs_4_.refs_0_, ...), custom_call_target="tpu_custom_call" | custom-call | flops 339738624 | bytes 4000000 | tf_op jit(solution)/shard_map/pallas_call | solution.py:212
  64.4 0.1 collective-permute-start.14
  64.5 0.6 shard_map.83
  65.1 1.6 %collective-permute-done.14 = bf16[4,144,576]{2,1,0:T(8,128)(2,1)S(1)} collective-permute-done((bf16[4,144,576]{2,1,0:T(8,128)(2,1)S(1)}, bf16[4,144,576]{2,1,0:T(8,128)(2,1)S(1)}, u32[]{:S(2)}, u32[]{:S(2)}) %collective-permute-start.14) | collective-permute-done | bytes 663584 | tf_op jit(solution)/shard_map/ppermute | solution.py:365
  66.7 0.2 add_convert_fusion
  66.9 0.1 slice_bitcast_fusion.2
  67.0 1.6 %collective-permute-start.15 = (bf16[144,576]{1,0:T(8,128)(2,1)S(1)}, bf16[144,576]{1,0:T(8,128)(2,1)S(1)}, u32[]{:S(2)}, u32[]{:S(2)}) collective-permute-start(bf16[144,576]{1,0:T(8,128)(2,1)S(1)} %get-tuple-element.43), channel_id=1, source_target_pairs={{0,2},{1,3},{2,0},{3,1},{4,6},{5,7},{6,4},{7,5},{8,10},{9,11},{10,... | collective-permute-start | bytes 497672 | tf_op jit(solution)/shard_map/ppermute | solution.py:377
  68.6 1.5 %collective-permute-start.17 = (bf16[144,576]{1,0:T(8,128)(2,1)S(1)}, bf16[144,576]{1,0:T(8,128)(2,1)S(1)}, u32[]{:S(2)}, u32[]{:S(2)}) collective-permute-start(bf16[144,576]{1,0:T(8,128)(2,1)S(1)} %get-tuple-element.44), channel_id=1, source_target_pairs={{0,6},{1,7},{2,4},{3,5},{4,2},{5,3},{6,0},{7,1},{8,14},{9,15},{10,... | collective-permute-start | bytes 497672 | tf_op jit(solution)/shard_map/ppermute | solution.py:377
  70.0 0.5 collective-permute-start.16
  70.5 0.7 shard_map.82
  71.3 0.6 reduce
  71.8 2.7 %collective-permute-done.15 = bf16[144,576]{1,0:T(8,128)(2,1)S(1)} collective-permute-done((bf16[144,576]{1,0:T(8,128)(2,1)S(1)}, bf16[144,576]{1,0:T(8,128)(2,1)S(1)}, u32[]{:S(2)}, u32[]{:S(2)}) %collective-permute-start.15) | collective-permute-done | bytes 165920 | tf_op jit(solution)/shard_map/ppermute | solution.py:377
  74.5 4.3 %collective-permute-done.17 = bf16[144,576]{1,0:T(8,128)(2,1)S(1)} collective-permute-done((bf16[144,576]{1,0:T(8,128)(2,1)S(1)}, bf16[144,576]{1,0:T(8,128)(2,1)S(1)}, u32[]{:S(2)}, u32[]{:S(2)}) %collective-permute-start.17) | collective-permute-done | bytes 165920 | tf_op jit(solution)/shard_map/ppermute | solution.py:377
  78.8 1.4 %collective-permute-done.16 = bf16[144,576]{1,0:T(8,128)(2,1)S(1)} collective-permute-done((bf16[144,576]{1,0:T(8,128)(2,1)S(1)}, bf16[144,576]{1,0:T(8,128)(2,1)S(1)}, u32[]{:S(2)}, u32[]{:S(2)}) %collective-permute-start.16) | collective-permute-done | bytes 165920 | tf_op jit(solution)/shard_map/ppermute | solution.py:377
  80.1 0.1 fusion.1
  80.2 1.1 %reshape.11 = f32[144,2,288]{2,1,0:T(2,128)} reshape(f32[144,576]{1,0:T(8,128)S(1)} %fusion.1) | data formatting | bytes 663552 | tf_op jit(solution)/shard_map/reshape | solution.py:380
  (13 shorter events, 0.2 us)
Async XLA Ops:
  1.6 26.4 %collective-permute-start.4 = (bf16[1024,128]{1,0:T(8,128)(2,1)S(1)}, bf16[1024,128]{1,0:T(8,128)(2,1)S(1)}, u32[]{:S(2)}, u32[]{:S(2)}) collective-permute-start(bf16[1024,128]{1,0:T(8,128)(2,1)S(1)} %pad_maximum_fusion.refs_4_.refs_0_), channel_id=1, source_target_pairs={{0,16},{8,24},{16,0},{24,8},{1,17},{9,25},{17,1},{25,9},{2,18},{10... | collective-permute-start | bytes 786440 | tf_op jit(solution)/shard_map/ppermute | solution.py:251
  5.7 2.0 %copy-start = (bf16[2,1152,768]{2,1,0:T(8,128)(2,1)S(1)}, bf16[2,1152,768]{2,1,0:T(8,128)(2,1)}, u32[]{:S(2)}) copy-start(bf16[2,1152,768]{2,1,0:T(8,128)(2,1)} %refs_10_.1) | copy-start | bytes 10616836
  7.7 1.0 %copy-start.2 = (bf16[1,128,1152]{2,1,0:T(8,128)(2,1)S(1)}, bf16[1,128,1152]{2,1,0:T(8,128)(2,1)}, u32[]{:S(2)}) copy-start(bf16[1,128,1152]{2,1,0:T(8,128)(2,1)} %param.5) | copy-start | bytes 884740
  8.7 0.7 copy-start.3
  10.3 17.7 %collective-permute-start.2 = (bf16[144,768]{1,0:T(8,128)(2,1)S(1)}, bf16[144,768]{1,0:T(8,128)(2,1)S(1)}, u32[]{:S(2)}, u32[]{:S(2)}) collective-permute-start(bf16[144,768]{1,0:T(8,128)(2,1)S(1)} %shard_map.76.refs_0_), channel_id=1, source_target_pairs={{0,24},{8,16},{16,8},{24,0},{1,25},{9,17},{17,9},{25,1},{2,26},{10... | collective-permute-start | bytes 663560 | tf_op jit(solution)/shard_map/ppermute | solution.py:251
  11.7 25.1 %collective-permute-start.1 = (bf16[144,768]{1,0:T(8,128)(2,1)S(1)}, bf16[144,768]{1,0:T(8,128)(2,1)S(1)}, u32[]{:S(2)}, u32[]{:S(2)}) collective-permute-start(bf16[144,768]{1,0:T(8,128)(2,1)S(1)} %shard_map.76.refs_0_), channel_id=1, source_target_pairs={{0,16},{8,24},{16,0},{24,8},{1,17},{9,25},{17,1},{25,9},{2,18},{10... | collective-permute-start | bytes 663560 | tf_op jit(solution)/shard_map/ppermute | solution.py:251
  13.4 23.4 %collective-permute-start = (bf16[144,768]{1,0:T(8,128)(2,1)S(1)}, bf16[144,768]{1,0:T(8,128)(2,1)S(1)}, u32[]{:S(2)}, u32[]{:S(2)}) collective-permute-start(bf16[144,768]{1,0:T(8,128)(2,1)S(1)} %shard_map.76.refs_0_), channel_id=1, source_target_pairs={{0,8},{8,0},{16,24},{24,16},{1,9},{9,1},{17,25},{25,17},{2,10},{10... | collective-permute-start | bytes 663560 | tf_op jit(solution)/shard_map/ppermute | solution.py:251
  14.8 22.8 %collective-permute-start.3 = (bf16[1024,128]{1,0:T(8,128)(2,1)S(1)}, bf16[1024,128]{1,0:T(8,128)(2,1)S(1)}, u32[]{:S(2)}, u32[]{:S(2)}) collective-permute-start(bf16[1024,128]{1,0:T(8,128)(2,1)S(1)} %pad_maximum_fusion.refs_4_.refs_0_), channel_id=1, source_target_pairs={{0,8},{8,0},{16,24},{24,16},{1,9},{9,1},{17,25},{25,17},{2,10},{10... | collective-permute-start | bytes 786440 | tf_op jit(solution)/shard_map/ppermute | solution.py:251
  28.0 15.1 %collective-permute-start.5 = (bf16[1024,128]{1,0:T(8,128)(2,1)S(1)}, bf16[1024,128]{1,0:T(8,128)(2,1)S(1)}, u32[]{:S(2)}, u32[]{:S(2)}) collective-permute-start(bf16[1024,128]{1,0:T(8,128)(2,1)S(1)} %collective-permute-done.4.refs_6_.refs_2_), channel_id=1, source_target_pairs={{0,8},{8,0},{16,24},{24,16},{1,9},{9,1},{17,25},{25,17},{2,10},{10... | collective-permute-start | bytes 786440 | tf_op jit(solution)/shard_map/ppermute | solution.py:251
  37.6 11.5 %copy-start.1 = (bf16[2,1152,768]{2,1,0:T(8,128)(2,1)S(1)}, bf16[2,1152,768]{2,1,0:T(8,128)(2,1)}, u32[]{:S(2)}) copy-start(bf16[2,1152,768]{2,1,0:T(8,128)(2,1)} %refs_10_.1) | copy-start | bytes 10616836
  44.2 1.2 %collective-permute-start.6 = (f32[3,384]{1,0:T(4,128)S(1)}, f32[3,384]{1,0:T(4,128)S(1)}, u32[]{:S(2)}, u32[]{:S(2)}) collective-permute-start(f32[3,384]{1,0:T(4,128)S(1)} %get-tuple-element.24), channel_id=1, source_target_pairs={{0,1},{1,0},{2,3},{3,2},{4,5},{5,4},{6,7},{7,6},{8,9},{9,8},{10,11... | collective-permute-start | bytes 13832 | tf_op jit(solution)/shard_map/ppermute | solution.py:238
  45.5 4.6 %collective-permute-start.9 = (f32[3,384]{1,0:T(4,128)S(1)}, f32[3,384]{1,0:T(4,128)S(1)}, u32[]{:S(2)}, u32[]{:S(2)}) collective-permute-start(f32[3,384]{1,0:T(4,128)S(1)} %pad_maximum_fusion.1), channel_id=1, source_target_pairs={{0,6},{1,7},{2,4},{3,5},{4,2},{5,3},{6,0},{7,1},{8,14},{9,15},{10,... | collective-permute-start | bytes 13832 | tf_op jit(solution)/shard_map/ppermute | solution.py:241
  48.1 3.6 %collective-permute-start.8 = (f32[3,384]{1,0:T(4,128)S(1)}, f32[3,384]{1,0:T(4,128)S(1)}, u32[]{:S(2)}, u32[]{:S(2)}) collective-permute-start(f32[3,384]{1,0:T(4,128)S(1)} %pad_maximum_fusion.1), channel_id=1, source_target_pairs={{0,4},{1,5},{2,6},{3,7},{4,0},{5,1},{6,2},{7,3},{8,12},{9,13},{10,... | collective-permute-start | bytes 13832 | tf_op jit(solution)/shard_map/ppermute | solution.py:241
  48.6 3.6 %collective-permute-start.7 = (f32[3,384]{1,0:T(4,128)S(1)}, f32[3,384]{1,0:T(4,128)S(1)}, u32[]{:S(2)}, u32[]{:S(2)}) collective-permute-start(f32[3,384]{1,0:T(4,128)S(1)} %pad_maximum_fusion.1), channel_id=1, source_target_pairs={{0,2},{1,3},{2,0},{3,1},{4,6},{5,7},{6,4},{7,5},{8,10},{9,11},{10,... | collective-permute-start | bytes 13832 | tf_op jit(solution)/shard_map/ppermute | solution.py:241
  54.7 1.2 %collective-permute-start.10 = (f32[3,384]{1,0:T(4,128)S(1)}, f32[3,384]{1,0:T(4,128)S(1)}, u32[]{:S(2)}, u32[]{:S(2)}) collective-permute-start(f32[3,384]{1,0:T(4,128)S(1)} %get-tuple-element.25), channel_id=1, source_target_pairs={{0,1},{1,0},{2,3},{3,2},{4,5},{5,4},{6,7},{7,6},{8,9},{9,8},{10,11... | collective-permute-start | bytes 13832 | tf_op jit(solution)/shard_map/ppermute | solution.py:238
  56.0 4.6 %collective-permute-start.13 = (f32[3,384]{1,0:T(4,128)S(1)}, f32[3,384]{1,0:T(4,128)S(1)}, u32[]{:S(2)}, u32[]{:S(2)}) collective-permute-start(f32[3,384]{1,0:T(4,128)S(1)} %pad_maximum_fusion.3), channel_id=1, source_target_pairs={{0,6},{1,7},{2,4},{3,5},{4,2},{5,3},{6,0},{7,1},{8,14},{9,15},{10,... | collective-permute-start | bytes 13832 | tf_op jit(solution)/shard_map/ppermute | solution.py:241
  57.5 3.6 %collective-permute-start.12 = (f32[3,384]{1,0:T(4,128)S(1)}, f32[3,384]{1,0:T(4,128)S(1)}, u32[]{:S(2)}, u32[]{:S(2)}) collective-permute-start(f32[3,384]{1,0:T(4,128)S(1)} %pad_maximum_fusion.3), channel_id=1, source_target_pairs={{0,4},{1,5},{2,6},{3,7},{4,0},{5,1},{6,2},{7,3},{8,12},{9,13},{10,... | collective-permute-start | bytes 13832 | tf_op jit(solution)/shard_map/ppermute | solution.py:241
  58.0 3.6 %collective-permute-start.11 = (f32[3,384]{1,0:T(4,128)S(1)}, f32[3,384]{1,0:T(4,128)S(1)}, u32[]{:S(2)}, u32[]{:S(2)}) collective-permute-start(f32[3,384]{1,0:T(4,128)S(1)} %pad_maximum_fusion.3), channel_id=1, source_target_pairs={{0,2},{1,3},{2,0},{3,1},{4,6},{5,7},{6,4},{7,5},{8,10},{9,11},{10,... | collective-permute-start | bytes 13832 | tf_op jit(solution)/shard_map/ppermute | solution.py:241
  64.4 2.3 %collective-permute-start.14 = (bf16[4,144,576]{2,1,0:T(8,128)(2,1)S(1)}, bf16[4,144,576]{2,1,0:T(8,128)(2,1)S(1)}, u32[]{:S(2)}, u32[]{:S(2)}) collective-permute-start(bf16[4,144,576]{2,1,0:T(8,128)(2,1)S(1)} %get-tuple-element.34), channel_id=1, source_target_pairs={{0,1},{1,0},{2,3},{3,2},{4,5},{5,4},{6,7},{7,6},{8,9},{9,8},{10,11... | collective-permute-start | bytes 1990664 | tf_op jit(solution)/shard_map/ppermute | solution.py:365
  67.0 7.5 %collective-permute-start.15 = (bf16[144,576]{1,0:T(8,128)(2,1)S(1)}, bf16[144,576]{1,0:T(8,128)(2,1)S(1)}, u32[]{:S(2)}, u32[]{:S(2)}) collective-permute-start(bf16[144,576]{1,0:T(8,128)(2,1)S(1)} %get-tuple-element.43), channel_id=1, source_target_pairs={{0,2},{1,3},{2,0},{3,1},{4,6},{5,7},{6,4},{7,5},{8,10},{9,11},{10,... | collective-permute-start | bytes 497672 | tf_op jit(solution)/shard_map/ppermute | solution.py:377
  68.6 10.2 %collective-permute-start.17 = (bf16[144,576]{1,0:T(8,128)(2,1)S(1)}, bf16[144,576]{1,0:T(8,128)(2,1)S(1)}, u32[]{:S(2)}, u32[]{:S(2)}) collective-permute-start(bf16[144,576]{1,0:T(8,128)(2,1)S(1)} %get-tuple-element.44), channel_id=1, source_target_pairs={{0,6},{1,7},{2,4},{3,5},{4,2},{5,3},{6,0},{7,1},{8,14},{9,15},{10,... | collective-permute-start | bytes 497672 | tf_op jit(solution)/shard_map/ppermute | solution.py:377
  70.0 10.1 %collective-permute-start.16 = (bf16[144,576]{1,0:T(8,128)(2,1)S(1)}, bf16[144,576]{1,0:T(8,128)(2,1)S(1)}, u32[]{:S(2)}, u32[]{:S(2)}) collective-permute-start(bf16[144,576]{1,0:T(8,128)(2,1)S(1)} %get-tuple-element.45), channel_id=1, source_target_pairs={{0,4},{1,5},{2,6},{3,7},{4,0},{5,1},{6,2},{7,3},{8,12},{9,13},{10,... | collective-permute-start | bytes 497672 | tf_op jit(solution)/shard_map/ppermute | solution.py:377

commit v9 on v7

--- a/solution.py
+++ b/solution.py
@@ -81,14 +81,17 @@
     return pl.BlockSpec(memory_space=pltpu.HBM)
 
 
-def turn_kernel(modes, cols, current, coeffs, out_ref):
-    rows, columns = out_ref.shape[0] - 16, out_ref.shape[1]
-    lane = lax.broadcasted_iota(jnp.int32, (16, columns), 1)
-    tag = jnp.zeros((16, columns), jnp.int32)
+def turn_kernel(cols, current, coeffs, out_ref):
+    rows, edge = current.shape[0], out_ref.shape[1]
+    turned = jnp.dot(current[...], coeffs[0], preferred_element_type=f32).astype(bf16)
+    blocks = turned.shape[1] // edge
+    for b in range(blocks):
+        out_ref[b * rows : (b + 1) * rows, :] = turned[:, b * edge : (b + 1) * edge]
+    lane = lax.broadcasted_iota(jnp.int32, (16, edge), 1)
+    tag = jnp.zeros((16, edge), jnp.int32)
     for s in range(cols.shape[1]):
         tag = jnp.where(lane == s, cols[0, s], tag)
-    out_ref[rows : rows + 16, :] = tag.astype(f32).astype(bf16)
-    out_ref[0:rows, :] = jnp.dot(current[...], coeffs[0], preferred_element_type=f32).astype(bf16)
+    out_ref[blocks * rows : blocks * rows + 16, :] = tag.astype(f32).astype(bf16)
 
 
 def rows_kernel(nz, slots, edge, modes, cols, *refs):
@@ -96,7 +99,9 @@
     placed, stiff_ref, mass_ref = refs[2 * nz - 1 :]
     z = lax.axis_index("blk")
     for k in range(nz):
-        placed[pl.ds(pl.multiple_of((z ^ k) * edge, edge), edge), :] = t_refs[k][:edge, :]
+        at = pl.ds(pl.multiple_of((z ^ k) * edge, edge), edge)
+        for b in range(placed.shape[1] // edge):
+            placed[at, b * edge : (b + 1) * edge] = t_refs[k][b * edge : (b + 1) * edge, :]
     for k in range(nz - 1):
         both = block_dot(km_refs[k], slots, edge, cols, k, placed, slice(0, modes))
         stiff_ref[k] = both[:edge]
@@ -160,6 +165,11 @@
     block_stats(z, pairs, sums, stats_ref)
 
 
+def dense_order(width):
+    whole = width // 128 * 128
+    return [(0, 0, whole), (1, 0, whole), (0, whole, width), (1, whole, width)]
+
+
 def gram_rows(full_t, applied, chips, core, out_ref):
     chip = lax.div(lax.axis_index("grp"), 2)
     block = full_t.shape[0] // (2 * chips)
@@ -167,37 +177,65 @@
         full_t[pl.ds(pl.multiple_of((2 * j + core) * block, 16), block), :] for j in range(chips)
     ]
     gram = jnp.dot(jnp.concatenate(rows, axis=0), applied[...], preferred_element_type=f32)
-    gram = gram.astype(bf16)
+    whole = gram.shape[1] // 128
     for j in range(chips):
-        out_ref[j ^ chip] = gram[j * block : (j + 1) * block]
+        mine = gram[j * block : (j + 1) * block]
+        for b in range(whole):
+            part = mine[:, b * 128 : (b + 1) * 128].astype(bf16)
+            out_ref[j ^ chip, b * block : (b + 1) * block, :] = part
+        left = mine[:, whole * 128 :]
+        left = jnp.concatenate([left[: block // 2], left[block // 2 :]], axis=1).astype(bf16)
+        out_ref[j ^ chip, whole * block : whole * block + block // 2, :] = left
+
+
+def finish_kernel(block, width, *refs):
+    out_ref = refs[-1]
+    total = refs[0][...].astype(f32)
+    for ref in refs[1:-1]:
+        total = total + ref[...].astype(f32)
+    whole = width // 128
+    left = total[2 * whole * block :, :]
+    left = jnp.concatenate([left[:, :64], left[:, 64:]], axis=0)
+    for op in range(2):
+        for b in range(whole):
+            at = (op * whole + b) * block
+            out_ref[:, op, b * 128 : (b + 1) * 128] = total[at : at + block]
+        out_ref[:, op, whole * 128 :] = left[:, op * 32 : (op + 1) * 32]
 
 
 def gram_kernel(nz, chips, slots, edge, modes, total_rows, split, cols, *refs):
     km_refs = refs[:nz]
     turned, stiff, mass, stats = refs[nz : nz + 4]
-    basis_ref, ritz_ref, gram_ref, full_t, applied, full, chosen = refs[nz + 4 :]
+    gram_ref, full, full_t, applied, chosen = refs[nz + 4 :]
     z = lax.axis_index("blk")
     at = [pl.ds(pl.multiple_of((z ^ k) * edge, edge), edge) for k in range(nz)]
     width = 3 * modes // nz
     shift, scale = shift_and_scale(stats, total_rows)
-    ritz_ref[...] = shift
     full[:, 0:modes] = turned[:, 0:modes]
     full[:, modes : 2 * modes] = ((stiff[...] - shift * mass[...]) * scale).astype(bf16)
     full[:, 2 * modes : 3 * modes] = turned[:, modes : 2 * modes]
-    basis_ref[...] = full[at[0], :]
     window = chosen.shape[1]
     start = z * width // 128 * 128
     picked = full[:, pl.ds(pl.multiple_of(start, 128), window)].astype(f32)
     chosen[...] = pltpu.roll(picked, window - (z * width - start), 1).astype(bf16)
     for k in range(nz):
         both = block_dot(km_refs[k], slots, edge, cols, k, chosen, slice(0, width)).astype(bf16)
-        applied[at[k], 0:width] = both[:edge]
-        applied[at[k], width : 2 * width] = both[edge:]
+        column = 0
+        for op, first, last in dense_order(width) if split else [(0, 0, width), (1, 0, width)]:
+            part = both[op * edge : (op + 1) * edge, first:last]
+            applied[at[k], column : column + last - first] = part
+            column += last - first
     full_t[...] = full[...].T
     if split:
         gram_rows(full_t, applied, chips, 1 - lax.rem(lax.axis_index("grp"), 2), gram_ref)
     else:
         gram_ref[...] = jnp.dot(full_t[...], applied[...], preferred_element_type=f32).astype(bf16)
+
+
+def results_kernel(edge, total_rows, stats, full, basis_ref, ritz_ref):
+    z = lax.axis_index("blk")
+    basis_ref[...] = full[pl.ds(pl.multiple_of(z * edge, edge), edge), :]
+    ritz_ref[...] = shift_and_scale(stats, total_rows)[0]
 
 
 def gram_rest_kernel(chips, full_t, applied, gram_ref):
@@ -295,16 +333,16 @@
         axis=0,
     )
     turned = call(
-        functools.partial(turn_kernel, modes),
+        turn_kernel,
         [block_cols[0], current, coeffs],
         1,
-        jax.ShapeDtypeStruct((edge + 16, 2 * modes), bf16),
+        jax.ShapeDtypeStruct((2 * modes + 16, edge), bf16),
         [],
         2 * edge * columns * 2 * modes,
     )
     km_parts, t_parts = gather((payload, turned), nz)
 
-    cols = jnp.stack([p[edge, :slots] for p in t_parts]).astype(jnp.int32)
+    cols = jnp.stack([p[2 * modes, :slots] for p in t_parts]).astype(jnp.int32)
     some = jax.ShapeDtypeStruct((nz - 1, edge, modes), f32)
     last = jax.ShapeDtypeStruct((edge, modes), f32)
     stats_shape = jax.ShapeDtypeStruct((3, modes), f32)
@@ -351,24 +389,31 @@
 
     chips = ng // 2
     block = columns // ng
-    split = block % 16 == 0
+    split = block % 16 == 0 and width % 128 == 32
     gram_shape = jax.ShapeDtypeStruct(
-        (chips, block, 2 * width) if split else (columns, 2 * width), bf16
+        (chips, block * 2 * width // 128, 128) if split else (columns, 2 * width), bf16
     )
     window = -(-(width + max(i * width % 128 for i in range(nz))) // 128) * 128
-    basis_out, ritz, gram, full_t, applied = call(
+    gram, full, full_t, applied = call(
         functools.partial(gram_kernel, nz, chips, slots, edge, modes, total_rows, split),
         [cols, *km_parts, turned, stiff_x, mass_x, stats],
         1,
         (
-            jax.ShapeDtypeStruct((edge, columns), bf16),
-            jax.ShapeDtypeStruct((1, modes), f32),
             gram_shape,
+            jax.ShapeDtypeStruct((rows, columns), bf16),
             jax.ShapeDtypeStruct((columns, rows), bf16),
             jax.ShapeDtypeStruct((rows, 2 * width), bf16),
         ),
-        [pltpu.VMEM((rows, columns), bf16), pltpu.VMEM((rows, window), bf16)],
+        [pltpu.VMEM((rows, window), bf16)],
         2 * rows * columns * width,
+    )
+    basis_out, ritz = call(
+        functools.partial(results_kernel, edge, total_rows),
+        [stats, full],
+        0,
+        (jax.ShapeDtypeStruct((edge, columns), bf16), jax.ShapeDtypeStruct((1, modes), f32)),
+        [],
+        0,
     )
     if split:
         got = lax.ppermute(gram, "grp", by_xor(ng, 1))
@@ -381,12 +426,21 @@
             2 * rows * columns * width,
         )
         mine = (keep.astype(f32) + got.astype(f32)).astype(bf16)
-        total = mine[0].astype(f32)
-        for k in range(1, chips):
-            total = total + lax.ppermute(mine[k], "grp", by_xor(ng, 2 * k)).astype(f32)
+        pieces = [mine[0]] + [
+            lax.ppermute(mine[k], "grp", by_xor(ng, 2 * k)) for k in range(1, chips)
+        ]
+        total = call(
+            functools.partial(finish_kernel, block, width),
+            pieces,
+            0,
+            jax.ShapeDtypeStruct((block, 2, width), f32),
+            [],
+            0,
+        )
     else:
-        total = lax.psum_scatter(gram, "grp", scatter_dimension=0, tiled=True).astype(f32)
-    return (basis_out[None], ritz[0], total.reshape(block, 2, width))
+        total = lax.psum_scatter(gram, "grp", scatter_dimension=0, tiled=True)
+        total = total.astype(f32).reshape(block, 2, width)
+    return (basis_out[None], ritz[0], total)
 
 
 def solution(mesh):

time: 80.6 us -> 76.4 us (0.948)
  waiting for transfers between devices: 42.9 us -> 38.4 us
  Pallas kernels: 10.7 us -> 12.2 us
  local copies, waits for them, and re-layouts: 4.77 us -> 3.67 us
    ppermute x3, waiting for transfers between devices: 8.96 us -> 6 us  [body(): lax.ppermute(mine[k], 'grp', by_xor(ng, 2 * k))]
    pallas_call x7 -> x9, Pallas kernels: 10.7 us -> 12.2 us  [call(): pl.pallas_call(kernel, out_shape=out_shape, in_specs=[smem()] * n_smem +...]
    ppermute x6, waiting for transfers between devices: 25.8 us -> 24.4 us  [send(): return tuple((lax.ppermute(a, 'blk', by_xor(nz, step)) for a in held))]
    reshape x1 -> x0, local copies, waits for them, and re-layouts: 1.09 us -> none  [body(): return (basis_out[None], ritz[0], total.reshape(block, 2, width))]
  transfers between devices with their start and end apart: 18 -> 18, of which waited for: 15 -> 15; matrix products, arithmetic and copies ran while one was open for 1% -> 1% of each run, Pallas kernels for 5% -> 6%
where the time goes in v9:
time: 76.4 us; the launch traced here: 76.2 us
  waiting for transfers between devices  38.4 us (50%)
  starting transfers between devices  19.2 us (25%)
  Pallas kernels  12.2 us (16%)
  local copies, waits for them, and re-layouts  3.67 us (5%)
  other arithmetic  1.98 us (3%)
  between operations  0.79 us (1%)
    ppermute x6, waiting for transfers between devices, send(): return tuple((lax.ppermute(a, 'blk', by_xor(nz, step)) for a in held))  24.4 us
    pallas_call x9, Pallas kernels, call(): pl.pallas_call(kernel, out_shape=out_shape, in_specs=[smem()] * n_smem +...  12.2 us
    ppermute x6, starting transfers between devices, send(): return tuple((lax.ppermute(a, 'blk', by_xor(nz, step)) for a in held))  8.35 us
    ppermute x6, starting transfers between devices, merge_over(): got = [lax.ppermute(stats, axis, by_xor(size, 2 * k)) for k in (1, 2, 3)]  7.11 us
    ppermute x3, waiting for transfers between devices, body(): lax.ppermute(mine[k], 'grp', by_xor(ng, 2 * k))  6 us
    ppermute x6, waiting for transfers between devices, merge_over(): got = [lax.ppermute(stats, axis, by_xor(size, 2 * k)) for k in (1, 2, 3)]  4.25 us
    unnamed x8, local copies, waits for them, and re-layouts  3.62 us
    ppermute x3, starting transfers between devices, body(): lax.ppermute(mine[k], 'grp', by_xor(ng, 2 * k))  3.55 us
  transfers between devices with their start and end apart: 18, of which 15 were waited for; matrix products, arithmetic and copies ran while one was open for 1% of the time, Pallas kernels for 6%

profile of v9, /device:TPU:0, one launch (start us, length us, event | category | flops | bytes accessed | tf_op | source)
XLA Modules:
  0.0 76.2 jit_solution(920264375422878901)
XLA Ops:
  0.6 1.0 %pad_maximum_fusion.refs_4_.refs_0_ = bf16[1024,128]{1,0:T(8,128)(2,1)S(1)} fusion(bf16[512,128]{1,0:T(8,128)(2,1)} %bitcast.15, bf16[512,128]{1,0:T(8,128)(2,1)} %bitcast.16), kind=kLoop, calls=%fused_computation.1 | loop fusion | flops 524288 | bytes 524288 | tf_op jit(solution)/shard_map/concatenate | solution.py:328
  1.6 3.1 %collective-permute-start.3 = (bf16[1024,128]{1,0:T(8,128)(2,1)S(1)}, bf16[1024,128]{1,0:T(8,128)(2,1)S(1)}, u32[]{:S(2)}, u32[]{:S(2)}) collective-permute-start(bf16[1024,128]{1,0:T(8,128)(2,1)S(1)} %pad_maximum_fusion.refs_4_.refs_0_), channel_id=1, source_target_pairs={{0,8},{8,0},{16,24},{24,16},{1,9},{9,1},{17,25},{25,17},{2,10},{10... | collective-permute-start | bytes 786440 | tf_op jit(solution)/shard_map/ppermute | solution.py:304
  4.7 2.6 %collective-permute-start.1 = (bf16[1024,128]{1,0:T(8,128)(2,1)S(1)}, bf16[1024,128]{1,0:T(8,128)(2,1)S(1)}, u32[]{:S(2)}, u32[]{:S(2)}) collective-permute-start(bf16[1024,128]{1,0:T(8,128)(2,1)S(1)} %pad_maximum_fusion.refs_4_.refs_0_), channel_id=1, source_target_pairs={{0,16},{8,24},{16,0},{24,8},{1,17},{9,25},{17,1},{25,9},{2,18},{10... | collective-permute-start | bytes 786440 | tf_op jit(solution)/shard_map/ppermute | solution.py:304
  7.3 0.0 copy-start
  7.3 2.0 %copy-done = bf16[2,1152,768]{2,1,0:T(8,128)(2,1)S(1)} copy-done((bf16[2,1152,768]{2,1,0:T(8,128)(2,1)S(1)}, bf16[2,1152,768]{2,1,0:T(8,128)(2,1)}, u32[]{:S(2)}) %copy-start) | copy-done | bytes 3538968
  9.3 0.0 copy-start.2
  9.3 1.0 %copy-done.2 = bf16[1,128,1152]{2,1,0:T(8,128)(2,1)S(1)} copy-done((bf16[1,128,1152]{2,1,0:T(8,128)(2,1)S(1)}, bf16[1,128,1152]{2,1,0:T(8,128)(2,1)}, u32[]{:S(2)}) %copy-start.2) | copy-done | bytes 294936
  10.3 0.0 copy-start.3
  10.3 0.7 copy-done.3
  10.9 1.0 %shard_map.76.refs_0_ = bf16[784,128]{1,0:T(8,128)(2,1)S(1)} custom-call(s32[1,4]{1,0:T(1,128)S(1)} %bitcast.14, bf16[128,1152]{1,0:T(8,128)(2,1)S(1)} %bitcast.13, bf16[2,1152,768]{2,1,0:T(8,128)(2,1)S(1)} %copy-done), custom_call_target="tpu_custom_call" | custom-call | flops 226492416 | bytes 4000000 | tf_op jit(solution)/shard_map/pallas_call | solution.py:246
  11.9 0.4 collective-permute-start.2
  12.3 0.2 collective-permute-start
  12.5 15.2 %collective-permute-done.2.refs_1_ = bf16[784,128]{1,0:T(8,128)(2,1)S(1)} collective-permute-done((bf16[784,128]{1,0:T(8,128)(2,1)S(1)}, bf16[784,128]{1,0:T(8,128)(2,1)S(1)}, u32[]{:S(2)}, u32[]{:S(2)}) %collective-permute-start.2) | collective-permute-done | bytes 200736 | tf_op jit(solution)/shard_map/ppermute | solution.py:304
  27.6 0.0 collective-permute-done.refs_3_.refs_1_
  27.6 0.0 collective-permute-done.3.refs_2_.refs_5_.refs_1_
  27.6 0.0 collective-permute-done.1.refs_0_
  27.7 0.1 collective-permute-start.4
  27.7 2.0 %collective-permute-start.5 = (bf16[1024,128]{1,0:T(8,128)(2,1)S(1)}, bf16[1024,128]{1,0:T(8,128)(2,1)S(1)}, u32[]{:S(2)}, u32[]{:S(2)}) collective-permute-start(bf16[1024,128]{1,0:T(8,128)(2,1)S(1)} %get-tuple-element.22.refs_6_.refs_2_), channel_id=1, source_target_pairs={{0,8},{8,0},{16,24},{24,16},{1,9},{9,1},{17,25},{25,17},{2,10},{10... | collective-permute-start | bytes 786440 | tf_op jit(solution)/shard_map/ppermute | solution.py:304
  29.8 5.8 %collective-permute-done.4.refs_3_ = bf16[784,128]{1,0:T(8,128)(2,1)S(1)} collective-permute-done((bf16[784,128]{1,0:T(8,128)(2,1)S(1)}, bf16[784,128]{1,0:T(8,128)(2,1)S(1)}, u32[]{:S(2)}, u32[]{:S(2)}) %collective-permute-start.4) | collective-permute-done | bytes 200736 | tf_op jit(solution)/shard_map/ppermute | solution.py:304
  35.6 0.0 copy-start.1
  35.6 1.3 %shard_map.78 = (bf16[512,768]{1,0:T(8,128)(2,1)S(1)}, f32[3,128,384]{2,1,0:T(8,128)S(1)}, f32[3,128,384]{2,1,0:T(8,128)S(1)}) custom-call(s32[4,4]{1,0:T(4,128)S(1)} %maximum_convert_fusion.cols, bf16[784,128]{1,0:T(8,128)(2,1)S(1)} %shard_map.76.refs_0_, bf16[784,128]{1,0:T(8,128)(2,1)S(1)} %collective-permute-done.refs_3_.refs_1_, ...), custom_call_target="tpu_custom_call" | custom-call | flops 301989888 | bytes 4000000 | tf_op jit(solution)/shard_map/pallas_call | solution.py:246
  36.9 3.4 %collective-permute-done.5.km_last.refs_3_ = bf16[1024,128]{1,0:T(8,128)(2,1)S(1)} collective-permute-done((bf16[1024,128]{1,0:T(8,128)(2,1)S(1)}, bf16[1024,128]{1,0:T(8,128)(2,1)S(1)}, u32[]{:S(2)}, u32[]{:S(2)}) %collective-permute-start.5) | collective-permute-done | bytes 262176 | tf_op jit(solution)/shard_map/ppermute | solution.py:304
  40.3 1.1 %shard_map.80 = (f32[128,384]{1,0:T(8,128)S(1)}, f32[128,384]{1,0:T(8,128)S(1)}, f32[3,384]{1,0:T(4,128)S(1)}) custom-call(s32[4,4]{1,0:T(4,128)S(1)} %maximum_convert_fusion.cols, bf16[1024,128]{1,0:T(8,128)(2,1)S(1)} %collective-permute-done.5.km_last.refs_3_, bf16[512,768]{1,0:T(8,128)(2,1)S(1)} %get-tuple-element.23.placed, ...), custom_call_target="tpu_custom_call" | custom-call | flops 100663296 | bytes 4000000 | tf_op jit(solution)/shard_map/pallas_call | solution.py:246
  41.4 0.1 collective-permute-start.6
  41.5 1.2 %collective-permute-done.6 = f32[3,384]{1,0:T(4,128)S(1)} collective-permute-done((f32[3,384]{1,0:T(4,128)S(1)}, f32[3,384]{1,0:T(4,128)S(1)}, u32[]{:S(2)}, u32[]{:S(2)}) %collective-permute-start.6) | collective-permute-done | bytes 4640 | tf_op jit(solution)/shard_map/ppermute | solution.py:272
  42.7 2.5 %collective-permute-start.9 = (f32[3,384]{1,0:T(4,128)S(1)}, f32[3,384]{1,0:T(4,128)S(1)}, u32[]{:S(2)}, u32[]{:S(2)}) collective-permute-start(f32[3,384]{1,0:T(4,128)S(1)} %pad_maximum_fusion.1), channel_id=1, source_target_pairs={{0,6},{1,7},{2,4},{3,5},{4,2},{5,3},{6,0},{7,1},{8,14},{9,15},{10,... | collective-permute-start | bytes 13832 | tf_op jit(solution)/shard_map/ppermute | solution.py:275
  45.2 0.5 collective-permute-start.8
  45.7 0.5 collective-permute-start.7
  46.2 0.0 copy-done.1
  46.2 1.0 %shard_map.79.refs_4_ = f32[512,768]{1,0:T(8,128)S(1)} custom-call(bf16[512,768]{1,0:T(8,128)(2,1)S(1)} %get-tuple-element.23.placed, bf16[2,1152,768]{2,1,0:T(8,128)(2,1)S(1)} %copy-done.1), custom_call_target="tpu_custom_call" | custom-call | flops 603979776 | bytes 4000000 | tf_op jit(solution)/shard_map/pallas_call | solution.py:246
  47.2 0.1 collective-permute-done.9
  47.3 1.5 %collective-permute-done.8 = f32[3,384]{1,0:T(4,128)S(1)} collective-permute-done((f32[3,384]{1,0:T(4,128)S(1)}, f32[3,384]{1,0:T(4,128)S(1)}, u32[]{:S(2)}, u32[]{:S(2)}) %collective-permute-start.8) | collective-permute-done | bytes 4640 | tf_op jit(solution)/shard_map/ppermute | solution.py:275
  48.8 0.5 collective-permute-done.7
  49.4 2.4 %shard_map.81 = (bf16[512,768]{1,0:T(8,128)(2,1)S(1)}, f32[512,384]{1,0:T(8,128)S(1)}, f32[512,384]{1,0:T(8,128)S(1)}, f32[3,384]{1,0:T(4,128)S(1)}) custom-call(s32[4,4]{1,0:T(4,128)S(1)} %maximum_convert_fusion.cols, bf16[1024,128]{1,0:T(8,128)(2,1)S(1)} %pad_maximum_fusion.refs_4_.refs_0_, ...), custom_call_target="tpu_custom_call" | custom-call | flops 704643072 | bytes 4000000 | tf_op jit(solution)/shard_map/pallas_call | solution.py:246
  51.8 0.1 collective-permute-start.10
  51.9 1.2 %collective-permute-done.10 = f32[3,384]{1,0:T(4,128)S(1)} collective-permute-done((f32[3,384]{1,0:T(4,128)S(1)}, f32[3,384]{1,0:T(4,128)S(1)}, u32[]{:S(2)}, u32[]{:S(2)}) %collective-permute-start.10) | collective-permute-done | bytes 4640 | tf_op jit(solution)/shard_map/ppermute | solution.py:272
  53.1 1.6 %collective-permute-start.13 = (f32[3,384]{1,0:T(4,128)S(1)}, f32[3,384]{1,0:T(4,128)S(1)}, u32[]{:S(2)}, u32[]{:S(2)}) collective-permute-start(f32[3,384]{1,0:T(4,128)S(1)} %pad_maximum_fusion.3), channel_id=1, source_target_pairs={{0,6},{1,7},{2,4},{3,5},{4,2},{5,3},{6,0},{7,1},{8,14},{9,15},{10,... | collective-permute-start | bytes 13832 | tf_op jit(solution)/shard_map/ppermute | solution.py:275
  54.7 0.5 collective-permute-start.12
  55.2 1.5 %collective-permute-start.11 = (f32[3,384]{1,0:T(4,128)S(1)}, f32[3,384]{1,0:T(4,128)S(1)}, u32[]{:S(2)}, u32[]{:S(2)}) collective-permute-start(f32[3,384]{1,0:T(4,128)S(1)} %pad_maximum_fusion.3), channel_id=1, source_target_pairs={{0,2},{1,3},{2,0},{3,1},{4,6},{5,7},{6,4},{7,5},{8,10},{9,11},{10,... | collective-permute-start | bytes 13832 | tf_op jit(solution)/shard_map/ppermute | solution.py:275
  56.7 1.0 %collective-permute-done.13 = f32[3,384]{1,0:T(4,128)S(1)} collective-permute-done((f32[3,384]{1,0:T(4,128)S(1)}, f32[3,384]{1,0:T(4,128)S(1)}, u32[]{:S(2)}, u32[]{:S(2)}) %collective-permute-start.13) | collective-permute-done | bytes 4640 | tf_op jit(solution)/shard_map/ppermute | solution.py:275
  57.7 0.6 collective-permute-done.12
  58.3 0.5 collective-permute-done.11
  58.9 2.8 %shard_map.82 = (bf16[4,648,128]{2,1,0:T(8,128)(2,1)S(1)}, bf16[512,1152]{1,0:T(8,128)(2,1)S(1)}, bf16[1152,512]{1,0:T(8,128)(2,1)S(1)}, bf16[512,576]{1,0:T(8,128)(2,1)S(1)}) custom-call(s32[4,4]{1,0:T(4,128)S(1)} %maximum_convert_fusion.cols, bf16[1024,128]{1,0:T(8,128)(2,1)S(1)} %pad_maximum_fusion.refs_4_.refs_0_, ...), custom_call_target="tpu_custom_call" | custom-call | flops 339738624 | bytes 4000000 | tf_op jit(solution)/shard_map/pallas_call | solution.py:246
  61.7 0.1 collective-permute-start.14
  61.8 0.7 shard_map.84
  62.5 1.4 %collective-permute-done.14 = bf16[4,648,128]{2,1,0:T(8,128)(2,1)S(1)} collective-permute-done((bf16[4,648,128]{2,1,0:T(8,128)(2,1)S(1)}, bf16[4,648,128]{2,1,0:T(8,128)(2,1)S(1)}, u32[]{:S(2)}, u32[]{:S(2)}) %collective-permute-start.14) | collective-permute-done | bytes 663584 | tf_op jit(solution)/shard_map/ppermute | solution.py:419
  63.9 0.2 add_convert_fusion
  64.1 2.5 %collective-permute-start.17 = (bf16[648,128]{1,0:T(8,128)(2,1)S(1)}, bf16[648,128]{1,0:T(8,128)(2,1)S(1)}, u32[]{:S(2)}, u32[]{:S(2)}) collective-permute-start(bf16[648,128]{1,0:T(8,128)(2,1)S(1)} %get-tuple-element.47), channel_id=1, source_target_pairs={{0,6},{1,7},{2,4},{3,5},{4,2},{5,3},{6,0},{7,1},{8,14},{9,15},{10,... | collective-permute-start | bytes 497672 | tf_op jit(solution)/shard_map/ppermute | solution.py:430
  66.6 0.5 collective-permute-start.16
  67.1 0.5 collective-permute-start.15
  67.7 0.7 shard_map.83
  68.4 0.6 reduce
  69.0 3.2 %collective-permute-done.17.refs_3_ = bf16[648,128]{1,0:T(8,128)(2,1)S(1)} collective-permute-done((bf16[648,128]{1,0:T(8,128)(2,1)S(1)}, bf16[648,128]{1,0:T(8,128)(2,1)S(1)}, u32[]{:S(2)}, u32[]{:S(2)}) %collective-permute-start.17) | collective-permute-done | bytes 165920 | tf_op jit(solution)/shard_map/ppermute | solution.py:430
  72.2 2.8 %collective-permute-done.16.refs_2_ = bf16[648,128]{1,0:T(8,128)(2,1)S(1)} collective-permute-done((bf16[648,128]{1,0:T(8,128)(2,1)S(1)}, bf16[648,128]{1,0:T(8,128)(2,1)S(1)}, u32[]{:S(2)}, u32[]{:S(2)}) %collective-permute-start.16) | collective-permute-done | bytes 165920 | tf_op jit(solution)/shard_map/ppermute | solution.py:430
  74.9 0.1 collective-permute-done.15.refs_1_
  75.0 1.2 %shard_map.85 = f32[144,2,288]{2,1,0:T(2,128)} custom-call(bf16[648,128]{1,0:T(8,128)(2,1)S(1)} %get-tuple-element.50.refs_0_, bf16[648,128]{1,0:T(8,128)(2,1)S(1)} %collective-permute-done.15.refs_1_, bf16[648,128]{1,0:T(8,128)(2,1)S(1)} %collective-permute-done.16.refs_2_, bf16[648,128]{1,0:T(8,128)(2,1)S(1)} %collective-permute-done.17.refs_3_), custom_call_target="tpu_custom_call" | custom-call | bytes 4000000 | tf_op jit(solution)/shard_map/pallas_call | solution.py:246
  (15 shorter events, 0.3 us)
Async XLA Ops:
  1.6 26.0 %collective-permute-start.3 = (bf16[1024,128]{1,0:T(8,128)(2,1)S(1)}, bf16[1024,128]{1,0:T(8,128)(2,1)S(1)}, u32[]{:S(2)}, u32[]{:S(2)}) collective-permute-start(bf16[1024,128]{1,0:T(8,128)(2,1)S(1)} %pad_maximum_fusion.refs_4_.refs_0_), channel_id=1, source_target_pairs={{0,8},{8,0},{16,24},{24,16},{1,9},{9,1},{17,25},{25,17},{2,10},{10... | collective-permute-start | bytes 786440 | tf_op jit(solution)/shard_map/ppermute | solution.py:304
  4.7 22.9 %collective-permute-start.1 = (bf16[1024,128]{1,0:T(8,128)(2,1)S(1)}, bf16[1024,128]{1,0:T(8,128)(2,1)S(1)}, u32[]{:S(2)}, u32[]{:S(2)}) collective-permute-start(bf16[1024,128]{1,0:T(8,128)(2,1)S(1)} %pad_maximum_fusion.refs_4_.refs_0_), channel_id=1, source_target_pairs={{0,16},{8,24},{16,0},{24,8},{1,17},{9,25},{17,1},{25,9},{2,18},{10... | collective-permute-start | bytes 786440 | tf_op jit(solution)/shard_map/ppermute | solution.py:304
  7.3 2.0 %copy-start = (bf16[2,1152,768]{2,1,0:T(8,128)(2,1)S(1)}, bf16[2,1152,768]{2,1,0:T(8,128)(2,1)}, u32[]{:S(2)}) copy-start(bf16[2,1152,768]{2,1,0:T(8,128)(2,1)} %refs_10_.1) | copy-start | bytes 10616836
  9.3 1.0 %copy-start.2 = (bf16[1,128,1152]{2,1,0:T(8,128)(2,1)S(1)}, bf16[1,128,1152]{2,1,0:T(8,128)(2,1)}, u32[]{:S(2)}) copy-start(bf16[1,128,1152]{2,1,0:T(8,128)(2,1)} %param.5) | copy-start | bytes 884740
  10.3 0.7 copy-start.3
  11.9 15.7 %collective-permute-start.2 = (bf16[784,128]{1,0:T(8,128)(2,1)S(1)}, bf16[784,128]{1,0:T(8,128)(2,1)S(1)}, u32[]{:S(2)}, u32[]{:S(2)}) collective-permute-start(bf16[784,128]{1,0:T(8,128)(2,1)S(1)} %shard_map.76.refs_0_), channel_id=1, source_target_pairs={{0,16},{8,24},{16,0},{24,8},{1,17},{9,25},{17,1},{25,9},{2,18},{10... | collective-permute-start | bytes 602120 | tf_op jit(solution)/shard_map/ppermute | solution.py:304
  12.3 15.4 %collective-permute-start = (bf16[784,128]{1,0:T(8,128)(2,1)S(1)}, bf16[784,128]{1,0:T(8,128)(2,1)S(1)}, u32[]{:S(2)}, u32[]{:S(2)}) collective-permute-start(bf16[784,128]{1,0:T(8,128)(2,1)S(1)} %shard_map.76.refs_0_), channel_id=1, source_target_pairs={{0,8},{8,0},{16,24},{24,16},{1,9},{9,1},{17,25},{25,17},{2,10},{10... | collective-permute-start | bytes 602120 | tf_op jit(solution)/shard_map/ppermute | solution.py:304
  27.7 7.9 %collective-permute-start.4 = (bf16[784,128]{1,0:T(8,128)(2,1)S(1)}, bf16[784,128]{1,0:T(8,128)(2,1)S(1)}, u32[]{:S(2)}, u32[]{:S(2)}) collective-permute-start(bf16[784,128]{1,0:T(8,128)(2,1)S(1)} %get-tuple-element.21.refs_2_), channel_id=1, source_target_pairs={{0,8},{8,0},{16,24},{24,16},{1,9},{9,1},{17,25},{25,17},{2,10},{10... | collective-permute-start | bytes 602120 | tf_op jit(solution)/shard_map/ppermute | solution.py:304
  27.7 12.6 %collective-permute-start.5 = (bf16[1024,128]{1,0:T(8,128)(2,1)S(1)}, bf16[1024,128]{1,0:T(8,128)(2,1)S(1)}, u32[]{:S(2)}, u32[]{:S(2)}) collective-permute-start(bf16[1024,128]{1,0:T(8,128)(2,1)S(1)} %get-tuple-element.22.refs_6_.refs_2_), channel_id=1, source_target_pairs={{0,8},{8,0},{16,24},{24,16},{1,9},{9,1},{17,25},{25,17},{2,10},{10... | collective-permute-start | bytes 786440 | tf_op jit(solution)/shard_map/ppermute | solution.py:304
  35.6 10.6 %copy-start.1 = (bf16[2,1152,768]{2,1,0:T(8,128)(2,1)S(1)}, bf16[2,1152,768]{2,1,0:T(8,128)(2,1)}, u32[]{:S(2)}) copy-start(bf16[2,1152,768]{2,1,0:T(8,128)(2,1)} %refs_10_.1) | copy-start | bytes 10616836
  41.4 1.2 %collective-permute-start.6 = (f32[3,384]{1,0:T(4,128)S(1)}, f32[3,384]{1,0:T(4,128)S(1)}, u32[]{:S(2)}, u32[]{:S(2)}) collective-permute-start(f32[3,384]{1,0:T(4,128)S(1)} %get-tuple-element.28), channel_id=1, source_target_pairs={{0,1},{1,0},{2,3},{3,2},{4,5},{5,4},{6,7},{7,6},{8,9},{9,8},{10,11... | collective-permute-start | bytes 13832 | tf_op jit(solution)/shard_map/ppermute | solution.py:272
  42.7 4.6 %collective-permute-start.9 = (f32[3,384]{1,0:T(4,128)S(1)}, f32[3,384]{1,0:T(4,128)S(1)}, u32[]{:S(2)}, u32[]{:S(2)}) collective-permute-start(f32[3,384]{1,0:T(4,128)S(1)} %pad_maximum_fusion.1), channel_id=1, source_target_pairs={{0,6},{1,7},{2,4},{3,5},{4,2},{5,3},{6,0},{7,1},{8,14},{9,15},{10,... | collective-permute-start | bytes 13832 | tf_op jit(solution)/shard_map/ppermute | solution.py:275
  45.2 3.6 %collective-permute-start.8 = (f32[3,384]{1,0:T(4,128)S(1)}, f32[3,384]{1,0:T(4,128)S(1)}, u32[]{:S(2)}, u32[]{:S(2)}) collective-permute-start(f32[3,384]{1,0:T(4,128)S(1)} %pad_maximum_fusion.1), channel_id=1, source_target_pairs={{0,4},{1,5},{2,6},{3,7},{4,0},{5,1},{6,2},{7,3},{8,12},{9,13},{10,... | collective-permute-start | bytes 13832 | tf_op jit(solution)/shard_map/ppermute | solution.py:275
  45.7 3.6 %collective-permute-start.7 = (f32[3,384]{1,0:T(4,128)S(1)}, f32[3,384]{1,0:T(4,128)S(1)}, u32[]{:S(2)}, u32[]{:S(2)}) collective-permute-start(f32[3,384]{1,0:T(4,128)S(1)} %pad_maximum_fusion.1), channel_id=1, source_target_pairs={{0,2},{1,3},{2,0},{3,1},{4,6},{5,7},{6,4},{7,5},{8,10},{9,11},{10,... | collective-permute-start | bytes 13832 | tf_op jit(solution)/shard_map/ppermute | solution.py:275
  51.8 1.2 %collective-permute-start.10 = (f32[3,384]{1,0:T(4,128)S(1)}, f32[3,384]{1,0:T(4,128)S(1)}, u32[]{:S(2)}, u32[]{:S(2)}) collective-permute-start(f32[3,384]{1,0:T(4,128)S(1)} %get-tuple-element.29), channel_id=1, source_target_pairs={{0,1},{1,0},{2,3},{3,2},{4,5},{5,4},{6,7},{7,6},{8,9},{9,8},{10,11... | collective-permute-start | bytes 13832 | tf_op jit(solution)/shard_map/ppermute | solution.py:272
  53.1 4.6 %collective-permute-start.13 = (f32[3,384]{1,0:T(4,128)S(1)}, f32[3,384]{1,0:T(4,128)S(1)}, u32[]{:S(2)}, u32[]{:S(2)}) collective-permute-start(f32[3,384]{1,0:T(4,128)S(1)} %pad_maximum_fusion.3), channel_id=1, source_target_pairs={{0,6},{1,7},{2,4},{3,5},{4,2},{5,3},{6,0},{7,1},{8,14},{9,15},{10,... | collective-permute-start | bytes 13832 | tf_op jit(solution)/shard_map/ppermute | solution.py:275
  54.7 3.6 %collective-permute-start.12 = (f32[3,384]{1,0:T(4,128)S(1)}, f32[3,384]{1,0:T(4,128)S(1)}, u32[]{:S(2)}, u32[]{:S(2)}) collective-permute-start(f32[3,384]{1,0:T(4,128)S(1)} %pad_maximum_fusion.3), channel_id=1, source_target_pairs={{0,4},{1,5},{2,6},{3,7},{4,0},{5,1},{6,2},{7,3},{8,12},{9,13},{10,... | collective-permute-start | bytes 13832 | tf_op jit(solution)/shard_map/ppermute | solution.py:275
  55.2 3.6 %collective-permute-start.11 = (f32[3,384]{1,0:T(4,128)S(1)}, f32[3,384]{1,0:T(4,128)S(1)}, u32[]{:S(2)}, u32[]{:S(2)}) collective-permute-start(f32[3,384]{1,0:T(4,128)S(1)} %pad_maximum_fusion.3), channel_id=1, source_target_pairs={{0,2},{1,3},{2,0},{3,1},{4,6},{5,7},{6,4},{7,5},{8,10},{9,11},{10,... | collective-permute-start | bytes 13832 | tf_op jit(solution)/shard_map/ppermute | solution.py:275
  61.7 2.2 %collective-permute-start.14 = (bf16[4,648,128]{2,1,0:T(8,128)(2,1)S(1)}, bf16[4,648,128]{2,1,0:T(8,128)(2,1)S(1)}, u32[]{:S(2)}, u32[]{:S(2)}) collective-permute-start(bf16[4,648,128]{2,1,0:T(8,128)(2,1)S(1)} %get-tuple-element.38), channel_id=1, source_target_pairs={{0,1},{1,0},{2,3},{3,2},{4,5},{5,4},{6,7},{7,6},{8,9},{9,8},{10,11... | collective-permute-start | bytes 1990664 | tf_op jit(solution)/shard_map/ppermute | solution.py:419
  64.1 8.1 %collective-permute-start.17 = (bf16[648,128]{1,0:T(8,128)(2,1)S(1)}, bf16[648,128]{1,0:T(8,128)(2,1)S(1)}, u32[]{:S(2)}, u32[]{:S(2)}) collective-permute-start(bf16[648,128]{1,0:T(8,128)(2,1)S(1)} %get-tuple-element.47), channel_id=1, source_target_pairs={{0,6},{1,7},{2,4},{3,5},{4,2},{5,3},{6,0},{7,1},{8,14},{9,15},{10,... | collective-permute-start | bytes 497672 | tf_op jit(solution)/shard_map/ppermute | solution.py:430
  66.6 8.3 %collective-permute-start.16 = (bf16[648,128]{1,0:T(8,128)(2,1)S(1)}, bf16[648,128]{1,0:T(8,128)(2,1)S(1)}, u32[]{:S(2)}, u32[]{:S(2)}) collective-permute-start(bf16[648,128]{1,0:T(8,128)(2,1)S(1)} %get-tuple-element.48), channel_id=1, source_target_pairs={{0,4},{1,5},{2,6},{3,7},{4,0},{5,1},{6,2},{7,3},{8,12},{9,13},{10,... | collective-permute-start | bytes 497672 | tf_op jit(solution)/shard_map/ppermute | solution.py:430
  67.1 7.9 %collective-permute-start.15 = (bf16[648,128]{1,0:T(8,128)(2,1)S(1)}, bf16[648,128]{1,0:T(8,128)(2,1)S(1)}, u32[]{:S(2)}, u32[]{:S(2)}) collective-permute-start(bf16[648,128]{1,0:T(8,128)(2,1)S(1)} %get-tuple-element.49), channel_id=1, source_target_pairs={{0,2},{1,3},{2,0},{3,1},{4,6},{5,7},{6,4},{7,5},{8,10},{9,11},{10,... | collective-permute-start | bytes 497672 | tf_op jit(solution)/shard_map/ppermute | solution.py:430

commit v10 on v9

--- a/solution.py
+++ b/solution.py
@@ -12,6 +12,7 @@
 f32 = jnp.float32
 bf16 = jnp.bfloat16
 VMEM_BYTES = 24 * 1024 * 1024
+FIRST_VMEM_BYTES = 61 * 1024 * 1024
 
 
 def vmem():
@@ -81,17 +82,52 @@
     return pl.BlockSpec(memory_space=pltpu.HBM)
 
 
-def turn_kernel(cols, current, coeffs, out_ref):
+def turn_kernel(chunks, cols, current_hbm, coeffs_hbm, out_ref, current, coeffs, sems):
+    depth = current.shape[1] // chunks
+    copies = [pltpu.make_async_copy(current_hbm, current, sems.at[0])]
+    for c in range(chunks):
+        part = pl.ds(c * depth, depth)
+        copies.append(pltpu.make_async_copy(coeffs_hbm.at[0, part], coeffs.at[part], sems.at[c + 1]))
+    for copy in copies:
+        copy.start()
     rows, edge = current.shape[0], out_ref.shape[1]
-    turned = jnp.dot(current[...], coeffs[0], preferred_element_type=f32).astype(bf16)
-    blocks = turned.shape[1] // edge
-    for b in range(blocks):
-        out_ref[b * rows : (b + 1) * rows, :] = turned[:, b * edge : (b + 1) * edge]
     lane = lax.broadcasted_iota(jnp.int32, (16, edge), 1)
     tag = jnp.zeros((16, edge), jnp.int32)
     for s in range(cols.shape[1]):
         tag = jnp.where(lane == s, cols[0, s], tag)
+    copies[0].wait()
+    turned = None
+    for c in range(chunks):
+        copies[c + 1].wait()
+        part = slice(c * depth, (c + 1) * depth)
+        more = jnp.dot(current[:, part], coeffs[part, :], preferred_element_type=f32)
+        turned = more if turned is None else turned + more
+    turned = turned.astype(bf16)
+    blocks = turned.shape[1] // edge
+    for b in range(blocks):
+        out_ref[b * rows : (b + 1) * rows, :] = turned[:, b * edge : (b + 1) * edge]
     out_ref[blocks * rows : blocks * rows + 16, :] = tag.astype(f32).astype(bf16)
+
+
+def turn_first(cols, current, coeffs, modes):
+    rows, columns = current.shape
+    chunks = 3
+    in_hbm = pl.BlockSpec(memory_space=pltpu.HBM)
+    return pl.pallas_call(
+        functools.partial(turn_kernel, chunks),
+        out_shape=jax.ShapeDtypeStruct((2 * modes + 16, rows), bf16),
+        in_specs=[smem(), in_hbm, in_hbm],
+        out_specs=vmem(),
+        scratch_shapes=[
+            pltpu.VMEM((rows, columns), bf16),
+            pltpu.VMEM((columns, 2 * modes), bf16),
+            pltpu.SemaphoreType.DMA((chunks + 1,)),
+        ],
+        compiler_params=pltpu.CompilerParams(vmem_limit_bytes=FIRST_VMEM_BYTES),
+        cost_estimate=pl.CostEstimate(
+            flops=4 * rows * columns * modes, bytes_accessed=4 * columns * modes, transcendentals=0
+        ),
+    )(cols, current, coeffs)
 
 
 def rows_kernel(nz, slots, edge, modes, cols, *refs):
@@ -297,22 +333,22 @@
     )(*arrays, *until)
 
 
-def gather(arrays, nz):
-    far = nz // 2
-
-    def send(held, step):
-        return tuple(lax.ppermute(a, "blk", by_xor(nz, step)) for a in held)
-
-    parts = {0: tuple(arrays)}
+def gather(operators, turned, nz):
+    def send(x, step):
+        return lax.ppermute(x, "blk", by_xor(nz, step))
+
     if nz == 4:
-        parts[2], parts[1] = send(arrays, 2), send(arrays, 1)
-        parts[2] = hold(parts[2], parts[1])
-        parts[3] = send(parts[2], 1)
-    else:
-        while far:
-            parts |= {k ^ far: send(held, far) for k, held in parts.items()}
-            far //= 2
-    return [[parts[k][i] for k in range(nz)] for i in range(len(arrays))]
+        km_2, km_1 = send(operators, 2), send(operators, 1)
+        t_2, t_1 = send(turned, 2), send(turned, 1)
+        (km_2,) = hold((km_2,), (km_1,))
+        km_3 = send(km_2, 1)
+        (t_2,) = hold((t_2,), (t_1,))
+        return [operators, km_1, km_2, km_3], [turned, t_1, t_2, send(t_2, 1)]
+    parts, far = {0: (operators, turned)}, nz // 2
+    while far:
+        parts |= {k ^ far: tuple(send(x, far) for x in held) for k, held in parts.items()}
+        far //= 2
+    return [[parts[k][i] for k in range(nz)] for i in range(2)]
 
 
 def body(basis, coeffs, stiff_blocks, mass_blocks, block_cols):
@@ -332,15 +368,8 @@
         ],
         axis=0,
     )
-    turned = call(
-        turn_kernel,
-        [block_cols[0], current, coeffs],
-        1,
-        jax.ShapeDtypeStruct((2 * modes + 16, edge), bf16),
-        [],
-        2 * edge * columns * 2 * modes,
-    )
-    km_parts, t_parts = gather((payload, turned), nz)
+    turned = turn_first(block_cols[0], current, coeffs, modes)
+    km_parts, t_parts = gather(payload, turned, nz)
 
     cols = jnp.stack([p[2 * modes, :slots] for p in t_parts]).astype(jnp.int32)
     some = jax.ShapeDtypeStruct((nz - 1, edge, modes), f32)

time: 76.4 us -> 75.2 us (0.984)
  local copies, waits for them, and re-layouts: 3.67 us -> 0.07 us
  Pallas kernels: 12.2 us -> 14.6 us
  waiting for transfers between devices: 38.4 us -> 40.2 us
  other arithmetic: 1.98 us -> 1 us
  starting transfers between devices: 19.2 us -> 18.4 us
    unnamed x8, local copies, waits for them, and re-layouts: 3.62 us -> 0.02 us
    pallas_call x0 -> x1, Pallas kernels: none -> 3.43 us  [turn_first(): pl.pallas_call(functools.partial(turn_kernel, chunks), out_shape=jax.Shap...]
    ppermute x6, waiting for transfers between devices: 24.4 us -> 26.2 us  [send(): return lax.ppermute(x, 'blk', by_xor(nz, step))]
    pallas_call x9 -> x8, Pallas kernels: 12.2 us -> 11.2 us  [call(): pl.pallas_call(kernel, out_shape=out_shape, in_specs=[smem()] * n_smem +...]
    concatenate x1, other arithmetic: 0.99 us -> 0.02 us  [body(): jnp.concatenate([stiff_blocks[0, 0].reshape(slots * edge, edge), mass_blo...]
    ppermute x6, starting transfers between devices: 8.35 us -> 7.49 us  [send(): return lax.ppermute(x, 'blk', by_xor(nz, step))]
  transfers between devices with their start and end apart: 18 -> 18, of which waited for: 15 -> 18; matrix products, arithmetic and copies ran while one was open for 1% -> 1% of each run, Pallas kernels for 6% -> 5%
where the time goes in v10:
time: 75.2 us; the launch traced here: 75.1 us
  waiting for transfers between devices  40.2 us (53%)
  starting transfers between devices  18.4 us (24%)
  Pallas kernels  14.6 us (19%)
  other arithmetic  1 us (1%)
  between operations  0.8 us (1%)
    ppermute x6, waiting for transfers between devices, send(): return lax.ppermute(x, 'blk', by_xor(nz, step))  26.2 us
    pallas_call x8, Pallas kernels, call(): pl.pallas_call(kernel, out_shape=out_shape, in_specs=[smem()] * n_smem +...  11.2 us
    ppermute x6, starting transfers between devices, send(): return lax.ppermute(x, 'blk', by_xor(nz, step))  7.49 us
    ppermute x6, starting transfers between devices, merge_over(): got = [lax.ppermute(stats, axis, by_xor(size, 2 * k)) for k in (1, 2, 3)]  7.11 us
    ppermute x3, waiting for transfers between devices, body(): lax.ppermute(mine[k], 'grp', by_xor(ng, 2 * k))  6.06 us
    ppermute x6, waiting for transfers between devices, merge_over(): got = [lax.ppermute(stats, axis, by_xor(size, 2 * k)) for k in (1, 2, 3)]  4.25 us
    ppermute x3, starting transfers between devices, body(): lax.ppermute(mine[k], 'grp', by_xor(ng, 2 * k))  3.55 us
    pallas_call x1, Pallas kernels, turn_first(): pl.pallas_call(functools.partial(turn_kernel, chunks), out_shape=jax.Shap...  3.43 us
  transfers between devices with their start and end apart: 18, of which 18 were waited for; matrix products, arithmetic and copies ran while one was open for 1% of the time, Pallas kernels for 5%

profile of v10, /device:TPU:0, one launch (start us, length us, event | category | flops | bytes accessed | tf_op | source)
XLA Modules:
  0.0 75.1 jit_solution(4633023108185883678)
XLA Ops:
  0.6 0.0 copy-start.2
  0.6 0.0 copy-start.3
  0.7 3.4 %shard_map.76.refs_0_ = bf16[784,128]{1,0:T(8,128)(2,1)} custom-call(s32[1,4]{1,0:T(1,128)} %bitcast.16, bf16[128,1152]{1,0:T(8,128)(2,1)} %bitcast.13, bf16[2,1152,768]{2,1,0:T(8,128)(2,1)} %refs_10_.1), custom_call_target="tpu_custom_call" | custom-call | flops 226492416 | bytes 1769472 | tf_op jit(solution)/shard_map/pallas_call | solution.py:116
  4.1 0.0 copy-start.1
  4.1 4.1 %collective-permute-start.1 = (bf16[784,128]{1,0:T(8,128)(2,1)}, bf16[784,128]{1,0:T(8,128)(2,1)S(1)}, u32[]{:S(2)}, u32[]{:S(2)}) collective-permute-start(bf16[784,128]{1,0:T(8,128)(2,1)} %shard_map.76.refs_0_), channel_id=1, source_target_pairs={{0,16},{8,24},{16,0},{24,8},{1,17},{9,25},{17,1},{25,9},{2,18},{10... | collective-permute-start | bytes 602120 | tf_op jit(solution)/shard_map/ppermute | solution.py:338
  8.2 1.6 %collective-permute-start = (bf16[784,128]{1,0:T(8,128)(2,1)}, bf16[784,128]{1,0:T(8,128)(2,1)S(1)}, u32[]{:S(2)}, u32[]{:S(2)}) collective-permute-start(bf16[784,128]{1,0:T(8,128)(2,1)} %shard_map.76.refs_0_), channel_id=1, source_target_pairs={{0,8},{8,0},{16,24},{24,16},{1,9},{9,1},{17,25},{25,17},{2,10},{10... | collective-permute-start | bytes 602120 | tf_op jit(solution)/shard_map/ppermute | solution.py:338
  9.8 0.0 copy-done.2
  9.8 0.0 copy-done.3
  9.8 0.4 collective-permute-start.4
  10.2 0.2 collective-permute-start.3
  10.4 9.1 %collective-permute-done.1.refs_0_ = bf16[784,128]{1,0:T(8,128)(2,1)S(1)} collective-permute-done((bf16[784,128]{1,0:T(8,128)(2,1)}, bf16[784,128]{1,0:T(8,128)(2,1)S(1)}, u32[]{:S(2)}, u32[]{:S(2)}) %collective-permute-start.1) | collective-permute-done | bytes 200736 | tf_op jit(solution)/shard_map/ppermute | solution.py:338
  19.5 1.2 %collective-permute-done.refs_1_ = bf16[784,128]{1,0:T(8,128)(2,1)S(1)} collective-permute-done((bf16[784,128]{1,0:T(8,128)(2,1)}, bf16[784,128]{1,0:T(8,128)(2,1)S(1)}, u32[]{:S(2)}, u32[]{:S(2)}) %collective-permute-start) | collective-permute-done | bytes 200736 | tf_op jit(solution)/shard_map/ppermute | solution.py:338
  20.6 0.0 collective-permute-start.2
  20.6 8.4 %collective-permute-done.4.refs_0_ = bf16[1024,128]{1,0:T(8,128)(2,1)S(1)} collective-permute-done((bf16[1024,128]{1,0:T(8,128)(2,1)S(1)}, bf16[1024,128]{1,0:T(8,128)(2,1)S(1)}, u32[]{:S(2)}, u32[]{:S(2)}) %collective-permute-start.4) | collective-permute-done | bytes 262176 | tf_op jit(solution)/shard_map/ppermute | solution.py:338
  29.1 1.6 %collective-permute-done.3.refs_1_.refs_5_ = bf16[1024,128]{1,0:T(8,128)(2,1)S(1)} collective-permute-done((bf16[1024,128]{1,0:T(8,128)(2,1)S(1)}, bf16[1024,128]{1,0:T(8,128)(2,1)S(1)}, u32[]{:S(2)}, u32[]{:S(2)}) %collective-permute-start.3) | collective-permute-done | bytes 262176 | tf_op jit(solution)/shard_map/ppermute | solution.py:338
  30.7 1.2 %collective-permute-start.5 = (bf16[1024,128]{1,0:T(8,128)(2,1)S(1)}, bf16[1024,128]{1,0:T(8,128)(2,1)S(1)}, u32[]{:S(2)}, u32[]{:S(2)}) collective-permute-start(bf16[1024,128]{1,0:T(8,128)(2,1)S(1)} %shard_map.78.refs_6_.refs_2_), channel_id=1, source_target_pairs={{0,8},{8,0},{16,24},{24,16},{1,9},{9,1},{17,25},{25,17},{2,10},{10... | collective-permute-start | bytes 786440 | tf_op jit(solution)/shard_map/ppermute | solution.py:338
  31.9 0.0 copy-done.1
  31.9 3.1 %collective-permute-done.2.refs_3_ = bf16[784,128]{1,0:T(8,128)(2,1)S(1)} collective-permute-done((bf16[784,128]{1,0:T(8,128)(2,1)S(1)}, bf16[784,128]{1,0:T(8,128)(2,1)S(1)}, u32[]{:S(2)}, u32[]{:S(2)}) %collective-permute-start.2) | collective-permute-done | bytes 200736 | tf_op jit(solution)/shard_map/ppermute | solution.py:338
  35.0 0.0 copy-start
  35.0 1.3 %shard_map.79 = (bf16[512,768]{1,0:T(8,128)(2,1)S(1)}, f32[3,128,384]{2,1,0:T(8,128)S(1)}, f32[3,128,384]{2,1,0:T(8,128)S(1)}) custom-call(s32[4,4]{1,0:T(4,128)S(1)} %maximum_convert_fusion.cols, bf16[784,128]{1,0:T(8,128)(2,1)S(1)} %copy-done.1, bf16[784,128]{1,0:T(8,128)(2,1)S(1)} %collective-permute-done.refs_1_, ...), custom_call_target="tpu_custom_call" | custom-call | flops 301989888 | bytes 4000000 | tf_op jit(solution)/shard_map/pallas_call | solution.py:282
  36.3 2.8 %collective-permute-done.5.km_last.refs_3_ = bf16[1024,128]{1,0:T(8,128)(2,1)S(1)} collective-permute-done((bf16[1024,128]{1,0:T(8,128)(2,1)S(1)}, bf16[1024,128]{1,0:T(8,128)(2,1)S(1)}, u32[]{:S(2)}, u32[]{:S(2)}) %collective-permute-start.5) | collective-permute-done | bytes 262176 | tf_op jit(solution)/shard_map/ppermute | solution.py:338
  39.1 1.1 %shard_map.81 = (f32[128,384]{1,0:T(8,128)S(1)}, f32[128,384]{1,0:T(8,128)S(1)}, f32[3,384]{1,0:T(4,128)S(1)}) custom-call(s32[4,4]{1,0:T(4,128)S(1)} %maximum_convert_fusion.cols, bf16[1024,128]{1,0:T(8,128)(2,1)S(1)} %collective-permute-done.5.km_last.refs_3_, bf16[512,768]{1,0:T(8,128)(2,1)S(1)} %get-tuple-element.19.placed, ...), custom_call_target="tpu_custom_call" | custom-call | flops 100663296 | bytes 4000000 | tf_op jit(solution)/shard_map/pallas_call | solution.py:282
  40.2 0.1 collective-permute-start.6
  40.3 1.2 %collective-permute-done.6 = f32[3,384]{1,0:T(4,128)S(1)} collective-permute-done((f32[3,384]{1,0:T(4,128)S(1)}, f32[3,384]{1,0:T(4,128)S(1)}, u32[]{:S(2)}, u32[]{:S(2)}) %collective-permute-start.6) | collective-permute-done | bytes 4640 | tf_op jit(solution)/shard_map/ppermute | solution.py:308
  41.5 2.6 %collective-permute-start.9 = (f32[3,384]{1,0:T(4,128)S(1)}, f32[3,384]{1,0:T(4,128)S(1)}, u32[]{:S(2)}, u32[]{:S(2)}) collective-permute-start(f32[3,384]{1,0:T(4,128)S(1)} %pad_maximum_fusion.1), channel_id=1, source_target_pairs={{0,6},{1,7},{2,4},{3,5},{4,2},{5,3},{6,0},{7,1},{8,14},{9,15},{10,... | collective-permute-start | bytes 13832 | tf_op jit(solution)/shard_map/ppermute | solution.py:311
  44.1 0.5 collective-permute-start.8
  44.6 0.5 collective-permute-start.7
  45.1 0.0 copy-done
  45.1 1.0 %shard_map.80.refs_4_ = f32[512,768]{1,0:T(8,128)S(1)} custom-call(bf16[512,768]{1,0:T(8,128)(2,1)S(1)} %get-tuple-element.19.placed, bf16[2,1152,768]{2,1,0:T(8,128)(2,1)S(1)} %copy-done), custom_call_target="tpu_custom_call" | custom-call | flops 603979776 | bytes 4000000 | tf_op jit(solution)/shard_map/pallas_call | solution.py:282
  46.0 0.1 collective-permute-done.9
  46.1 1.6 %collective-permute-done.8 = f32[3,384]{1,0:T(4,128)S(1)} collective-permute-done((f32[3,384]{1,0:T(4,128)S(1)}, f32[3,384]{1,0:T(4,128)S(1)}, u32[]{:S(2)}, u32[]{:S(2)}) %collective-permute-start.8) | collective-permute-done | bytes 4640 | tf_op jit(solution)/shard_map/ppermute | solution.py:311
  47.7 0.5 collective-permute-done.7
  48.3 2.4 %shard_map.82 = (bf16[512,768]{1,0:T(8,128)(2,1)S(1)}, f32[512,384]{1,0:T(8,128)S(1)}, f32[512,384]{1,0:T(8,128)S(1)}, f32[3,384]{1,0:T(4,128)S(1)}) custom-call(s32[4,4]{1,0:T(4,128)S(1)} %maximum_convert_fusion.cols, bf16[1024,128]{1,0:T(8,128)(2,1)S(1)} %pad_maximum_fusion.refs_4_.refs_0_, bf16[1024,128]{1,0:T(8,128)(2,1)S(1)} %collective-permute-done.3.refs_1_.refs_5_, ...), custom_call_target="tpu_custom_call" | custom-call | flops 704643072 | bytes 4000000 | tf_op jit(solution)/shard_map/pallas_call | solution.py:282
  50.7 0.1 collective-permute-start.10
  50.8 1.2 %collective-permute-done.10 = f32[3,384]{1,0:T(4,128)S(1)} collective-permute-done((f32[3,384]{1,0:T(4,128)S(1)}, f32[3,384]{1,0:T(4,128)S(1)}, u32[]{:S(2)}, u32[]{:S(2)}) %collective-permute-start.10) | collective-permute-done | bytes 4640 | tf_op jit(solution)/shard_map/ppermute | solution.py:308
  52.0 1.5 %collective-permute-start.13 = (f32[3,384]{1,0:T(4,128)S(1)}, f32[3,384]{1,0:T(4,128)S(1)}, u32[]{:S(2)}, u32[]{:S(2)}) collective-permute-start(f32[3,384]{1,0:T(4,128)S(1)} %pad_maximum_fusion.3), channel_id=1, source_target_pairs={{0,6},{1,7},{2,4},{3,5},{4,2},{5,3},{6,0},{7,1},{8,14},{9,15},{10,... | collective-permute-start | bytes 13832 | tf_op jit(solution)/shard_map/ppermute | solution.py:311
  53.5 0.5 collective-permute-start.12
  54.0 1.5 %collective-permute-start.11 = (f32[3,384]{1,0:T(4,128)S(1)}, f32[3,384]{1,0:T(4,128)S(1)}, u32[]{:S(2)}, u32[]{:S(2)}) collective-permute-start(f32[3,384]{1,0:T(4,128)S(1)} %pad_maximum_fusion.3), channel_id=1, source_target_pairs={{0,2},{1,3},{2,0},{3,1},{4,6},{5,7},{6,4},{7,5},{8,10},{9,11},{10,... | collective-permute-start | bytes 13832 | tf_op jit(solution)/shard_map/ppermute | solution.py:311
  55.5 1.0 %collective-permute-done.13 = f32[3,384]{1,0:T(4,128)S(1)} collective-permute-done((f32[3,384]{1,0:T(4,128)S(1)}, f32[3,384]{1,0:T(4,128)S(1)}, u32[]{:S(2)}, u32[]{:S(2)}) %collective-permute-start.13) | collective-permute-done | bytes 4640 | tf_op jit(solution)/shard_map/ppermute | solution.py:311
  56.6 0.6 collective-permute-done.12
  57.2 0.5 collective-permute-done.11
  57.7 2.8 %shard_map.83 = (bf16[4,648,128]{2,1,0:T(8,128)(2,1)S(1)}, bf16[512,1152]{1,0:T(8,128)(2,1)S(1)}, bf16[1152,512]{1,0:T(8,128)(2,1)S(1)}, bf16[512,576]{1,0:T(8,128)(2,1)S(1)}) custom-call(s32[4,4]{1,0:T(4,128)S(1)} %maximum_convert_fusion.cols, bf16[1024,128]{1,0:T(8,128)(2,1)S(1)} %pad_maximum_fusion.refs_4_.refs_0_, ...), custom_call_target="tpu_custom_call" | custom-call | flops 339738624 | bytes 4000000 | tf_op jit(solution)/shard_map/pallas_call | solution.py:282
  60.5 0.1 collective-permute-start.14
  60.6 0.7 shard_map.85
  61.3 1.4 %collective-permute-done.14 = bf16[4,648,128]{2,1,0:T(8,128)(2,1)S(1)} collective-permute-done((bf16[4,648,128]{2,1,0:T(8,128)(2,1)S(1)}, bf16[4,648,128]{2,1,0:T(8,128)(2,1)S(1)}, u32[]{:S(2)}, u32[]{:S(2)}) %collective-permute-start.14) | collective-permute-done | bytes 663584 | tf_op jit(solution)/shard_map/ppermute | solution.py:448
  62.7 0.2 add_convert_fusion
  62.9 2.6 %collective-permute-start.17 = (bf16[648,128]{1,0:T(8,128)(2,1)S(1)}, bf16[648,128]{1,0:T(8,128)(2,1)S(1)}, u32[]{:S(2)}, u32[]{:S(2)}) collective-permute-start(bf16[648,128]{1,0:T(8,128)(2,1)S(1)} %get-tuple-element.43), channel_id=1, source_target_pairs={{0,6},{1,7},{2,4},{3,5},{4,2},{5,3},{6,0},{7,1},{8,14},{9,15},{10,... | collective-permute-start | bytes 497672 | tf_op jit(solution)/shard_map/ppermute | solution.py:459
  65.5 0.5 collective-permute-start.16
  66.0 0.5 collective-permute-start.15
  66.5 0.7 shard_map.84
  67.2 0.6 reduce
  67.8 3.2 %collective-permute-done.17.refs_3_ = bf16[648,128]{1,0:T(8,128)(2,1)S(1)} collective-permute-done((bf16[648,128]{1,0:T(8,128)(2,1)S(1)}, bf16[648,128]{1,0:T(8,128)(2,1)S(1)}, u32[]{:S(2)}, u32[]{:S(2)}) %collective-permute-start.17) | collective-permute-done | bytes 165920 | tf_op jit(solution)/shard_map/ppermute | solution.py:459
  71.0 2.8 %collective-permute-done.16.refs_2_ = bf16[648,128]{1,0:T(8,128)(2,1)S(1)} collective-permute-done((bf16[648,128]{1,0:T(8,128)(2,1)S(1)}, bf16[648,128]{1,0:T(8,128)(2,1)S(1)}, u32[]{:S(2)}, u32[]{:S(2)}) %collective-permute-start.16) | collective-permute-done | bytes 165920 | tf_op jit(solution)/shard_map/ppermute | solution.py:459
  73.7 0.1 collective-permute-done.15.refs_1_
  73.9 1.2 %shard_map.86 = f32[144,2,288]{2,1,0:T(2,128)} custom-call(bf16[648,128]{1,0:T(8,128)(2,1)S(1)} %get-tuple-element.46.refs_0_, bf16[648,128]{1,0:T(8,128)(2,1)S(1)} %collective-permute-done.15.refs_1_, bf16[648,128]{1,0:T(8,128)(2,1)S(1)} %collective-permute-done.16.refs_2_, bf16[648,128]{1,0:T(8,128)(2,1)S(1)} %collective-permute-done.17.refs_3_), custom_call_target="tpu_custom_call" | custom-call | bytes 4000000 | tf_op jit(solution)/shard_map/pallas_call | solution.py:282
  (17 shorter events, 0.3 us)
Async XLA Ops:
  0.6 9.1 %copy-start.2 = (bf16[1,1,4,128,128]{4,3,2,1,0:T(8,128)(2,1)S(1)}, bf16[1,1,4,128,128]{4,3,2,1,0:T(8,128)(2,1)}, u32[]{:S(2)}) copy-start(bf16[1,1,4,128,128]{4,3,2,1,0:T(8,128)(2,1)} %param.8) | copy-start | bytes 393220
  0.6 9.1 %copy-start.3 = (bf16[1,1,4,128,128]{4,3,2,1,0:T(8,128)(2,1)S(1)}, bf16[1,1,4,128,128]{4,3,2,1,0:T(8,128)(2,1)}, u32[]{:S(2)}) copy-start(bf16[1,1,4,128,128]{4,3,2,1,0:T(8,128)(2,1)} %param.7) | copy-start | bytes 393220
  4.1 27.8 %copy-start.1 = (bf16[784,128]{1,0:T(8,128)(2,1)S(1)}, bf16[784,128]{1,0:T(8,128)(2,1)}, u32[]{:S(2)}) copy-start(bf16[784,128]{1,0:T(8,128)(2,1)} %shard_map.76.refs_0_) | copy-start | bytes 602116
  4.1 15.4 %collective-permute-start.1 = (bf16[784,128]{1,0:T(8,128)(2,1)}, bf16[784,128]{1,0:T(8,128)(2,1)S(1)}, u32[]{:S(2)}, u32[]{:S(2)}) collective-permute-start(bf16[784,128]{1,0:T(8,128)(2,1)} %shard_map.76.refs_0_), channel_id=1, source_target_pairs={{0,16},{8,24},{16,0},{24,8},{1,17},{9,25},{17,1},{25,9},{2,18},{10... | collective-permute-start | bytes 602120 | tf_op jit(solution)/shard_map/ppermute | solution.py:338
  8.2 12.4 %collective-permute-start = (bf16[784,128]{1,0:T(8,128)(2,1)}, bf16[784,128]{1,0:T(8,128)(2,1)S(1)}, u32[]{:S(2)}, u32[]{:S(2)}) collective-permute-start(bf16[784,128]{1,0:T(8,128)(2,1)} %shard_map.76.refs_0_), channel_id=1, source_target_pairs={{0,8},{8,0},{16,24},{24,16},{1,9},{9,1},{17,25},{25,17},{2,10},{10... | collective-permute-start | bytes 602120 | tf_op jit(solution)/shard_map/ppermute | solution.py:338
  9.8 19.3 %collective-permute-start.4 = (bf16[1024,128]{1,0:T(8,128)(2,1)S(1)}, bf16[1024,128]{1,0:T(8,128)(2,1)S(1)}, u32[]{:S(2)}, u32[]{:S(2)}) collective-permute-start(bf16[1024,128]{1,0:T(8,128)(2,1)S(1)} %pad_maximum_fusion.refs_4_.refs_0_), channel_id=1, source_target_pairs={{0,16},{8,24},{16,0},{24,8},{1,17},{9,25},{17,1},{25,9},{2,18},{10... | collective-permute-start | bytes 786440 | tf_op jit(solution)/shard_map/ppermute | solution.py:338
  10.2 20.5 %collective-permute-start.3 = (bf16[1024,128]{1,0:T(8,128)(2,1)S(1)}, bf16[1024,128]{1,0:T(8,128)(2,1)S(1)}, u32[]{:S(2)}, u32[]{:S(2)}) collective-permute-start(bf16[1024,128]{1,0:T(8,128)(2,1)S(1)} %pad_maximum_fusion.refs_4_.refs_0_), channel_id=1, source_target_pairs={{0,8},{8,0},{16,24},{24,16},{1,9},{9,1},{17,25},{25,17},{2,10},{10... | collective-permute-start | bytes 786440 | tf_op jit(solution)/shard_map/ppermute | solution.py:338
  20.6 14.4 %collective-permute-start.2 = (bf16[784,128]{1,0:T(8,128)(2,1)S(1)}, bf16[784,128]{1,0:T(8,128)(2,1)S(1)}, u32[]{:S(2)}, u32[]{:S(2)}) collective-permute-start(bf16[784,128]{1,0:T(8,128)(2,1)S(1)} %shard_map.77.refs_2_), channel_id=1, source_target_pairs={{0,8},{8,0},{16,24},{24,16},{1,9},{9,1},{17,25},{25,17},{2,10},{10... | collective-permute-start | bytes 602120 | tf_op jit(solution)/shard_map/ppermute | solution.py:338
  30.7 8.4 %collective-permute-start.5 = (bf16[1024,128]{1,0:T(8,128)(2,1)S(1)}, bf16[1024,128]{1,0:T(8,128)(2,1)S(1)}, u32[]{:S(2)}, u32[]{:S(2)}) collective-permute-start(bf16[1024,128]{1,0:T(8,128)(2,1)S(1)} %shard_map.78.refs_6_.refs_2_), channel_id=1, source_target_pairs={{0,8},{8,0},{16,24},{24,16},{1,9},{9,1},{17,25},{25,17},{2,10},{10... | collective-permute-start | bytes 786440 | tf_op jit(solution)/shard_map/ppermute | solution.py:338
  35.0 10.0 %copy-start = (bf16[2,1152,768]{2,1,0:T(8,128)(2,1)S(1)}, bf16[2,1152,768]{2,1,0:T(8,128)(2,1)}, u32[]{:S(2)}) copy-start(bf16[2,1152,768]{2,1,0:T(8,128)(2,1)} %refs_10_.1) | copy-start | bytes 10616836
  40.2 1.2 %collective-permute-start.6 = (f32[3,384]{1,0:T(4,128)S(1)}, f32[3,384]{1,0:T(4,128)S(1)}, u32[]{:S(2)}, u32[]{:S(2)}) collective-permute-start(f32[3,384]{1,0:T(4,128)S(1)} %get-tuple-element.24), channel_id=1, source_target_pairs={{0,1},{1,0},{2,3},{3,2},{4,5},{5,4},{6,7},{7,6},{8,9},{9,8},{10,11... | collective-permute-start | bytes 13832 | tf_op jit(solution)/shard_map/ppermute | solution.py:308
  41.5 4.6 %collective-permute-start.9 = (f32[3,384]{1,0:T(4,128)S(1)}, f32[3,384]{1,0:T(4,128)S(1)}, u32[]{:S(2)}, u32[]{:S(2)}) collective-permute-start(f32[3,384]{1,0:T(4,128)S(1)} %pad_maximum_fusion.1), channel_id=1, source_target_pairs={{0,6},{1,7},{2,4},{3,5},{4,2},{5,3},{6,0},{7,1},{8,14},{9,15},{10,... | collective-permute-start | bytes 13832 | tf_op jit(solution)/shard_map/ppermute | solution.py:311
  44.1 3.6 %collective-permute-start.8 = (f32[3,384]{1,0:T(4,128)S(1)}, f32[3,384]{1,0:T(4,128)S(1)}, u32[]{:S(2)}, u32[]{:S(2)}) collective-permute-start(f32[3,384]{1,0:T(4,128)S(1)} %pad_maximum_fusion.1), channel_id=1, source_target_pairs={{0,4},{1,5},{2,6},{3,7},{4,0},{5,1},{6,2},{7,3},{8,12},{9,13},{10,... | collective-permute-start | bytes 13832 | tf_op jit(solution)/shard_map/ppermute | solution.py:311
  44.6 3.6 %collective-permute-start.7 = (f32[3,384]{1,0:T(4,128)S(1)}, f32[3,384]{1,0:T(4,128)S(1)}, u32[]{:S(2)}, u32[]{:S(2)}) collective-permute-start(f32[3,384]{1,0:T(4,128)S(1)} %pad_maximum_fusion.1), channel_id=1, source_target_pairs={{0,2},{1,3},{2,0},{3,1},{4,6},{5,7},{6,4},{7,5},{8,10},{9,11},{10,... | collective-permute-start | bytes 13832 | tf_op jit(solution)/shard_map/ppermute | solution.py:311
  50.7 1.2 %collective-permute-start.10 = (f32[3,384]{1,0:T(4,128)S(1)}, f32[3,384]{1,0:T(4,128)S(1)}, u32[]{:S(2)}, u32[]{:S(2)}) collective-permute-start(f32[3,384]{1,0:T(4,128)S(1)} %get-tuple-element.25), channel_id=1, source_target_pairs={{0,1},{1,0},{2,3},{3,2},{4,5},{5,4},{6,7},{7,6},{8,9},{9,8},{10,11... | collective-permute-start | bytes 13832 | tf_op jit(solution)/shard_map/ppermute | solution.py:308
  52.0 4.6 %collective-permute-start.13 = (f32[3,384]{1,0:T(4,128)S(1)}, f32[3,384]{1,0:T(4,128)S(1)}, u32[]{:S(2)}, u32[]{:S(2)}) collective-permute-start(f32[3,384]{1,0:T(4,128)S(1)} %pad_maximum_fusion.3), channel_id=1, source_target_pairs={{0,6},{1,7},{2,4},{3,5},{4,2},{5,3},{6,0},{7,1},{8,14},{9,15},{10,... | collective-permute-start | bytes 13832 | tf_op jit(solution)/shard_map/ppermute | solution.py:311
  53.5 3.6 %collective-permute-start.12 = (f32[3,384]{1,0:T(4,128)S(1)}, f32[3,384]{1,0:T(4,128)S(1)}, u32[]{:S(2)}, u32[]{:S(2)}) collective-permute-start(f32[3,384]{1,0:T(4,128)S(1)} %pad_maximum_fusion.3), channel_id=1, source_target_pairs={{0,4},{1,5},{2,6},{3,7},{4,0},{5,1},{6,2},{7,3},{8,12},{9,13},{10,... | collective-permute-start | bytes 13832 | tf_op jit(solution)/shard_map/ppermute | solution.py:311
  54.0 3.6 %collective-permute-start.11 = (f32[3,384]{1,0:T(4,128)S(1)}, f32[3,384]{1,0:T(4,128)S(1)}, u32[]{:S(2)}, u32[]{:S(2)}) collective-permute-start(f32[3,384]{1,0:T(4,128)S(1)} %pad_maximum_fusion.3), channel_id=1, source_target_pairs={{0,2},{1,3},{2,0},{3,1},{4,6},{5,7},{6,4},{7,5},{8,10},{9,11},{10,... | collective-permute-start | bytes 13832 | tf_op jit(solution)/shard_map/ppermute | solution.py:311
  60.5 2.2 %collective-permute-start.14 = (bf16[4,648,128]{2,1,0:T(8,128)(2,1)S(1)}, bf16[4,648,128]{2,1,0:T(8,128)(2,1)S(1)}, u32[]{:S(2)}, u32[]{:S(2)}) collective-permute-start(bf16[4,648,128]{2,1,0:T(8,128)(2,1)S(1)} %get-tuple-element.34), channel_id=1, source_target_pairs={{0,1},{1,0},{2,3},{3,2},{4,5},{5,4},{6,7},{7,6},{8,9},{9,8},{10,11... | collective-permute-start | bytes 1990664 | tf_op jit(solution)/shard_map/ppermute | solution.py:448
  62.9 8.1 %collective-permute-start.17 = (bf16[648,128]{1,0:T(8,128)(2,1)S(1)}, bf16[648,128]{1,0:T(8,128)(2,1)S(1)}, u32[]{:S(2)}, u32[]{:S(2)}) collective-permute-start(bf16[648,128]{1,0:T(8,128)(2,1)S(1)} %get-tuple-element.43), channel_id=1, source_target_pairs={{0,6},{1,7},{2,4},{3,5},{4,2},{5,3},{6,0},{7,1},{8,14},{9,15},{10,... | collective-permute-start | bytes 497672 | tf_op jit(solution)/shard_map/ppermute | solution.py:459
  65.5 8.2 %collective-permute-start.16 = (bf16[648,128]{1,0:T(8,128)(2,1)S(1)}, bf16[648,128]{1,0:T(8,128)(2,1)S(1)}, u32[]{:S(2)}, u32[]{:S(2)}) collective-permute-start(bf16[648,128]{1,0:T(8,128)(2,1)S(1)} %get-tuple-element.44), channel_id=1, source_target_pairs={{0,4},{1,5},{2,6},{3,7},{4,0},{5,1},{6,2},{7,3},{8,12},{9,13},{10,... | collective-permute-start | bytes 497672 | tf_op jit(solution)/shard_map/ppermute | solution.py:459
  66.0 7.9 %collective-permute-start.15 = (bf16[648,128]{1,0:T(8,128)(2,1)S(1)}, bf16[648,128]{1,0:T(8,128)(2,1)S(1)}, u32[]{:S(2)}, u32[]{:S(2)}) collective-permute-start(bf16[648,128]{1,0:T(8,128)(2,1)S(1)} %get-tuple-element.45), channel_id=1, source_target_pairs={{0,2},{1,3},{2,0},{3,1},{4,6},{5,7},{6,4},{7,5},{8,10},{9,11},{10,... | collective-permute-start | bytes 497672 | tf_op jit(solution)/shard_map/ppermute | solution.py:459

commit v11 on v10

--- a/solution.py
+++ b/solution.py
@@ -82,26 +82,30 @@
     return pl.BlockSpec(memory_space=pltpu.HBM)
 
 
-def turn_kernel(chunks, cols, current_hbm, coeffs_hbm, out_ref, current, coeffs, sems):
+def turn_kernel(chunks, copies_each, cols_hbm, current_hbm, coeffs_hbm, out_ref, current, coeffs, cols, sems):
     depth = current.shape[1] // chunks
+    piece = depth // copies_each
     copies = [pltpu.make_async_copy(current_hbm, current, sems.at[0])]
-    for c in range(chunks):
-        part = pl.ds(c * depth, depth)
+    for c in range(chunks * copies_each):
+        part = pl.ds(c * piece, piece)
         copies.append(pltpu.make_async_copy(coeffs_hbm.at[0, part], coeffs.at[part], sems.at[c + 1]))
+    copies.append(pltpu.make_async_copy(cols_hbm, cols, sems.at[chunks * copies_each + 1]))
     for copy in copies:
         copy.start()
     rows, edge = current.shape[0], out_ref.shape[1]
+    copies[0].wait()
+    turned = None
+    for c in range(chunks):
+        for d in range(copies_each):
+            copies[c * copies_each + d + 1].wait()
+        part = slice(c * depth, (c + 1) * depth)
+        more = jnp.dot(current[:, part], coeffs[part, :], preferred_element_type=f32)
+        turned = more if turned is None else turned + more
+    copies[-1].wait()
     lane = lax.broadcasted_iota(jnp.int32, (16, edge), 1)
     tag = jnp.zeros((16, edge), jnp.int32)
     for s in range(cols.shape[1]):
         tag = jnp.where(lane == s, cols[0, s], tag)
-    copies[0].wait()
-    turned = None
-    for c in range(chunks):
-        copies[c + 1].wait()
-        part = slice(c * depth, (c + 1) * depth)
-        more = jnp.dot(current[:, part], coeffs[part, :], preferred_element_type=f32)
-        turned = more if turned is None else turned + more
     turned = turned.astype(bf16)
     blocks = turned.shape[1] // edge
     for b in range(blocks):
@@ -111,17 +115,18 @@
 
 def turn_first(cols, current, coeffs, modes):
     rows, columns = current.shape
-    chunks = 3
+    chunks, copies_each = 3, 2
     in_hbm = pl.BlockSpec(memory_space=pltpu.HBM)
     return pl.pallas_call(
-        functools.partial(turn_kernel, chunks),
+        functools.partial(turn_kernel, chunks, copies_each),
         out_shape=jax.ShapeDtypeStruct((2 * modes + 16, rows), bf16),
-        in_specs=[smem(), in_hbm, in_hbm],
+        in_specs=[in_hbm, in_hbm, in_hbm],
         out_specs=vmem(),
         scratch_shapes=[
             pltpu.VMEM((rows, columns), bf16),
             pltpu.VMEM((columns, 2 * modes), bf16),
-            pltpu.SemaphoreType.DMA((chunks + 1,)),
+            pltpu.SMEM(cols.shape, jnp.int32),
+            pltpu.SemaphoreType.DMA((chunks * copies_each + 2,)),
         ],
         compiler_params=pltpu.CompilerParams(vmem_limit_bytes=FIRST_VMEM_BYTES),
         cost_estimate=pl.CostEstimate(

time: 75.2 us -> 74.5 us (level)
  no operation moved by 1% of the time
where the time goes in v11:
time: 74.5 us; the launch traced here: 74.4 us
  waiting for transfers between devices  40.2 us (54%)
  starting transfers between devices  18.4 us (25%)
  Pallas kernels  13.9 us (19%)
  other arithmetic  1 us (1%)
  between operations  0.8 us (1%)
    ppermute x6, waiting for transfers between devices, send(): return lax.ppermute(x, 'blk', by_xor(nz, step))  26.2 us
    pallas_call x8, Pallas kernels, call(): pl.pallas_call(kernel, out_shape=out_shape, in_specs=[smem()] * n_smem +...  11.2 us
    ppermute x6, starting transfers between devices, send(): return lax.ppermute(x, 'blk', by_xor(nz, step))  7.49 us
    ppermute x6, starting transfers between devices, merge_over(): got = [lax.ppermute(stats, axis, by_xor(size, 2 * k)) for k in (1, 2, 3)]  7.11 us
    ppermute x3, waiting for transfers between devices, body(): lax.ppermute(mine[k], 'grp', by_xor(ng, 2 * k))  6.06 us
    ppermute x6, waiting for transfers between devices, merge_over(): got = [lax.ppermute(stats, axis, by_xor(size, 2 * k)) for k in (1, 2, 3)]  4.25 us
    ppermute x3, starting transfers between devices, body(): lax.ppermute(mine[k], 'grp', by_xor(ng, 2 * k))  3.55 us
    pallas_call x1, Pallas kernels, turn_first(): pl.pallas_call(functools.partial(turn_kernel, chunks, copies_each), out_s...  2.71 us
  transfers between devices with their start and end apart: 18, of which 18 were waited for; matrix products, arithmetic and copies ran while one was open for 1% of the time, Pallas kernels for 5%

profile of v11, /device:TPU:0, one launch (start us, length us, event | category | flops | bytes accessed | tf_op | source)
XLA Modules:
  0.0 74.4 jit_solution(5050453598160458658)
XLA Ops:
  0.6 0.0 copy-start.2
  0.6 0.0 copy-start.3
  0.7 2.7 %shard_map.76.refs_0_ = bf16[784,128]{1,0:T(8,128)(2,1)} custom-call(s32[1,4]{1,0:T(1,128)} %bitcast.16, bf16[128,1152]{1,0:T(8,128)(2,1)} %bitcast.13, bf16[2,1152,768]{2,1,0:T(8,128)(2,1)} %refs_10_.1), custom_call_target="tpu_custom_call" | custom-call | flops 226492416 | bytes 1769472 | tf_op jit(solution)/shard_map/pallas_call | solution.py:120
  3.4 0.0 copy-start.1
  3.4 4.1 %collective-permute-start.1 = (bf16[784,128]{1,0:T(8,128)(2,1)}, bf16[784,128]{1,0:T(8,128)(2,1)S(1)}, u32[]{:S(2)}, u32[]{:S(2)}) collective-permute-start(bf16[784,128]{1,0:T(8,128)(2,1)} %shard_map.76.refs_0_), channel_id=1, source_target_pairs={{0,16},{8,24},{16,0},{24,8},{1,17},{9,25},{17,1},{25,9},{2,18},{10... | collective-permute-start | bytes 602120 | tf_op jit(solution)/shard_map/ppermute | solution.py:343
  7.5 1.6 %collective-permute-start = (bf16[784,128]{1,0:T(8,128)(2,1)}, bf16[784,128]{1,0:T(8,128)(2,1)S(1)}, u32[]{:S(2)}, u32[]{:S(2)}) collective-permute-start(bf16[784,128]{1,0:T(8,128)(2,1)} %shard_map.76.refs_0_), channel_id=1, source_target_pairs={{0,8},{8,0},{16,24},{24,16},{1,9},{9,1},{17,25},{25,17},{2,10},{10... | collective-permute-start | bytes 602120 | tf_op jit(solution)/shard_map/ppermute | solution.py:343
  9.1 0.0 copy-done.2
  9.1 0.0 copy-done.3
  9.1 0.4 collective-permute-start.4
  9.5 0.2 collective-permute-start.3
  9.7 9.0 %collective-permute-done.1.refs_0_ = bf16[784,128]{1,0:T(8,128)(2,1)S(1)} collective-permute-done((bf16[784,128]{1,0:T(8,128)(2,1)}, bf16[784,128]{1,0:T(8,128)(2,1)S(1)}, u32[]{:S(2)}, u32[]{:S(2)}) %collective-permute-start.1) | collective-permute-done | bytes 200736 | tf_op jit(solution)/shard_map/ppermute | solution.py:343
  18.7 1.2 %collective-permute-done.refs_1_ = bf16[784,128]{1,0:T(8,128)(2,1)S(1)} collective-permute-done((bf16[784,128]{1,0:T(8,128)(2,1)}, bf16[784,128]{1,0:T(8,128)(2,1)S(1)}, u32[]{:S(2)}, u32[]{:S(2)}) %collective-permute-start) | collective-permute-done | bytes 200736 | tf_op jit(solution)/shard_map/ppermute | solution.py:343
  19.9 0.0 collective-permute-start.2
  19.9 8.5 %collective-permute-done.4.refs_0_ = bf16[1024,128]{1,0:T(8,128)(2,1)S(1)} collective-permute-done((bf16[1024,128]{1,0:T(8,128)(2,1)S(1)}, bf16[1024,128]{1,0:T(8,128)(2,1)S(1)}, u32[]{:S(2)}, u32[]{:S(2)}) %collective-permute-start.4) | collective-permute-done | bytes 262176 | tf_op jit(solution)/shard_map/ppermute | solution.py:343
  28.4 1.6 %collective-permute-done.3.refs_1_.refs_5_ = bf16[1024,128]{1,0:T(8,128)(2,1)S(1)} collective-permute-done((bf16[1024,128]{1,0:T(8,128)(2,1)S(1)}, bf16[1024,128]{1,0:T(8,128)(2,1)S(1)}, u32[]{:S(2)}, u32[]{:S(2)}) %collective-permute-start.3) | collective-permute-done | bytes 262176 | tf_op jit(solution)/shard_map/ppermute | solution.py:343
  30.0 1.2 %collective-permute-start.5 = (bf16[1024,128]{1,0:T(8,128)(2,1)S(1)}, bf16[1024,128]{1,0:T(8,128)(2,1)S(1)}, u32[]{:S(2)}, u32[]{:S(2)}) collective-permute-start(bf16[1024,128]{1,0:T(8,128)(2,1)S(1)} %shard_map.78.refs_6_.refs_2_), channel_id=1, source_target_pairs={{0,8},{8,0},{16,24},{24,16},{1,9},{9,1},{17,25},{25,17},{2,10},{10... | collective-permute-start | bytes 786440 | tf_op jit(solution)/shard_map/ppermute | solution.py:343
  31.2 0.0 copy-done.1
  31.2 3.1 %collective-permute-done.2.refs_3_ = bf16[784,128]{1,0:T(8,128)(2,1)S(1)} collective-permute-done((bf16[784,128]{1,0:T(8,128)(2,1)S(1)}, bf16[784,128]{1,0:T(8,128)(2,1)S(1)}, u32[]{:S(2)}, u32[]{:S(2)}) %collective-permute-start.2) | collective-permute-done | bytes 200736 | tf_op jit(solution)/shard_map/ppermute | solution.py:343
  34.3 0.0 copy-start
  34.3 1.3 %shard_map.79 = (bf16[512,768]{1,0:T(8,128)(2,1)S(1)}, f32[3,128,384]{2,1,0:T(8,128)S(1)}, f32[3,128,384]{2,1,0:T(8,128)S(1)}) custom-call(s32[4,4]{1,0:T(4,128)S(1)} %maximum_convert_fusion.cols, bf16[784,128]{1,0:T(8,128)(2,1)S(1)} %copy-done.1, bf16[784,128]{1,0:T(8,128)(2,1)S(1)} %collective-permute-done.refs_1_, ...), custom_call_target="tpu_custom_call" | custom-call | flops 301989888 | bytes 4000000 | tf_op jit(solution)/shard_map/pallas_call | solution.py:287
  35.6 2.9 %collective-permute-done.5.km_last.refs_3_ = bf16[1024,128]{1,0:T(8,128)(2,1)S(1)} collective-permute-done((bf16[1024,128]{1,0:T(8,128)(2,1)S(1)}, bf16[1024,128]{1,0:T(8,128)(2,1)S(1)}, u32[]{:S(2)}, u32[]{:S(2)}) %collective-permute-start.5) | collective-permute-done | bytes 262176 | tf_op jit(solution)/shard_map/ppermute | solution.py:343
  38.4 1.1 %shard_map.81 = (f32[128,384]{1,0:T(8,128)S(1)}, f32[128,384]{1,0:T(8,128)S(1)}, f32[3,384]{1,0:T(4,128)S(1)}) custom-call(s32[4,4]{1,0:T(4,128)S(1)} %maximum_convert_fusion.cols, bf16[1024,128]{1,0:T(8,128)(2,1)S(1)} %collective-permute-done.5.km_last.refs_3_, bf16[512,768]{1,0:T(8,128)(2,1)S(1)} %get-tuple-element.19.placed, ...), custom_call_target="tpu_custom_call" | custom-call | flops 100663296 | bytes 4000000 | tf_op jit(solution)/shard_map/pallas_call | solution.py:287
  39.5 0.1 collective-permute-start.6
  39.6 1.2 %collective-permute-done.6 = f32[3,384]{1,0:T(4,128)S(1)} collective-permute-done((f32[3,384]{1,0:T(4,128)S(1)}, f32[3,384]{1,0:T(4,128)S(1)}, u32[]{:S(2)}, u32[]{:S(2)}) %collective-permute-start.6) | collective-permute-done | bytes 4640 | tf_op jit(solution)/shard_map/ppermute | solution.py:313
  40.8 2.6 %collective-permute-start.9 = (f32[3,384]{1,0:T(4,128)S(1)}, f32[3,384]{1,0:T(4,128)S(1)}, u32[]{:S(2)}, u32[]{:S(2)}) collective-permute-start(f32[3,384]{1,0:T(4,128)S(1)} %pad_maximum_fusion.1), channel_id=1, source_target_pairs={{0,6},{1,7},{2,4},{3,5},{4,2},{5,3},{6,0},{7,1},{8,14},{9,15},{10,... | collective-permute-start | bytes 13832 | tf_op jit(solution)/shard_map/ppermute | solution.py:316
  43.4 0.5 collective-permute-start.8
  43.9 0.5 collective-permute-start.7
  44.4 0.0 copy-done
  44.4 1.0 %shard_map.80.refs_4_ = f32[512,768]{1,0:T(8,128)S(1)} custom-call(bf16[512,768]{1,0:T(8,128)(2,1)S(1)} %get-tuple-element.19.placed, bf16[2,1152,768]{2,1,0:T(8,128)(2,1)S(1)} %copy-done), custom_call_target="tpu_custom_call" | custom-call | flops 603979776 | bytes 4000000 | tf_op jit(solution)/shard_map/pallas_call | solution.py:287
  45.3 0.1 collective-permute-done.9
  45.4 1.6 %collective-permute-done.8 = f32[3,384]{1,0:T(4,128)S(1)} collective-permute-done((f32[3,384]{1,0:T(4,128)S(1)}, f32[3,384]{1,0:T(4,128)S(1)}, u32[]{:S(2)}, u32[]{:S(2)}) %collective-permute-start.8) | collective-permute-done | bytes 4640 | tf_op jit(solution)/shard_map/ppermute | solution.py:316
  47.0 0.5 collective-permute-done.7
  47.6 2.4 %shard_map.82 = (bf16[512,768]{1,0:T(8,128)(2,1)S(1)}, f32[512,384]{1,0:T(8,128)S(1)}, f32[512,384]{1,0:T(8,128)S(1)}, f32[3,384]{1,0:T(4,128)S(1)}) custom-call(s32[4,4]{1,0:T(4,128)S(1)} %maximum_convert_fusion.cols, bf16[1024,128]{1,0:T(8,128)(2,1)S(1)} %pad_maximum_fusion.refs_4_.refs_0_, bf16[1024,128]{1,0:T(8,128)(2,1)S(1)} %collective-permute-done.3.refs_1_.refs_5_, ...), custom_call_target="tpu_custom_call" | custom-call | flops 704643072 | bytes 4000000 | tf_op jit(solution)/shard_map/pallas_call | solution.py:287
  50.0 0.1 collective-permute-start.10
  50.1 1.2 %collective-permute-done.10 = f32[3,384]{1,0:T(4,128)S(1)} collective-permute-done((f32[3,384]{1,0:T(4,128)S(1)}, f32[3,384]{1,0:T(4,128)S(1)}, u32[]{:S(2)}, u32[]{:S(2)}) %collective-permute-start.10) | collective-permute-done | bytes 4640 | tf_op jit(solution)/shard_map/ppermute | solution.py:313
  51.3 1.6 %collective-permute-start.13 = (f32[3,384]{1,0:T(4,128)S(1)}, f32[3,384]{1,0:T(4,128)S(1)}, u32[]{:S(2)}, u32[]{:S(2)}) collective-permute-start(f32[3,384]{1,0:T(4,128)S(1)} %pad_maximum_fusion.3), channel_id=1, source_target_pairs={{0,6},{1,7},{2,4},{3,5},{4,2},{5,3},{6,0},{7,1},{8,14},{9,15},{10,... | collective-permute-start | bytes 13832 | tf_op jit(solution)/shard_map/ppermute | solution.py:316
  52.8 0.5 collective-permute-start.12
  53.3 1.5 %collective-permute-start.11 = (f32[3,384]{1,0:T(4,128)S(1)}, f32[3,384]{1,0:T(4,128)S(1)}, u32[]{:S(2)}, u32[]{:S(2)}) collective-permute-start(f32[3,384]{1,0:T(4,128)S(1)} %pad_maximum_fusion.3), channel_id=1, source_target_pairs={{0,2},{1,3},{2,0},{3,1},{4,6},{5,7},{6,4},{7,5},{8,10},{9,11},{10,... | collective-permute-start | bytes 13832 | tf_op jit(solution)/shard_map/ppermute | solution.py:316
  54.8 1.0 %collective-permute-done.13 = f32[3,384]{1,0:T(4,128)S(1)} collective-permute-done((f32[3,384]{1,0:T(4,128)S(1)}, f32[3,384]{1,0:T(4,128)S(1)}, u32[]{:S(2)}, u32[]{:S(2)}) %collective-permute-start.13) | collective-permute-done | bytes 4640 | tf_op jit(solution)/shard_map/ppermute | solution.py:316
  55.9 0.6 collective-permute-done.12
  56.5 0.5 collective-permute-done.11
  57.0 2.8 %shard_map.83 = (bf16[4,648,128]{2,1,0:T(8,128)(2,1)S(1)}, bf16[512,1152]{1,0:T(8,128)(2,1)S(1)}, bf16[1152,512]{1,0:T(8,128)(2,1)S(1)}, bf16[512,576]{1,0:T(8,128)(2,1)S(1)}) custom-call(s32[4,4]{1,0:T(4,128)S(1)} %maximum_convert_fusion.cols, bf16[1024,128]{1,0:T(8,128)(2,1)S(1)} %pad_maximum_fusion.refs_4_.refs_0_, ...), custom_call_target="tpu_custom_call" | custom-call | flops 339738624 | bytes 4000000 | tf_op jit(solution)/shard_map/pallas_call | solution.py:287
  59.8 0.1 collective-permute-start.14
  59.9 0.7 shard_map.85
  60.6 1.4 %collective-permute-done.14 = bf16[4,648,128]{2,1,0:T(8,128)(2,1)S(1)} collective-permute-done((bf16[4,648,128]{2,1,0:T(8,128)(2,1)S(1)}, bf16[4,648,128]{2,1,0:T(8,128)(2,1)S(1)}, u32[]{:S(2)}, u32[]{:S(2)}) %collective-permute-start.14) | collective-permute-done | bytes 663584 | tf_op jit(solution)/shard_map/ppermute | solution.py:453
  62.0 0.2 add_convert_fusion
  62.2 2.6 %collective-permute-start.17 = (bf16[648,128]{1,0:T(8,128)(2,1)S(1)}, bf16[648,128]{1,0:T(8,128)(2,1)S(1)}, u32[]{:S(2)}, u32[]{:S(2)}) collective-permute-start(bf16[648,128]{1,0:T(8,128)(2,1)S(1)} %get-tuple-element.43), channel_id=1, source_target_pairs={{0,6},{1,7},{2,4},{3,5},{4,2},{5,3},{6,0},{7,1},{8,14},{9,15},{10,... | collective-permute-start | bytes 497672 | tf_op jit(solution)/shard_map/ppermute | solution.py:464
  64.8 0.5 collective-permute-start.16
  65.3 0.5 collective-permute-start.15
  65.8 0.7 shard_map.84
  66.5 0.6 reduce
  67.1 3.2 %collective-permute-done.17.refs_3_ = bf16[648,128]{1,0:T(8,128)(2,1)S(1)} collective-permute-done((bf16[648,128]{1,0:T(8,128)(2,1)S(1)}, bf16[648,128]{1,0:T(8,128)(2,1)S(1)}, u32[]{:S(2)}, u32[]{:S(2)}) %collective-permute-start.17) | collective-permute-done | bytes 165920 | tf_op jit(solution)/shard_map/ppermute | solution.py:464
  70.2 2.8 %collective-permute-done.16.refs_2_ = bf16[648,128]{1,0:T(8,128)(2,1)S(1)} collective-permute-done((bf16[648,128]{1,0:T(8,128)(2,1)S(1)}, bf16[648,128]{1,0:T(8,128)(2,1)S(1)}, u32[]{:S(2)}, u32[]{:S(2)}) %collective-permute-start.16) | collective-permute-done | bytes 165920 | tf_op jit(solution)/shard_map/ppermute | solution.py:464
  73.0 0.1 collective-permute-done.15.refs_1_
  73.1 1.2 %shard_map.86 = f32[144,2,288]{2,1,0:T(2,128)} custom-call(bf16[648,128]{1,0:T(8,128)(2,1)S(1)} %get-tuple-element.46.refs_0_, bf16[648,128]{1,0:T(8,128)(2,1)S(1)} %collective-permute-done.15.refs_1_, bf16[648,128]{1,0:T(8,128)(2,1)S(1)} %collective-permute-done.16.refs_2_, bf16[648,128]{1,0:T(8,128)(2,1)S(1)} %collective-permute-done.17.refs_3_), custom_call_target="tpu_custom_call" | custom-call | bytes 4000000 | tf_op jit(solution)/shard_map/pallas_call | solution.py:287
  (17 shorter events, 0.3 us)
Async XLA Ops:
  0.6 8.4 %copy-start.2 = (bf16[1,1,4,128,128]{4,3,2,1,0:T(8,128)(2,1)S(1)}, bf16[1,1,4,128,128]{4,3,2,1,0:T(8,128)(2,1)}, u32[]{:S(2)}) copy-start(bf16[1,1,4,128,128]{4,3,2,1,0:T(8,128)(2,1)} %param.8) | copy-start | bytes 393220
  0.6 8.4 %copy-start.3 = (bf16[1,1,4,128,128]{4,3,2,1,0:T(8,128)(2,1)S(1)}, bf16[1,1,4,128,128]{4,3,2,1,0:T(8,128)(2,1)}, u32[]{:S(2)}) copy-start(bf16[1,1,4,128,128]{4,3,2,1,0:T(8,128)(2,1)} %param.7) | copy-start | bytes 393220
  3.4 27.8 %copy-start.1 = (bf16[784,128]{1,0:T(8,128)(2,1)S(1)}, bf16[784,128]{1,0:T(8,128)(2,1)}, u32[]{:S(2)}) copy-start(bf16[784,128]{1,0:T(8,128)(2,1)} %shard_map.76.refs_0_) | copy-start | bytes 602116
  3.4 15.3 %collective-permute-start.1 = (bf16[784,128]{1,0:T(8,128)(2,1)}, bf16[784,128]{1,0:T(8,128)(2,1)S(1)}, u32[]{:S(2)}, u32[]{:S(2)}) collective-permute-start(bf16[784,128]{1,0:T(8,128)(2,1)} %shard_map.76.refs_0_), channel_id=1, source_target_pairs={{0,16},{8,24},{16,0},{24,8},{1,17},{9,25},{17,1},{25,9},{2,18},{10... | collective-permute-start | bytes 602120 | tf_op jit(solution)/shard_map/ppermute | solution.py:343
  7.5 12.4 %collective-permute-start = (bf16[784,128]{1,0:T(8,128)(2,1)}, bf16[784,128]{1,0:T(8,128)(2,1)S(1)}, u32[]{:S(2)}, u32[]{:S(2)}) collective-permute-start(bf16[784,128]{1,0:T(8,128)(2,1)} %shard_map.76.refs_0_), channel_id=1, source_target_pairs={{0,8},{8,0},{16,24},{24,16},{1,9},{9,1},{17,25},{25,17},{2,10},{10... | collective-permute-start | bytes 602120 | tf_op jit(solution)/shard_map/ppermute | solution.py:343
  9.1 19.3 %collective-permute-start.4 = (bf16[1024,128]{1,0:T(8,128)(2,1)S(1)}, bf16[1024,128]{1,0:T(8,128)(2,1)S(1)}, u32[]{:S(2)}, u32[]{:S(2)}) collective-permute-start(bf16[1024,128]{1,0:T(8,128)(2,1)S(1)} %pad_maximum_fusion.refs_4_.refs_0_), channel_id=1, source_target_pairs={{0,16},{8,24},{16,0},{24,8},{1,17},{9,25},{17,1},{25,9},{2,18},{10... | collective-permute-start | bytes 786440 | tf_op jit(solution)/shard_map/ppermute | solution.py:343
  9.5 20.5 %collective-permute-start.3 = (bf16[1024,128]{1,0:T(8,128)(2,1)S(1)}, bf16[1024,128]{1,0:T(8,128)(2,1)S(1)}, u32[]{:S(2)}, u32[]{:S(2)}) collective-permute-start(bf16[1024,128]{1,0:T(8,128)(2,1)S(1)} %pad_maximum_fusion.refs_4_.refs_0_), channel_id=1, source_target_pairs={{0,8},{8,0},{16,24},{24,16},{1,9},{9,1},{17,25},{25,17},{2,10},{10... | collective-permute-start | bytes 786440 | tf_op jit(solution)/shard_map/ppermute | solution.py:343
  19.9 14.4 %collective-permute-start.2 = (bf16[784,128]{1,0:T(8,128)(2,1)S(1)}, bf16[784,128]{1,0:T(8,128)(2,1)S(1)}, u32[]{:S(2)}, u32[]{:S(2)}) collective-permute-start(bf16[784,128]{1,0:T(8,128)(2,1)S(1)} %shard_map.77.refs_2_), channel_id=1, source_target_pairs={{0,8},{8,0},{16,24},{24,16},{1,9},{9,1},{17,25},{25,17},{2,10},{10... | collective-permute-start | bytes 602120 | tf_op jit(solution)/shard_map/ppermute | solution.py:343
  30.0 8.5 %collective-permute-start.5 = (bf16[1024,128]{1,0:T(8,128)(2,1)S(1)}, bf16[1024,128]{1,0:T(8,128)(2,1)S(1)}, u32[]{:S(2)}, u32[]{:S(2)}) collective-permute-start(bf16[1024,128]{1,0:T(8,128)(2,1)S(1)} %shard_map.78.refs_6_.refs_2_), channel_id=1, source_target_pairs={{0,8},{8,0},{16,24},{24,16},{1,9},{9,1},{17,25},{25,17},{2,10},{10... | collective-permute-start | bytes 786440 | tf_op jit(solution)/shard_map/ppermute | solution.py:343
  34.3 10.1 %copy-start = (bf16[2,1152,768]{2,1,0:T(8,128)(2,1)S(1)}, bf16[2,1152,768]{2,1,0:T(8,128)(2,1)}, u32[]{:S(2)}) copy-start(bf16[2,1152,768]{2,1,0:T(8,128)(2,1)} %refs_10_.1) | copy-start | bytes 10616836
  39.5 1.2 %collective-permute-start.6 = (f32[3,384]{1,0:T(4,128)S(1)}, f32[3,384]{1,0:T(4,128)S(1)}, u32[]{:S(2)}, u32[]{:S(2)}) collective-permute-start(f32[3,384]{1,0:T(4,128)S(1)} %get-tuple-element.24), channel_id=1, source_target_pairs={{0,1},{1,0},{2,3},{3,2},{4,5},{5,4},{6,7},{7,6},{8,9},{9,8},{10,11... | collective-permute-start | bytes 13832 | tf_op jit(solution)/shard_map/ppermute | solution.py:313
  40.8 4.6 %collective-permute-start.9 = (f32[3,384]{1,0:T(4,128)S(1)}, f32[3,384]{1,0:T(4,128)S(1)}, u32[]{:S(2)}, u32[]{:S(2)}) collective-permute-start(f32[3,384]{1,0:T(4,128)S(1)} %pad_maximum_fusion.1), channel_id=1, source_target_pairs={{0,6},{1,7},{2,4},{3,5},{4,2},{5,3},{6,0},{7,1},{8,14},{9,15},{10,... | collective-permute-start | bytes 13832 | tf_op jit(solution)/shard_map/ppermute | solution.py:316
  43.4 3.6 %collective-permute-start.8 = (f32[3,384]{1,0:T(4,128)S(1)}, f32[3,384]{1,0:T(4,128)S(1)}, u32[]{:S(2)}, u32[]{:S(2)}) collective-permute-start(f32[3,384]{1,0:T(4,128)S(1)} %pad_maximum_fusion.1), channel_id=1, source_target_pairs={{0,4},{1,5},{2,6},{3,7},{4,0},{5,1},{6,2},{7,3},{8,12},{9,13},{10,... | collective-permute-start | bytes 13832 | tf_op jit(solution)/shard_map/ppermute | solution.py:316
  43.9 3.6 %collective-permute-start.7 = (f32[3,384]{1,0:T(4,128)S(1)}, f32[3,384]{1,0:T(4,128)S(1)}, u32[]{:S(2)}, u32[]{:S(2)}) collective-permute-start(f32[3,384]{1,0:T(4,128)S(1)} %pad_maximum_fusion.1), channel_id=1, source_target_pairs={{0,2},{1,3},{2,0},{3,1},{4,6},{5,7},{6,4},{7,5},{8,10},{9,11},{10,... | collective-permute-start | bytes 13832 | tf_op jit(solution)/shard_map/ppermute | solution.py:316
  50.0 1.2 %collective-permute-start.10 = (f32[3,384]{1,0:T(4,128)S(1)}, f32[3,384]{1,0:T(4,128)S(1)}, u32[]{:S(2)}, u32[]{:S(2)}) collective-permute-start(f32[3,384]{1,0:T(4,128)S(1)} %get-tuple-element.25), channel_id=1, source_target_pairs={{0,1},{1,0},{2,3},{3,2},{4,5},{5,4},{6,7},{7,6},{8,9},{9,8},{10,11... | collective-permute-start | bytes 13832 | tf_op jit(solution)/shard_map/ppermute | solution.py:313
  51.3 4.6 %collective-permute-start.13 = (f32[3,384]{1,0:T(4,128)S(1)}, f32[3,384]{1,0:T(4,128)S(1)}, u32[]{:S(2)}, u32[]{:S(2)}) collective-permute-start(f32[3,384]{1,0:T(4,128)S(1)} %pad_maximum_fusion.3), channel_id=1, source_target_pairs={{0,6},{1,7},{2,4},{3,5},{4,2},{5,3},{6,0},{7,1},{8,14},{9,15},{10,... | collective-permute-start | bytes 13832 | tf_op jit(solution)/shard_map/ppermute | solution.py:316
  52.8 3.6 %collective-permute-start.12 = (f32[3,384]{1,0:T(4,128)S(1)}, f32[3,384]{1,0:T(4,128)S(1)}, u32[]{:S(2)}, u32[]{:S(2)}) collective-permute-start(f32[3,384]{1,0:T(4,128)S(1)} %pad_maximum_fusion.3), channel_id=1, source_target_pairs={{0,4},{1,5},{2,6},{3,7},{4,0},{5,1},{6,2},{7,3},{8,12},{9,13},{10,... | collective-permute-start | bytes 13832 | tf_op jit(solution)/shard_map/ppermute | solution.py:316
  53.3 3.6 %collective-permute-start.11 = (f32[3,384]{1,0:T(4,128)S(1)}, f32[3,384]{1,0:T(4,128)S(1)}, u32[]{:S(2)}, u32[]{:S(2)}) collective-permute-start(f32[3,384]{1,0:T(4,128)S(1)} %pad_maximum_fusion.3), channel_id=1, source_target_pairs={{0,2},{1,3},{2,0},{3,1},{4,6},{5,7},{6,4},{7,5},{8,10},{9,11},{10,... | collective-permute-start | bytes 13832 | tf_op jit(solution)/shard_map/ppermute | solution.py:316
  59.8 2.2 %collective-permute-start.14 = (bf16[4,648,128]{2,1,0:T(8,128)(2,1)S(1)}, bf16[4,648,128]{2,1,0:T(8,128)(2,1)S(1)}, u32[]{:S(2)}, u32[]{:S(2)}) collective-permute-start(bf16[4,648,128]{2,1,0:T(8,128)(2,1)S(1)} %get-tuple-element.34), channel_id=1, source_target_pairs={{0,1},{1,0},{2,3},{3,2},{4,5},{5,4},{6,7},{7,6},{8,9},{9,8},{10,11... | collective-permute-start | bytes 1990664 | tf_op jit(solution)/shard_map/ppermute | solution.py:453
  62.2 8.1 %collective-permute-start.17 = (bf16[648,128]{1,0:T(8,128)(2,1)S(1)}, bf16[648,128]{1,0:T(8,128)(2,1)S(1)}, u32[]{:S(2)}, u32[]{:S(2)}) collective-permute-start(bf16[648,128]{1,0:T(8,128)(2,1)S(1)} %get-tuple-element.43), channel_id=1, source_target_pairs={{0,6},{1,7},{2,4},{3,5},{4,2},{5,3},{6,0},{7,1},{8,14},{9,15},{10,... | collective-permute-start | bytes 497672 | tf_op jit(solution)/shard_map/ppermute | solution.py:464
  64.8 8.2 %collective-permute-start.16 = (bf16[648,128]{1,0:T(8,128)(2,1)S(1)}, bf16[648,128]{1,0:T(8,128)(2,1)S(1)}, u32[]{:S(2)}, u32[]{:S(2)}) collective-permute-start(bf16[648,128]{1,0:T(8,128)(2,1)S(1)} %get-tuple-element.44), channel_id=1, source_target_pairs={{0,4},{1,5},{2,6},{3,7},{4,0},{5,1},{6,2},{7,3},{8,12},{9,13},{10,... | collective-permute-start | bytes 497672 | tf_op jit(solution)/shard_map/ppermute | solution.py:464
  65.3 7.9 %collective-permute-start.15 = (bf16[648,128]{1,0:T(8,128)(2,1)S(1)}, bf16[648,128]{1,0:T(8,128)(2,1)S(1)}, u32[]{:S(2)}, u32[]{:S(2)}) collective-permute-start(bf16[648,128]{1,0:T(8,128)(2,1)S(1)} %get-tuple-element.45), channel_id=1, source_target_pairs={{0,2},{1,3},{2,0},{3,1},{4,6},{5,7},{6,4},{7,5},{8,10},{9,11},{10,... | collective-permute-start | bytes 497672 | tf_op jit(solution)/shard_map/ppermute | solution.py:464

commit v12 on v11

--- a/solution.py
+++ b/solution.py
@@ -149,10 +149,12 @@
         mass_ref[k] = both[edge:]
 
 
+def block_products(place, stiff_x, mass_x, sums):
+    sums[place, 0:1, :] = jnp.sum(stiff_x * mass_x, axis=0, keepdims=True)
+    sums[place, 1:2, :] = jnp.sum(mass_x * mass_x, axis=0, keepdims=True)
+
+
 def block_stats(z, pairs, sums, stats_ref):
-    for k, (stiff_x, mass_x) in enumerate(pairs):
-        sums[z ^ k, 0:1, :] = jnp.sum(stiff_x * mass_x, axis=0, keepdims=True)
-        sums[z ^ k, 1:2, :] = jnp.sum(mass_x * mass_x, axis=0, keepdims=True)
     total = sums[0]
     for r in range(1, len(pairs)):
         total = total + sums[r]
@@ -167,13 +169,21 @@
     stats_ref[2:3, :] = about
 
 
-def stats_kernel(nz, slots, edge, modes, cols, km_last, placed, stiff, mass, stiff_ref, mass_ref, stats_ref, sums):
+def stats_kernel(
+    nz, slots, edge, modes, cols_ref, km_last, placed, stiff, mass, stiff_ref, mass_ref, stats_ref, sums, cols, sem
+):
+    fetch = pltpu.make_async_copy(cols_ref, cols, sem)
+    fetch.start()
     z = lax.axis_index("blk")
+    sums[...] = jnp.zeros_like(sums)
+    for k in range(nz - 1):
+        block_products(z ^ k, stiff[k], mass[k], sums)
+    fetch.wait()
     both = block_dot(km_last, slots, edge, cols, nz - 1, placed, slice(0, modes))
     stiff_ref[...] = both[:edge]
     mass_ref[...] = both[edge:]
+    block_products(z ^ (nz - 1), both[:edge], both[edge:], sums)
     pairs = [(stiff[k], mass[k]) for k in range(nz - 1)] + [(both[:edge], both[edge:])]
-    sums[...] = jnp.zeros_like(sums)
     block_stats(z, pairs, sums, stats_ref)
 
 
@@ -183,7 +193,10 @@
     ) + jnp.dot(placed[:, modes:], coeffs[1, 2 * modes :, :], preferred_element_type=f32)
 
 
-def sweep_kernel(nz, slots, edge, modes, total_rows, cols, *refs):
+def sweep_kernel(nz, slots, edge, modes, total_rows, cols_ref, *refs):
+    *refs, cols, sem = refs
+    fetch = pltpu.make_async_copy(cols_ref, cols, sem)
+    fetch.start()
     km_refs = refs[:nz]
     early, stiff, mass, stiff_last, mass_last, stats, coeffs = refs[nz : nz + 7]
     turned_ref, stiff_ref, mass_ref, stats_ref, search, sums = refs[nz + 7 :]
@@ -196,13 +209,15 @@
         search[at[k], :] = ((stiff_x - shift * mass_x) * scale).astype(bf16)
     late = jnp.dot(search[...], coeffs[1, modes : 2 * modes, :], preferred_element_type=f32)
     turned_ref[...] = (early[...] + late).astype(bf16)
+    sums[...] = jnp.zeros_like(sums)
+    fetch.wait()
     pairs = []
     for k in range(nz):
         both = block_dot(km_refs[k], slots, edge, cols, k, turned_ref, slice(0, modes))
         stiff_ref[at[k], :] = both[:edge]
         mass_ref[at[k], :] = both[edge:]
+        block_products(z ^ k, both[:edge], both[edge:], sums)
         pairs.append((both[:edge], both[edge:]))
-    sums[...] = jnp.zeros_like(sums)
     block_stats(z, pairs, sums, stats_ref)
 
 
@@ -244,7 +259,10 @@
         out_ref[:, op, whole * 128 :] = left[:, op * 32 : (op + 1) * 32]
 
 
-def gram_kernel(nz, chips, slots, edge, modes, total_rows, split, cols, *refs):
+def gram_kernel(nz, chips, slots, edge, modes, total_rows, split, cols_ref, *refs):
+    *refs, cols, sem = refs
+    fetch = pltpu.make_async_copy(cols_ref, cols, sem)
+    fetch.start()
     km_refs = refs[:nz]
     turned, stiff, mass, stats = refs[nz : nz + 4]
     gram_ref, full, full_t, applied, chosen = refs[nz + 4 :]
@@ -255,10 +273,12 @@
     full[:, 0:modes] = turned[:, 0:modes]
     full[:, modes : 2 * modes] = ((stiff[...] - shift * mass[...]) * scale).astype(bf16)
     full[:, 2 * modes : 3 * modes] = turned[:, modes : 2 * modes]
+    full_t[...] = full[...].T
     window = chosen.shape[1]
     start = z * width // 128 * 128
     picked = full[:, pl.ds(pl.multiple_of(start, 128), window)].astype(f32)
     chosen[...] = pltpu.roll(picked, window - (z * width - start), 1).astype(bf16)
+    fetch.wait()
     for k in range(nz):
         both = block_dot(km_refs[k], slots, edge, cols, k, chosen, slice(0, width)).astype(bf16)
         column = 0
@@ -266,7 +286,6 @@
             part = both[op * edge : (op + 1) * edge, first:last]
             applied[at[k], column : column + last - first] = part
             column += last - first
-    full_t[...] = full[...].T
     if split:
         gram_rows(full_t, applied, chips, 1 - lax.rem(lax.axis_index("grp"), 2), gram_ref)
     else:
@@ -283,11 +302,13 @@
     gram_rows(full_t, applied, chips, lax.rem(lax.axis_index("grp"), 2), gram_ref)
 
 
-def call(kernel, inputs, n_smem, out_shape, scratch, flops):
+def call(kernel, inputs, n_smem, out_shape, scratch, flops, n_any=0):
     return pl.pallas_call(
         kernel,
         out_shape=out_shape,
-        in_specs=[smem()] * n_smem + [vmem()] * (len(inputs) - n_smem),
+        in_specs=[smem()] * n_smem
+        + [pl.BlockSpec(memory_space=pl.ANY)] * n_any
+        + [vmem()] * (len(inputs) - n_smem - n_any),
         out_specs=jax.tree.map(lambda _: vmem(), out_shape),
         scratch_shapes=scratch,
         compiler_params=pltpu.CompilerParams(vmem_limit_bytes=VMEM_BYTES),
@@ -389,13 +410,15 @@
         [],
         (nz - 1) * work,
     )
+    fetched = [pltpu.SMEM((nz, slots), jnp.int32), pltpu.SemaphoreType.DMA(())]
     stiff_last, mass_last, stats = call(
         functools.partial(stats_kernel, nz, slots, edge, modes),
         [cols, km_parts[-1], placed, stiff_some, mass_some],
-        1,
+        0,
         (last, last, stats_shape),
-        [pltpu.VMEM((nz, 8, modes), f32)],
+        [pltpu.VMEM((nz, 8, modes), f32), *fetched],
         work,
+        n_any=1,
     )
     stats = merge_over("grp", ng, stats)
     early = call(
@@ -409,15 +432,16 @@
     turned, stiff_x, mass_x, stats = call(
         functools.partial(sweep_kernel, nz, slots, edge, modes, total_rows),
         [cols, *km_parts, early, stiff_some, mass_some, stiff_last, mass_last, stats, coeffs],
-        1,
+        0,
         (
             jax.ShapeDtypeStruct((rows, 2 * modes), bf16),
             jax.ShapeDtypeStruct((rows, modes), f32),
             jax.ShapeDtypeStruct((rows, modes), f32),
             stats_shape,
         ),
-        [pltpu.VMEM((rows, modes), bf16), pltpu.VMEM((nz, 8, modes), f32)],
+        [pltpu.VMEM((rows, modes), bf16), pltpu.VMEM((nz, 8, modes), f32), *fetched],
         4 * rows * modes * modes + nz * work,
+        n_any=1,
     )
     stats = merge_over("grp", ng, stats)
 
@@ -431,15 +455,16 @@
     gram, full, full_t, applied = call(
         functools.partial(gram_kernel, nz, chips, slots, edge, modes, total_rows, split),
         [cols, *km_parts, turned, stiff_x, mass_x, stats],
-        1,
+        0,
         (
             gram_shape,
             jax.ShapeDtypeStruct((rows, columns), bf16),
             jax.ShapeDtypeStruct((columns, rows), bf16),
             jax.ShapeDtypeStruct((rows, 2 * width), bf16),
         ),
-        [pltpu.VMEM((rows, window), bf16)],
+        [pltpu.VMEM((rows, window), bf16), *fetched],
         2 * rows * columns * width,
+        n_any=1,
     )
     basis_out, ritz = call(
         functools.partial(results_kernel, edge, total_rows),

time: 74.5 us -> 73.5 us (0.987)
  Pallas kernels: 13.9 us -> 12.9 us
    pallas_call x8, Pallas kernels: 11.2 us -> 10.2 us  [call(): pl.pallas_call(kernel, out_shape=out_shape, in_specs=[smem()] * n_smem +...]
where the time goes in v12:
time: 73.5 us; the launch traced here: 73.4 us
  waiting for transfers between devices  40.2 us (55%)
  starting transfers between devices  18.4 us (25%)
  Pallas kernels  12.9 us (18%)
  other arithmetic  1 us (1%)
  between operations  0.82 us (1%)
    ppermute x6, waiting for transfers between devices, send(): return lax.ppermute(x, 'blk', by_xor(nz, step))  26.2 us
    pallas_call x8, Pallas kernels, call(): pl.pallas_call(kernel, out_shape=out_shape, in_specs=[smem()] * n_smem +...  10.2 us
    ppermute x6, starting transfers between devices, send(): return lax.ppermute(x, 'blk', by_xor(nz, step))  7.49 us
    ppermute x6, starting transfers between devices, merge_over(): got = [lax.ppermute(stats, axis, by_xor(size, 2 * k)) for k in (1, 2, 3)]  7.11 us
    ppermute x3, waiting for transfers between devices, body(): lax.ppermute(mine[k], 'grp', by_xor(ng, 2 * k))  6.06 us
    ppermute x6, waiting for transfers between devices, merge_over(): got = [lax.ppermute(stats, axis, by_xor(size, 2 * k)) for k in (1, 2, 3)]  4.26 us
    ppermute x3, starting transfers between devices, body(): lax.ppermute(mine[k], 'grp', by_xor(ng, 2 * k))  3.55 us
    pallas_call x1, Pallas kernels, turn_first(): pl.pallas_call(functools.partial(turn_kernel, chunks, copies_each), out_s...  2.71 us
  transfers between devices with their start and end apart: 18, of which 18 were waited for; matrix products, arithmetic and copies ran while one was open for 1% of the time, Pallas kernels for 5%

profile of v12, /device:TPU:0, one launch (start us, length us, event | category | flops | bytes accessed | tf_op | source)
XLA Modules:
  0.0 73.4 jit_solution(5112138195160591611)
XLA Ops:
  0.6 0.0 copy-start.2
  0.6 0.0 copy-start.3
  0.7 2.7 %shard_map.76.refs_0_ = bf16[784,128]{1,0:T(8,128)(2,1)} custom-call(s32[1,4]{1,0:T(1,128)} %bitcast.16, bf16[128,1152]{1,0:T(8,128)(2,1)} %bitcast.13, bf16[2,1152,768]{2,1,0:T(8,128)(2,1)} %refs_10_.1), custom_call_target="tpu_custom_call" | custom-call | flops 226492416 | bytes 1769472 | tf_op jit(solution)/shard_map/pallas_call | solution.py:120
  3.4 0.0 copy-start.1
  3.4 4.1 %collective-permute-start.1 = (bf16[784,128]{1,0:T(8,128)(2,1)}, bf16[784,128]{1,0:T(8,128)(2,1)S(1)}, u32[]{:S(2)}, u32[]{:S(2)}) collective-permute-start(bf16[784,128]{1,0:T(8,128)(2,1)} %shard_map.76.refs_0_), channel_id=1, source_target_pairs={{0,16},{8,24},{16,0},{24,8},{1,17},{9,25},{17,1},{25,9},{2,18},{10... | collective-permute-start | bytes 602120 | tf_op jit(solution)/shard_map/ppermute | solution.py:364
  7.5 1.6 %collective-permute-start = (bf16[784,128]{1,0:T(8,128)(2,1)}, bf16[784,128]{1,0:T(8,128)(2,1)S(1)}, u32[]{:S(2)}, u32[]{:S(2)}) collective-permute-start(bf16[784,128]{1,0:T(8,128)(2,1)} %shard_map.76.refs_0_), channel_id=1, source_target_pairs={{0,8},{8,0},{16,24},{24,16},{1,9},{9,1},{17,25},{25,17},{2,10},{10... | collective-permute-start | bytes 602120 | tf_op jit(solution)/shard_map/ppermute | solution.py:364
  9.1 0.0 copy-done.2
  9.1 0.0 copy-done.3
  9.1 0.4 collective-permute-start.4
  9.5 0.2 collective-permute-start.3
  9.7 9.0 %collective-permute-done.1.refs_0_ = bf16[784,128]{1,0:T(8,128)(2,1)S(1)} collective-permute-done((bf16[784,128]{1,0:T(8,128)(2,1)}, bf16[784,128]{1,0:T(8,128)(2,1)S(1)}, u32[]{:S(2)}, u32[]{:S(2)}) %collective-permute-start.1) | collective-permute-done | bytes 200736 | tf_op jit(solution)/shard_map/ppermute | solution.py:364
  18.7 1.2 %collective-permute-done.refs_1_ = bf16[784,128]{1,0:T(8,128)(2,1)S(1)} collective-permute-done((bf16[784,128]{1,0:T(8,128)(2,1)}, bf16[784,128]{1,0:T(8,128)(2,1)S(1)}, u32[]{:S(2)}, u32[]{:S(2)}) %collective-permute-start) | collective-permute-done | bytes 200736 | tf_op jit(solution)/shard_map/ppermute | solution.py:364
  19.9 0.0 collective-permute-start.2
  19.9 8.5 %collective-permute-done.4.refs_0_ = bf16[1024,128]{1,0:T(8,128)(2,1)S(1)} collective-permute-done((bf16[1024,128]{1,0:T(8,128)(2,1)S(1)}, bf16[1024,128]{1,0:T(8,128)(2,1)S(1)}, u32[]{:S(2)}, u32[]{:S(2)}) %collective-permute-start.4) | collective-permute-done | bytes 262176 | tf_op jit(solution)/shard_map/ppermute | solution.py:364
  28.4 1.6 %collective-permute-done.3.refs_1_.refs_5_ = bf16[1024,128]{1,0:T(8,128)(2,1)S(1)} collective-permute-done((bf16[1024,128]{1,0:T(8,128)(2,1)S(1)}, bf16[1024,128]{1,0:T(8,128)(2,1)S(1)}, u32[]{:S(2)}, u32[]{:S(2)}) %collective-permute-start.3) | collective-permute-done | bytes 262176 | tf_op jit(solution)/shard_map/ppermute | solution.py:364
  30.0 1.2 %collective-permute-start.5 = (bf16[1024,128]{1,0:T(8,128)(2,1)S(1)}, bf16[1024,128]{1,0:T(8,128)(2,1)S(1)}, u32[]{:S(2)}, u32[]{:S(2)}) collective-permute-start(bf16[1024,128]{1,0:T(8,128)(2,1)S(1)} %shard_map.78.refs_6_.refs_2_), channel_id=1, source_target_pairs={{0,8},{8,0},{16,24},{24,16},{1,9},{9,1},{17,25},{25,17},{2,10},{10... | collective-permute-start | bytes 786440 | tf_op jit(solution)/shard_map/ppermute | solution.py:364
  31.2 0.0 copy-done.1
  31.2 3.1 %collective-permute-done.2.refs_3_ = bf16[784,128]{1,0:T(8,128)(2,1)S(1)} collective-permute-done((bf16[784,128]{1,0:T(8,128)(2,1)S(1)}, bf16[784,128]{1,0:T(8,128)(2,1)S(1)}, u32[]{:S(2)}, u32[]{:S(2)}) %collective-permute-start.2) | collective-permute-done | bytes 200736 | tf_op jit(solution)/shard_map/ppermute | solution.py:364
  34.3 0.0 copy-start
  34.3 1.3 %shard_map.79 = (bf16[512,768]{1,0:T(8,128)(2,1)S(1)}, f32[3,128,384]{2,1,0:T(8,128)S(1)}, f32[3,128,384]{2,1,0:T(8,128)S(1)}) custom-call(s32[4,4]{1,0:T(4,128)S(1)} %maximum_convert_fusion.cols.cols_ref, bf16[784,128]{1,0:T(8,128)(2,1)S(1)} %copy-done.1, bf16[784,128]{1,0:T(8,128)(2,1)S(1)} %collective-permute-done.refs_1_, ...), custom_call_target="tpu_custom_call" | custom-call | flops 301989888 | bytes 4000000 | tf_op jit(solution)/shard_map/pallas_call | solution.py:306
  35.6 2.9 %collective-permute-done.5.km_last.refs_3_ = bf16[1024,128]{1,0:T(8,128)(2,1)S(1)} collective-permute-done((bf16[1024,128]{1,0:T(8,128)(2,1)S(1)}, bf16[1024,128]{1,0:T(8,128)(2,1)S(1)}, u32[]{:S(2)}, u32[]{:S(2)}) %collective-permute-start.5) | collective-permute-done | bytes 262176 | tf_op jit(solution)/shard_map/ppermute | solution.py:364
  38.4 1.0 %shard_map.81 = (f32[128,384]{1,0:T(8,128)S(1)}, f32[128,384]{1,0:T(8,128)S(1)}, f32[3,384]{1,0:T(4,128)S(1)}) custom-call(s32[4,4]{1,0:T(4,128)S(1)} %maximum_convert_fusion.cols.cols_ref, bf16[1024,128]{1,0:T(8,128)(2,1)S(1)} %collective-permute-done.5.km_last.refs_3_, bf16[512,768]{1,0:T(8,128)(2,1)S(1)} %get-tuple-element.19.placed, ...), custom_call_target="tpu_custom_call" | custom-call | flops 100663296 | bytes 4000000 | tf_op jit(solution)/shard_map/pallas_call | solution.py:306
  39.5 0.1 collective-permute-start.6
  39.6 1.2 %collective-permute-done.6 = f32[3,384]{1,0:T(4,128)S(1)} collective-permute-done((f32[3,384]{1,0:T(4,128)S(1)}, f32[3,384]{1,0:T(4,128)S(1)}, u32[]{:S(2)}, u32[]{:S(2)}) %collective-permute-start.6) | collective-permute-done | bytes 4640 | tf_op jit(solution)/shard_map/ppermute | solution.py:334
  40.8 2.6 %collective-permute-start.9 = (f32[3,384]{1,0:T(4,128)S(1)}, f32[3,384]{1,0:T(4,128)S(1)}, u32[]{:S(2)}, u32[]{:S(2)}) collective-permute-start(f32[3,384]{1,0:T(4,128)S(1)} %pad_maximum_fusion.1), channel_id=1, source_target_pairs={{0,6},{1,7},{2,4},{3,5},{4,2},{5,3},{6,0},{7,1},{8,14},{9,15},{10,... | collective-permute-start | bytes 13832 | tf_op jit(solution)/shard_map/ppermute | solution.py:337
  43.3 0.5 collective-permute-start.8
  43.8 0.5 collective-permute-start.7
  44.3 0.0 copy-done
  44.3 1.0 %shard_map.80.refs_4_ = f32[512,768]{1,0:T(8,128)S(1)} custom-call(bf16[512,768]{1,0:T(8,128)(2,1)S(1)} %get-tuple-element.19.placed, bf16[2,1152,768]{2,1,0:T(8,128)(2,1)S(1)} %copy-done), custom_call_target="tpu_custom_call" | custom-call | flops 603979776 | bytes 4000000 | tf_op jit(solution)/shard_map/pallas_call | solution.py:306
  45.3 0.1 collective-permute-done.9
  45.4 1.6 %collective-permute-done.8 = f32[3,384]{1,0:T(4,128)S(1)} collective-permute-done((f32[3,384]{1,0:T(4,128)S(1)}, f32[3,384]{1,0:T(4,128)S(1)}, u32[]{:S(2)}, u32[]{:S(2)}) %collective-permute-start.8) | collective-permute-done | bytes 4640 | tf_op jit(solution)/shard_map/ppermute | solution.py:337
  47.0 0.5 collective-permute-done.7
  47.5 1.9 %shard_map.82 = (bf16[512,768]{1,0:T(8,128)(2,1)S(1)}, f32[512,384]{1,0:T(8,128)S(1)}, f32[512,384]{1,0:T(8,128)S(1)}, f32[3,384]{1,0:T(4,128)S(1)}) custom-call(s32[4,4]{1,0:T(4,128)S(1)} %maximum_convert_fusion.cols.cols_ref, bf16[1024,128]{1,0:T(8,128)(2,1)S(1)} %pad_maximum_fusion.refs_4_.refs_0_, ...), custom_call_target="tpu_custom_call" | custom-call | flops 704643072 | bytes 4000000 | tf_op jit(solution)/shard_map/pallas_call | solution.py:306
  49.4 0.1 collective-permute-start.10
  49.5 1.2 %collective-permute-done.10 = f32[3,384]{1,0:T(4,128)S(1)} collective-permute-done((f32[3,384]{1,0:T(4,128)S(1)}, f32[3,384]{1,0:T(4,128)S(1)}, u32[]{:S(2)}, u32[]{:S(2)}) %collective-permute-start.10) | collective-permute-done | bytes 4640 | tf_op jit(solution)/shard_map/ppermute | solution.py:334
  50.7 1.6 %collective-permute-start.13 = (f32[3,384]{1,0:T(4,128)S(1)}, f32[3,384]{1,0:T(4,128)S(1)}, u32[]{:S(2)}, u32[]{:S(2)}) collective-permute-start(f32[3,384]{1,0:T(4,128)S(1)} %pad_maximum_fusion.3), channel_id=1, source_target_pairs={{0,6},{1,7},{2,4},{3,5},{4,2},{5,3},{6,0},{7,1},{8,14},{9,15},{10,... | collective-permute-start | bytes 13832 | tf_op jit(solution)/shard_map/ppermute | solution.py:337
  52.3 0.5 collective-permute-start.12
  52.7 1.5 %collective-permute-start.11 = (f32[3,384]{1,0:T(4,128)S(1)}, f32[3,384]{1,0:T(4,128)S(1)}, u32[]{:S(2)}, u32[]{:S(2)}) collective-permute-start(f32[3,384]{1,0:T(4,128)S(1)} %pad_maximum_fusion.3), channel_id=1, source_target_pairs={{0,2},{1,3},{2,0},{3,1},{4,6},{5,7},{6,4},{7,5},{8,10},{9,11},{10,... | collective-permute-start | bytes 13832 | tf_op jit(solution)/shard_map/ppermute | solution.py:337
  54.3 1.0 %collective-permute-done.13 = f32[3,384]{1,0:T(4,128)S(1)} collective-permute-done((f32[3,384]{1,0:T(4,128)S(1)}, f32[3,384]{1,0:T(4,128)S(1)}, u32[]{:S(2)}, u32[]{:S(2)}) %collective-permute-start.13) | collective-permute-done | bytes 4640 | tf_op jit(solution)/shard_map/ppermute | solution.py:337
  55.3 0.6 collective-permute-done.12
  55.9 0.5 collective-permute-done.11
  56.4 2.3 %shard_map.83 = (bf16[4,648,128]{2,1,0:T(8,128)(2,1)S(1)}, bf16[512,1152]{1,0:T(8,128)(2,1)S(1)}, bf16[1152,512]{1,0:T(8,128)(2,1)S(1)}, bf16[512,576]{1,0:T(8,128)(2,1)S(1)}) custom-call(s32[4,4]{1,0:T(4,128)S(1)} %maximum_convert_fusion.cols.cols_ref, bf16[1024,128]{1,0:T(8,128)(2,1)S(1)} %pad_maximum_fusion.refs_4_.refs_0_, ...), custom_call_target="tpu_custom_call" | custom-call | flops 339738624 | bytes 4000000 | tf_op jit(solution)/shard_map/pallas_call | solution.py:306
  58.8 0.1 collective-permute-start.14
  58.9 0.7 shard_map.85
  59.6 1.4 %collective-permute-done.14 = bf16[4,648,128]{2,1,0:T(8,128)(2,1)S(1)} collective-permute-done((bf16[4,648,128]{2,1,0:T(8,128)(2,1)S(1)}, bf16[4,648,128]{2,1,0:T(8,128)(2,1)S(1)}, u32[]{:S(2)}, u32[]{:S(2)}) %collective-permute-start.14) | collective-permute-done | bytes 663584 | tf_op jit(solution)/shard_map/ppermute | solution.py:478
  61.0 0.2 add_convert_fusion
  61.2 2.6 %collective-permute-start.17 = (bf16[648,128]{1,0:T(8,128)(2,1)S(1)}, bf16[648,128]{1,0:T(8,128)(2,1)S(1)}, u32[]{:S(2)}, u32[]{:S(2)}) collective-permute-start(bf16[648,128]{1,0:T(8,128)(2,1)S(1)} %get-tuple-element.43), channel_id=1, source_target_pairs={{0,6},{1,7},{2,4},{3,5},{4,2},{5,3},{6,0},{7,1},{8,14},{9,15},{10,... | collective-permute-start | bytes 497672 | tf_op jit(solution)/shard_map/ppermute | solution.py:489
  63.8 0.5 collective-permute-start.16
  64.3 0.5 collective-permute-start.15
  64.7 0.7 %shard_map.84 = (bf16[128,1152]{1,0:T(8,128)(2,1)}, f32[1,384]{1,0:T(1,128)S(1)}) custom-call(f32[3,384]{1,0:T(4,128)S(1)} %pad_maximum_fusion.4.refs_7_.stats, bf16[512,1152]{1,0:T(8,128)(2,1)S(1)} %get-tuple-element.29.full), custom_call_target="tpu_custom_call" | custom-call | bytes 4000000 | tf_op jit(solution)/shard_map/pallas_call | solution.py:306
  65.5 0.6 reduce
  66.1 3.2 %collective-permute-done.17.refs_3_ = bf16[648,128]{1,0:T(8,128)(2,1)S(1)} collective-permute-done((bf16[648,128]{1,0:T(8,128)(2,1)S(1)}, bf16[648,128]{1,0:T(8,128)(2,1)S(1)}, u32[]{:S(2)}, u32[]{:S(2)}) %collective-permute-start.17) | collective-permute-done | bytes 165920 | tf_op jit(solution)/shard_map/ppermute | solution.py:489
  69.2 2.8 %collective-permute-done.16.refs_2_ = bf16[648,128]{1,0:T(8,128)(2,1)S(1)} collective-permute-done((bf16[648,128]{1,0:T(8,128)(2,1)S(1)}, bf16[648,128]{1,0:T(8,128)(2,1)S(1)}, u32[]{:S(2)}, u32[]{:S(2)}) %collective-permute-start.16) | collective-permute-done | bytes 165920 | tf_op jit(solution)/shard_map/ppermute | solution.py:489
  72.0 0.1 collective-permute-done.15.refs_1_
  72.1 1.2 %shard_map.86 = f32[144,2,288]{2,1,0:T(2,128)} custom-call(bf16[648,128]{1,0:T(8,128)(2,1)S(1)} %get-tuple-element.46.refs_0_, bf16[648,128]{1,0:T(8,128)(2,1)S(1)} %collective-permute-done.15.refs_1_, bf16[648,128]{1,0:T(8,128)(2,1)S(1)} %collective-permute-done.16.refs_2_, bf16[648,128]{1,0:T(8,128)(2,1)S(1)} %collective-permute-done.17.refs_3_), custom_call_target="tpu_custom_call" | custom-call | bytes 4000000 | tf_op jit(solution)/shard_map/pallas_call | solution.py:306
  (17 shorter events, 0.3 us)
Async XLA Ops:
  0.6 8.4 %copy-start.2 = (bf16[1,1,4,128,128]{4,3,2,1,0:T(8,128)(2,1)S(1)}, bf16[1,1,4,128,128]{4,3,2,1,0:T(8,128)(2,1)}, u32[]{:S(2)}) copy-start(bf16[1,1,4,128,128]{4,3,2,1,0:T(8,128)(2,1)} %param.8) | copy-start | bytes 393220
  0.6 8.4 %copy-start.3 = (bf16[1,1,4,128,128]{4,3,2,1,0:T(8,128)(2,1)S(1)}, bf16[1,1,4,128,128]{4,3,2,1,0:T(8,128)(2,1)}, u32[]{:S(2)}) copy-start(bf16[1,1,4,128,128]{4,3,2,1,0:T(8,128)(2,1)} %param.7) | copy-start | bytes 393220
  3.4 27.8 %copy-start.1 = (bf16[784,128]{1,0:T(8,128)(2,1)S(1)}, bf16[784,128]{1,0:T(8,128)(2,1)}, u32[]{:S(2)}) copy-start(bf16[784,128]{1,0:T(8,128)(2,1)} %shard_map.76.refs_0_) | copy-start | bytes 602116
  3.4 15.3 %collective-permute-start.1 = (bf16[784,128]{1,0:T(8,128)(2,1)}, bf16[784,128]{1,0:T(8,128)(2,1)S(1)}, u32[]{:S(2)}, u32[]{:S(2)}) collective-permute-start(bf16[784,128]{1,0:T(8,128)(2,1)} %shard_map.76.refs_0_), channel_id=1, source_target_pairs={{0,16},{8,24},{16,0},{24,8},{1,17},{9,25},{17,1},{25,9},{2,18},{10... | collective-permute-start | bytes 602120 | tf_op jit(solution)/shard_map/ppermute | solution.py:364
  7.5 12.4 %collective-permute-start = (bf16[784,128]{1,0:T(8,128)(2,1)}, bf16[784,128]{1,0:T(8,128)(2,1)S(1)}, u32[]{:S(2)}, u32[]{:S(2)}) collective-permute-start(bf16[784,128]{1,0:T(8,128)(2,1)} %shard_map.76.refs_0_), channel_id=1, source_target_pairs={{0,8},{8,0},{16,24},{24,16},{1,9},{9,1},{17,25},{25,17},{2,10},{10... | collective-permute-start | bytes 602120 | tf_op jit(solution)/shard_map/ppermute | solution.py:364
  9.1 19.3 %collective-permute-start.4 = (bf16[1024,128]{1,0:T(8,128)(2,1)S(1)}, bf16[1024,128]{1,0:T(8,128)(2,1)S(1)}, u32[]{:S(2)}, u32[]{:S(2)}) collective-permute-start(bf16[1024,128]{1,0:T(8,128)(2,1)S(1)} %pad_maximum_fusion.refs_4_.refs_0_), channel_id=1, source_target_pairs={{0,16},{8,24},{16,0},{24,8},{1,17},{9,25},{17,1},{25,9},{2,18},{10... | collective-permute-start | bytes 786440 | tf_op jit(solution)/shard_map/ppermute | solution.py:364
  9.5 20.5 %collective-permute-start.3 = (bf16[1024,128]{1,0:T(8,128)(2,1)S(1)}, bf16[1024,128]{1,0:T(8,128)(2,1)S(1)}, u32[]{:S(2)}, u32[]{:S(2)}) collective-permute-start(bf16[1024,128]{1,0:T(8,128)(2,1)S(1)} %pad_maximum_fusion.refs_4_.refs_0_), channel_id=1, source_target_pairs={{0,8},{8,0},{16,24},{24,16},{1,9},{9,1},{17,25},{25,17},{2,10},{10... | collective-permute-start | bytes 786440 | tf_op jit(solution)/shard_map/ppermute | solution.py:364
  19.9 14.4 %collective-permute-start.2 = (bf16[784,128]{1,0:T(8,128)(2,1)S(1)}, bf16[784,128]{1,0:T(8,128)(2,1)S(1)}, u32[]{:S(2)}, u32[]{:S(2)}) collective-permute-start(bf16[784,128]{1,0:T(8,128)(2,1)S(1)} %shard_map.77.refs_2_), channel_id=1, source_target_pairs={{0,8},{8,0},{16,24},{24,16},{1,9},{9,1},{17,25},{25,17},{2,10},{10... | collective-permute-start | bytes 602120 | tf_op jit(solution)/shard_map/ppermute | solution.py:364
  30.0 8.5 %collective-permute-start.5 = (bf16[1024,128]{1,0:T(8,128)(2,1)S(1)}, bf16[1024,128]{1,0:T(8,128)(2,1)S(1)}, u32[]{:S(2)}, u32[]{:S(2)}) collective-permute-start(bf16[1024,128]{1,0:T(8,128)(2,1)S(1)} %shard_map.78.refs_6_.refs_2_), channel_id=1, source_target_pairs={{0,8},{8,0},{16,24},{24,16},{1,9},{9,1},{17,25},{25,17},{2,10},{10... | collective-permute-start | bytes 786440 | tf_op jit(solution)/shard_map/ppermute | solution.py:364
  34.3 10.0 %copy-start = (bf16[2,1152,768]{2,1,0:T(8,128)(2,1)S(1)}, bf16[2,1152,768]{2,1,0:T(8,128)(2,1)}, u32[]{:S(2)}) copy-start(bf16[2,1152,768]{2,1,0:T(8,128)(2,1)} %refs_10_.1) | copy-start | bytes 10616836
  39.5 1.2 %collective-permute-start.6 = (f32[3,384]{1,0:T(4,128)S(1)}, f32[3,384]{1,0:T(4,128)S(1)}, u32[]{:S(2)}, u32[]{:S(2)}) collective-permute-start(f32[3,384]{1,0:T(4,128)S(1)} %get-tuple-element.24), channel_id=1, source_target_pairs={{0,1},{1,0},{2,3},{3,2},{4,5},{5,4},{6,7},{7,6},{8,9},{9,8},{10,11... | collective-permute-start | bytes 13832 | tf_op jit(solution)/shard_map/ppermute | solution.py:334
  40.8 4.6 %collective-permute-start.9 = (f32[3,384]{1,0:T(4,128)S(1)}, f32[3,384]{1,0:T(4,128)S(1)}, u32[]{:S(2)}, u32[]{:S(2)}) collective-permute-start(f32[3,384]{1,0:T(4,128)S(1)} %pad_maximum_fusion.1), channel_id=1, source_target_pairs={{0,6},{1,7},{2,4},{3,5},{4,2},{5,3},{6,0},{7,1},{8,14},{9,15},{10,... | collective-permute-start | bytes 13832 | tf_op jit(solution)/shard_map/ppermute | solution.py:337
  43.3 3.6 %collective-permute-start.8 = (f32[3,384]{1,0:T(4,128)S(1)}, f32[3,384]{1,0:T(4,128)S(1)}, u32[]{:S(2)}, u32[]{:S(2)}) collective-permute-start(f32[3,384]{1,0:T(4,128)S(1)} %pad_maximum_fusion.1), channel_id=1, source_target_pairs={{0,4},{1,5},{2,6},{3,7},{4,0},{5,1},{6,2},{7,3},{8,12},{9,13},{10,... | collective-permute-start | bytes 13832 | tf_op jit(solution)/shard_map/ppermute | solution.py:337
  43.8 3.6 %collective-permute-start.7 = (f32[3,384]{1,0:T(4,128)S(1)}, f32[3,384]{1,0:T(4,128)S(1)}, u32[]{:S(2)}, u32[]{:S(2)}) collective-permute-start(f32[3,384]{1,0:T(4,128)S(1)} %pad_maximum_fusion.1), channel_id=1, source_target_pairs={{0,2},{1,3},{2,0},{3,1},{4,6},{5,7},{6,4},{7,5},{8,10},{9,11},{10,... | collective-permute-start | bytes 13832 | tf_op jit(solution)/shard_map/ppermute | solution.py:337
  49.4 1.2 %collective-permute-start.10 = (f32[3,384]{1,0:T(4,128)S(1)}, f32[3,384]{1,0:T(4,128)S(1)}, u32[]{:S(2)}, u32[]{:S(2)}) collective-permute-start(f32[3,384]{1,0:T(4,128)S(1)} %get-tuple-element.25), channel_id=1, source_target_pairs={{0,1},{1,0},{2,3},{3,2},{4,5},{5,4},{6,7},{7,6},{8,9},{9,8},{10,11... | collective-permute-start | bytes 13832 | tf_op jit(solution)/shard_map/ppermute | solution.py:334
  50.7 4.6 %collective-permute-start.13 = (f32[3,384]{1,0:T(4,128)S(1)}, f32[3,384]{1,0:T(4,128)S(1)}, u32[]{:S(2)}, u32[]{:S(2)}) collective-permute-start(f32[3,384]{1,0:T(4,128)S(1)} %pad_maximum_fusion.3), channel_id=1, source_target_pairs={{0,6},{1,7},{2,4},{3,5},{4,2},{5,3},{6,0},{7,1},{8,14},{9,15},{10,... | collective-permute-start | bytes 13832 | tf_op jit(solution)/shard_map/ppermute | solution.py:337
  52.3 3.6 %collective-permute-start.12 = (f32[3,384]{1,0:T(4,128)S(1)}, f32[3,384]{1,0:T(4,128)S(1)}, u32[]{:S(2)}, u32[]{:S(2)}) collective-permute-start(f32[3,384]{1,0:T(4,128)S(1)} %pad_maximum_fusion.3), channel_id=1, source_target_pairs={{0,4},{1,5},{2,6},{3,7},{4,0},{5,1},{6,2},{7,3},{8,12},{9,13},{10,... | collective-permute-start | bytes 13832 | tf_op jit(solution)/shard_map/ppermute | solution.py:337
  52.7 3.6 %collective-permute-start.11 = (f32[3,384]{1,0:T(4,128)S(1)}, f32[3,384]{1,0:T(4,128)S(1)}, u32[]{:S(2)}, u32[]{:S(2)}) collective-permute-start(f32[3,384]{1,0:T(4,128)S(1)} %pad_maximum_fusion.3), channel_id=1, source_target_pairs={{0,2},{1,3},{2,0},{3,1},{4,6},{5,7},{6,4},{7,5},{8,10},{9,11},{10,... | collective-permute-start | bytes 13832 | tf_op jit(solution)/shard_map/ppermute | solution.py:337
  58.8 2.2 %collective-permute-start.14 = (bf16[4,648,128]{2,1,0:T(8,128)(2,1)S(1)}, bf16[4,648,128]{2,1,0:T(8,128)(2,1)S(1)}, u32[]{:S(2)}, u32[]{:S(2)}) collective-permute-start(bf16[4,648,128]{2,1,0:T(8,128)(2,1)S(1)} %get-tuple-element.34), channel_id=1, source_target_pairs={{0,1},{1,0},{2,3},{3,2},{4,5},{5,4},{6,7},{7,6},{8,9},{9,8},{10,11... | collective-permute-start | bytes 1990664 | tf_op jit(solution)/shard_map/ppermute | solution.py:478
  61.2 8.1 %collective-permute-start.17 = (bf16[648,128]{1,0:T(8,128)(2,1)S(1)}, bf16[648,128]{1,0:T(8,128)(2,1)S(1)}, u32[]{:S(2)}, u32[]{:S(2)}) collective-permute-start(bf16[648,128]{1,0:T(8,128)(2,1)S(1)} %get-tuple-element.43), channel_id=1, source_target_pairs={{0,6},{1,7},{2,4},{3,5},{4,2},{5,3},{6,0},{7,1},{8,14},{9,15},{10,... | collective-permute-start | bytes 497672 | tf_op jit(solution)/shard_map/ppermute | solution.py:489
  63.8 8.2 %collective-permute-start.16 = (bf16[648,128]{1,0:T(8,128)(2,1)S(1)}, bf16[648,128]{1,0:T(8,128)(2,1)S(1)}, u32[]{:S(2)}, u32[]{:S(2)}) collective-permute-start(bf16[648,128]{1,0:T(8,128)(2,1)S(1)} %get-tuple-element.44), channel_id=1, source_target_pairs={{0,4},{1,5},{2,6},{3,7},{4,0},{5,1},{6,2},{7,3},{8,12},{9,13},{10,... | collective-permute-start | bytes 497672 | tf_op jit(solution)/shard_map/ppermute | solution.py:489
  64.3 7.9 %collective-permute-start.15 = (bf16[648,128]{1,0:T(8,128)(2,1)S(1)}, bf16[648,128]{1,0:T(8,128)(2,1)S(1)}, u32[]{:S(2)}, u32[]{:S(2)}) collective-permute-start(bf16[648,128]{1,0:T(8,128)(2,1)S(1)} %get-tuple-element.45), channel_id=1, source_target_pairs={{0,2},{1,3},{2,0},{3,1},{4,6},{5,7},{6,4},{7,5},{8,10},{9,11},{10,... | collective-permute-start | bytes 497672 | tf_op jit(solution)/shard_map/ppermute | solution.py:489

commit v13 on v12

--- a/solution.py
+++ b/solution.py
@@ -226,7 +226,7 @@
     return [(0, 0, whole), (1, 0, whole), (0, whole, width), (1, whole, width)]
 
 
-def gram_rows(full_t, applied, chips, core, out_ref):
+def gram_rows(full_t, applied, chips, core, bounds, out_refs):
     chip = lax.div(lax.axis_index("grp"), 2)
     block = full_t.shape[0] // (2 * chips)
     rows = [
@@ -234,38 +234,43 @@
     ]
     gram = jnp.dot(jnp.concatenate(rows, axis=0), applied[...], preferred_element_type=f32)
     whole = gram.shape[1] // 128
-    for j in range(chips):
-        mine = gram[j * block : (j + 1) * block]
-        for b in range(whole):
-            part = mine[:, b * 128 : (b + 1) * 128].astype(bf16)
-            out_ref[j ^ chip, b * block : (b + 1) * block, :] = part
-        left = mine[:, whole * 128 :]
-        left = jnp.concatenate([left[: block // 2], left[block // 2 :]], axis=1).astype(bf16)
-        out_ref[j ^ chip, whole * block : whole * block + block // 2, :] = left
-
-
-def finish_kernel(block, width, *refs):
-    out_ref = refs[-1]
-    total = refs[0][...].astype(f32)
-    for ref in refs[1:-1]:
-        total = total + ref[...].astype(f32)
+    for (low, high), out_ref in zip(bounds, out_refs):
+        size = high - low
+        for j in range(chips):
+            mine = gram[j * block + low : j * block + high]
+            for b in range(whole):
+                part = mine[:, b * 128 : (b + 1) * 128].astype(bf16)
+                out_ref[j ^ chip, b * size : (b + 1) * size, :] = part
+            left = mine[:, whole * 128 :]
+            left = jnp.concatenate([left[: size // 2], left[size // 2 :]], axis=1).astype(bf16)
+            out_ref[j ^ chip, whole * size : whole * size + size // 2, :] = left
+
+
+def finish_kernel(bounds, width, *refs):
+    *refs, out_ref = refs
+    each = len(refs) // len(bounds)
     whole = width // 128
-    left = total[2 * whole * block :, :]
-    left = jnp.concatenate([left[:, :64], left[:, 64:]], axis=0)
-    for op in range(2):
-        for b in range(whole):
-            at = (op * whole + b) * block
-            out_ref[:, op, b * 128 : (b + 1) * 128] = total[at : at + block]
-        out_ref[:, op, whole * 128 :] = left[:, op * 32 : (op + 1) * 32]
-
-
-def gram_kernel(nz, chips, slots, edge, modes, total_rows, split, cols_ref, *refs):
+    for i, (low, high) in enumerate(bounds):
+        size = high - low
+        total = refs[i * each][...].astype(f32)
+        for ref in refs[i * each + 1 : (i + 1) * each]:
+            total = total + ref[...].astype(f32)
+        left = total[2 * whole * size :, :]
+        left = jnp.concatenate([left[:, :64], left[:, 64:]], axis=0)
+        for op in range(2):
+            for b in range(whole):
+                at = (op * whole + b) * size
+                out_ref[low:high, op, b * 128 : (b + 1) * 128] = total[at : at + size]
+            out_ref[low:high, op, whole * 128 :] = left[:, op * 32 : (op + 1) * 32]
+
+
+def gram_kernel(nz, chips, slots, edge, modes, total_rows, bounds, cols_ref, *refs):
     *refs, cols, sem = refs
     fetch = pltpu.make_async_copy(cols_ref, cols, sem)
     fetch.start()
     km_refs = refs[:nz]
     turned, stiff, mass, stats = refs[nz : nz + 4]
-    gram_ref, full, full_t, applied, chosen = refs[nz + 4 :]
+    *gram_refs, full, full_t, applied, chosen = refs[nz + 4 :]
     z = lax.axis_index("blk")
     at = [pl.ds(pl.multiple_of((z ^ k) * edge, edge), edge) for k in range(nz)]
     width = 3 * modes // nz
@@ -282,14 +287,15 @@
     for k in range(nz):
         both = block_dot(km_refs[k], slots, edge, cols, k, chosen, slice(0, width)).astype(bf16)
         column = 0
-        for op, first, last in dense_order(width) if split else [(0, 0, width), (1, 0, width)]:
+        for op, first, last in dense_order(width) if bounds else [(0, 0, width), (1, 0, width)]:
             part = both[op * edge : (op + 1) * edge, first:last]
             applied[at[k], column : column + last - first] = part
             column += last - first
-    if split:
-        gram_rows(full_t, applied, chips, 1 - lax.rem(lax.axis_index("grp"), 2), gram_ref)
+    if bounds:
+        other = 1 - lax.rem(lax.axis_index("grp"), 2)
+        gram_rows(full_t, applied, chips, other, bounds, gram_refs)
     else:
-        gram_ref[...] = jnp.dot(full_t[...], applied[...], preferred_element_type=f32).astype(bf16)
+        gram_refs[0][...] = jnp.dot(full_t[...], applied[...], preferred_element_type=f32).astype(bf16)
 
 
 def results_kernel(edge, total_rows, stats, full, basis_ref, ritz_ref):
@@ -298,8 +304,9 @@
     ritz_ref[...] = shift_and_scale(stats, total_rows)[0]
 
 
-def gram_rest_kernel(chips, full_t, applied, gram_ref):
-    gram_rows(full_t, applied, chips, lax.rem(lax.axis_index("grp"), 2), gram_ref)
+def gram_rest_kernel(chips, bounds, full_t, applied, *gram_refs):
+    own = lax.rem(lax.axis_index("grp"), 2)
+    gram_rows(full_t, applied, chips, own, bounds, gram_refs)
 
 
 def call(kernel, inputs, n_smem, out_shape, scratch, flops, n_any=0):
@@ -447,17 +454,21 @@
 
     chips = ng // 2
     block = columns // ng
-    split = block % 16 == 0 and width % 128 == 32
-    gram_shape = jax.ShapeDtypeStruct(
-        (chips, block * 2 * width // 128, 128) if split else (columns, 2 * width), bf16
-    )
+    bounds = []
+    if block % 32 == 16 and width % 128 == 32:
+        first_rows = (block + 16) // 32 * 16
+        bounds = [(0, first_rows), (first_rows, block)]
+    gram_shapes = tuple(
+        jax.ShapeDtypeStruct((chips, (high - low) * 2 * width // 128, 128), bf16)
+        for low, high in bounds
+    ) or (jax.ShapeDtypeStruct((columns, 2 * width), bf16),)
     window = -(-(width + max(i * width % 128 for i in range(nz))) // 128) * 128
-    gram, full, full_t, applied = call(
-        functools.partial(gram_kernel, nz, chips, slots, edge, modes, total_rows, split),
+    *grams, full, full_t, applied = call(
+        functools.partial(gram_kernel, nz, chips, slots, edge, modes, total_rows, bounds),
         [cols, *km_parts, turned, stiff_x, mass_x, stats],
         0,
         (
-            gram_shape,
+            *gram_shapes,
             jax.ShapeDtypeStruct((rows, columns), bf16),
             jax.ShapeDtypeStruct((columns, rows), bf16),
             jax.ShapeDtypeStruct((rows, 2 * width), bf16),
@@ -474,22 +485,24 @@
         [],
         0,
     )
-    if split:
-        got = lax.ppermute(gram, "grp", by_xor(ng, 1))
+    if bounds:
+        got = [lax.ppermute(x, "grp", by_xor(ng, 1)) for x in grams]
         keep = call(
-            functools.partial(gram_rest_kernel, chips),
+            functools.partial(gram_rest_kernel, chips, bounds),
             [full_t, applied],
             0,
-            gram_shape,
+            gram_shapes,
             [],
             2 * rows * columns * width,
         )
-        mine = (keep.astype(f32) + got.astype(f32)).astype(bf16)
-        pieces = [mine[0]] + [
-            lax.ppermute(mine[k], "grp", by_xor(ng, 2 * k)) for k in range(1, chips)
-        ]
+        pieces = []
+        for one, two in zip(keep, got):
+            mine = (one.astype(f32) + two.astype(f32)).astype(bf16)
+            pieces += [mine[0]] + [
+                lax.ppermute(mine[k], "grp", by_xor(ng, 2 * k)) for k in range(1, chips)
+            ]
         total = call(
-            functools.partial(finish_kernel, block, width),
+            functools.partial(finish_kernel, bounds, width),
             pieces,
             0,
             jax.ShapeDtypeStruct((block, 2, width), f32),
@@ -497,7 +510,7 @@
             0,
         )
     else:
-        total = lax.psum_scatter(gram, "grp", scatter_dimension=0, tiled=True)
+        total = lax.psum_scatter(grams[0], "grp", scatter_dimension=0, tiled=True)
         total = total.astype(f32).reshape(block, 2, width)
     return (basis_out[None], ritz[0], total)
 

time: 73.5 us -> 73.1 us (level)
  waiting for transfers between devices: 40.2 us -> 35.7 us
  starting transfers between devices: 18.4 us -> 22.4 us
    ppermute x3 -> x6, starting transfers between devices: 3.55 us -> 7.11 us  [body(): lax.ppermute(mine[k], 'grp', by_xor(ng, 2 * k))]
    ppermute x3 -> x6, waiting for transfers between devices: 6.06 us -> 2.54 us  [body(): lax.ppermute(mine[k], 'grp', by_xor(ng, 2 * k))]
    ppermute x1 -> x2, waiting for transfers between devices: 1.39 us -> 0.38 us  [body(): got = [lax.ppermute(x, 'grp', by_xor(ng, 1)) for x in grams]]
  transfers between devices with their start and end apart: 18 -> 22, of which waited for: 18 -> 16; matrix products, arithmetic and copies ran while one was open for 1% -> 1% of each run, Pallas kernels for 5% -> 5%
where the time goes in v13:
time: 73.1 us; the launch traced here: 72.9 us
  waiting for transfers between devices  35.7 us (49%)
  starting transfers between devices  22.4 us (31%)
  Pallas kernels  12.9 us (18%)
  other arithmetic  1.01 us (1%)
  between operations  0.83 us (1%)
    ppermute x6, waiting for transfers between devices, send(): return lax.ppermute(x, 'blk', by_xor(nz, step))  26.2 us
    pallas_call x8, Pallas kernels, call(): pl.pallas_call(kernel, out_shape=out_shape, in_specs=[smem()] * n_smem +...  10.2 us
    ppermute x6, starting transfers between devices, send(): return lax.ppermute(x, 'blk', by_xor(nz, step))  7.49 us
    ppermute x6, starting transfers between devices, body(): lax.ppermute(mine[k], 'grp', by_xor(ng, 2 * k))  7.11 us
    ppermute x6, starting transfers between devices, merge_over(): got = [lax.ppermute(stats, axis, by_xor(size, 2 * k)) for k in (1, 2, 3)]  7.11 us
    ppermute x6, waiting for transfers between devices, merge_over(): got = [lax.ppermute(stats, axis, by_xor(size, 2 * k)) for k in (1, 2, 3)]  4.26 us
    pallas_call x1, Pallas kernels, turn_first(): pl.pallas_call(functools.partial(turn_kernel, chunks, copies_each), out_s...  2.71 us
    ppermute x6, waiting for transfers between devices, body(): lax.ppermute(mine[k], 'grp', by_xor(ng, 2 * k))  2.54 us
  transfers between devices with their start and end apart: 22, of which 16 were waited for; matrix products, arithmetic and copies ran while one was open for 1% of the time, Pallas kernels for 5%

profile of v13, /device:TPU:0, one launch (start us, length us, event | category | flops | bytes accessed | tf_op | source)
XLA Modules:
  0.0 72.9 jit_solution(6025234008675012878)
XLA Ops:
  0.6 0.0 copy-start.2
  0.6 0.0 copy-start.3
  0.7 2.7 %shard_map.76.refs_0_ = bf16[784,128]{1,0:T(8,128)(2,1)} custom-call(s32[1,4]{1,0:T(1,128)} %bitcast.24, bf16[128,1152]{1,0:T(8,128)(2,1)} %bitcast.21, bf16[2,1152,768]{2,1,0:T(8,128)(2,1)} %refs_10_.1), custom_call_target="tpu_custom_call" | custom-call | flops 226492416 | bytes 1769472 | tf_op jit(solution)/shard_map/pallas_call | solution.py:120
  3.4 0.0 copy-start.1
  3.4 4.1 %collective-permute-start.1 = (bf16[784,128]{1,0:T(8,128)(2,1)}, bf16[784,128]{1,0:T(8,128)(2,1)S(1)}, u32[]{:S(2)}, u32[]{:S(2)}) collective-permute-start(bf16[784,128]{1,0:T(8,128)(2,1)} %shard_map.76.refs_0_), channel_id=1, source_target_pairs={{0,16},{8,24},{16,0},{24,8},{1,17},{9,25},{17,1},{25,9},{2,18},{10... | collective-permute-start | bytes 602120 | tf_op jit(solution)/shard_map/ppermute | solution.py:371
  7.5 1.6 %collective-permute-start = (bf16[784,128]{1,0:T(8,128)(2,1)}, bf16[784,128]{1,0:T(8,128)(2,1)S(1)}, u32[]{:S(2)}, u32[]{:S(2)}) collective-permute-start(bf16[784,128]{1,0:T(8,128)(2,1)} %shard_map.76.refs_0_), channel_id=1, source_target_pairs={{0,8},{8,0},{16,24},{24,16},{1,9},{9,1},{17,25},{25,17},{2,10},{10... | collective-permute-start | bytes 602120 | tf_op jit(solution)/shard_map/ppermute | solution.py:371
  9.1 0.0 copy-done.2
  9.1 0.0 copy-done.3
  9.1 0.4 collective-permute-start.4
  9.5 0.2 collective-permute-start.3
  9.7 9.0 %collective-permute-done.1.refs_0_ = bf16[784,128]{1,0:T(8,128)(2,1)S(1)} collective-permute-done((bf16[784,128]{1,0:T(8,128)(2,1)}, bf16[784,128]{1,0:T(8,128)(2,1)S(1)}, u32[]{:S(2)}, u32[]{:S(2)}) %collective-permute-start.1) | collective-permute-done | bytes 200736 | tf_op jit(solution)/shard_map/ppermute | solution.py:371
  18.7 1.2 %collective-permute-done.refs_1_ = bf16[784,128]{1,0:T(8,128)(2,1)S(1)} collective-permute-done((bf16[784,128]{1,0:T(8,128)(2,1)}, bf16[784,128]{1,0:T(8,128)(2,1)S(1)}, u32[]{:S(2)}, u32[]{:S(2)}) %collective-permute-start) | collective-permute-done | bytes 200736 | tf_op jit(solution)/shard_map/ppermute | solution.py:371
  19.9 0.0 collective-permute-start.2
  19.9 8.5 %collective-permute-done.4.refs_0_ = bf16[1024,128]{1,0:T(8,128)(2,1)S(1)} collective-permute-done((bf16[1024,128]{1,0:T(8,128)(2,1)S(1)}, bf16[1024,128]{1,0:T(8,128)(2,1)S(1)}, u32[]{:S(2)}, u32[]{:S(2)}) %collective-permute-start.4) | collective-permute-done | bytes 262176 | tf_op jit(solution)/shard_map/ppermute | solution.py:371
  28.4 1.6 %collective-permute-done.3.refs_1_.refs_5_ = bf16[1024,128]{1,0:T(8,128)(2,1)S(1)} collective-permute-done((bf16[1024,128]{1,0:T(8,128)(2,1)S(1)}, bf16[1024,128]{1,0:T(8,128)(2,1)S(1)}, u32[]{:S(2)}, u32[]{:S(2)}) %collective-permute-start.3) | collective-permute-done | bytes 262176 | tf_op jit(solution)/shard_map/ppermute | solution.py:371
  30.0 1.2 %collective-permute-start.5 = (bf16[1024,128]{1,0:T(8,128)(2,1)S(1)}, bf16[1024,128]{1,0:T(8,128)(2,1)S(1)}, u32[]{:S(2)}, u32[]{:S(2)}) collective-permute-start(bf16[1024,128]{1,0:T(8,128)(2,1)S(1)} %shard_map.78.refs_6_.refs_2_), channel_id=1, source_target_pairs={{0,8},{8,0},{16,24},{24,16},{1,9},{9,1},{17,25},{25,17},{2,10},{10... | collective-permute-start | bytes 786440 | tf_op jit(solution)/shard_map/ppermute | solution.py:371
  31.2 0.0 copy-done.1
  31.2 3.1 %collective-permute-done.2.refs_3_ = bf16[784,128]{1,0:T(8,128)(2,1)S(1)} collective-permute-done((bf16[784,128]{1,0:T(8,128)(2,1)S(1)}, bf16[784,128]{1,0:T(8,128)(2,1)S(1)}, u32[]{:S(2)}, u32[]{:S(2)}) %collective-permute-start.2) | collective-permute-done | bytes 200736 | tf_op jit(solution)/shard_map/ppermute | solution.py:371
  34.3 0.0 copy-start
  34.3 1.3 %shard_map.79 = (bf16[512,768]{1,0:T(8,128)(2,1)S(1)}, f32[3,128,384]{2,1,0:T(8,128)S(1)}, f32[3,128,384]{2,1,0:T(8,128)S(1)}) custom-call(s32[4,4]{1,0:T(4,128)S(1)} %maximum_convert_fusion.cols.cols_ref, bf16[784,128]{1,0:T(8,128)(2,1)S(1)} %copy-done.1, bf16[784,128]{1,0:T(8,128)(2,1)S(1)} %collective-permute-done.refs_1_, ...), custom_call_target="tpu_custom_call" | custom-call | flops 301989888 | bytes 4000000 | tf_op jit(solution)/shard_map/pallas_call | solution.py:313
  35.6 2.9 %collective-permute-done.5.km_last.refs_3_ = bf16[1024,128]{1,0:T(8,128)(2,1)S(1)} collective-permute-done((bf16[1024,128]{1,0:T(8,128)(2,1)S(1)}, bf16[1024,128]{1,0:T(8,128)(2,1)S(1)}, u32[]{:S(2)}, u32[]{:S(2)}) %collective-permute-start.5) | collective-permute-done | bytes 262176 | tf_op jit(solution)/shard_map/ppermute | solution.py:371
  38.4 1.0 %shard_map.81 = (f32[128,384]{1,0:T(8,128)S(1)}, f32[128,384]{1,0:T(8,128)S(1)}, f32[3,384]{1,0:T(4,128)S(1)}) custom-call(s32[4,4]{1,0:T(4,128)S(1)} %maximum_convert_fusion.cols.cols_ref, bf16[1024,128]{1,0:T(8,128)(2,1)S(1)} %collective-permute-done.5.km_last.refs_3_, bf16[512,768]{1,0:T(8,128)(2,1)S(1)} %get-tuple-element.22.placed, ...), custom_call_target="tpu_custom_call" | custom-call | flops 100663296 | bytes 4000000 | tf_op jit(solution)/shard_map/pallas_call | solution.py:313
  39.5 0.1 collective-permute-start.6
  39.6 1.2 %collective-permute-done.6 = f32[3,384]{1,0:T(4,128)S(1)} collective-permute-done((f32[3,384]{1,0:T(4,128)S(1)}, f32[3,384]{1,0:T(4,128)S(1)}, u32[]{:S(2)}, u32[]{:S(2)}) %collective-permute-start.6) | collective-permute-done | bytes 4640 | tf_op jit(solution)/shard_map/ppermute | solution.py:341
  40.8 2.6 %collective-permute-start.9 = (f32[3,384]{1,0:T(4,128)S(1)}, f32[3,384]{1,0:T(4,128)S(1)}, u32[]{:S(2)}, u32[]{:S(2)}) collective-permute-start(f32[3,384]{1,0:T(4,128)S(1)} %pad_maximum_fusion.1), channel_id=1, source_target_pairs={{0,6},{1,7},{2,4},{3,5},{4,2},{5,3},{6,0},{7,1},{8,14},{9,15},{10,... | collective-permute-start | bytes 13832 | tf_op jit(solution)/shard_map/ppermute | solution.py:344
  43.3 0.5 collective-permute-start.8
  43.8 0.5 collective-permute-start.7
  44.3 0.0 copy-done
  44.3 1.0 %shard_map.80.refs_4_ = f32[512,768]{1,0:T(8,128)S(1)} custom-call(bf16[512,768]{1,0:T(8,128)(2,1)S(1)} %get-tuple-element.22.placed, bf16[2,1152,768]{2,1,0:T(8,128)(2,1)S(1)} %copy-done), custom_call_target="tpu_custom_call" | custom-call | flops 603979776 | bytes 4000000 | tf_op jit(solution)/shard_map/pallas_call | solution.py:313
  45.3 0.1 collective-permute-done.9
  45.4 1.6 %collective-permute-done.8 = f32[3,384]{1,0:T(4,128)S(1)} collective-permute-done((f32[3,384]{1,0:T(4,128)S(1)}, f32[3,384]{1,0:T(4,128)S(1)}, u32[]{:S(2)}, u32[]{:S(2)}) %collective-permute-start.8) | collective-permute-done | bytes 4640 | tf_op jit(solution)/shard_map/ppermute | solution.py:344
  47.0 0.5 collective-permute-done.7
  47.5 1.9 %shard_map.82 = (bf16[512,768]{1,0:T(8,128)(2,1)S(1)}, f32[512,384]{1,0:T(8,128)S(1)}, f32[512,384]{1,0:T(8,128)S(1)}, f32[3,384]{1,0:T(4,128)S(1)}) custom-call(s32[4,4]{1,0:T(4,128)S(1)} %maximum_convert_fusion.cols.cols_ref, bf16[1024,128]{1,0:T(8,128)(2,1)S(1)} %pad_maximum_fusion.refs_4_.refs_0_, ...), custom_call_target="tpu_custom_call" | custom-call | flops 704643072 | bytes 4000000 | tf_op jit(solution)/shard_map/pallas_call | solution.py:313
  49.4 0.1 collective-permute-start.10
  49.5 1.2 %collective-permute-done.10 = f32[3,384]{1,0:T(4,128)S(1)} collective-permute-done((f32[3,384]{1,0:T(4,128)S(1)}, f32[3,384]{1,0:T(4,128)S(1)}, u32[]{:S(2)}, u32[]{:S(2)}) %collective-permute-start.10) | collective-permute-done | bytes 4640 | tf_op jit(solution)/shard_map/ppermute | solution.py:341
  50.7 1.6 %collective-permute-start.13 = (f32[3,384]{1,0:T(4,128)S(1)}, f32[3,384]{1,0:T(4,128)S(1)}, u32[]{:S(2)}, u32[]{:S(2)}) collective-permute-start(f32[3,384]{1,0:T(4,128)S(1)} %pad_maximum_fusion.3), channel_id=1, source_target_pairs={{0,6},{1,7},{2,4},{3,5},{4,2},{5,3},{6,0},{7,1},{8,14},{9,15},{10,... | collective-permute-start | bytes 13832 | tf_op jit(solution)/shard_map/ppermute | solution.py:344
  52.3 0.5 collective-permute-start.12
  52.7 1.5 %collective-permute-start.11 = (f32[3,384]{1,0:T(4,128)S(1)}, f32[3,384]{1,0:T(4,128)S(1)}, u32[]{:S(2)}, u32[]{:S(2)}) collective-permute-start(f32[3,384]{1,0:T(4,128)S(1)} %pad_maximum_fusion.3), channel_id=1, source_target_pairs={{0,2},{1,3},{2,0},{3,1},{4,6},{5,7},{6,4},{7,5},{8,10},{9,11},{10,... | collective-permute-start | bytes 13832 | tf_op jit(solution)/shard_map/ppermute | solution.py:344
  54.3 1.0 %collective-permute-done.13 = f32[3,384]{1,0:T(4,128)S(1)} collective-permute-done((f32[3,384]{1,0:T(4,128)S(1)}, f32[3,384]{1,0:T(4,128)S(1)}, u32[]{:S(2)}, u32[]{:S(2)}) %collective-permute-start.13) | collective-permute-done | bytes 4640 | tf_op jit(solution)/shard_map/ppermute | solution.py:344
  55.3 0.6 collective-permute-done.12
  55.9 0.5 collective-permute-done.11
  56.4 2.4 %shard_map.83 = (bf16[4,360,128]{2,1,0:T(8,128)(2,1)S(1)}, bf16[4,288,128]{2,1,0:T(8,128)(2,1)S(1)}, bf16[512,1152]{1,0:T(8,128)(2,1)S(1)}, bf16[1152,512]{1,0:T(8,128)(2,1)S(1)}, bf16[512,576]{1,0:T(8,128)(2,1)S(1)}) custom-call(s32[4,4]{1,0:T(4,128)S(1)} %maximum_convert_fusion.cols.cols_ref, bf16[1024,128]{1,0:T(8,128)(2,1)S(1)} %pad_maximum_fusion.refs_4_.refs_0_, ...), custom_call_target="tpu_custom_call" | custom-call | flops 339738624 | bytes 4000000 | tf_op jit(solution)/shard_map/pallas_call | solution.py:313
  58.8 0.1 collective-permute-start.18
  58.9 0.5 collective-permute-start.14
  59.4 0.7 shard_map.85
  60.1 0.4 collective-permute-done.18
  60.4 0.1 add_convert_fusion.1
  60.6 2.6 %collective-permute-start.21 = (bf16[288,128]{1,0:T(8,128)(2,1)S(1)}, bf16[288,128]{1,0:T(8,128)(2,1)S(1)}, u32[]{:S(2)}, u32[]{:S(2)}) collective-permute-start(bf16[288,128]{1,0:T(8,128)(2,1)S(1)} %get-tuple-element.53), channel_id=1, source_target_pairs={{0,6},{1,7},{2,4},{3,5},{4,2},{5,3},{6,0},{7,1},{8,14},{9,15},{10,... | collective-permute-start | bytes 221192 | tf_op jit(solution)/shard_map/ppermute | solution.py:502
  63.1 0.0 collective-permute-done.14
  63.1 0.1 add_convert_fusion
  63.3 0.5 collective-permute-start.17
  63.8 1.6 %collective-permute-start.16 = (bf16[360,128]{1,0:T(8,128)(2,1)S(1)}, bf16[360,128]{1,0:T(8,128)(2,1)S(1)}, u32[]{:S(2)}, u32[]{:S(2)}) collective-permute-start(bf16[360,128]{1,0:T(8,128)(2,1)S(1)} %get-tuple-element.50), channel_id=1, source_target_pairs={{0,4},{1,5},{2,6},{3,7},{4,0},{5,1},{6,2},{7,3},{8,12},{9,13},{10,... | collective-permute-start | bytes 276488 | tf_op jit(solution)/shard_map/ppermute | solution.py:502
  65.3 1.5 %collective-permute-start.15 = (bf16[360,128]{1,0:T(8,128)(2,1)S(1)}, bf16[360,128]{1,0:T(8,128)(2,1)S(1)}, u32[]{:S(2)}, u32[]{:S(2)}) collective-permute-start(bf16[360,128]{1,0:T(8,128)(2,1)S(1)} %get-tuple-element.51), channel_id=1, source_target_pairs={{0,2},{1,3},{2,0},{3,1},{4,6},{5,7},{6,4},{7,5},{8,10},{9,11},{10,... | collective-permute-start | bytes 276488 | tf_op jit(solution)/shard_map/ppermute | solution.py:502
  66.8 0.5 collective-permute-start.20
  67.3 0.0 collective-permute-done.21.refs_7_
  67.3 0.5 collective-permute-start.19
  67.8 0.7 %shard_map.84 = (bf16[128,1152]{1,0:T(8,128)(2,1)}, f32[1,384]{1,0:T(1,128)S(1)}) custom-call(f32[3,384]{1,0:T(4,128)S(1)} %pad_maximum_fusion.4.refs_7_.stats, bf16[512,1152]{1,0:T(8,128)(2,1)S(1)} %get-tuple-element.32.full), custom_call_target="tpu_custom_call" | custom-call | bytes 4000000 | tf_op jit(solution)/shard_map/pallas_call | solution.py:313
  68.6 0.6 reduce
  69.2 2.5 %collective-permute-done.20.refs_6_ = bf16[288,128]{1,0:T(8,128)(2,1)S(1)} collective-permute-done((bf16[288,128]{1,0:T(8,128)(2,1)S(1)}, bf16[288,128]{1,0:T(8,128)(2,1)S(1)}, u32[]{:S(2)}, u32[]{:S(2)}) %collective-permute-start.20) | collective-permute-done | bytes 73760 | tf_op jit(solution)/shard_map/ppermute | solution.py:502
  71.7 0.0 collective-permute-done.19.refs_5_
  71.7 0.0 collective-permute-done.17.refs_3_
  71.7 0.0 collective-permute-done.16.refs_2_
  71.7 0.0 collective-permute-done.15.refs_1_
  71.7 1.2 %shard_map.86 = f32[144,2,288]{2,1,0:T(2,128)} custom-call(bf16[360,128]{1,0:T(8,128)(2,1)S(1)} %get-tuple-element.52.refs_0_, bf16[360,128]{1,0:T(8,128)(2,1)S(1)} %collective-permute-done.15.refs_1_, bf16[360,128]{1,0:T(8,128)(2,1)S(1)} %collective-permute-done.16.refs_2_, bf16[360,128]{1,0:T(8,128)(2,1)S(1)} %collective-permute-done.17.refs_3_, ...), custom_call_target="tpu_custom_call" | custom-call | bytes 4000000 | tf_op jit(solution)/shard_map/pallas_call | solution.py:313
  (18 shorter events, 0.3 us)
Async XLA Ops:
  0.6 8.4 %copy-start.2 = (bf16[1,1,4,128,128]{4,3,2,1,0:T(8,128)(2,1)S(1)}, bf16[1,1,4,128,128]{4,3,2,1,0:T(8,128)(2,1)}, u32[]{:S(2)}) copy-start(bf16[1,1,4,128,128]{4,3,2,1,0:T(8,128)(2,1)} %param.8) | copy-start | bytes 393220
  0.6 8.4 %copy-start.3 = (bf16[1,1,4,128,128]{4,3,2,1,0:T(8,128)(2,1)S(1)}, bf16[1,1,4,128,128]{4,3,2,1,0:T(8,128)(2,1)}, u32[]{:S(2)}) copy-start(bf16[1,1,4,128,128]{4,3,2,1,0:T(8,128)(2,1)} %param.7) | copy-start | bytes 393220
  3.4 27.8 %copy-start.1 = (bf16[784,128]{1,0:T(8,128)(2,1)S(1)}, bf16[784,128]{1,0:T(8,128)(2,1)}, u32[]{:S(2)}) copy-start(bf16[784,128]{1,0:T(8,128)(2,1)} %shard_map.76.refs_0_) | copy-start | bytes 602116
  3.4 15.3 %collective-permute-start.1 = (bf16[784,128]{1,0:T(8,128)(2,1)}, bf16[784,128]{1,0:T(8,128)(2,1)S(1)}, u32[]{:S(2)}, u32[]{:S(2)}) collective-permute-start(bf16[784,128]{1,0:T(8,128)(2,1)} %shard_map.76.refs_0_), channel_id=1, source_target_pairs={{0,16},{8,24},{16,0},{24,8},{1,17},{9,25},{17,1},{25,9},{2,18},{10... | collective-permute-start | bytes 602120 | tf_op jit(solution)/shard_map/ppermute | solution.py:371
  7.5 12.4 %collective-permute-start = (bf16[784,128]{1,0:T(8,128)(2,1)}, bf16[784,128]{1,0:T(8,128)(2,1)S(1)}, u32[]{:S(2)}, u32[]{:S(2)}) collective-permute-start(bf16[784,128]{1,0:T(8,128)(2,1)} %shard_map.76.refs_0_), channel_id=1, source_target_pairs={{0,8},{8,0},{16,24},{24,16},{1,9},{9,1},{17,25},{25,17},{2,10},{10... | collective-permute-start | bytes 602120 | tf_op jit(solution)/shard_map/ppermute | solution.py:371
  9.1 19.3 %collective-permute-start.4 = (bf16[1024,128]{1,0:T(8,128)(2,1)S(1)}, bf16[1024,128]{1,0:T(8,128)(2,1)S(1)}, u32[]{:S(2)}, u32[]{:S(2)}) collective-permute-start(bf16[1024,128]{1,0:T(8,128)(2,1)S(1)} %pad_maximum_fusion.refs_4_.refs_0_), channel_id=1, source_target_pairs={{0,16},{8,24},{16,0},{24,8},{1,17},{9,25},{17,1},{25,9},{2,18},{10... | collective-permute-start | bytes 786440 | tf_op jit(solution)/shard_map/ppermute | solution.py:371
  9.5 20.5 %collective-permute-start.3 = (bf16[1024,128]{1,0:T(8,128)(2,1)S(1)}, bf16[1024,128]{1,0:T(8,128)(2,1)S(1)}, u32[]{:S(2)}, u32[]{:S(2)}) collective-permute-start(bf16[1024,128]{1,0:T(8,128)(2,1)S(1)} %pad_maximum_fusion.refs_4_.refs_0_), channel_id=1, source_target_pairs={{0,8},{8,0},{16,24},{24,16},{1,9},{9,1},{17,25},{25,17},{2,10},{10... | collective-permute-start | bytes 786440 | tf_op jit(solution)/shard_map/ppermute | solution.py:371
  19.9 14.4 %collective-permute-start.2 = (bf16[784,128]{1,0:T(8,128)(2,1)S(1)}, bf16[784,128]{1,0:T(8,128)(2,1)S(1)}, u32[]{:S(2)}, u32[]{:S(2)}) collective-permute-start(bf16[784,128]{1,0:T(8,128)(2,1)S(1)} %shard_map.77.refs_2_), channel_id=1, source_target_pairs={{0,8},{8,0},{16,24},{24,16},{1,9},{9,1},{17,25},{25,17},{2,10},{10... | collective-permute-start | bytes 602120 | tf_op jit(solution)/shard_map/ppermute | solution.py:371
  30.0 8.5 %collective-permute-start.5 = (bf16[1024,128]{1,0:T(8,128)(2,1)S(1)}, bf16[1024,128]{1,0:T(8,128)(2,1)S(1)}, u32[]{:S(2)}, u32[]{:S(2)}) collective-permute-start(bf16[1024,128]{1,0:T(8,128)(2,1)S(1)} %shard_map.78.refs_6_.refs_2_), channel_id=1, source_target_pairs={{0,8},{8,0},{16,24},{24,16},{1,9},{9,1},{17,25},{25,17},{2,10},{10... | collective-permute-start | bytes 786440 | tf_op jit(solution)/shard_map/ppermute | solution.py:371
  34.3 10.0 %copy-start = (bf16[2,1152,768]{2,1,0:T(8,128)(2,1)S(1)}, bf16[2,1152,768]{2,1,0:T(8,128)(2,1)}, u32[]{:S(2)}) copy-start(bf16[2,1152,768]{2,1,0:T(8,128)(2,1)} %refs_10_.1) | copy-start | bytes 10616836
  39.5 1.2 %collective-permute-start.6 = (f32[3,384]{1,0:T(4,128)S(1)}, f32[3,384]{1,0:T(4,128)S(1)}, u32[]{:S(2)}, u32[]{:S(2)}) collective-permute-start(f32[3,384]{1,0:T(4,128)S(1)} %get-tuple-element.27), channel_id=1, source_target_pairs={{0,1},{1,0},{2,3},{3,2},{4,5},{5,4},{6,7},{7,6},{8,9},{9,8},{10,11... | collective-permute-start | bytes 13832 | tf_op jit(solution)/shard_map/ppermute | solution.py:341
  40.8 4.6 %collective-permute-start.9 = (f32[3,384]{1,0:T(4,128)S(1)}, f32[3,384]{1,0:T(4,128)S(1)}, u32[]{:S(2)}, u32[]{:S(2)}) collective-permute-start(f32[3,384]{1,0:T(4,128)S(1)} %pad_maximum_fusion.1), channel_id=1, source_target_pairs={{0,6},{1,7},{2,4},{3,5},{4,2},{5,3},{6,0},{7,1},{8,14},{9,15},{10,... | collective-permute-start | bytes 13832 | tf_op jit(solution)/shard_map/ppermute | solution.py:344
  43.3 3.6 %collective-permute-start.8 = (f32[3,384]{1,0:T(4,128)S(1)}, f32[3,384]{1,0:T(4,128)S(1)}, u32[]{:S(2)}, u32[]{:S(2)}) collective-permute-start(f32[3,384]{1,0:T(4,128)S(1)} %pad_maximum_fusion.1), channel_id=1, source_target_pairs={{0,4},{1,5},{2,6},{3,7},{4,0},{5,1},{6,2},{7,3},{8,12},{9,13},{10,... | collective-permute-start | bytes 13832 | tf_op jit(solution)/shard_map/ppermute | solution.py:344
  43.8 3.6 %collective-permute-start.7 = (f32[3,384]{1,0:T(4,128)S(1)}, f32[3,384]{1,0:T(4,128)S(1)}, u32[]{:S(2)}, u32[]{:S(2)}) collective-permute-start(f32[3,384]{1,0:T(4,128)S(1)} %pad_maximum_fusion.1), channel_id=1, source_target_pairs={{0,2},{1,3},{2,0},{3,1},{4,6},{5,7},{6,4},{7,5},{8,10},{9,11},{10,... | collective-permute-start | bytes 13832 | tf_op jit(solution)/shard_map/ppermute | solution.py:344
  49.4 1.2 %collective-permute-start.10 = (f32[3,384]{1,0:T(4,128)S(1)}, f32[3,384]{1,0:T(4,128)S(1)}, u32[]{:S(2)}, u32[]{:S(2)}) collective-permute-start(f32[3,384]{1,0:T(4,128)S(1)} %get-tuple-element.28), channel_id=1, source_target_pairs={{0,1},{1,0},{2,3},{3,2},{4,5},{5,4},{6,7},{7,6},{8,9},{9,8},{10,11... | collective-permute-start | bytes 13832 | tf_op jit(solution)/shard_map/ppermute | solution.py:341
  50.7 4.6 %collective-permute-start.13 = (f32[3,384]{1,0:T(4,128)S(1)}, f32[3,384]{1,0:T(4,128)S(1)}, u32[]{:S(2)}, u32[]{:S(2)}) collective-permute-start(f32[3,384]{1,0:T(4,128)S(1)} %pad_maximum_fusion.3), channel_id=1, source_target_pairs={{0,6},{1,7},{2,4},{3,5},{4,2},{5,3},{6,0},{7,1},{8,14},{9,15},{10,... | collective-permute-start | bytes 13832 | tf_op jit(solution)/shard_map/ppermute | solution.py:344
  52.3 3.6 %collective-permute-start.12 = (f32[3,384]{1,0:T(4,128)S(1)}, f32[3,384]{1,0:T(4,128)S(1)}, u32[]{:S(2)}, u32[]{:S(2)}) collective-permute-start(f32[3,384]{1,0:T(4,128)S(1)} %pad_maximum_fusion.3), channel_id=1, source_target_pairs={{0,4},{1,5},{2,6},{3,7},{4,0},{5,1},{6,2},{7,3},{8,12},{9,13},{10,... | collective-permute-start | bytes 13832 | tf_op jit(solution)/shard_map/ppermute | solution.py:344
  52.7 3.6 %collective-permute-start.11 = (f32[3,384]{1,0:T(4,128)S(1)}, f32[3,384]{1,0:T(4,128)S(1)}, u32[]{:S(2)}, u32[]{:S(2)}) collective-permute-start(f32[3,384]{1,0:T(4,128)S(1)} %pad_maximum_fusion.3), channel_id=1, source_target_pairs={{0,2},{1,3},{2,0},{3,1},{4,6},{5,7},{6,4},{7,5},{8,10},{9,11},{10,... | collective-permute-start | bytes 13832 | tf_op jit(solution)/shard_map/ppermute | solution.py:344
  58.8 1.6 %collective-permute-start.18 = (bf16[4,288,128]{2,1,0:T(8,128)(2,1)S(1)}, bf16[4,288,128]{2,1,0:T(8,128)(2,1)S(1)}, u32[]{:S(2)}, u32[]{:S(2)}) collective-permute-start(bf16[4,288,128]{2,1,0:T(8,128)(2,1)S(1)} %get-tuple-element.40), channel_id=1, source_target_pairs={{0,1},{1,0},{2,3},{3,2},{4,5},{5,4},{6,7},{7,6},{8,9},{9,8},{10,11... | collective-permute-start | bytes 884744 | tf_op jit(solution)/shard_map/ppermute | solution.py:489
  58.9 4.2 %collective-permute-start.14 = (bf16[4,360,128]{2,1,0:T(8,128)(2,1)S(1)}, bf16[4,360,128]{2,1,0:T(8,128)(2,1)S(1)}, u32[]{:S(2)}, u32[]{:S(2)}) collective-permute-start(bf16[4,360,128]{2,1,0:T(8,128)(2,1)S(1)} %get-tuple-element.38), channel_id=1, source_target_pairs={{0,1},{1,0},{2,3},{3,2},{4,5},{5,4},{6,7},{7,6},{8,9},{9,8},{10,11... | collective-permute-start | bytes 1105928 | tf_op jit(solution)/shard_map/ppermute | solution.py:489
  60.6 6.8 %collective-permute-start.21 = (bf16[288,128]{1,0:T(8,128)(2,1)S(1)}, bf16[288,128]{1,0:T(8,128)(2,1)S(1)}, u32[]{:S(2)}, u32[]{:S(2)}) collective-permute-start(bf16[288,128]{1,0:T(8,128)(2,1)S(1)} %get-tuple-element.53), channel_id=1, source_target_pairs={{0,6},{1,7},{2,4},{3,5},{4,2},{5,3},{6,0},{7,1},{8,14},{9,15},{10,... | collective-permute-start | bytes 221192 | tf_op jit(solution)/shard_map/ppermute | solution.py:502
  63.3 8.4 %collective-permute-start.17 = (bf16[360,128]{1,0:T(8,128)(2,1)S(1)}, bf16[360,128]{1,0:T(8,128)(2,1)S(1)}, u32[]{:S(2)}, u32[]{:S(2)}) collective-permute-start(bf16[360,128]{1,0:T(8,128)(2,1)S(1)} %get-tuple-element.49), channel_id=1, source_target_pairs={{0,6},{1,7},{2,4},{3,5},{4,2},{5,3},{6,0},{7,1},{8,14},{9,15},{10,... | collective-permute-start | bytes 276488 | tf_op jit(solution)/shard_map/ppermute | solution.py:502
  63.8 7.9 %collective-permute-start.16 = (bf16[360,128]{1,0:T(8,128)(2,1)S(1)}, bf16[360,128]{1,0:T(8,128)(2,1)S(1)}, u32[]{:S(2)}, u32[]{:S(2)}) collective-permute-start(bf16[360,128]{1,0:T(8,128)(2,1)S(1)} %get-tuple-element.50), channel_id=1, source_target_pairs={{0,4},{1,5},{2,6},{3,7},{4,0},{5,1},{6,2},{7,3},{8,12},{9,13},{10,... | collective-permute-start | bytes 276488 | tf_op jit(solution)/shard_map/ppermute | solution.py:502
  65.3 6.4 %collective-permute-start.15 = (bf16[360,128]{1,0:T(8,128)(2,1)S(1)}, bf16[360,128]{1,0:T(8,128)(2,1)S(1)}, u32[]{:S(2)}, u32[]{:S(2)}) collective-permute-start(bf16[360,128]{1,0:T(8,128)(2,1)S(1)} %get-tuple-element.51), channel_id=1, source_target_pairs={{0,2},{1,3},{2,0},{3,1},{4,6},{5,7},{6,4},{7,5},{8,10},{9,11},{10,... | collective-permute-start | bytes 276488 | tf_op jit(solution)/shard_map/ppermute | solution.py:502
  66.8 4.8 %collective-permute-start.20 = (bf16[288,128]{1,0:T(8,128)(2,1)S(1)}, bf16[288,128]{1,0:T(8,128)(2,1)S(1)}, u32[]{:S(2)}, u32[]{:S(2)}) collective-permute-start(bf16[288,128]{1,0:T(8,128)(2,1)S(1)} %get-tuple-element.54), channel_id=1, source_target_pairs={{0,4},{1,5},{2,6},{3,7},{4,0},{5,1},{6,2},{7,3},{8,12},{9,13},{10,... | collective-permute-start | bytes 221192 | tf_op jit(solution)/shard_map/ppermute | solution.py:502
  67.3 4.4 %collective-permute-start.19 = (bf16[288,128]{1,0:T(8,128)(2,1)S(1)}, bf16[288,128]{1,0:T(8,128)(2,1)S(1)}, u32[]{:S(2)}, u32[]{:S(2)}) collective-permute-start(bf16[288,128]{1,0:T(8,128)(2,1)S(1)} %get-tuple-element.55), channel_id=1, source_target_pairs={{0,2},{1,3},{2,0},{3,1},{4,6},{5,7},{6,4},{7,5},{8,10},{9,11},{10,... | collective-permute-start | bytes 221192 | tf_op jit(solution)/shard_map/ppermute | solution.py:502

commit v14 on v13

--- a/solution.py
+++ b/solution.py
@@ -12,7 +12,7 @@
 f32 = jnp.float32
 bf16 = jnp.bfloat16
 VMEM_BYTES = 24 * 1024 * 1024
-FIRST_VMEM_BYTES = 61 * 1024 * 1024
+FIRST_VMEM_BYTES = 58 * 1024 * 1024
 
 
 def vmem():
@@ -119,7 +119,7 @@
     in_hbm = pl.BlockSpec(memory_space=pltpu.HBM)
     return pl.pallas_call(
         functools.partial(turn_kernel, chunks, copies_each),
-        out_shape=jax.ShapeDtypeStruct((2 * modes + 16, rows), bf16),
+        out_shape=pltpu.VMEM((2 * modes + 16, rows), bf16),
         in_specs=[in_hbm, in_hbm, in_hbm],
         out_specs=vmem(),
         scratch_shapes=[
@@ -247,9 +247,10 @@
 
 
 def finish_kernel(bounds, width, *refs):
-    *refs, out_ref = refs
+    *refs, out_hbm, out_ref, sems = refs
     each = len(refs) // len(bounds)
     whole = width // 128
+    writes = []
     for i, (low, high) in enumerate(bounds):
         size = high - low
         total = refs[i * each][...].astype(f32)
@@ -262,6 +263,11 @@
                 at = (op * whole + b) * size
                 out_ref[low:high, op, b * 128 : (b + 1) * 128] = total[at : at + size]
             out_ref[low:high, op, whole * 128 :] = left[:, op * 32 : (op + 1) * 32]
+        part = pl.ds(low, size)
+        writes.append(pltpu.make_async_copy(out_ref.at[part], out_hbm.at[part], sems.at[i]))
+        writes[-1].start()
+    for write in writes:
+        write.wait()
 
 
 def gram_kernel(nz, chips, slots, edge, modes, total_rows, bounds, cols_ref, *refs):
@@ -501,14 +507,17 @@
             pieces += [mine[0]] + [
                 lax.ppermute(mine[k], "grp", by_xor(ng, 2 * k)) for k in range(1, chips)
             ]
-        total = call(
+        total = pl.pallas_call(
             functools.partial(finish_kernel, bounds, width),
-            pieces,
-            0,
-            jax.ShapeDtypeStruct((block, 2, width), f32),
-            [],
-            0,
-        )
+            out_shape=jax.ShapeDtypeStruct((block, 2, width), f32),
+            in_specs=[vmem()] * len(pieces),
+            out_specs=pl.BlockSpec(memory_space=pl.ANY),
+            scratch_shapes=[
+                pltpu.VMEM((block, 2, width), f32),
+                pltpu.SemaphoreType.DMA((len(bounds),)),
+            ],
+            compiler_params=pltpu.CompilerParams(vmem_limit_bytes=VMEM_BYTES),
+        )(*pieces)
     else:
         total = lax.psum_scatter(grams[0], "grp", scatter_dimension=0, tiled=True)
         total = total.astype(f32).reshape(block, 2, width)

time: 73.1 us -> 72.3 us (0.989)
    pallas_call x0 -> x1, Pallas kernels: none -> 1.25 us  [body(): pl.pallas_call(functools.partial(finish_kernel, bounds, width), out_shape...]
    pallas_call x8 -> x7, Pallas kernels: 10.2 us -> 9.02 us  [call(): pl.pallas_call(kernel, out_shape=out_shape, in_specs=[smem()] * n_smem +...]
where the time goes in v14:
time: 72.3 us; the launch traced here: 72.1 us
  waiting for transfers between devices  35.5 us (49%)
  starting transfers between devices  22.4 us (31%)
  Pallas kernels  12.3 us (17%)
  other arithmetic  1.02 us (1%)
  between operations  0.82 us (1%)
    ppermute x6, waiting for transfers between devices, send(): return lax.ppermute(x, 'blk', by_xor(nz, step))  26 us
    pallas_call x7, Pallas kernels, call(): pl.pallas_call(kernel, out_shape=out_shape, in_specs=[smem()] * n_smem +...  9.02 us
    ppermute x6, starting transfers between devices, send(): return lax.ppermute(x, 'blk', by_xor(nz, step))  7.49 us
    ppermute x6, starting transfers between devices, merge_over(): got = [lax.ppermute(stats, axis, by_xor(size, 2 * k)) for k in (1, 2, 3)]  7.11 us
    ppermute x6, starting transfers between devices, body(): lax.ppermute(mine[k], 'grp', by_xor(ng, 2 * k))  7.11 us
    ppermute x6, waiting for transfers between devices, merge_over(): got = [lax.ppermute(stats, axis, by_xor(size, 2 * k)) for k in (1, 2, 3)]  4.25 us
    ppermute x6, waiting for transfers between devices, body(): lax.ppermute(mine[k], 'grp', by_xor(ng, 2 * k))  2.54 us
    ppermute x2, waiting for transfers between devices, merge_over(): stats = merge(stats, lax.ppermute(stats, axis, by_xor(size, 1)))  2.31 us
  transfers between devices with their start and end apart: 22, of which 16 were waited for; matrix products, arithmetic and copies ran while one was open for 1% of the time, Pallas kernels for 5%

profile of v14, /device:TPU:0, one launch (start us, length us, event | category | flops | bytes accessed | tf_op | source)
XLA Modules:
  0.0 72.1 jit_solution(8083291371491382534)
XLA Ops:
  0.6 0.0 copy-start.1
  0.6 0.0 copy-start.2
  0.7 2.0 %shard_map.76.refs_0_ = bf16[784,128]{1,0:T(8,128)(2,1)S(1)} custom-call(s32[1,4]{1,0:T(1,128)} %bitcast.24, bf16[128,1152]{1,0:T(8,128)(2,1)} %bitcast.21, bf16[2,1152,768]{2,1,0:T(8,128)(2,1)} %refs_10_.1), custom_call_target="tpu_custom_call" | custom-call | flops 226492416 | bytes 1769472 | tf_op jit(solution)/shard_map/pallas_call | solution.py:120
  2.7 4.1 %collective-permute-start.1 = (bf16[784,128]{1,0:T(8,128)(2,1)S(1)}, bf16[784,128]{1,0:T(8,128)(2,1)S(1)}, u32[]{:S(2)}, u32[]{:S(2)}) collective-permute-start(bf16[784,128]{1,0:T(8,128)(2,1)S(1)} %shard_map.76.refs_0_), channel_id=1, source_target_pairs={{0,16},{8,24},{16,0},{24,8},{1,17},{9,25},{17,1},{25,9},{2,18},{10... | collective-permute-start | bytes 602120 | tf_op jit(solution)/shard_map/ppermute | solution.py:377
  6.8 1.6 %collective-permute-start = (bf16[784,128]{1,0:T(8,128)(2,1)S(1)}, bf16[784,128]{1,0:T(8,128)(2,1)S(1)}, u32[]{:S(2)}, u32[]{:S(2)}) collective-permute-start(bf16[784,128]{1,0:T(8,128)(2,1)S(1)} %shard_map.76.refs_0_), channel_id=1, source_target_pairs={{0,8},{8,0},{16,24},{24,16},{1,9},{9,1},{17,25},{25,17},{2,10},{10... | collective-permute-start | bytes 602120 | tf_op jit(solution)/shard_map/ppermute | solution.py:377
  8.4 0.0 copy-done.1
  8.4 0.0 copy-done.2
  8.4 0.4 collective-permute-start.4
  8.8 0.2 collective-permute-start.3
  9.0 8.8 %collective-permute-done.1.refs_0_ = bf16[784,128]{1,0:T(8,128)(2,1)S(1)} collective-permute-done((bf16[784,128]{1,0:T(8,128)(2,1)S(1)}, bf16[784,128]{1,0:T(8,128)(2,1)S(1)}, u32[]{:S(2)}, u32[]{:S(2)}) %collective-permute-start.1) | collective-permute-done | bytes 200736 | tf_op jit(solution)/shard_map/ppermute | solution.py:377
  17.8 1.2 %collective-permute-done.refs_1_ = bf16[784,128]{1,0:T(8,128)(2,1)S(1)} collective-permute-done((bf16[784,128]{1,0:T(8,128)(2,1)S(1)}, bf16[784,128]{1,0:T(8,128)(2,1)S(1)}, u32[]{:S(2)}, u32[]{:S(2)}) %collective-permute-start) | collective-permute-done | bytes 200736 | tf_op jit(solution)/shard_map/ppermute | solution.py:377
  19.0 0.0 collective-permute-start.2
  19.0 8.5 %collective-permute-done.4.refs_0_ = bf16[1024,128]{1,0:T(8,128)(2,1)S(1)} collective-permute-done((bf16[1024,128]{1,0:T(8,128)(2,1)S(1)}, bf16[1024,128]{1,0:T(8,128)(2,1)S(1)}, u32[]{:S(2)}, u32[]{:S(2)}) %collective-permute-start.4) | collective-permute-done | bytes 262176 | tf_op jit(solution)/shard_map/ppermute | solution.py:377
  27.5 1.6 %collective-permute-done.3.refs_1_.refs_5_ = bf16[1024,128]{1,0:T(8,128)(2,1)S(1)} collective-permute-done((bf16[1024,128]{1,0:T(8,128)(2,1)S(1)}, bf16[1024,128]{1,0:T(8,128)(2,1)S(1)}, u32[]{:S(2)}, u32[]{:S(2)}) %collective-permute-start.3) | collective-permute-done | bytes 262176 | tf_op jit(solution)/shard_map/ppermute | solution.py:377
  29.1 1.2 %collective-permute-start.5 = (bf16[1024,128]{1,0:T(8,128)(2,1)S(1)}, bf16[1024,128]{1,0:T(8,128)(2,1)S(1)}, u32[]{:S(2)}, u32[]{:S(2)}) collective-permute-start(bf16[1024,128]{1,0:T(8,128)(2,1)S(1)} %shard_map.78.refs_6_.refs_2_), channel_id=1, source_target_pairs={{0,8},{8,0},{16,24},{24,16},{1,9},{9,1},{17,25},{25,17},{2,10},{10... | collective-permute-start | bytes 786440 | tf_op jit(solution)/shard_map/ppermute | solution.py:377
  30.3 3.1 %collective-permute-done.2.refs_3_ = bf16[784,128]{1,0:T(8,128)(2,1)S(1)} collective-permute-done((bf16[784,128]{1,0:T(8,128)(2,1)S(1)}, bf16[784,128]{1,0:T(8,128)(2,1)S(1)}, u32[]{:S(2)}, u32[]{:S(2)}) %collective-permute-start.2) | collective-permute-done | bytes 200736 | tf_op jit(solution)/shard_map/ppermute | solution.py:377
  33.4 0.0 copy-start
  33.4 1.3 %shard_map.79 = (bf16[512,768]{1,0:T(8,128)(2,1)S(1)}, f32[3,128,384]{2,1,0:T(8,128)S(1)}, f32[3,128,384]{2,1,0:T(8,128)S(1)}) custom-call(s32[4,4]{1,0:T(4,128)S(1)} %maximum_convert_fusion.cols.cols_ref, bf16[784,128]{1,0:T(8,128)(2,1)S(1)} %shard_map.76.refs_0_, bf16[784,128]{1,0:T(8,128)(2,1)S(1)} %collective-permute-done.refs_1_, ...), custom_call_target="tpu_custom_call" | custom-call | flops 301989888 | bytes 4000000 | tf_op jit(solution)/shard_map/pallas_call | solution.py:319
  34.7 2.8 %collective-permute-done.5.km_last.refs_3_ = bf16[1024,128]{1,0:T(8,128)(2,1)S(1)} collective-permute-done((bf16[1024,128]{1,0:T(8,128)(2,1)S(1)}, bf16[1024,128]{1,0:T(8,128)(2,1)S(1)}, u32[]{:S(2)}, u32[]{:S(2)}) %collective-permute-start.5) | collective-permute-done | bytes 262176 | tf_op jit(solution)/shard_map/ppermute | solution.py:377
  37.5 1.1 %shard_map.81 = (f32[128,384]{1,0:T(8,128)S(1)}, f32[128,384]{1,0:T(8,128)S(1)}, f32[3,384]{1,0:T(4,128)S(1)}) custom-call(s32[4,4]{1,0:T(4,128)S(1)} %maximum_convert_fusion.cols.cols_ref, bf16[1024,128]{1,0:T(8,128)(2,1)S(1)} %collective-permute-done.5.km_last.refs_3_, bf16[512,768]{1,0:T(8,128)(2,1)S(1)} %get-tuple-element.22.placed, ...), custom_call_target="tpu_custom_call" | custom-call | flops 100663296 | bytes 4000000 | tf_op jit(solution)/shard_map/pallas_call | solution.py:319
  38.6 0.1 collective-permute-start.6
  38.7 1.2 %collective-permute-done.6 = f32[3,384]{1,0:T(4,128)S(1)} collective-permute-done((f32[3,384]{1,0:T(4,128)S(1)}, f32[3,384]{1,0:T(4,128)S(1)}, u32[]{:S(2)}, u32[]{:S(2)}) %collective-permute-start.6) | collective-permute-done | bytes 4640 | tf_op jit(solution)/shard_map/ppermute | solution.py:347
  39.9 2.6 %collective-permute-start.9 = (f32[3,384]{1,0:T(4,128)S(1)}, f32[3,384]{1,0:T(4,128)S(1)}, u32[]{:S(2)}, u32[]{:S(2)}) collective-permute-start(f32[3,384]{1,0:T(4,128)S(1)} %pad_maximum_fusion.1), channel_id=1, source_target_pairs={{0,6},{1,7},{2,4},{3,5},{4,2},{5,3},{6,0},{7,1},{8,14},{9,15},{10,... | collective-permute-start | bytes 13832 | tf_op jit(solution)/shard_map/ppermute | solution.py:350
  42.4 0.5 collective-permute-start.8
  42.9 0.5 collective-permute-start.7
  43.4 0.0 copy-done
  43.4 1.0 %shard_map.80.refs_4_ = f32[512,768]{1,0:T(8,128)S(1)} custom-call(bf16[512,768]{1,0:T(8,128)(2,1)S(1)} %get-tuple-element.22.placed, bf16[2,1152,768]{2,1,0:T(8,128)(2,1)S(1)} %copy-done), custom_call_target="tpu_custom_call" | custom-call | flops 603979776 | bytes 4000000 | tf_op jit(solution)/shard_map/pallas_call | solution.py:319
  44.4 0.1 collective-permute-done.9
  44.5 1.6 %collective-permute-done.8 = f32[3,384]{1,0:T(4,128)S(1)} collective-permute-done((f32[3,384]{1,0:T(4,128)S(1)}, f32[3,384]{1,0:T(4,128)S(1)}, u32[]{:S(2)}, u32[]{:S(2)}) %collective-permute-start.8) | collective-permute-done | bytes 4640 | tf_op jit(solution)/shard_map/ppermute | solution.py:350
  46.1 0.5 collective-permute-done.7
  46.6 1.9 %shard_map.82 = (bf16[512,768]{1,0:T(8,128)(2,1)S(1)}, f32[512,384]{1,0:T(8,128)S(1)}, f32[512,384]{1,0:T(8,128)S(1)}, f32[3,384]{1,0:T(4,128)S(1)}) custom-call(s32[4,4]{1,0:T(4,128)S(1)} %maximum_convert_fusion.cols.cols_ref, bf16[1024,128]{1,0:T(8,128)(2,1)S(1)} %pad_maximum_fusion.refs_4_.refs_0_, ...), custom_call_target="tpu_custom_call" | custom-call | flops 704643072 | bytes 4000000 | tf_op jit(solution)/shard_map/pallas_call | solution.py:319
  48.6 0.1 collective-permute-start.10
  48.6 1.2 %collective-permute-done.10 = f32[3,384]{1,0:T(4,128)S(1)} collective-permute-done((f32[3,384]{1,0:T(4,128)S(1)}, f32[3,384]{1,0:T(4,128)S(1)}, u32[]{:S(2)}, u32[]{:S(2)}) %collective-permute-start.10) | collective-permute-done | bytes 4640 | tf_op jit(solution)/shard_map/ppermute | solution.py:347
  49.9 1.6 %collective-permute-start.13 = (f32[3,384]{1,0:T(4,128)S(1)}, f32[3,384]{1,0:T(4,128)S(1)}, u32[]{:S(2)}, u32[]{:S(2)}) collective-permute-start(f32[3,384]{1,0:T(4,128)S(1)} %pad_maximum_fusion.3), channel_id=1, source_target_pairs={{0,6},{1,7},{2,4},{3,5},{4,2},{5,3},{6,0},{7,1},{8,14},{9,15},{10,... | collective-permute-start | bytes 13832 | tf_op jit(solution)/shard_map/ppermute | solution.py:350
  51.4 0.5 collective-permute-start.12
  51.9 1.5 %collective-permute-start.11 = (f32[3,384]{1,0:T(4,128)S(1)}, f32[3,384]{1,0:T(4,128)S(1)}, u32[]{:S(2)}, u32[]{:S(2)}) collective-permute-start(f32[3,384]{1,0:T(4,128)S(1)} %pad_maximum_fusion.3), channel_id=1, source_target_pairs={{0,2},{1,3},{2,0},{3,1},{4,6},{5,7},{6,4},{7,5},{8,10},{9,11},{10,... | collective-permute-start | bytes 13832 | tf_op jit(solution)/shard_map/ppermute | solution.py:350
  53.4 1.0 %collective-permute-done.13 = f32[3,384]{1,0:T(4,128)S(1)} collective-permute-done((f32[3,384]{1,0:T(4,128)S(1)}, f32[3,384]{1,0:T(4,128)S(1)}, u32[]{:S(2)}, u32[]{:S(2)}) %collective-permute-start.13) | collective-permute-done | bytes 4640 | tf_op jit(solution)/shard_map/ppermute | solution.py:350
  54.4 0.6 collective-permute-done.12
  55.0 0.5 collective-permute-done.11
  55.6 2.4 %shard_map.83 = (bf16[4,360,128]{2,1,0:T(8,128)(2,1)S(1)}, bf16[4,288,128]{2,1,0:T(8,128)(2,1)S(1)}, bf16[512,1152]{1,0:T(8,128)(2,1)S(1)}, bf16[1152,512]{1,0:T(8,128)(2,1)S(1)}, bf16[512,576]{1,0:T(8,128)(2,1)S(1)}) custom-call(s32[4,4]{1,0:T(4,128)S(1)} %maximum_convert_fusion.cols.cols_ref, bf16[1024,128]{1,0:T(8,128)(2,1)S(1)} %pad_maximum_fusion.refs_4_.refs_0_, ...), custom_call_target="tpu_custom_call" | custom-call | flops 339738624 | bytes 4000000 | tf_op jit(solution)/shard_map/pallas_call | solution.py:319
  57.9 0.1 collective-permute-start.18
  58.0 0.5 collective-permute-start.14
  58.5 0.7 shard_map.85
  59.2 0.4 collective-permute-done.18
  59.6 0.1 add_convert_fusion.1
  59.7 2.6 %collective-permute-start.21 = (bf16[288,128]{1,0:T(8,128)(2,1)S(1)}, bf16[288,128]{1,0:T(8,128)(2,1)S(1)}, u32[]{:S(2)}, u32[]{:S(2)}) collective-permute-start(bf16[288,128]{1,0:T(8,128)(2,1)S(1)} %get-tuple-element.53), channel_id=1, source_target_pairs={{0,6},{1,7},{2,4},{3,5},{4,2},{5,3},{6,0},{7,1},{8,14},{9,15},{10,... | collective-permute-start | bytes 221192 | tf_op jit(solution)/shard_map/ppermute | solution.py:508
  62.3 0.0 collective-permute-done.14
  62.3 0.1 add_convert_fusion
  62.4 0.5 collective-permute-start.17
  62.9 1.6 %collective-permute-start.16 = (bf16[360,128]{1,0:T(8,128)(2,1)S(1)}, bf16[360,128]{1,0:T(8,128)(2,1)S(1)}, u32[]{:S(2)}, u32[]{:S(2)}) collective-permute-start(bf16[360,128]{1,0:T(8,128)(2,1)S(1)} %get-tuple-element.50), channel_id=1, source_target_pairs={{0,4},{1,5},{2,6},{3,7},{4,0},{5,1},{6,2},{7,3},{8,12},{9,13},{10,... | collective-permute-start | bytes 276488 | tf_op jit(solution)/shard_map/ppermute | solution.py:508
  64.5 1.5 %collective-permute-start.15 = (bf16[360,128]{1,0:T(8,128)(2,1)S(1)}, bf16[360,128]{1,0:T(8,128)(2,1)S(1)}, u32[]{:S(2)}, u32[]{:S(2)}) collective-permute-start(bf16[360,128]{1,0:T(8,128)(2,1)S(1)} %get-tuple-element.51), channel_id=1, source_target_pairs={{0,2},{1,3},{2,0},{3,1},{4,6},{5,7},{6,4},{7,5},{8,10},{9,11},{10,... | collective-permute-start | bytes 276488 | tf_op jit(solution)/shard_map/ppermute | solution.py:508
  66.0 0.5 collective-permute-start.20
  66.5 0.0 collective-permute-done.21.refs_7_
  66.5 0.5 collective-permute-start.19
  67.0 0.7 %shard_map.84 = (bf16[128,1152]{1,0:T(8,128)(2,1)}, f32[1,384]{1,0:T(1,128)S(1)}) custom-call(f32[3,384]{1,0:T(4,128)S(1)} %pad_maximum_fusion.4.refs_7_.stats, bf16[512,1152]{1,0:T(8,128)(2,1)S(1)} %get-tuple-element.32.full), custom_call_target="tpu_custom_call" | custom-call | bytes 4000000 | tf_op jit(solution)/shard_map/pallas_call | solution.py:319
  67.7 0.6 reduce
  68.3 2.5 %collective-permute-done.20.refs_6_ = bf16[288,128]{1,0:T(8,128)(2,1)S(1)} collective-permute-done((bf16[288,128]{1,0:T(8,128)(2,1)S(1)}, bf16[288,128]{1,0:T(8,128)(2,1)S(1)}, u32[]{:S(2)}, u32[]{:S(2)}) %collective-permute-start.20) | collective-permute-done | bytes 73760 | tf_op jit(solution)/shard_map/ppermute | solution.py:508
  70.8 0.0 collective-permute-done.19.refs_5_
  70.8 0.0 collective-permute-done.17.refs_3_
  70.8 0.0 collective-permute-done.16.refs_2_
  70.9 0.0 collective-permute-done.15.refs_1_
  70.9 1.2 %shard_map.86 = f32[144,2,288]{2,1,0:T(2,128)} custom-call(bf16[360,128]{1,0:T(8,128)(2,1)S(1)} %get-tuple-element.52.refs_0_, bf16[360,128]{1,0:T(8,128)(2,1)S(1)} %collective-permute-done.15.refs_1_, bf16[360,128]{1,0:T(8,128)(2,1)S(1)} %collective-permute-done.16.refs_2_, bf16[360,128]{1,0:T(8,128)(2,1)S(1)} %collective-permute-done.17.refs_3_, ...), custom_call_target="tpu_custom_call" | custom-call | tf_op jit(solution)/shard_map/pallas_call | solution.py:510
  (18 shorter events, 0.3 us)
Async XLA Ops:
  0.6 7.7 %copy-start.1 = (bf16[1,1,4,128,128]{4,3,2,1,0:T(8,128)(2,1)S(1)}, bf16[1,1,4,128,128]{4,3,2,1,0:T(8,128)(2,1)}, u32[]{:S(2)}) copy-start(bf16[1,1,4,128,128]{4,3,2,1,0:T(8,128)(2,1)} %param.8) | copy-start | bytes 393220
  0.6 7.7 %copy-start.2 = (bf16[1,1,4,128,128]{4,3,2,1,0:T(8,128)(2,1)S(1)}, bf16[1,1,4,128,128]{4,3,2,1,0:T(8,128)(2,1)}, u32[]{:S(2)}) copy-start(bf16[1,1,4,128,128]{4,3,2,1,0:T(8,128)(2,1)} %param.7) | copy-start | bytes 393220
  2.7 15.1 %collective-permute-start.1 = (bf16[784,128]{1,0:T(8,128)(2,1)S(1)}, bf16[784,128]{1,0:T(8,128)(2,1)S(1)}, u32[]{:S(2)}, u32[]{:S(2)}) collective-permute-start(bf16[784,128]{1,0:T(8,128)(2,1)S(1)} %shard_map.76.refs_0_), channel_id=1, source_target_pairs={{0,16},{8,24},{16,0},{24,8},{1,17},{9,25},{17,1},{25,9},{2,18},{10... | collective-permute-start | bytes 602120 | tf_op jit(solution)/shard_map/ppermute | solution.py:377
  6.8 12.2 %collective-permute-start = (bf16[784,128]{1,0:T(8,128)(2,1)S(1)}, bf16[784,128]{1,0:T(8,128)(2,1)S(1)}, u32[]{:S(2)}, u32[]{:S(2)}) collective-permute-start(bf16[784,128]{1,0:T(8,128)(2,1)S(1)} %shard_map.76.refs_0_), channel_id=1, source_target_pairs={{0,8},{8,0},{16,24},{24,16},{1,9},{9,1},{17,25},{25,17},{2,10},{10... | collective-permute-start | bytes 602120 | tf_op jit(solution)/shard_map/ppermute | solution.py:377
  8.4 19.1 %collective-permute-start.4 = (bf16[1024,128]{1,0:T(8,128)(2,1)S(1)}, bf16[1024,128]{1,0:T(8,128)(2,1)S(1)}, u32[]{:S(2)}, u32[]{:S(2)}) collective-permute-start(bf16[1024,128]{1,0:T(8,128)(2,1)S(1)} %pad_maximum_fusion.refs_4_.refs_0_), channel_id=1, source_target_pairs={{0,16},{8,24},{16,0},{24,8},{1,17},{9,25},{17,1},{25,9},{2,18},{10... | collective-permute-start | bytes 786440 | tf_op jit(solution)/shard_map/ppermute | solution.py:377
  8.8 20.3 %collective-permute-start.3 = (bf16[1024,128]{1,0:T(8,128)(2,1)S(1)}, bf16[1024,128]{1,0:T(8,128)(2,1)S(1)}, u32[]{:S(2)}, u32[]{:S(2)}) collective-permute-start(bf16[1024,128]{1,0:T(8,128)(2,1)S(1)} %pad_maximum_fusion.refs_4_.refs_0_), channel_id=1, source_target_pairs={{0,8},{8,0},{16,24},{24,16},{1,9},{9,1},{17,25},{25,17},{2,10},{10... | collective-permute-start | bytes 786440 | tf_op jit(solution)/shard_map/ppermute | solution.py:377
  19.0 14.4 %collective-permute-start.2 = (bf16[784,128]{1,0:T(8,128)(2,1)S(1)}, bf16[784,128]{1,0:T(8,128)(2,1)S(1)}, u32[]{:S(2)}, u32[]{:S(2)}) collective-permute-start(bf16[784,128]{1,0:T(8,128)(2,1)S(1)} %shard_map.77.refs_2_), channel_id=1, source_target_pairs={{0,8},{8,0},{16,24},{24,16},{1,9},{9,1},{17,25},{25,17},{2,10},{10... | collective-permute-start | bytes 602120 | tf_op jit(solution)/shard_map/ppermute | solution.py:377
  29.1 8.5 %collective-permute-start.5 = (bf16[1024,128]{1,0:T(8,128)(2,1)S(1)}, bf16[1024,128]{1,0:T(8,128)(2,1)S(1)}, u32[]{:S(2)}, u32[]{:S(2)}) collective-permute-start(bf16[1024,128]{1,0:T(8,128)(2,1)S(1)} %shard_map.78.refs_6_.refs_2_), channel_id=1, source_target_pairs={{0,8},{8,0},{16,24},{24,16},{1,9},{9,1},{17,25},{25,17},{2,10},{10... | collective-permute-start | bytes 786440 | tf_op jit(solution)/shard_map/ppermute | solution.py:377
  33.4 10.0 %copy-start = (bf16[2,1152,768]{2,1,0:T(8,128)(2,1)S(1)}, bf16[2,1152,768]{2,1,0:T(8,128)(2,1)}, u32[]{:S(2)}) copy-start(bf16[2,1152,768]{2,1,0:T(8,128)(2,1)} %refs_10_.1) | copy-start | bytes 10616836
  38.6 1.2 %collective-permute-start.6 = (f32[3,384]{1,0:T(4,128)S(1)}, f32[3,384]{1,0:T(4,128)S(1)}, u32[]{:S(2)}, u32[]{:S(2)}) collective-permute-start(f32[3,384]{1,0:T(4,128)S(1)} %get-tuple-element.27), channel_id=1, source_target_pairs={{0,1},{1,0},{2,3},{3,2},{4,5},{5,4},{6,7},{7,6},{8,9},{9,8},{10,11... | collective-permute-start | bytes 13832 | tf_op jit(solution)/shard_map/ppermute | solution.py:347
  39.9 4.6 %collective-permute-start.9 = (f32[3,384]{1,0:T(4,128)S(1)}, f32[3,384]{1,0:T(4,128)S(1)}, u32[]{:S(2)}, u32[]{:S(2)}) collective-permute-start(f32[3,384]{1,0:T(4,128)S(1)} %pad_maximum_fusion.1), channel_id=1, source_target_pairs={{0,6},{1,7},{2,4},{3,5},{4,2},{5,3},{6,0},{7,1},{8,14},{9,15},{10,... | collective-permute-start | bytes 13832 | tf_op jit(solution)/shard_map/ppermute | solution.py:350
  42.4 3.6 %collective-permute-start.8 = (f32[3,384]{1,0:T(4,128)S(1)}, f32[3,384]{1,0:T(4,128)S(1)}, u32[]{:S(2)}, u32[]{:S(2)}) collective-permute-start(f32[3,384]{1,0:T(4,128)S(1)} %pad_maximum_fusion.1), channel_id=1, source_target_pairs={{0,4},{1,5},{2,6},{3,7},{4,0},{5,1},{6,2},{7,3},{8,12},{9,13},{10,... | collective-permute-start | bytes 13832 | tf_op jit(solution)/shard_map/ppermute | solution.py:350
  42.9 3.6 %collective-permute-start.7 = (f32[3,384]{1,0:T(4,128)S(1)}, f32[3,384]{1,0:T(4,128)S(1)}, u32[]{:S(2)}, u32[]{:S(2)}) collective-permute-start(f32[3,384]{1,0:T(4,128)S(1)} %pad_maximum_fusion.1), channel_id=1, source_target_pairs={{0,2},{1,3},{2,0},{3,1},{4,6},{5,7},{6,4},{7,5},{8,10},{9,11},{10,... | collective-permute-start | bytes 13832 | tf_op jit(solution)/shard_map/ppermute | solution.py:350
  48.6 1.2 %collective-permute-start.10 = (f32[3,384]{1,0:T(4,128)S(1)}, f32[3,384]{1,0:T(4,128)S(1)}, u32[]{:S(2)}, u32[]{:S(2)}) collective-permute-start(f32[3,384]{1,0:T(4,128)S(1)} %get-tuple-element.28), channel_id=1, source_target_pairs={{0,1},{1,0},{2,3},{3,2},{4,5},{5,4},{6,7},{7,6},{8,9},{9,8},{10,11... | collective-permute-start | bytes 13832 | tf_op jit(solution)/shard_map/ppermute | solution.py:347
  49.9 4.6 %collective-permute-start.13 = (f32[3,384]{1,0:T(4,128)S(1)}, f32[3,384]{1,0:T(4,128)S(1)}, u32[]{:S(2)}, u32[]{:S(2)}) collective-permute-start(f32[3,384]{1,0:T(4,128)S(1)} %pad_maximum_fusion.3), channel_id=1, source_target_pairs={{0,6},{1,7},{2,4},{3,5},{4,2},{5,3},{6,0},{7,1},{8,14},{9,15},{10,... | collective-permute-start | bytes 13832 | tf_op jit(solution)/shard_map/ppermute | solution.py:350
  51.4 3.6 %collective-permute-start.12 = (f32[3,384]{1,0:T(4,128)S(1)}, f32[3,384]{1,0:T(4,128)S(1)}, u32[]{:S(2)}, u32[]{:S(2)}) collective-permute-start(f32[3,384]{1,0:T(4,128)S(1)} %pad_maximum_fusion.3), channel_id=1, source_target_pairs={{0,4},{1,5},{2,6},{3,7},{4,0},{5,1},{6,2},{7,3},{8,12},{9,13},{10,... | collective-permute-start | bytes 13832 | tf_op jit(solution)/shard_map/ppermute | solution.py:350
  51.9 3.6 %collective-permute-start.11 = (f32[3,384]{1,0:T(4,128)S(1)}, f32[3,384]{1,0:T(4,128)S(1)}, u32[]{:S(2)}, u32[]{:S(2)}) collective-permute-start(f32[3,384]{1,0:T(4,128)S(1)} %pad_maximum_fusion.3), channel_id=1, source_target_pairs={{0,2},{1,3},{2,0},{3,1},{4,6},{5,7},{6,4},{7,5},{8,10},{9,11},{10,... | collective-permute-start | bytes 13832 | tf_op jit(solution)/shard_map/ppermute | solution.py:350
  57.9 1.6 %collective-permute-start.18 = (bf16[4,288,128]{2,1,0:T(8,128)(2,1)S(1)}, bf16[4,288,128]{2,1,0:T(8,128)(2,1)S(1)}, u32[]{:S(2)}, u32[]{:S(2)}) collective-permute-start(bf16[4,288,128]{2,1,0:T(8,128)(2,1)S(1)} %get-tuple-element.40), channel_id=1, source_target_pairs={{0,1},{1,0},{2,3},{3,2},{4,5},{5,4},{6,7},{7,6},{8,9},{9,8},{10,11... | collective-permute-start | bytes 884744 | tf_op jit(solution)/shard_map/ppermute | solution.py:495
  58.0 4.3 %collective-permute-start.14 = (bf16[4,360,128]{2,1,0:T(8,128)(2,1)S(1)}, bf16[4,360,128]{2,1,0:T(8,128)(2,1)S(1)}, u32[]{:S(2)}, u32[]{:S(2)}) collective-permute-start(bf16[4,360,128]{2,1,0:T(8,128)(2,1)S(1)} %get-tuple-element.38), channel_id=1, source_target_pairs={{0,1},{1,0},{2,3},{3,2},{4,5},{5,4},{6,7},{7,6},{8,9},{9,8},{10,11... | collective-permute-start | bytes 1105928 | tf_op jit(solution)/shard_map/ppermute | solution.py:495
  59.7 6.8 %collective-permute-start.21 = (bf16[288,128]{1,0:T(8,128)(2,1)S(1)}, bf16[288,128]{1,0:T(8,128)(2,1)S(1)}, u32[]{:S(2)}, u32[]{:S(2)}) collective-permute-start(bf16[288,128]{1,0:T(8,128)(2,1)S(1)} %get-tuple-element.53), channel_id=1, source_target_pairs={{0,6},{1,7},{2,4},{3,5},{4,2},{5,3},{6,0},{7,1},{8,14},{9,15},{10,... | collective-permute-start | bytes 221192 | tf_op jit(solution)/shard_map/ppermute | solution.py:508
  62.4 8.4 %collective-permute-start.17 = (bf16[360,128]{1,0:T(8,128)(2,1)S(1)}, bf16[360,128]{1,0:T(8,128)(2,1)S(1)}, u32[]{:S(2)}, u32[]{:S(2)}) collective-permute-start(bf16[360,128]{1,0:T(8,128)(2,1)S(1)} %get-tuple-element.49), channel_id=1, source_target_pairs={{0,6},{1,7},{2,4},{3,5},{4,2},{5,3},{6,0},{7,1},{8,14},{9,15},{10,... | collective-permute-start | bytes 276488 | tf_op jit(solution)/shard_map/ppermute | solution.py:508
  62.9 7.9 %collective-permute-start.16 = (bf16[360,128]{1,0:T(8,128)(2,1)S(1)}, bf16[360,128]{1,0:T(8,128)(2,1)S(1)}, u32[]{:S(2)}, u32[]{:S(2)}) collective-permute-start(bf16[360,128]{1,0:T(8,128)(2,1)S(1)} %get-tuple-element.50), channel_id=1, source_target_pairs={{0,4},{1,5},{2,6},{3,7},{4,0},{5,1},{6,2},{7,3},{8,12},{9,13},{10,... | collective-permute-start | bytes 276488 | tf_op jit(solution)/shard_map/ppermute | solution.py:508
  64.5 6.4 %collective-permute-start.15 = (bf16[360,128]{1,0:T(8,128)(2,1)S(1)}, bf16[360,128]{1,0:T(8,128)(2,1)S(1)}, u32[]{:S(2)}, u32[]{:S(2)}) collective-permute-start(bf16[360,128]{1,0:T(8,128)(2,1)S(1)} %get-tuple-element.51), channel_id=1, source_target_pairs={{0,2},{1,3},{2,0},{3,1},{4,6},{5,7},{6,4},{7,5},{8,10},{9,11},{10,... | collective-permute-start | bytes 276488 | tf_op jit(solution)/shard_map/ppermute | solution.py:508
  66.0 4.8 %collective-permute-start.20 = (bf16[288,128]{1,0:T(8,128)(2,1)S(1)}, bf16[288,128]{1,0:T(8,128)(2,1)S(1)}, u32[]{:S(2)}, u32[]{:S(2)}) collective-permute-start(bf16[288,128]{1,0:T(8,128)(2,1)S(1)} %get-tuple-element.54), channel_id=1, source_target_pairs={{0,4},{1,5},{2,6},{3,7},{4,0},{5,1},{6,2},{7,3},{8,12},{9,13},{10,... | collective-permute-start | bytes 221192 | tf_op jit(solution)/shard_map/ppermute | solution.py:508
  66.5 4.4 %collective-permute-start.19 = (bf16[288,128]{1,0:T(8,128)(2,1)S(1)}, bf16[288,128]{1,0:T(8,128)(2,1)S(1)}, u32[]{:S(2)}, u32[]{:S(2)}) collective-permute-start(bf16[288,128]{1,0:T(8,128)(2,1)S(1)} %get-tuple-element.55), channel_id=1, source_target_pairs={{0,2},{1,3},{2,0},{3,1},{4,6},{5,7},{6,4},{7,5},{8,10},{9,11},{10,... | collective-permute-start | bytes 221192 | tf_op jit(solution)/shard_map/ppermute | solution.py:508

commit v15 on v14

--- a/solution.py
+++ b/solution.py
@@ -37,6 +37,21 @@
         jnp.concatenate(rows, axis=0),
         preferred_element_type=f32,
     )
+
+
+def merge_parts(one, two):
+    num, den = one[0] + two[0], one[1] + two[1]
+    apart = one[0] / jnp.maximum(one[1], tiny) - two[0] / jnp.maximum(two[1], tiny)
+    weight = jnp.sqrt(one[1]) * jnp.sqrt(two[1]) * lax.rsqrt(jnp.maximum(den, tiny))
+    gap = apart * weight
+    return num, den, (one[2] + two[2]) + gap * gap
+
+
+def own_stats(stiff_x, mass_x):
+    num = jnp.sum(stiff_x * mass_x, axis=0, keepdims=True)
+    den = jnp.sum(mass_x * mass_x, axis=0, keepdims=True)
+    rest = stiff_x - (num / jnp.maximum(den, tiny)) * mass_x
+    return num, den, jnp.sum(rest * rest, axis=0, keepdims=True)
 
 
 def shift_and_scale(stats, total_rows):
@@ -137,7 +152,7 @@
 
 def rows_kernel(nz, slots, edge, modes, cols, *refs):
     t_refs, km_refs = refs[:nz], refs[nz : 2 * nz - 1]
-    placed, stiff_ref, mass_ref = refs[2 * nz - 1 :]
+    placed, stiff_ref, mass_ref, some_ref = refs[2 * nz - 1 :]
     z = lax.axis_index("blk")
     for k in range(nz):
         at = pl.ds(pl.multiple_of((z ^ k) * edge, edge), edge)
@@ -147,6 +162,8 @@
         both = block_dot(km_refs[k], slots, edge, cols, k, placed, slice(0, modes))
         stiff_ref[k] = both[:edge]
         mass_ref[k] = both[edge:]
+        for row, value in enumerate(own_stats(both[:edge], both[edge:])):
+            some_ref[k, row : row + 1, :] = value
 
 
 def block_products(place, stiff_x, mass_x, sums):
@@ -170,21 +187,20 @@
 
 
 def stats_kernel(
-    nz, slots, edge, modes, cols_ref, km_last, placed, stiff, mass, stiff_ref, mass_ref, stats_ref, sums, cols, sem
+    nz, slots, edge, modes, cols_ref, km_last, placed, some, stiff_ref, mass_ref, stats_ref, cols, sem
 ):
     fetch = pltpu.make_async_copy(cols_ref, cols, sem)
     fetch.start()
-    z = lax.axis_index("blk")
-    sums[...] = jnp.zeros_like(sums)
-    for k in range(nz - 1):
-        block_products(z ^ k, stiff[k], mass[k], sums)
+    parts = [tuple(some[k, r : r + 1, :] for r in range(3)) for k in range(nz - 1)]
     fetch.wait()
     both = block_dot(km_last, slots, edge, cols, nz - 1, placed, slice(0, modes))
     stiff_ref[...] = both[:edge]
     mass_ref[...] = both[edge:]
-    block_products(z ^ (nz - 1), both[:edge], both[edge:], sums)
-    pairs = [(stiff[k], mass[k]) for k in range(nz - 1)] + [(both[:edge], both[edge:])]
-    block_stats(z, pairs, sums, stats_ref)
+    parts.append(own_stats(both[:edge], both[edge:]))
+    while len(parts) > 1:
+        parts = [merge_parts(*parts[k : k + 2]) for k in range(0, len(parts), 2)]
+    for row, value in enumerate(parts[0]):
+        stats_ref[row : row + 1, :] = value
 
 
 def early_turn_kernel(modes, placed, coeffs, out_ref):
@@ -334,11 +350,7 @@
 
 
 def merge(one, two):
-    num, den = one[0] + two[0], one[1] + two[1]
-    apart = one[0] / jnp.maximum(one[1], tiny) - two[0] / jnp.maximum(two[1], tiny)
-    weight = jnp.sqrt(one[1]) * jnp.sqrt(two[1]) * lax.rsqrt(jnp.maximum(den, tiny))
-    gap = apart * weight
-    return jnp.stack([num, den, (one[2] + two[2]) + gap * gap])
+    return jnp.stack(merge_parts(one, two))
 
 
 def merge_over(axis, size, stats):
@@ -415,21 +427,26 @@
     last = jax.ShapeDtypeStruct((edge, modes), f32)
     stats_shape = jax.ShapeDtypeStruct((3, modes), f32)
     work = 4 * edge * slots * edge * modes
-    placed, stiff_some, mass_some = call(
+    placed, stiff_some, mass_some, stats_some = call(
         functools.partial(rows_kernel, nz, slots, edge, modes),
         [cols, *t_parts, *km_parts[:-1]],
         1,
-        (jax.ShapeDtypeStruct((rows, 2 * modes), bf16), some, some),
+        (
+            jax.ShapeDtypeStruct((rows, 2 * modes), bf16),
+            some,
+            some,
+            jax.ShapeDtypeStruct((nz - 1, 8, modes), f32),
+        ),
         [],
         (nz - 1) * work,
     )
     fetched = [pltpu.SMEM((nz, slots), jnp.int32), pltpu.SemaphoreType.DMA(())]
     stiff_last, mass_last, stats = call(
         functools.partial(stats_kernel, nz, slots, edge, modes),
-        [cols, km_parts[-1], placed, stiff_some, mass_some],
+        [cols, km_parts[-1], placed, stats_some],
         0,
         (last, last, stats_shape),
-        [pltpu.VMEM((nz, 8, modes), f32), *fetched],
+        fetched,
         work,
         n_any=1,
     )

time: 72.3 us -> 72.1 us (level)
  no operation moved by 1% of the time
where the time goes in v15:
time: 72.1 us; the launch traced here: 72 us
  waiting for transfers between devices  35.4 us (49%)
  starting transfers between devices  22.4 us (31%)
  Pallas kernels  12.3 us (17%)
  other arithmetic  1 us (1%)
  between operations  0.81 us (1%)
    ppermute x6, waiting for transfers between devices, send(): return lax.ppermute(x, 'blk', by_xor(nz, step))  26 us
    pallas_call x7, Pallas kernels, call(): pl.pallas_call(kernel, out_shape=out_shape, in_specs=[smem()] * n_smem +...  8.97 us
    ppermute x6, starting transfers between devices, send(): return lax.ppermute(x, 'blk', by_xor(nz, step))  7.49 us
    ppermute x6, starting transfers between devices, body(): lax.ppermute(mine[k], 'grp', by_xor(ng, 2 * k))  7.11 us
    ppermute x6, starting transfers between devices, merge_over(): got = [lax.ppermute(stats, axis, by_xor(size, 2 * k)) for k in (1, 2, 3)]  7.11 us
    ppermute x6, waiting for transfers between devices, merge_over(): got = [lax.ppermute(stats, axis, by_xor(size, 2 * k)) for k in (1, 2, 3)]  4.25 us
    ppermute x6, waiting for transfers between devices, body(): lax.ppermute(mine[k], 'grp', by_xor(ng, 2 * k))  2.54 us
    ppermute x2, waiting for transfers between devices, merge_over(): stats = merge(stats, lax.ppermute(stats, axis, by_xor(size, 1)))  2.31 us
  transfers between devices with their start and end apart: 22, of which 16 were waited for; matrix products, arithmetic and copies ran while one was open for 1% of the time, Pallas kernels for 5%

profile of v15, /device:TPU:0, one launch (start us, length us, event | category | flops | bytes accessed | tf_op | source)
XLA Modules:
  0.0 72.0 jit_solution(10448605527611801814)
XLA Ops:
  0.6 0.0 copy-start.1
  0.6 0.0 copy-start.2
  0.7 2.0 %shard_map.76.refs_0_ = bf16[784,128]{1,0:T(8,128)(2,1)S(1)} custom-call(s32[1,4]{1,0:T(1,128)} %bitcast.24, bf16[128,1152]{1,0:T(8,128)(2,1)} %bitcast.21, bf16[2,1152,768]{2,1,0:T(8,128)(2,1)} %refs_10_.1), custom_call_target="tpu_custom_call" | custom-call | flops 226492416 | bytes 1769472 | tf_op jit(solution)/shard_map/pallas_call | solution.py:135
  2.7 4.1 %collective-permute-start.1 = (bf16[784,128]{1,0:T(8,128)(2,1)S(1)}, bf16[784,128]{1,0:T(8,128)(2,1)S(1)}, u32[]{:S(2)}, u32[]{:S(2)}) collective-permute-start(bf16[784,128]{1,0:T(8,128)(2,1)S(1)} %shard_map.76.refs_0_), channel_id=1, source_target_pairs={{0,16},{8,24},{16,0},{24,8},{1,17},{9,25},{17,1},{25,9},{2,18},{10... | collective-permute-start | bytes 602120 | tf_op jit(solution)/shard_map/ppermute | solution.py:389
  6.8 1.6 %collective-permute-start = (bf16[784,128]{1,0:T(8,128)(2,1)S(1)}, bf16[784,128]{1,0:T(8,128)(2,1)S(1)}, u32[]{:S(2)}, u32[]{:S(2)}) collective-permute-start(bf16[784,128]{1,0:T(8,128)(2,1)S(1)} %shard_map.76.refs_0_), channel_id=1, source_target_pairs={{0,8},{8,0},{16,24},{24,16},{1,9},{9,1},{17,25},{25,17},{2,10},{10... | collective-permute-start | bytes 602120 | tf_op jit(solution)/shard_map/ppermute | solution.py:389
  8.4 0.0 copy-done.1
  8.4 0.0 copy-done.2
  8.4 0.4 collective-permute-start.4
  8.8 0.2 collective-permute-start.3
  9.0 8.8 %collective-permute-done.1.refs_0_ = bf16[784,128]{1,0:T(8,128)(2,1)S(1)} collective-permute-done((bf16[784,128]{1,0:T(8,128)(2,1)S(1)}, bf16[784,128]{1,0:T(8,128)(2,1)S(1)}, u32[]{:S(2)}, u32[]{:S(2)}) %collective-permute-start.1) | collective-permute-done | bytes 200736 | tf_op jit(solution)/shard_map/ppermute | solution.py:389
  17.8 1.2 %collective-permute-done.refs_1_ = bf16[784,128]{1,0:T(8,128)(2,1)S(1)} collective-permute-done((bf16[784,128]{1,0:T(8,128)(2,1)S(1)}, bf16[784,128]{1,0:T(8,128)(2,1)S(1)}, u32[]{:S(2)}, u32[]{:S(2)}) %collective-permute-start) | collective-permute-done | bytes 200736 | tf_op jit(solution)/shard_map/ppermute | solution.py:389
  19.0 0.0 copy-start
  19.0 0.0 collective-permute-start.2
  19.0 8.5 %collective-permute-done.4.refs_0_ = bf16[1024,128]{1,0:T(8,128)(2,1)S(1)} collective-permute-done((bf16[1024,128]{1,0:T(8,128)(2,1)S(1)}, bf16[1024,128]{1,0:T(8,128)(2,1)S(1)}, u32[]{:S(2)}, u32[]{:S(2)}) %collective-permute-start.4) | collective-permute-done | bytes 262176 | tf_op jit(solution)/shard_map/ppermute | solution.py:389
  27.5 1.6 %collective-permute-done.3.refs_1_.refs_5_ = bf16[1024,128]{1,0:T(8,128)(2,1)S(1)} collective-permute-done((bf16[1024,128]{1,0:T(8,128)(2,1)S(1)}, bf16[1024,128]{1,0:T(8,128)(2,1)S(1)}, u32[]{:S(2)}, u32[]{:S(2)}) %collective-permute-start.3) | collective-permute-done | bytes 262176 | tf_op jit(solution)/shard_map/ppermute | solution.py:389
  29.1 1.2 %collective-permute-start.5 = (bf16[1024,128]{1,0:T(8,128)(2,1)S(1)}, bf16[1024,128]{1,0:T(8,128)(2,1)S(1)}, u32[]{:S(2)}, u32[]{:S(2)}) collective-permute-start(bf16[1024,128]{1,0:T(8,128)(2,1)S(1)} %shard_map.78.refs_6_.refs_2_), channel_id=1, source_target_pairs={{0,8},{8,0},{16,24},{24,16},{1,9},{9,1},{17,25},{25,17},{2,10},{10... | collective-permute-start | bytes 786440 | tf_op jit(solution)/shard_map/ppermute | solution.py:389
  30.3 3.1 %collective-permute-done.2.refs_3_ = bf16[784,128]{1,0:T(8,128)(2,1)S(1)} collective-permute-done((bf16[784,128]{1,0:T(8,128)(2,1)S(1)}, bf16[784,128]{1,0:T(8,128)(2,1)S(1)}, u32[]{:S(2)}, u32[]{:S(2)}) %collective-permute-start.2) | collective-permute-done | bytes 200736 | tf_op jit(solution)/shard_map/ppermute | solution.py:389
  33.4 1.3 %shard_map.79 = (bf16[512,768]{1,0:T(8,128)(2,1)S(1)}, f32[3,128,384]{2,1,0:T(8,128)S(1)}, f32[3,128,384]{2,1,0:T(8,128)S(1)}, f32[3,8,384]{2,1,0:T(8,128)S(1)}) custom-call(s32[4,4]{1,0:T(4,128)S(1)} %maximum_convert_fusion.cols.cols_ref, bf16[784,128]{1,0:T(8,128)(2,1)S(1)} %shard_map.76.refs_0_, bf16[784,128]{1,0:T(8,128)(2,1)S(1)} %collective-permute-done.refs_1_, ...), custom_call_target="tpu_custom_call" | custom-call | flops 301989888 | bytes 4000000 | tf_op jit(solution)/shard_map/pallas_call | solution.py:335
  34.7 2.8 %collective-permute-done.5.km_last.refs_3_ = bf16[1024,128]{1,0:T(8,128)(2,1)S(1)} collective-permute-done((bf16[1024,128]{1,0:T(8,128)(2,1)S(1)}, bf16[1024,128]{1,0:T(8,128)(2,1)S(1)}, u32[]{:S(2)}, u32[]{:S(2)}) %collective-permute-start.5) | collective-permute-done | bytes 262176 | tf_op jit(solution)/shard_map/ppermute | solution.py:389
  37.5 0.9 %shard_map.81 = (f32[128,384]{1,0:T(8,128)S(1)}, f32[128,384]{1,0:T(8,128)S(1)}, f32[3,384]{1,0:T(4,128)S(1)}) custom-call(s32[4,4]{1,0:T(4,128)S(1)} %maximum_convert_fusion.cols.cols_ref, bf16[1024,128]{1,0:T(8,128)(2,1)S(1)} %collective-permute-done.5.km_last.refs_3_, bf16[512,768]{1,0:T(8,128)(2,1)S(1)} %get-tuple-element.23.placed, ...), custom_call_target="tpu_custom_call" | custom-call | flops 100663296 | bytes 4000000 | tf_op jit(solution)/shard_map/pallas_call | solution.py:335
  38.5 0.1 collective-permute-start.6
  38.6 1.2 %collective-permute-done.6 = f32[3,384]{1,0:T(4,128)S(1)} collective-permute-done((f32[3,384]{1,0:T(4,128)S(1)}, f32[3,384]{1,0:T(4,128)S(1)}, u32[]{:S(2)}, u32[]{:S(2)}) %collective-permute-start.6) | collective-permute-done | bytes 4640 | tf_op jit(solution)/shard_map/ppermute | solution.py:359
  39.8 2.6 %collective-permute-start.9 = (f32[3,384]{1,0:T(4,128)S(1)}, f32[3,384]{1,0:T(4,128)S(1)}, u32[]{:S(2)}, u32[]{:S(2)}) collective-permute-start(f32[3,384]{1,0:T(4,128)S(1)} %pad_maximum_fusion.1), channel_id=1, source_target_pairs={{0,6},{1,7},{2,4},{3,5},{4,2},{5,3},{6,0},{7,1},{8,14},{9,15},{10,... | collective-permute-start | bytes 13832 | tf_op jit(solution)/shard_map/ppermute | solution.py:362
  42.3 0.5 collective-permute-start.8
  42.8 0.5 collective-permute-start.7
  43.3 0.0 copy-done
  43.3 1.0 %shard_map.80.refs_4_ = f32[512,768]{1,0:T(8,128)S(1)} custom-call(bf16[512,768]{1,0:T(8,128)(2,1)S(1)} %get-tuple-element.23.placed, bf16[2,1152,768]{2,1,0:T(8,128)(2,1)S(1)} %copy-done), custom_call_target="tpu_custom_call" | custom-call | flops 603979776 | bytes 4000000 | tf_op jit(solution)/shard_map/pallas_call | solution.py:335
  44.3 0.1 collective-permute-done.9
  44.4 1.6 %collective-permute-done.8 = f32[3,384]{1,0:T(4,128)S(1)} collective-permute-done((f32[3,384]{1,0:T(4,128)S(1)}, f32[3,384]{1,0:T(4,128)S(1)}, u32[]{:S(2)}, u32[]{:S(2)}) %collective-permute-start.8) | collective-permute-done | bytes 4640 | tf_op jit(solution)/shard_map/ppermute | solution.py:362
  46.0 0.5 collective-permute-done.7
  46.5 1.9 %shard_map.82 = (bf16[512,768]{1,0:T(8,128)(2,1)S(1)}, f32[512,384]{1,0:T(8,128)S(1)}, f32[512,384]{1,0:T(8,128)S(1)}, f32[3,384]{1,0:T(4,128)S(1)}) custom-call(s32[4,4]{1,0:T(4,128)S(1)} %maximum_convert_fusion.cols.cols_ref, bf16[1024,128]{1,0:T(8,128)(2,1)S(1)} %pad_maximum_fusion.refs_4_.refs_0_, ...), custom_call_target="tpu_custom_call" | custom-call | flops 704643072 | bytes 4000000 | tf_op jit(solution)/shard_map/pallas_call | solution.py:335
  48.5 0.1 collective-permute-start.10
  48.5 1.2 %collective-permute-done.10 = f32[3,384]{1,0:T(4,128)S(1)} collective-permute-done((f32[3,384]{1,0:T(4,128)S(1)}, f32[3,384]{1,0:T(4,128)S(1)}, u32[]{:S(2)}, u32[]{:S(2)}) %collective-permute-start.10) | collective-permute-done | bytes 4640 | tf_op jit(solution)/shard_map/ppermute | solution.py:359
  49.7 1.6 %collective-permute-start.13 = (f32[3,384]{1,0:T(4,128)S(1)}, f32[3,384]{1,0:T(4,128)S(1)}, u32[]{:S(2)}, u32[]{:S(2)}) collective-permute-start(f32[3,384]{1,0:T(4,128)S(1)} %pad_maximum_fusion.3), channel_id=1, source_target_pairs={{0,6},{1,7},{2,4},{3,5},{4,2},{5,3},{6,0},{7,1},{8,14},{9,15},{10,... | collective-permute-start | bytes 13832 | tf_op jit(solution)/shard_map/ppermute | solution.py:362
  51.3 0.5 collective-permute-start.12
  51.8 1.5 %collective-permute-start.11 = (f32[3,384]{1,0:T(4,128)S(1)}, f32[3,384]{1,0:T(4,128)S(1)}, u32[]{:S(2)}, u32[]{:S(2)}) collective-permute-start(f32[3,384]{1,0:T(4,128)S(1)} %pad_maximum_fusion.3), channel_id=1, source_target_pairs={{0,2},{1,3},{2,0},{3,1},{4,6},{5,7},{6,4},{7,5},{8,10},{9,11},{10,... | collective-permute-start | bytes 13832 | tf_op jit(solution)/shard_map/ppermute | solution.py:362
  53.3 1.0 %collective-permute-done.13 = f32[3,384]{1,0:T(4,128)S(1)} collective-permute-done((f32[3,384]{1,0:T(4,128)S(1)}, f32[3,384]{1,0:T(4,128)S(1)}, u32[]{:S(2)}, u32[]{:S(2)}) %collective-permute-start.13) | collective-permute-done | bytes 4640 | tf_op jit(solution)/shard_map/ppermute | solution.py:362
  54.3 0.6 collective-permute-done.12
  54.9 0.5 collective-permute-done.11
  55.5 2.4 %shard_map.83 = (bf16[4,360,128]{2,1,0:T(8,128)(2,1)S(1)}, bf16[4,288,128]{2,1,0:T(8,128)(2,1)S(1)}, bf16[512,1152]{1,0:T(8,128)(2,1)S(1)}, bf16[1152,512]{1,0:T(8,128)(2,1)S(1)}, bf16[512,576]{1,0:T(8,128)(2,1)S(1)}) custom-call(s32[4,4]{1,0:T(4,128)S(1)} %maximum_convert_fusion.cols.cols_ref, bf16[1024,128]{1,0:T(8,128)(2,1)S(1)} %pad_maximum_fusion.refs_4_.refs_0_, ...), custom_call_target="tpu_custom_call" | custom-call | flops 339738624 | bytes 4000000 | tf_op jit(solution)/shard_map/pallas_call | solution.py:335
  57.8 0.1 collective-permute-start.18
  57.9 0.5 collective-permute-start.14
  58.4 0.7 shard_map.85
  59.1 0.4 collective-permute-done.18
  59.5 0.1 add_convert_fusion.1
  59.6 2.6 %collective-permute-start.21 = (bf16[288,128]{1,0:T(8,128)(2,1)S(1)}, bf16[288,128]{1,0:T(8,128)(2,1)S(1)}, u32[]{:S(2)}, u32[]{:S(2)}) collective-permute-start(bf16[288,128]{1,0:T(8,128)(2,1)S(1)} %get-tuple-element.55), channel_id=1, source_target_pairs={{0,6},{1,7},{2,4},{3,5},{4,2},{5,3},{6,0},{7,1},{8,14},{9,15},{10,... | collective-permute-start | bytes 221192 | tf_op jit(solution)/shard_map/ppermute | solution.py:525
  62.2 0.0 collective-permute-done.14
  62.2 0.1 add_convert_fusion
  62.3 0.5 collective-permute-start.17
  62.8 1.6 %collective-permute-start.16 = (bf16[360,128]{1,0:T(8,128)(2,1)S(1)}, bf16[360,128]{1,0:T(8,128)(2,1)S(1)}, u32[]{:S(2)}, u32[]{:S(2)}) collective-permute-start(bf16[360,128]{1,0:T(8,128)(2,1)S(1)} %get-tuple-element.52), channel_id=1, source_target_pairs={{0,4},{1,5},{2,6},{3,7},{4,0},{5,1},{6,2},{7,3},{8,12},{9,13},{10,... | collective-permute-start | bytes 276488 | tf_op jit(solution)/shard_map/ppermute | solution.py:525
  64.4 1.5 %collective-permute-start.15 = (bf16[360,128]{1,0:T(8,128)(2,1)S(1)}, bf16[360,128]{1,0:T(8,128)(2,1)S(1)}, u32[]{:S(2)}, u32[]{:S(2)}) collective-permute-start(bf16[360,128]{1,0:T(8,128)(2,1)S(1)} %get-tuple-element.53), channel_id=1, source_target_pairs={{0,2},{1,3},{2,0},{3,1},{4,6},{5,7},{6,4},{7,5},{8,10},{9,11},{10,... | collective-permute-start | bytes 276488 | tf_op jit(solution)/shard_map/ppermute | solution.py:525
  65.9 0.5 collective-permute-start.20
  66.4 0.0 collective-permute-done.21.refs_7_
  66.4 0.5 collective-permute-start.19
  66.9 0.7 %shard_map.84 = (bf16[128,1152]{1,0:T(8,128)(2,1)}, f32[1,384]{1,0:T(1,128)S(1)}) custom-call(f32[3,384]{1,0:T(4,128)S(1)} %pad_maximum_fusion.4.refs_7_.stats, bf16[512,1152]{1,0:T(8,128)(2,1)S(1)} %get-tuple-element.34.full), custom_call_target="tpu_custom_call" | custom-call | bytes 4000000 | tf_op jit(solution)/shard_map/pallas_call | solution.py:335
  67.6 0.6 reduce
  68.2 2.5 %collective-permute-done.20.refs_6_ = bf16[288,128]{1,0:T(8,128)(2,1)S(1)} collective-permute-done((bf16[288,128]{1,0:T(8,128)(2,1)S(1)}, bf16[288,128]{1,0:T(8,128)(2,1)S(1)}, u32[]{:S(2)}, u32[]{:S(2)}) %collective-permute-start.20) | collective-permute-done | bytes 73760 | tf_op jit(solution)/shard_map/ppermute | solution.py:525
  70.7 0.0 collective-permute-done.19.refs_5_
  70.7 0.0 collective-permute-done.17.refs_3_
  70.7 0.0 collective-permute-done.16.refs_2_
  70.7 0.0 collective-permute-done.15.refs_1_
  70.7 1.2 %shard_map.86 = f32[144,2,288]{2,1,0:T(2,128)} custom-call(bf16[360,128]{1,0:T(8,128)(2,1)S(1)} %get-tuple-element.54.refs_0_, bf16[360,128]{1,0:T(8,128)(2,1)S(1)} %collective-permute-done.15.refs_1_, bf16[360,128]{1,0:T(8,128)(2,1)S(1)} %collective-permute-done.16.refs_2_, bf16[360,128]{1,0:T(8,128)(2,1)S(1)} %collective-permute-done.17.refs_3_, ...), custom_call_target="tpu_custom_call" | custom-call | tf_op jit(solution)/shard_map/pallas_call | solution.py:527
  (18 shorter events, 0.3 us)
Async XLA Ops:
  0.6 7.7 %copy-start.1 = (bf16[1,1,4,128,128]{4,3,2,1,0:T(8,128)(2,1)S(1)}, bf16[1,1,4,128,128]{4,3,2,1,0:T(8,128)(2,1)}, u32[]{:S(2)}) copy-start(bf16[1,1,4,128,128]{4,3,2,1,0:T(8,128)(2,1)} %param.8) | copy-start | bytes 393220
  0.6 7.7 %copy-start.2 = (bf16[1,1,4,128,128]{4,3,2,1,0:T(8,128)(2,1)S(1)}, bf16[1,1,4,128,128]{4,3,2,1,0:T(8,128)(2,1)}, u32[]{:S(2)}) copy-start(bf16[1,1,4,128,128]{4,3,2,1,0:T(8,128)(2,1)} %param.7) | copy-start | bytes 393220
  2.7 15.1 %collective-permute-start.1 = (bf16[784,128]{1,0:T(8,128)(2,1)S(1)}, bf16[784,128]{1,0:T(8,128)(2,1)S(1)}, u32[]{:S(2)}, u32[]{:S(2)}) collective-permute-start(bf16[784,128]{1,0:T(8,128)(2,1)S(1)} %shard_map.76.refs_0_), channel_id=1, source_target_pairs={{0,16},{8,24},{16,0},{24,8},{1,17},{9,25},{17,1},{25,9},{2,18},{10... | collective-permute-start | bytes 602120 | tf_op jit(solution)/shard_map/ppermute | solution.py:389
  6.8 12.2 %collective-permute-start = (bf16[784,128]{1,0:T(8,128)(2,1)S(1)}, bf16[784,128]{1,0:T(8,128)(2,1)S(1)}, u32[]{:S(2)}, u32[]{:S(2)}) collective-permute-start(bf16[784,128]{1,0:T(8,128)(2,1)S(1)} %shard_map.76.refs_0_), channel_id=1, source_target_pairs={{0,8},{8,0},{16,24},{24,16},{1,9},{9,1},{17,25},{25,17},{2,10},{10... | collective-permute-start | bytes 602120 | tf_op jit(solution)/shard_map/ppermute | solution.py:389
  8.4 19.1 %collective-permute-start.4 = (bf16[1024,128]{1,0:T(8,128)(2,1)S(1)}, bf16[1024,128]{1,0:T(8,128)(2,1)S(1)}, u32[]{:S(2)}, u32[]{:S(2)}) collective-permute-start(bf16[1024,128]{1,0:T(8,128)(2,1)S(1)} %pad_maximum_fusion.refs_4_.refs_0_), channel_id=1, source_target_pairs={{0,16},{8,24},{16,0},{24,8},{1,17},{9,25},{17,1},{25,9},{2,18},{10... | collective-permute-start | bytes 786440 | tf_op jit(solution)/shard_map/ppermute | solution.py:389
  8.8 20.3 %collective-permute-start.3 = (bf16[1024,128]{1,0:T(8,128)(2,1)S(1)}, bf16[1024,128]{1,0:T(8,128)(2,1)S(1)}, u32[]{:S(2)}, u32[]{:S(2)}) collective-permute-start(bf16[1024,128]{1,0:T(8,128)(2,1)S(1)} %pad_maximum_fusion.refs_4_.refs_0_), channel_id=1, source_target_pairs={{0,8},{8,0},{16,24},{24,16},{1,9},{9,1},{17,25},{25,17},{2,10},{10... | collective-permute-start | bytes 786440 | tf_op jit(solution)/shard_map/ppermute | solution.py:389
  19.0 24.3 %copy-start = (bf16[2,1152,768]{2,1,0:T(8,128)(2,1)S(1)}, bf16[2,1152,768]{2,1,0:T(8,128)(2,1)}, u32[]{:S(2)}) copy-start(bf16[2,1152,768]{2,1,0:T(8,128)(2,1)} %refs_10_.1) | copy-start | bytes 10616836
  19.0 14.4 %collective-permute-start.2 = (bf16[784,128]{1,0:T(8,128)(2,1)S(1)}, bf16[784,128]{1,0:T(8,128)(2,1)S(1)}, u32[]{:S(2)}, u32[]{:S(2)}) collective-permute-start(bf16[784,128]{1,0:T(8,128)(2,1)S(1)} %shard_map.77.refs_2_), channel_id=1, source_target_pairs={{0,8},{8,0},{16,24},{24,16},{1,9},{9,1},{17,25},{25,17},{2,10},{10... | collective-permute-start | bytes 602120 | tf_op jit(solution)/shard_map/ppermute | solution.py:389
  29.1 8.5 %collective-permute-start.5 = (bf16[1024,128]{1,0:T(8,128)(2,1)S(1)}, bf16[1024,128]{1,0:T(8,128)(2,1)S(1)}, u32[]{:S(2)}, u32[]{:S(2)}) collective-permute-start(bf16[1024,128]{1,0:T(8,128)(2,1)S(1)} %shard_map.78.refs_6_.refs_2_), channel_id=1, source_target_pairs={{0,8},{8,0},{16,24},{24,16},{1,9},{9,1},{17,25},{25,17},{2,10},{10... | collective-permute-start | bytes 786440 | tf_op jit(solution)/shard_map/ppermute | solution.py:389
  38.5 1.2 %collective-permute-start.6 = (f32[3,384]{1,0:T(4,128)S(1)}, f32[3,384]{1,0:T(4,128)S(1)}, u32[]{:S(2)}, u32[]{:S(2)}) collective-permute-start(f32[3,384]{1,0:T(4,128)S(1)} %get-tuple-element.29), channel_id=1, source_target_pairs={{0,1},{1,0},{2,3},{3,2},{4,5},{5,4},{6,7},{7,6},{8,9},{9,8},{10,11... | collective-permute-start | bytes 13832 | tf_op jit(solution)/shard_map/ppermute | solution.py:359
  39.8 4.6 %collective-permute-start.9 = (f32[3,384]{1,0:T(4,128)S(1)}, f32[3,384]{1,0:T(4,128)S(1)}, u32[]{:S(2)}, u32[]{:S(2)}) collective-permute-start(f32[3,384]{1,0:T(4,128)S(1)} %pad_maximum_fusion.1), channel_id=1, source_target_pairs={{0,6},{1,7},{2,4},{3,5},{4,2},{5,3},{6,0},{7,1},{8,14},{9,15},{10,... | collective-permute-start | bytes 13832 | tf_op jit(solution)/shard_map/ppermute | solution.py:362
  42.3 3.6 %collective-permute-start.8 = (f32[3,384]{1,0:T(4,128)S(1)}, f32[3,384]{1,0:T(4,128)S(1)}, u32[]{:S(2)}, u32[]{:S(2)}) collective-permute-start(f32[3,384]{1,0:T(4,128)S(1)} %pad_maximum_fusion.1), channel_id=1, source_target_pairs={{0,4},{1,5},{2,6},{3,7},{4,0},{5,1},{6,2},{7,3},{8,12},{9,13},{10,... | collective-permute-start | bytes 13832 | tf_op jit(solution)/shard_map/ppermute | solution.py:362
  42.8 3.6 %collective-permute-start.7 = (f32[3,384]{1,0:T(4,128)S(1)}, f32[3,384]{1,0:T(4,128)S(1)}, u32[]{:S(2)}, u32[]{:S(2)}) collective-permute-start(f32[3,384]{1,0:T(4,128)S(1)} %pad_maximum_fusion.1), channel_id=1, source_target_pairs={{0,2},{1,3},{2,0},{3,1},{4,6},{5,7},{6,4},{7,5},{8,10},{9,11},{10,... | collective-permute-start | bytes 13832 | tf_op jit(solution)/shard_map/ppermute | solution.py:362
  48.5 1.2 %collective-permute-start.10 = (f32[3,384]{1,0:T(4,128)S(1)}, f32[3,384]{1,0:T(4,128)S(1)}, u32[]{:S(2)}, u32[]{:S(2)}) collective-permute-start(f32[3,384]{1,0:T(4,128)S(1)} %get-tuple-element.30), channel_id=1, source_target_pairs={{0,1},{1,0},{2,3},{3,2},{4,5},{5,4},{6,7},{7,6},{8,9},{9,8},{10,11... | collective-permute-start | bytes 13832 | tf_op jit(solution)/shard_map/ppermute | solution.py:359
  49.7 4.6 %collective-permute-start.13 = (f32[3,384]{1,0:T(4,128)S(1)}, f32[3,384]{1,0:T(4,128)S(1)}, u32[]{:S(2)}, u32[]{:S(2)}) collective-permute-start(f32[3,384]{1,0:T(4,128)S(1)} %pad_maximum_fusion.3), channel_id=1, source_target_pairs={{0,6},{1,7},{2,4},{3,5},{4,2},{5,3},{6,0},{7,1},{8,14},{9,15},{10,... | collective-permute-start | bytes 13832 | tf_op jit(solution)/shard_map/ppermute | solution.py:362
  51.3 3.6 %collective-permute-start.12 = (f32[3,384]{1,0:T(4,128)S(1)}, f32[3,384]{1,0:T(4,128)S(1)}, u32[]{:S(2)}, u32[]{:S(2)}) collective-permute-start(f32[3,384]{1,0:T(4,128)S(1)} %pad_maximum_fusion.3), channel_id=1, source_target_pairs={{0,4},{1,5},{2,6},{3,7},{4,0},{5,1},{6,2},{7,3},{8,12},{9,13},{10,... | collective-permute-start | bytes 13832 | tf_op jit(solution)/shard_map/ppermute | solution.py:362
  51.8 3.6 %collective-permute-start.11 = (f32[3,384]{1,0:T(4,128)S(1)}, f32[3,384]{1,0:T(4,128)S(1)}, u32[]{:S(2)}, u32[]{:S(2)}) collective-permute-start(f32[3,384]{1,0:T(4,128)S(1)} %pad_maximum_fusion.3), channel_id=1, source_target_pairs={{0,2},{1,3},{2,0},{3,1},{4,6},{5,7},{6,4},{7,5},{8,10},{9,11},{10,... | collective-permute-start | bytes 13832 | tf_op jit(solution)/shard_map/ppermute | solution.py:362
  57.8 1.6 %collective-permute-start.18 = (bf16[4,288,128]{2,1,0:T(8,128)(2,1)S(1)}, bf16[4,288,128]{2,1,0:T(8,128)(2,1)S(1)}, u32[]{:S(2)}, u32[]{:S(2)}) collective-permute-start(bf16[4,288,128]{2,1,0:T(8,128)(2,1)S(1)} %get-tuple-element.42), channel_id=1, source_target_pairs={{0,1},{1,0},{2,3},{3,2},{4,5},{5,4},{6,7},{7,6},{8,9},{9,8},{10,11... | collective-permute-start | bytes 884744 | tf_op jit(solution)/shard_map/ppermute | solution.py:512
  57.9 4.2 %collective-permute-start.14 = (bf16[4,360,128]{2,1,0:T(8,128)(2,1)S(1)}, bf16[4,360,128]{2,1,0:T(8,128)(2,1)S(1)}, u32[]{:S(2)}, u32[]{:S(2)}) collective-permute-start(bf16[4,360,128]{2,1,0:T(8,128)(2,1)S(1)} %get-tuple-element.40), channel_id=1, source_target_pairs={{0,1},{1,0},{2,3},{3,2},{4,5},{5,4},{6,7},{7,6},{8,9},{9,8},{10,11... | collective-permute-start | bytes 1105928 | tf_op jit(solution)/shard_map/ppermute | solution.py:512
  59.6 6.8 %collective-permute-start.21 = (bf16[288,128]{1,0:T(8,128)(2,1)S(1)}, bf16[288,128]{1,0:T(8,128)(2,1)S(1)}, u32[]{:S(2)}, u32[]{:S(2)}) collective-permute-start(bf16[288,128]{1,0:T(8,128)(2,1)S(1)} %get-tuple-element.55), channel_id=1, source_target_pairs={{0,6},{1,7},{2,4},{3,5},{4,2},{5,3},{6,0},{7,1},{8,14},{9,15},{10,... | collective-permute-start | bytes 221192 | tf_op jit(solution)/shard_map/ppermute | solution.py:525
  62.3 8.4 %collective-permute-start.17 = (bf16[360,128]{1,0:T(8,128)(2,1)S(1)}, bf16[360,128]{1,0:T(8,128)(2,1)S(1)}, u32[]{:S(2)}, u32[]{:S(2)}) collective-permute-start(bf16[360,128]{1,0:T(8,128)(2,1)S(1)} %get-tuple-element.51), channel_id=1, source_target_pairs={{0,6},{1,7},{2,4},{3,5},{4,2},{5,3},{6,0},{7,1},{8,14},{9,15},{10,... | collective-permute-start | bytes 276488 | tf_op jit(solution)/shard_map/ppermute | solution.py:525
  62.8 7.9 %collective-permute-start.16 = (bf16[360,128]{1,0:T(8,128)(2,1)S(1)}, bf16[360,128]{1,0:T(8,128)(2,1)S(1)}, u32[]{:S(2)}, u32[]{:S(2)}) collective-permute-start(bf16[360,128]{1,0:T(8,128)(2,1)S(1)} %get-tuple-element.52), channel_id=1, source_target_pairs={{0,4},{1,5},{2,6},{3,7},{4,0},{5,1},{6,2},{7,3},{8,12},{9,13},{10,... | collective-permute-start | bytes 276488 | tf_op jit(solution)/shard_map/ppermute | solution.py:525
  64.4 6.4 %collective-permute-start.15 = (bf16[360,128]{1,0:T(8,128)(2,1)S(1)}, bf16[360,128]{1,0:T(8,128)(2,1)S(1)}, u32[]{:S(2)}, u32[]{:S(2)}) collective-permute-start(bf16[360,128]{1,0:T(8,128)(2,1)S(1)} %get-tuple-element.53), channel_id=1, source_target_pairs={{0,2},{1,3},{2,0},{3,1},{4,6},{5,7},{6,4},{7,5},{8,10},{9,11},{10,... | collective-permute-start | bytes 276488 | tf_op jit(solution)/shard_map/ppermute | solution.py:525
  65.9 4.8 %collective-permute-start.20 = (bf16[288,128]{1,0:T(8,128)(2,1)S(1)}, bf16[288,128]{1,0:T(8,128)(2,1)S(1)}, u32[]{:S(2)}, u32[]{:S(2)}) collective-permute-start(bf16[288,128]{1,0:T(8,128)(2,1)S(1)} %get-tuple-element.56), channel_id=1, source_target_pairs={{0,4},{1,5},{2,6},{3,7},{4,0},{5,1},{6,2},{7,3},{8,12},{9,13},{10,... | collective-permute-start | bytes 221192 | tf_op jit(solution)/shard_map/ppermute | solution.py:525
  66.4 4.4 %collective-permute-start.19 = (bf16[288,128]{1,0:T(8,128)(2,1)S(1)}, bf16[288,128]{1,0:T(8,128)(2,1)S(1)}, u32[]{:S(2)}, u32[]{:S(2)}) collective-permute-start(bf16[288,128]{1,0:T(8,128)(2,1)S(1)} %get-tuple-element.57), channel_id=1, source_target_pairs={{0,2},{1,3},{2,0},{3,1},{4,6},{5,7},{6,4},{7,5},{8,10},{9,11},{10,... | collective-permute-start | bytes 221192 | tf_op jit(solution)/shard_map/ppermute | solution.py:525

commit v16 on v15

--- a/solution.py
+++ b/solution.py
@@ -166,26 +166,6 @@
             some_ref[k, row : row + 1, :] = value
 
 
-def block_products(place, stiff_x, mass_x, sums):
-    sums[place, 0:1, :] = jnp.sum(stiff_x * mass_x, axis=0, keepdims=True)
-    sums[place, 1:2, :] = jnp.sum(mass_x * mass_x, axis=0, keepdims=True)
-
-
-def block_stats(z, pairs, sums, stats_ref):
-    total = sums[0]
-    for r in range(1, len(pairs)):
-        total = total + sums[r]
-    own_shift = total[0:1, :] / jnp.maximum(total[1:2, :], tiny)
-    for k, (stiff_x, mass_x) in enumerate(pairs):
-        rest = stiff_x - own_shift * mass_x
-        sums[z ^ k, 2:3, :] = jnp.sum(rest * rest, axis=0, keepdims=True)
-    about = sums[0, 2:3, :]
-    for r in range(1, len(pairs)):
-        about = about + sums[r, 2:3, :]
-    stats_ref[0:2, :] = total[0:2, :]
-    stats_ref[2:3, :] = about
-
-
 def stats_kernel(
     nz, slots, edge, modes, cols_ref, km_last, placed, some, stiff_ref, mass_ref, stats_ref, cols, sem
 ):
@@ -215,7 +195,7 @@
     fetch.start()
     km_refs = refs[:nz]
     early, stiff, mass, stiff_last, mass_last, stats, coeffs = refs[nz : nz + 7]
-    turned_ref, stiff_ref, mass_ref, stats_ref, search, sums = refs[nz + 7 :]
+    turned_ref, stiff_ref, mass_ref, stats_ref, search = refs[nz + 7 :]
     z = lax.axis_index("blk")
     at = [pl.ds(pl.multiple_of((z ^ k) * edge, edge), edge) for k in range(nz)]
     shift, scale = shift_and_scale(stats, total_rows)
@@ -225,16 +205,17 @@
         search[at[k], :] = ((stiff_x - shift * mass_x) * scale).astype(bf16)
     late = jnp.dot(search[...], coeffs[1, modes : 2 * modes, :], preferred_element_type=f32)
     turned_ref[...] = (early[...] + late).astype(bf16)
-    sums[...] = jnp.zeros_like(sums)
     fetch.wait()
-    pairs = []
+    parts = []
     for k in range(nz):
         both = block_dot(km_refs[k], slots, edge, cols, k, turned_ref, slice(0, modes))
         stiff_ref[at[k], :] = both[:edge]
         mass_ref[at[k], :] = both[edge:]
-        block_products(z ^ k, both[:edge], both[edge:], sums)
-        pairs.append((both[:edge], both[edge:]))
-    block_stats(z, pairs, sums, stats_ref)
+        parts.append(own_stats(both[:edge], both[edge:]))
+    while len(parts) > 1:
+        parts = [merge_parts(*parts[k : k + 2]) for k in range(0, len(parts), 2)]
+    for row, value in enumerate(parts[0]):
+        stats_ref[row : row + 1, :] = value
 
 
 def dense_order(width):
@@ -469,7 +450,7 @@
             jax.ShapeDtypeStruct((rows, modes), f32),
             stats_shape,
         ),
-        [pltpu.VMEM((rows, modes), bf16), pltpu.VMEM((nz, 8, modes), f32), *fetched],
+        [pltpu.VMEM((rows, modes), bf16), *fetched],
         4 * rows * modes * modes + nz * work,
         n_any=1,
     )

time: 72.1 us -> 72.1 us (level)
  no operation moved by 1% of the time
where the time goes in v16:
time: 72.1 us; the launch traced here: 71.9 us
  waiting for transfers between devices  35.4 us (49%)
  starting transfers between devices  22.4 us (31%)
  Pallas kernels  12.2 us (17%)
  other arithmetic  1 us (1%)
  between operations  0.81 us (1%)
    ppermute x6, waiting for transfers between devices, send(): return lax.ppermute(x, 'blk', by_xor(nz, step))  26 us
    pallas_call x7, Pallas kernels, call(): pl.pallas_call(kernel, out_shape=out_shape, in_specs=[smem()] * n_smem +...  8.9 us
    ppermute x6, starting transfers between devices, send(): return lax.ppermute(x, 'blk', by_xor(nz, step))  7.49 us
    ppermute x6, starting transfers between devices, merge_over(): got = [lax.ppermute(stats, axis, by_xor(size, 2 * k)) for k in (1, 2, 3)]  7.11 us
    ppermute x6, starting transfers between devices, body(): lax.ppermute(mine[k], 'grp', by_xor(ng, 2 * k))  7.11 us
    ppermute x6, waiting for transfers between devices, merge_over(): got = [lax.ppermute(stats, axis, by_xor(size, 2 * k)) for k in (1, 2, 3)]  4.25 us
    ppermute x6, waiting for transfers between devices, body(): lax.ppermute(mine[k], 'grp', by_xor(ng, 2 * k))  2.53 us
    ppermute x2, waiting for transfers between devices, merge_over(): stats = merge(stats, lax.ppermute(stats, axis, by_xor(size, 1)))  2.31 us
  transfers between devices with their start and end apart: 22, of which 16 were waited for; matrix products, arithmetic and copies ran while one was open for 1% of the time, Pallas kernels for 5%

profile of v16, /device:TPU:0, one launch (start us, length us, event | category | flops | bytes accessed | tf_op | source)
XLA Modules:
  0.0 71.9 jit_solution(15126852744652314699)
XLA Ops:
  0.6 0.0 copy-start.1
  0.6 0.0 copy-start.2
  0.7 2.0 %shard_map.76.refs_0_ = bf16[784,128]{1,0:T(8,128)(2,1)S(1)} custom-call(s32[1,4]{1,0:T(1,128)} %bitcast.24, bf16[128,1152]{1,0:T(8,128)(2,1)} %bitcast.21, bf16[2,1152,768]{2,1,0:T(8,128)(2,1)} %refs_10_.1), custom_call_target="tpu_custom_call" | custom-call | flops 226492416 | bytes 1769472 | tf_op jit(solution)/shard_map/pallas_call | solution.py:135
  2.7 4.1 %collective-permute-start.1 = (bf16[784,128]{1,0:T(8,128)(2,1)S(1)}, bf16[784,128]{1,0:T(8,128)(2,1)S(1)}, u32[]{:S(2)}, u32[]{:S(2)}) collective-permute-start(bf16[784,128]{1,0:T(8,128)(2,1)S(1)} %shard_map.76.refs_0_), channel_id=1, source_target_pairs={{0,16},{8,24},{16,0},{24,8},{1,17},{9,25},{17,1},{25,9},{2,18},{10... | collective-permute-start | bytes 602120 | tf_op jit(solution)/shard_map/ppermute | solution.py:370
  6.8 1.6 %collective-permute-start = (bf16[784,128]{1,0:T(8,128)(2,1)S(1)}, bf16[784,128]{1,0:T(8,128)(2,1)S(1)}, u32[]{:S(2)}, u32[]{:S(2)}) collective-permute-start(bf16[784,128]{1,0:T(8,128)(2,1)S(1)} %shard_map.76.refs_0_), channel_id=1, source_target_pairs={{0,8},{8,0},{16,24},{24,16},{1,9},{9,1},{17,25},{25,17},{2,10},{10... | collective-permute-start | bytes 602120 | tf_op jit(solution)/shard_map/ppermute | solution.py:370
  8.4 0.0 copy-done.1
  8.4 0.0 copy-done.2
  8.4 0.4 collective-permute-start.4
  8.8 0.2 collective-permute-start.3
  9.0 8.8 %collective-permute-done.1.refs_0_ = bf16[784,128]{1,0:T(8,128)(2,1)S(1)} collective-permute-done((bf16[784,128]{1,0:T(8,128)(2,1)S(1)}, bf16[784,128]{1,0:T(8,128)(2,1)S(1)}, u32[]{:S(2)}, u32[]{:S(2)}) %collective-permute-start.1) | collective-permute-done | bytes 200736 | tf_op jit(solution)/shard_map/ppermute | solution.py:370
  17.8 1.2 %collective-permute-done.refs_1_ = bf16[784,128]{1,0:T(8,128)(2,1)S(1)} collective-permute-done((bf16[784,128]{1,0:T(8,128)(2,1)S(1)}, bf16[784,128]{1,0:T(8,128)(2,1)S(1)}, u32[]{:S(2)}, u32[]{:S(2)}) %collective-permute-start) | collective-permute-done | bytes 200736 | tf_op jit(solution)/shard_map/ppermute | solution.py:370
  19.0 0.0 copy-start
  19.0 0.0 collective-permute-start.2
  19.0 8.5 %collective-permute-done.4.refs_0_ = bf16[1024,128]{1,0:T(8,128)(2,1)S(1)} collective-permute-done((bf16[1024,128]{1,0:T(8,128)(2,1)S(1)}, bf16[1024,128]{1,0:T(8,128)(2,1)S(1)}, u32[]{:S(2)}, u32[]{:S(2)}) %collective-permute-start.4) | collective-permute-done | bytes 262176 | tf_op jit(solution)/shard_map/ppermute | solution.py:370
  27.5 1.6 %collective-permute-done.3.refs_1_.refs_5_ = bf16[1024,128]{1,0:T(8,128)(2,1)S(1)} collective-permute-done((bf16[1024,128]{1,0:T(8,128)(2,1)S(1)}, bf16[1024,128]{1,0:T(8,128)(2,1)S(1)}, u32[]{:S(2)}, u32[]{:S(2)}) %collective-permute-start.3) | collective-permute-done | bytes 262176 | tf_op jit(solution)/shard_map/ppermute | solution.py:370
  29.1 1.2 %collective-permute-start.5 = (bf16[1024,128]{1,0:T(8,128)(2,1)S(1)}, bf16[1024,128]{1,0:T(8,128)(2,1)S(1)}, u32[]{:S(2)}, u32[]{:S(2)}) collective-permute-start(bf16[1024,128]{1,0:T(8,128)(2,1)S(1)} %shard_map.78.refs_6_.refs_2_), channel_id=1, source_target_pairs={{0,8},{8,0},{16,24},{24,16},{1,9},{9,1},{17,25},{25,17},{2,10},{10... | collective-permute-start | bytes 786440 | tf_op jit(solution)/shard_map/ppermute | solution.py:370
  30.3 3.1 %collective-permute-done.2.refs_3_ = bf16[784,128]{1,0:T(8,128)(2,1)S(1)} collective-permute-done((bf16[784,128]{1,0:T(8,128)(2,1)S(1)}, bf16[784,128]{1,0:T(8,128)(2,1)S(1)}, u32[]{:S(2)}, u32[]{:S(2)}) %collective-permute-start.2) | collective-permute-done | bytes 200736 | tf_op jit(solution)/shard_map/ppermute | solution.py:370
  33.4 1.3 %shard_map.79 = (bf16[512,768]{1,0:T(8,128)(2,1)S(1)}, f32[3,128,384]{2,1,0:T(8,128)S(1)}, f32[3,128,384]{2,1,0:T(8,128)S(1)}, f32[3,8,384]{2,1,0:T(8,128)S(1)}) custom-call(s32[4,4]{1,0:T(4,128)S(1)} %maximum_convert_fusion.cols.cols_ref, bf16[784,128]{1,0:T(8,128)(2,1)S(1)} %shard_map.76.refs_0_, bf16[784,128]{1,0:T(8,128)(2,1)S(1)} %collective-permute-done.refs_1_, ...), custom_call_target="tpu_custom_call" | custom-call | flops 301989888 | bytes 4000000 | tf_op jit(solution)/shard_map/pallas_call | solution.py:316
  34.7 2.8 %collective-permute-done.5.km_last.refs_3_ = bf16[1024,128]{1,0:T(8,128)(2,1)S(1)} collective-permute-done((bf16[1024,128]{1,0:T(8,128)(2,1)S(1)}, bf16[1024,128]{1,0:T(8,128)(2,1)S(1)}, u32[]{:S(2)}, u32[]{:S(2)}) %collective-permute-start.5) | collective-permute-done | bytes 262176 | tf_op jit(solution)/shard_map/ppermute | solution.py:370
  37.5 0.9 %shard_map.81 = (f32[128,384]{1,0:T(8,128)S(1)}, f32[128,384]{1,0:T(8,128)S(1)}, f32[3,384]{1,0:T(4,128)S(1)}) custom-call(s32[4,4]{1,0:T(4,128)S(1)} %maximum_convert_fusion.cols.cols_ref, bf16[1024,128]{1,0:T(8,128)(2,1)S(1)} %collective-permute-done.5.km_last.refs_3_, bf16[512,768]{1,0:T(8,128)(2,1)S(1)} %get-tuple-element.23.placed, ...), custom_call_target="tpu_custom_call" | custom-call | flops 100663296 | bytes 4000000 | tf_op jit(solution)/shard_map/pallas_call | solution.py:316
  38.5 0.1 collective-permute-start.6
  38.6 1.2 %collective-permute-done.6 = f32[3,384]{1,0:T(4,128)S(1)} collective-permute-done((f32[3,384]{1,0:T(4,128)S(1)}, f32[3,384]{1,0:T(4,128)S(1)}, u32[]{:S(2)}, u32[]{:S(2)}) %collective-permute-start.6) | collective-permute-done | bytes 4640 | tf_op jit(solution)/shard_map/ppermute | solution.py:340
  39.8 2.6 %collective-permute-start.9 = (f32[3,384]{1,0:T(4,128)S(1)}, f32[3,384]{1,0:T(4,128)S(1)}, u32[]{:S(2)}, u32[]{:S(2)}) collective-permute-start(f32[3,384]{1,0:T(4,128)S(1)} %pad_maximum_fusion.1), channel_id=1, source_target_pairs={{0,6},{1,7},{2,4},{3,5},{4,2},{5,3},{6,0},{7,1},{8,14},{9,15},{10,... | collective-permute-start | bytes 13832 | tf_op jit(solution)/shard_map/ppermute | solution.py:343
  42.3 0.5 collective-permute-start.8
  42.8 0.5 collective-permute-start.7
  43.3 0.0 copy-done
  43.3 1.0 %shard_map.80.refs_4_ = f32[512,768]{1,0:T(8,128)S(1)} custom-call(bf16[512,768]{1,0:T(8,128)(2,1)S(1)} %get-tuple-element.23.placed, bf16[2,1152,768]{2,1,0:T(8,128)(2,1)S(1)} %copy-done), custom_call_target="tpu_custom_call" | custom-call | flops 603979776 | bytes 4000000 | tf_op jit(solution)/shard_map/pallas_call | solution.py:316
  44.3 0.1 collective-permute-done.9
  44.4 1.6 %collective-permute-done.8 = f32[3,384]{1,0:T(4,128)S(1)} collective-permute-done((f32[3,384]{1,0:T(4,128)S(1)}, f32[3,384]{1,0:T(4,128)S(1)}, u32[]{:S(2)}, u32[]{:S(2)}) %collective-permute-start.8) | collective-permute-done | bytes 4640 | tf_op jit(solution)/shard_map/ppermute | solution.py:343
  46.0 0.5 collective-permute-done.7
  46.5 1.8 %shard_map.82 = (bf16[512,768]{1,0:T(8,128)(2,1)S(1)}, f32[512,384]{1,0:T(8,128)S(1)}, f32[512,384]{1,0:T(8,128)S(1)}, f32[3,384]{1,0:T(4,128)S(1)}) custom-call(s32[4,4]{1,0:T(4,128)S(1)} %maximum_convert_fusion.cols.cols_ref, bf16[1024,128]{1,0:T(8,128)(2,1)S(1)} %pad_maximum_fusion.refs_4_.refs_0_, ...), custom_call_target="tpu_custom_call" | custom-call | flops 704643072 | bytes 4000000 | tf_op jit(solution)/shard_map/pallas_call | solution.py:316
  48.4 0.1 collective-permute-start.10
  48.5 1.2 %collective-permute-done.10 = f32[3,384]{1,0:T(4,128)S(1)} collective-permute-done((f32[3,384]{1,0:T(4,128)S(1)}, f32[3,384]{1,0:T(4,128)S(1)}, u32[]{:S(2)}, u32[]{:S(2)}) %collective-permute-start.10) | collective-permute-done | bytes 4640 | tf_op jit(solution)/shard_map/ppermute | solution.py:340
  49.7 1.6 %collective-permute-start.13 = (f32[3,384]{1,0:T(4,128)S(1)}, f32[3,384]{1,0:T(4,128)S(1)}, u32[]{:S(2)}, u32[]{:S(2)}) collective-permute-start(f32[3,384]{1,0:T(4,128)S(1)} %pad_maximum_fusion.3), channel_id=1, source_target_pairs={{0,6},{1,7},{2,4},{3,5},{4,2},{5,3},{6,0},{7,1},{8,14},{9,15},{10,... | collective-permute-start | bytes 13832 | tf_op jit(solution)/shard_map/ppermute | solution.py:343
  51.2 0.5 collective-permute-start.12
  51.7 1.5 %collective-permute-start.11 = (f32[3,384]{1,0:T(4,128)S(1)}, f32[3,384]{1,0:T(4,128)S(1)}, u32[]{:S(2)}, u32[]{:S(2)}) collective-permute-start(f32[3,384]{1,0:T(4,128)S(1)} %pad_maximum_fusion.3), channel_id=1, source_target_pairs={{0,2},{1,3},{2,0},{3,1},{4,6},{5,7},{6,4},{7,5},{8,10},{9,11},{10,... | collective-permute-start | bytes 13832 | tf_op jit(solution)/shard_map/ppermute | solution.py:343
  53.2 1.0 %collective-permute-done.13 = f32[3,384]{1,0:T(4,128)S(1)} collective-permute-done((f32[3,384]{1,0:T(4,128)S(1)}, f32[3,384]{1,0:T(4,128)S(1)}, u32[]{:S(2)}, u32[]{:S(2)}) %collective-permute-start.13) | collective-permute-done | bytes 4640 | tf_op jit(solution)/shard_map/ppermute | solution.py:343
  54.3 0.6 collective-permute-done.12
  54.9 0.5 collective-permute-done.11
  55.4 2.4 %shard_map.83 = (bf16[4,360,128]{2,1,0:T(8,128)(2,1)S(1)}, bf16[4,288,128]{2,1,0:T(8,128)(2,1)S(1)}, bf16[512,1152]{1,0:T(8,128)(2,1)S(1)}, bf16[1152,512]{1,0:T(8,128)(2,1)S(1)}, bf16[512,576]{1,0:T(8,128)(2,1)S(1)}) custom-call(s32[4,4]{1,0:T(4,128)S(1)} %maximum_convert_fusion.cols.cols_ref, bf16[1024,128]{1,0:T(8,128)(2,1)S(1)} %pad_maximum_fusion.refs_4_.refs_0_, ...), custom_call_target="tpu_custom_call" | custom-call | flops 339738624 | bytes 4000000 | tf_op jit(solution)/shard_map/pallas_call | solution.py:316
  57.8 0.1 collective-permute-start.18
  57.8 0.5 collective-permute-start.14
  58.3 0.7 shard_map.85
  59.0 0.4 collective-permute-done.18
  59.4 0.1 add_convert_fusion.1
  59.5 2.6 %collective-permute-start.21 = (bf16[288,128]{1,0:T(8,128)(2,1)S(1)}, bf16[288,128]{1,0:T(8,128)(2,1)S(1)}, u32[]{:S(2)}, u32[]{:S(2)}) collective-permute-start(bf16[288,128]{1,0:T(8,128)(2,1)S(1)} %get-tuple-element.55), channel_id=1, source_target_pairs={{0,6},{1,7},{2,4},{3,5},{4,2},{5,3},{6,0},{7,1},{8,14},{9,15},{10,... | collective-permute-start | bytes 221192 | tf_op jit(solution)/shard_map/ppermute | solution.py:506
  62.1 0.0 collective-permute-done.14
  62.1 0.1 add_convert_fusion
  62.2 0.5 collective-permute-start.17
  62.7 1.6 %collective-permute-start.16 = (bf16[360,128]{1,0:T(8,128)(2,1)S(1)}, bf16[360,128]{1,0:T(8,128)(2,1)S(1)}, u32[]{:S(2)}, u32[]{:S(2)}) collective-permute-start(bf16[360,128]{1,0:T(8,128)(2,1)S(1)} %get-tuple-element.52), channel_id=1, source_target_pairs={{0,4},{1,5},{2,6},{3,7},{4,0},{5,1},{6,2},{7,3},{8,12},{9,13},{10,... | collective-permute-start | bytes 276488 | tf_op jit(solution)/shard_map/ppermute | solution.py:506
  64.3 1.5 %collective-permute-start.15 = (bf16[360,128]{1,0:T(8,128)(2,1)S(1)}, bf16[360,128]{1,0:T(8,128)(2,1)S(1)}, u32[]{:S(2)}, u32[]{:S(2)}) collective-permute-start(bf16[360,128]{1,0:T(8,128)(2,1)S(1)} %get-tuple-element.53), channel_id=1, source_target_pairs={{0,2},{1,3},{2,0},{3,1},{4,6},{5,7},{6,4},{7,5},{8,10},{9,11},{10,... | collective-permute-start | bytes 276488 | tf_op jit(solution)/shard_map/ppermute | solution.py:506
  65.8 0.5 collective-permute-start.20
  66.3 0.0 collective-permute-done.21.refs_7_
  66.3 0.5 collective-permute-start.19
  66.8 0.7 %shard_map.84 = (bf16[128,1152]{1,0:T(8,128)(2,1)}, f32[1,384]{1,0:T(1,128)S(1)}) custom-call(f32[3,384]{1,0:T(4,128)S(1)} %pad_maximum_fusion.4.refs_7_.stats, bf16[512,1152]{1,0:T(8,128)(2,1)S(1)} %get-tuple-element.34.full), custom_call_target="tpu_custom_call" | custom-call | bytes 4000000 | tf_op jit(solution)/shard_map/pallas_call | solution.py:316
  67.5 0.6 reduce
  68.1 2.5 %collective-permute-done.20.refs_6_ = bf16[288,128]{1,0:T(8,128)(2,1)S(1)} collective-permute-done((bf16[288,128]{1,0:T(8,128)(2,1)S(1)}, bf16[288,128]{1,0:T(8,128)(2,1)S(1)}, u32[]{:S(2)}, u32[]{:S(2)}) %collective-permute-start.20) | collective-permute-done | bytes 73760 | tf_op jit(solution)/shard_map/ppermute | solution.py:506
  70.6 0.0 collective-permute-done.19.refs_5_
  70.7 0.0 collective-permute-done.17.refs_3_
  70.7 0.0 collective-permute-done.16.refs_2_
  70.7 0.0 collective-permute-done.15.refs_1_
  70.7 1.2 %shard_map.86 = f32[144,2,288]{2,1,0:T(2,128)} custom-call(bf16[360,128]{1,0:T(8,128)(2,1)S(1)} %get-tuple-element.54.refs_0_, bf16[360,128]{1,0:T(8,128)(2,1)S(1)} %collective-permute-done.15.refs_1_, bf16[360,128]{1,0:T(8,128)(2,1)S(1)} %collective-permute-done.16.refs_2_, bf16[360,128]{1,0:T(8,128)(2,1)S(1)} %collective-permute-done.17.refs_3_, ...), custom_call_target="tpu_custom_call" | custom-call | tf_op jit(solution)/shard_map/pallas_call | solution.py:508
  (18 shorter events, 0.3 us)
Async XLA Ops:
  0.6 7.7 %copy-start.1 = (bf16[1,1,4,128,128]{4,3,2,1,0:T(8,128)(2,1)S(1)}, bf16[1,1,4,128,128]{4,3,2,1,0:T(8,128)(2,1)}, u32[]{:S(2)}) copy-start(bf16[1,1,4,128,128]{4,3,2,1,0:T(8,128)(2,1)} %param.8) | copy-start | bytes 393220
  0.6 7.7 %copy-start.2 = (bf16[1,1,4,128,128]{4,3,2,1,0:T(8,128)(2,1)S(1)}, bf16[1,1,4,128,128]{4,3,2,1,0:T(8,128)(2,1)}, u32[]{:S(2)}) copy-start(bf16[1,1,4,128,128]{4,3,2,1,0:T(8,128)(2,1)} %param.7) | copy-start | bytes 393220
  2.7 15.1 %collective-permute-start.1 = (bf16[784,128]{1,0:T(8,128)(2,1)S(1)}, bf16[784,128]{1,0:T(8,128)(2,1)S(1)}, u32[]{:S(2)}, u32[]{:S(2)}) collective-permute-start(bf16[784,128]{1,0:T(8,128)(2,1)S(1)} %shard_map.76.refs_0_), channel_id=1, source_target_pairs={{0,16},{8,24},{16,0},{24,8},{1,17},{9,25},{17,1},{25,9},{2,18},{10... | collective-permute-start | bytes 602120 | tf_op jit(solution)/shard_map/ppermute | solution.py:370
  6.8 12.2 %collective-permute-start = (bf16[784,128]{1,0:T(8,128)(2,1)S(1)}, bf16[784,128]{1,0:T(8,128)(2,1)S(1)}, u32[]{:S(2)}, u32[]{:S(2)}) collective-permute-start(bf16[784,128]{1,0:T(8,128)(2,1)S(1)} %shard_map.76.refs_0_), channel_id=1, source_target_pairs={{0,8},{8,0},{16,24},{24,16},{1,9},{9,1},{17,25},{25,17},{2,10},{10... | collective-permute-start | bytes 602120 | tf_op jit(solution)/shard_map/ppermute | solution.py:370
  8.4 19.1 %collective-permute-start.4 = (bf16[1024,128]{1,0:T(8,128)(2,1)S(1)}, bf16[1024,128]{1,0:T(8,128)(2,1)S(1)}, u32[]{:S(2)}, u32[]{:S(2)}) collective-permute-start(bf16[1024,128]{1,0:T(8,128)(2,1)S(1)} %pad_maximum_fusion.refs_4_.refs_0_), channel_id=1, source_target_pairs={{0,16},{8,24},{16,0},{24,8},{1,17},{9,25},{17,1},{25,9},{2,18},{10... | collective-permute-start | bytes 786440 | tf_op jit(solution)/shard_map/ppermute | solution.py:370
  8.8 20.3 %collective-permute-start.3 = (bf16[1024,128]{1,0:T(8,128)(2,1)S(1)}, bf16[1024,128]{1,0:T(8,128)(2,1)S(1)}, u32[]{:S(2)}, u32[]{:S(2)}) collective-permute-start(bf16[1024,128]{1,0:T(8,128)(2,1)S(1)} %pad_maximum_fusion.refs_4_.refs_0_), channel_id=1, source_target_pairs={{0,8},{8,0},{16,24},{24,16},{1,9},{9,1},{17,25},{25,17},{2,10},{10... | collective-permute-start | bytes 786440 | tf_op jit(solution)/shard_map/ppermute | solution.py:370
  19.0 24.3 %copy-start = (bf16[2,1152,768]{2,1,0:T(8,128)(2,1)S(1)}, bf16[2,1152,768]{2,1,0:T(8,128)(2,1)}, u32[]{:S(2)}) copy-start(bf16[2,1152,768]{2,1,0:T(8,128)(2,1)} %refs_10_.1) | copy-start | bytes 10616836
  19.0 14.4 %collective-permute-start.2 = (bf16[784,128]{1,0:T(8,128)(2,1)S(1)}, bf16[784,128]{1,0:T(8,128)(2,1)S(1)}, u32[]{:S(2)}, u32[]{:S(2)}) collective-permute-start(bf16[784,128]{1,0:T(8,128)(2,1)S(1)} %shard_map.77.refs_2_), channel_id=1, source_target_pairs={{0,8},{8,0},{16,24},{24,16},{1,9},{9,1},{17,25},{25,17},{2,10},{10... | collective-permute-start | bytes 602120 | tf_op jit(solution)/shard_map/ppermute | solution.py:370
  29.1 8.5 %collective-permute-start.5 = (bf16[1024,128]{1,0:T(8,128)(2,1)S(1)}, bf16[1024,128]{1,0:T(8,128)(2,1)S(1)}, u32[]{:S(2)}, u32[]{:S(2)}) collective-permute-start(bf16[1024,128]{1,0:T(8,128)(2,1)S(1)} %shard_map.78.refs_6_.refs_2_), channel_id=1, source_target_pairs={{0,8},{8,0},{16,24},{24,16},{1,9},{9,1},{17,25},{25,17},{2,10},{10... | collective-permute-start | bytes 786440 | tf_op jit(solution)/shard_map/ppermute | solution.py:370
  38.5 1.2 %collective-permute-start.6 = (f32[3,384]{1,0:T(4,128)S(1)}, f32[3,384]{1,0:T(4,128)S(1)}, u32[]{:S(2)}, u32[]{:S(2)}) collective-permute-start(f32[3,384]{1,0:T(4,128)S(1)} %get-tuple-element.29), channel_id=1, source_target_pairs={{0,1},{1,0},{2,3},{3,2},{4,5},{5,4},{6,7},{7,6},{8,9},{9,8},{10,11... | collective-permute-start | bytes 13832 | tf_op jit(solution)/shard_map/ppermute | solution.py:340
  39.8 4.6 %collective-permute-start.9 = (f32[3,384]{1,0:T(4,128)S(1)}, f32[3,384]{1,0:T(4,128)S(1)}, u32[]{:S(2)}, u32[]{:S(2)}) collective-permute-start(f32[3,384]{1,0:T(4,128)S(1)} %pad_maximum_fusion.1), channel_id=1, source_target_pairs={{0,6},{1,7},{2,4},{3,5},{4,2},{5,3},{6,0},{7,1},{8,14},{9,15},{10,... | collective-permute-start | bytes 13832 | tf_op jit(solution)/shard_map/ppermute | solution.py:343
  42.3 3.6 %collective-permute-start.8 = (f32[3,384]{1,0:T(4,128)S(1)}, f32[3,384]{1,0:T(4,128)S(1)}, u32[]{:S(2)}, u32[]{:S(2)}) collective-permute-start(f32[3,384]{1,0:T(4,128)S(1)} %pad_maximum_fusion.1), channel_id=1, source_target_pairs={{0,4},{1,5},{2,6},{3,7},{4,0},{5,1},{6,2},{7,3},{8,12},{9,13},{10,... | collective-permute-start | bytes 13832 | tf_op jit(solution)/shard_map/ppermute | solution.py:343
  42.8 3.6 %collective-permute-start.7 = (f32[3,384]{1,0:T(4,128)S(1)}, f32[3,384]{1,0:T(4,128)S(1)}, u32[]{:S(2)}, u32[]{:S(2)}) collective-permute-start(f32[3,384]{1,0:T(4,128)S(1)} %pad_maximum_fusion.1), channel_id=1, source_target_pairs={{0,2},{1,3},{2,0},{3,1},{4,6},{5,7},{6,4},{7,5},{8,10},{9,11},{10,... | collective-permute-start | bytes 13832 | tf_op jit(solution)/shard_map/ppermute | solution.py:343
  48.4 1.2 %collective-permute-start.10 = (f32[3,384]{1,0:T(4,128)S(1)}, f32[3,384]{1,0:T(4,128)S(1)}, u32[]{:S(2)}, u32[]{:S(2)}) collective-permute-start(f32[3,384]{1,0:T(4,128)S(1)} %get-tuple-element.30), channel_id=1, source_target_pairs={{0,1},{1,0},{2,3},{3,2},{4,5},{5,4},{6,7},{7,6},{8,9},{9,8},{10,11... | collective-permute-start | bytes 13832 | tf_op jit(solution)/shard_map/ppermute | solution.py:340
  49.7 4.6 %collective-permute-start.13 = (f32[3,384]{1,0:T(4,128)S(1)}, f32[3,384]{1,0:T(4,128)S(1)}, u32[]{:S(2)}, u32[]{:S(2)}) collective-permute-start(f32[3,384]{1,0:T(4,128)S(1)} %pad_maximum_fusion.3), channel_id=1, source_target_pairs={{0,6},{1,7},{2,4},{3,5},{4,2},{5,3},{6,0},{7,1},{8,14},{9,15},{10,... | collective-permute-start | bytes 13832 | tf_op jit(solution)/shard_map/ppermute | solution.py:343
  51.2 3.6 %collective-permute-start.12 = (f32[3,384]{1,0:T(4,128)S(1)}, f32[3,384]{1,0:T(4,128)S(1)}, u32[]{:S(2)}, u32[]{:S(2)}) collective-permute-start(f32[3,384]{1,0:T(4,128)S(1)} %pad_maximum_fusion.3), channel_id=1, source_target_pairs={{0,4},{1,5},{2,6},{3,7},{4,0},{5,1},{6,2},{7,3},{8,12},{9,13},{10,... | collective-permute-start | bytes 13832 | tf_op jit(solution)/shard_map/ppermute | solution.py:343
  51.7 3.6 %collective-permute-start.11 = (f32[3,384]{1,0:T(4,128)S(1)}, f32[3,384]{1,0:T(4,128)S(1)}, u32[]{:S(2)}, u32[]{:S(2)}) collective-permute-start(f32[3,384]{1,0:T(4,128)S(1)} %pad_maximum_fusion.3), channel_id=1, source_target_pairs={{0,2},{1,3},{2,0},{3,1},{4,6},{5,7},{6,4},{7,5},{8,10},{9,11},{10,... | collective-permute-start | bytes 13832 | tf_op jit(solution)/shard_map/ppermute | solution.py:343
  57.8 1.6 %collective-permute-start.18 = (bf16[4,288,128]{2,1,0:T(8,128)(2,1)S(1)}, bf16[4,288,128]{2,1,0:T(8,128)(2,1)S(1)}, u32[]{:S(2)}, u32[]{:S(2)}) collective-permute-start(bf16[4,288,128]{2,1,0:T(8,128)(2,1)S(1)} %get-tuple-element.42), channel_id=1, source_target_pairs={{0,1},{1,0},{2,3},{3,2},{4,5},{5,4},{6,7},{7,6},{8,9},{9,8},{10,11... | collective-permute-start | bytes 884744 | tf_op jit(solution)/shard_map/ppermute | solution.py:493
  57.8 4.2 %collective-permute-start.14 = (bf16[4,360,128]{2,1,0:T(8,128)(2,1)S(1)}, bf16[4,360,128]{2,1,0:T(8,128)(2,1)S(1)}, u32[]{:S(2)}, u32[]{:S(2)}) collective-permute-start(bf16[4,360,128]{2,1,0:T(8,128)(2,1)S(1)} %get-tuple-element.40), channel_id=1, source_target_pairs={{0,1},{1,0},{2,3},{3,2},{4,5},{5,4},{6,7},{7,6},{8,9},{9,8},{10,11... | collective-permute-start | bytes 1105928 | tf_op jit(solution)/shard_map/ppermute | solution.py:493
  59.5 6.8 %collective-permute-start.21 = (bf16[288,128]{1,0:T(8,128)(2,1)S(1)}, bf16[288,128]{1,0:T(8,128)(2,1)S(1)}, u32[]{:S(2)}, u32[]{:S(2)}) collective-permute-start(bf16[288,128]{1,0:T(8,128)(2,1)S(1)} %get-tuple-element.55), channel_id=1, source_target_pairs={{0,6},{1,7},{2,4},{3,5},{4,2},{5,3},{6,0},{7,1},{8,14},{9,15},{10,... | collective-permute-start | bytes 221192 | tf_op jit(solution)/shard_map/ppermute | solution.py:506
  62.2 8.4 %collective-permute-start.17 = (bf16[360,128]{1,0:T(8,128)(2,1)S(1)}, bf16[360,128]{1,0:T(8,128)(2,1)S(1)}, u32[]{:S(2)}, u32[]{:S(2)}) collective-permute-start(bf16[360,128]{1,0:T(8,128)(2,1)S(1)} %get-tuple-element.51), channel_id=1, source_target_pairs={{0,6},{1,7},{2,4},{3,5},{4,2},{5,3},{6,0},{7,1},{8,14},{9,15},{10,... | collective-permute-start | bytes 276488 | tf_op jit(solution)/shard_map/ppermute | solution.py:506
  62.7 7.9 %collective-permute-start.16 = (bf16[360,128]{1,0:T(8,128)(2,1)S(1)}, bf16[360,128]{1,0:T(8,128)(2,1)S(1)}, u32[]{:S(2)}, u32[]{:S(2)}) collective-permute-start(bf16[360,128]{1,0:T(8,128)(2,1)S(1)} %get-tuple-element.52), channel_id=1, source_target_pairs={{0,4},{1,5},{2,6},{3,7},{4,0},{5,1},{6,2},{7,3},{8,12},{9,13},{10,... | collective-permute-start | bytes 276488 | tf_op jit(solution)/shard_map/ppermute | solution.py:506
  64.3 6.4 %collective-permute-start.15 = (bf16[360,128]{1,0:T(8,128)(2,1)S(1)}, bf16[360,128]{1,0:T(8,128)(2,1)S(1)}, u32[]{:S(2)}, u32[]{:S(2)}) collective-permute-start(bf16[360,128]{1,0:T(8,128)(2,1)S(1)} %get-tuple-element.53), channel_id=1, source_target_pairs={{0,2},{1,3},{2,0},{3,1},{4,6},{5,7},{6,4},{7,5},{8,10},{9,11},{10,... | collective-permute-start | bytes 276488 | tf_op jit(solution)/shard_map/ppermute | solution.py:506
  65.8 4.8 %collective-permute-start.20 = (bf16[288,128]{1,0:T(8,128)(2,1)S(1)}, bf16[288,128]{1,0:T(8,128)(2,1)S(1)}, u32[]{:S(2)}, u32[]{:S(2)}) collective-permute-start(bf16[288,128]{1,0:T(8,128)(2,1)S(1)} %get-tuple-element.56), channel_id=1, source_target_pairs={{0,4},{1,5},{2,6},{3,7},{4,0},{5,1},{6,2},{7,3},{8,12},{9,13},{10,... | collective-permute-start | bytes 221192 | tf_op jit(solution)/shard_map/ppermute | solution.py:506
  66.3 4.4 %collective-permute-start.19 = (bf16[288,128]{1,0:T(8,128)(2,1)S(1)}, bf16[288,128]{1,0:T(8,128)(2,1)S(1)}, u32[]{:S(2)}, u32[]{:S(2)}) collective-permute-start(bf16[288,128]{1,0:T(8,128)(2,1)S(1)} %get-tuple-element.57), channel_id=1, source_target_pairs={{0,2},{1,3},{2,0},{3,1},{4,6},{5,7},{6,4},{7,5},{8,10},{9,11},{10,... | collective-permute-start | bytes 221192 | tf_op jit(solution)/shard_map/ppermute | solution.py:506
